TPU v7x, 32 devices: a whole 2x2x4 slice. The times are simulated.
32 devices in a mesh: fsdp: 4 (over y, core), ctx: 4 (over z), tp: 2 (over x).
Axes of the slice: x: 2, y: 2, z: 4, core: 2. Of those that a mesh axis runs over, the one named last changes fastest.
Arguments:
- tokens_in: bfloat16 [64, 512, 768], P('fsdp', 'ctx'), may hold values from -6 to 6
- seq_lengths: int32 [64], P('fsdp'), may hold values from 256 to 512, as said below
- query_weight: bfloat16 [768, 768], P('fsdp', 'tp'), may hold values from -0.21875 to 0.21875
- query_bias: bfloat16 [12, 64], P('tp', 'fsdp'), may hold values from -3 to 3
- key_weight: bfloat16 [768, 768], P('fsdp', 'tp'), may hold values from -0.21875 to 0.21875
- value_weight: bfloat16 [768, 768], P('fsdp', 'tp'), may hold values from -0.21875 to 0.21875
- value_bias: bfloat16 [12, 64], P('tp', 'fsdp'), may hold values from -1.1953125 to 1.1953125
- output_weight: bfloat16 [768, 768], P('tp', 'fsdp'), may hold values from -0.875 to 0.875
- output_bias: bfloat16 [768], P('fsdp'), may hold values from -3 to 3
- attn_gain: bfloat16 [768], P('fsdp'), may hold values from 0.5 to 1.5
- attn_shift: bfloat16 [768], P('fsdp'), may hold values from -2 to 2
- inner_weight: bfloat16 [768, 3072], P('fsdp', 'tp'), may hold values from -0.21875 to 0.21875
- inner_bias: bfloat16 [24, 128], P('tp', 'fsdp'), may hold values from -3 to 3
- outer_weight: bfloat16 [3072, 768], P('tp', 'fsdp'), may hold values from -0.109375 to 0.109375
- outer_bias: bfloat16 [768], P('fsdp'), may hold values from -2 to 2
- ffn_gain: bfloat16 [768], P('fsdp'), may hold values from 0.5 to 1.5
- ffn_shift: bfloat16 [768], P('fsdp'), may hold values from -2 to 2
- cotangent: bfloat16 [64, 512, 768], P('fsdp', 'ctx'), may hold values from -6 to 6
Outputs:
- layer_out: bfloat16 [64, 512, 768], P('fsdp', 'ctx')
- input_grad: float32 [64, 512, 768], P('fsdp', 'ctx')
- query_weight_grad: float32 [768, 768], P('fsdp', 'tp')
- query_bias_grad: float32 [12, 64], P('tp', 'fsdp')
- key_weight_grad: float32 [768, 768], P('fsdp', 'tp')
- value_weight_grad: float32 [768, 768], P('fsdp', 'tp')
- value_bias_grad: float32 [12, 64], P('tp', 'fsdp')
- output_weight_grad: float32 [768, 768], P('tp', 'fsdp')
- output_bias_grad: float32 [768], P('fsdp')
- attn_gain_grad: float32 [768], P('fsdp')
- attn_shift_grad: float32 [768], P('fsdp')
- inner_weight_grad: float32 [768, 3072], P('fsdp', 'tp')
- inner_bias_grad: float32 [24, 128], P('tp', 'fsdp')
- outer_weight_grad: float32 [3072, 768], P('tp', 'fsdp')
- outer_bias_grad: float32 [768], P('fsdp')
- ffn_gain_grad: float32 [768], P('fsdp')
- ffn_shift_grad: float32 [768], P('fsdp')
Inputs may be any that keep to these rules, and one draw needn't show every extreme that they name: `seq_lengths`: slots 0 to length - 1 of a sequence hold tokens, the rest padding. Some sequence has length 512 and some has length 256.
All inputs are finite; a program needn't handle non-finite values.
Results may differ from a plain program's by a relative error of at most 0.019.
Values may be sent and summed in bfloat16 or wider, within the bound.
No kernel may reach another device: no remote copies, remote signals or barrier semaphores. Data moves between devices by JAX's collectives and lax.ppermute only.
A program may use at most 256 MiB of HBM per device.

v0:
```python
from functools import partial
import math

import jax
import jax.numpy as jnp
from jax import lax
from jax.sharding import PartitionSpec as P

HD = 64


def layer_norm(values, gain_vec, offset_vec):
    centre = values - jnp.mean(values, axis=-1, keepdims=True)
    spread = jnp.mean(centre * centre, axis=-1, keepdims=True)
    return centre * lax.rsqrt(spread + 1e-12) * gain_vec + offset_vec


def matmul(left_side, right_side):
    return jnp.dot(left_side, right_side, preferred_element_type=jnp.float32)


def inner_rows(left_side, right_side):
    return lax.dot_general(
        left_side, right_side, (((0,), (0,)), ((), ())), preferred_element_type=jnp.float32
    )


def times_transposed(left_side, right_side):
    return lax.dot_general(
        left_side, right_side, (((1,), (1,)), ((), ())), preferred_element_type=jnp.float32
    )


def attention_probs(query_heads, key_heads, key_valid):
    scores = jnp.einsum(
        "sqhd,skhd->shqk", query_heads, key_heads, preferred_element_type=jnp.float32
    ) * (1.0 / math.sqrt(HD))
    masked = jnp.where(key_valid[:, None, None, :], scores, -1e30)
    largest = jnp.max(masked, axis=-1, keepdims=True)
    exponent = jnp.where(key_valid[:, None, None, :], jnp.exp(masked - largest), 0.0)
    return exponent / jnp.sum(exponent, axis=-1, keepdims=True)


def column_sums(matrix_low):
    return jnp.sum(matrix_low.astype(jnp.float32), axis=0)


def per_device(
    tokens_in,
    seq_lengths,
    query_weight,
    query_bias,
    key_weight,
    value_weight,
    value_bias,
    output_weight,
    output_bias,
    attn_gain,
    attn_shift,
    inner_weight,
    inner_bias,
    outer_weight,
    outer_bias,
    ffn_gain,
    ffn_shift,
    cotangent,
):
    (
        query_full,
        query_offset,
        key_full,
        value_full,
        value_offset,
        output_full,
        output_offset,
        attn_scale,
        attn_offset,
        inner_full,
        inner_offset,
        outer_full,
        outer_offset,
        ffn_scale,
        ffn_offset,
    ) = (
        lax.all_gather(query_weight, "fsdp", axis=0, tiled=True),
        lax.all_gather(query_bias, "fsdp", axis=1, tiled=True),
        lax.all_gather(key_weight, "fsdp", axis=0, tiled=True),
        lax.all_gather(value_weight, "fsdp", axis=0, tiled=True),
        lax.all_gather(value_bias, "fsdp", axis=1, tiled=True),
        lax.all_gather(output_weight, "fsdp", axis=1, tiled=True),
        lax.all_gather(output_bias, "fsdp", axis=0, tiled=True),
        lax.all_gather(attn_gain, "fsdp", axis=0, tiled=True),
        lax.all_gather(attn_shift, "fsdp", axis=0, tiled=True),
        lax.all_gather(inner_weight, "fsdp", axis=0, tiled=True),
        lax.all_gather(inner_bias, "fsdp", axis=1, tiled=True),
        lax.all_gather(outer_weight, "fsdp", axis=1, tiled=True),
        lax.all_gather(outer_bias, "fsdp", axis=0, tiled=True),
        lax.all_gather(ffn_gain, "fsdp", axis=0, tiled=True),
        lax.all_gather(ffn_shift, "fsdp", axis=0, tiled=True),
    )
    ctx_count = lax.axis_size("ctx")
    tokens_here, cotangent_here = (tokens_in, cotangent)
    seq_count = tokens_here.shape[0]
    first_slot = lax.axis_index("ctx") * tokens_here.shape[1]
    seq_total = tokens_here.shape[1] * ctx_count
    span_len = tokens_here.shape[1]
    model_width = tokens_here.shape[2]
    token_count = seq_count * span_len
    head_cols = query_full.shape[1]
    head_count = head_cols // HD
    slot_index = jnp.arange(seq_total, dtype=jnp.int32)
    key_valid = slot_index[None, :] < seq_lengths[:, None]
    local_valid = lax.dynamic_slice_in_dim(key_valid, first_slot, span_len, 1)
    row_keep = local_valid.astype(jnp.float32).reshape(token_count, 1)
    token_rows = tokens_here.reshape(token_count, model_width)
    scale_factor = 1.0 / math.sqrt(HD)
    queries = (
        matmul(token_rows, query_full) + query_offset.astype(jnp.float32).reshape(-1)
    ).astype(jnp.bfloat16)
    keys_local = (
        matmul(token_rows, key_full).astype(jnp.bfloat16).reshape(seq_count, span_len, head_cols)
    )
    values_local = (
        (matmul(token_rows, value_full) + value_offset.astype(jnp.float32).reshape(-1))
        .astype(jnp.bfloat16)
        .reshape(seq_count, span_len, head_cols)
    )
    key_whole, value_whole = (
        lax.all_gather(keys_local, "ctx", axis=1, tiled=True),
        lax.all_gather(values_local, "ctx", axis=1, tiled=True),
    )
    split_heads = (seq_count, seq_total, head_count, HD)
    query_heads = queries.reshape(seq_count, span_len, head_count, HD)
    attention = attention_probs(query_heads, key_whole.reshape(split_heads), key_valid)
    attention_low = attention.astype(jnp.bfloat16)
    mixed_heads = jnp.einsum(
        "shqk,skhd->sqhd",
        attention_low,
        value_whole.reshape(split_heads),
        preferred_element_type=jnp.float32,
    )
    mixed_low = mixed_heads.astype(jnp.bfloat16).reshape(token_count, head_cols)
    attn_out = lax.psum(matmul(mixed_low, output_full), "tp") + output_offset.astype(jnp.float32)
    before_first = token_rows.astype(jnp.float32) + attn_out
    normed = layer_norm(
        before_first, attn_scale.astype(jnp.float32), attn_offset.astype(jnp.float32)
    )
    normed_low = normed.astype(jnp.bfloat16)
    inner_pre = matmul(normed_low, inner_full) + inner_offset.astype(jnp.float32).reshape(-1)
    active_low = jax.nn.gelu(inner_pre, approximate=True).astype(jnp.bfloat16)
    outer_out = lax.psum(matmul(active_low, outer_full), "tp") + outer_offset.astype(jnp.float32)
    before_second = normed + outer_out
    layer_rows = (
        layer_norm(before_second, ffn_scale.astype(jnp.float32), ffn_offset.astype(jnp.float32))
        * row_keep
    )
    layer_out = layer_rows.astype(jnp.bfloat16).reshape(seq_count, span_len, model_width)
    (
        query_back,
        key_back,
        value_back,
        output_back,
        attn_scale_back,
        inner_back,
        outer_back,
        ffn_scale_back,
    ) = (
        lax.all_gather(query_weight, "fsdp", axis=0, tiled=True),
        lax.all_gather(key_weight, "fsdp", axis=0, tiled=True),
        lax.all_gather(value_weight, "fsdp", axis=0, tiled=True),
        lax.all_gather(output_weight, "fsdp", axis=1, tiled=True),
        lax.all_gather(attn_gain, "fsdp", axis=0, tiled=True),
        lax.all_gather(inner_weight, "fsdp", axis=0, tiled=True),
        lax.all_gather(outer_weight, "fsdp", axis=1, tiled=True),
        lax.all_gather(ffn_gain, "fsdp", axis=0, tiled=True),
    )
    out_grad = cotangent_here.reshape(token_count, model_width).astype(jnp.float32) * row_keep
    unused_second, second_pull = jax.vjp(
        layer_norm,
        before_second,
        ffn_scale_back.astype(jnp.float32),
        ffn_offset.astype(jnp.float32),
    )
    second_grad, ffn_gain_part, ffn_shift_part = second_pull(out_grad)
    outer_grad_low = second_grad.astype(jnp.bfloat16)
    outer_bias_part = column_sums(outer_grad_low)
    outer_weight_part = inner_rows(active_low, outer_grad_low)
    active_grad = times_transposed(outer_grad_low, outer_back)
    unused_gelu, gelu_pull = jax.vjp(partial(jax.nn.gelu, approximate=True), inner_pre)
    (inner_grad,) = gelu_pull(active_grad)
    inner_grad_low = inner_grad.astype(jnp.bfloat16)
    inner_bias_part = column_sums(inner_grad_low).reshape(inner_offset.shape)
    inner_weight_part = inner_rows(normed_low, inner_grad_low)
    normed_grad = lax.psum(times_transposed(inner_grad_low, inner_back), "tp") + second_grad
    unused_first, first_pull = jax.vjp(
        layer_norm,
        before_first,
        attn_scale_back.astype(jnp.float32),
        attn_offset.astype(jnp.float32),
    )
    first_grad, attn_gain_part, attn_shift_part = first_pull(normed_grad)
    attn_grad_low = first_grad.astype(jnp.bfloat16)
    output_bias_part = column_sums(attn_grad_low)
    output_weight_part = inner_rows(mixed_low, attn_grad_low)
    mixed_grad = (
        times_transposed(attn_grad_low, output_back)
        .astype(jnp.bfloat16)
        .reshape(seq_count, span_len, head_count, HD)
    )
    key_again, value_again = (key_whole, value_whole)
    key_heads = key_again.reshape(split_heads)
    value_heads = value_again.reshape(split_heads)
    attention_again = attention_probs(query_heads, key_heads, key_valid)
    attention_grad = jnp.einsum(
        "sqhd,skhd->shqk", mixed_grad, value_heads, preferred_element_type=jnp.float32
    )
    row_dot = jnp.sum(attention_again * attention_grad, axis=-1, keepdims=True)
    score_grad = (attention_again * (attention_grad - row_dot)).astype(jnp.bfloat16)
    query_grad = (
        (
            jnp.einsum("shqk,skhd->sqhd", score_grad, key_heads, preferred_element_type=jnp.float32)
            * scale_factor
        )
        .astype(jnp.bfloat16)
        .reshape(token_count, head_cols)
    )
    key_part = (
        jnp.einsum("shqk,sqhd->skhd", score_grad, query_heads, preferred_element_type=jnp.float32)
        * scale_factor
    )
    value_part = jnp.einsum(
        "shqk,sqhd->skhd",
        attention_again.astype(jnp.bfloat16),
        mixed_grad,
        preferred_element_type=jnp.float32,
    )
    key_sums, value_sums = (
        lax.psum_scatter(
            key_part.reshape(seq_count, seq_total, head_cols),
            "ctx",
            scatter_dimension=1,
            tiled=True,
        ),
        lax.psum_scatter(
            value_part.reshape(seq_count, seq_total, head_cols),
            "ctx",
            scatter_dimension=1,
            tiled=True,
        ),
    )
    key_grad_low = key_sums.reshape(token_count, head_cols).astype(jnp.bfloat16)
    value_grad_low = value_sums.reshape(token_count, head_cols).astype(jnp.bfloat16)
    query_weight_part = inner_rows(token_rows, query_grad)
    query_bias_part = column_sums(query_grad).reshape(head_count, HD)
    key_weight_part = inner_rows(token_rows, key_grad_low)
    value_weight_part = inner_rows(token_rows, value_grad_low)
    value_bias_part = column_sums(value_grad_low).reshape(head_count, HD)
    input_part = (
        times_transposed(query_grad, query_back)
        + times_transposed(key_grad_low, key_back)
        + times_transposed(value_grad_low, value_back)
    )
    input_grad = (
        lax.psum(input_part.astype(jnp.bfloat16), "tp").astype(jnp.float32) + first_grad
    ).reshape(seq_count, span_len, model_width)
    shard_sums = (
        lax.psum_scatter(
            query_weight_part.astype(jnp.bfloat16), "fsdp", scatter_dimension=0, tiled=True
        ).astype(jnp.float32),
        lax.psum_scatter(
            query_bias_part.astype(jnp.bfloat16), "fsdp", scatter_dimension=1, tiled=True
        ).astype(jnp.float32),
        lax.psum_scatter(
            key_weight_part.astype(jnp.bfloat16), "fsdp", scatter_dimension=0, tiled=True
        ).astype(jnp.float32),
        lax.psum_scatter(
            value_weight_part.astype(jnp.bfloat16), "fsdp", scatter_dimension=0, tiled=True
        ).astype(jnp.float32),
        lax.psum_scatter(
            value_bias_part.astype(jnp.bfloat16), "fsdp", scatter_dimension=1, tiled=True
        ).astype(jnp.float32),
        lax.psum_scatter(
            output_weight_part.astype(jnp.bfloat16), "fsdp", scatter_dimension=1, tiled=True
        ).astype(jnp.float32),
        lax.psum_scatter(
            output_bias_part.astype(jnp.bfloat16), "fsdp", scatter_dimension=0, tiled=True
        ).astype(jnp.float32),
        lax.psum_scatter(
            attn_gain_part.astype(jnp.bfloat16), "fsdp", scatter_dimension=0, tiled=True
        ).astype(jnp.float32),
        lax.psum_scatter(
            attn_shift_part.astype(jnp.bfloat16), "fsdp", scatter_dimension=0, tiled=True
        ).astype(jnp.float32),
        lax.psum_scatter(
            inner_weight_part.astype(jnp.bfloat16), "fsdp", scatter_dimension=0, tiled=True
        ).astype(jnp.float32),
        lax.psum_scatter(
            inner_bias_part.astype(jnp.bfloat16), "fsdp", scatter_dimension=1, tiled=True
        ).astype(jnp.float32),
        lax.psum_scatter(
            outer_weight_part.astype(jnp.bfloat16), "fsdp", scatter_dimension=1, tiled=True
        ).astype(jnp.float32),
        lax.psum_scatter(
            outer_bias_part.astype(jnp.bfloat16), "fsdp", scatter_dimension=0, tiled=True
        ).astype(jnp.float32),
        lax.psum_scatter(
            ffn_gain_part.astype(jnp.bfloat16), "fsdp", scatter_dimension=0, tiled=True
        ).astype(jnp.float32),
        lax.psum_scatter(
            ffn_shift_part.astype(jnp.bfloat16), "fsdp", scatter_dimension=0, tiled=True
        ).astype(jnp.float32),
    )
    group_sums = (
        lax.psum(shard_sums[0].astype(jnp.bfloat16), "ctx").astype(jnp.float32),
        lax.psum(shard_sums[1].astype(jnp.bfloat16), "ctx").astype(jnp.float32),
        lax.psum(shard_sums[2].astype(jnp.bfloat16), "ctx").astype(jnp.float32),
        lax.psum(shard_sums[3].astype(jnp.bfloat16), "ctx").astype(jnp.float32),
        lax.psum(shard_sums[4].astype(jnp.bfloat16), "ctx").astype(jnp.float32),
        lax.psum(shard_sums[5].astype(jnp.bfloat16), "ctx").astype(jnp.float32),
        lax.psum(shard_sums[6].astype(jnp.bfloat16), "ctx").astype(jnp.float32),
        lax.psum(shard_sums[7].astype(jnp.bfloat16), "ctx").astype(jnp.float32),
        lax.psum(shard_sums[8].astype(jnp.bfloat16), "ctx").astype(jnp.float32),
        lax.psum(shard_sums[9].astype(jnp.bfloat16), "ctx").astype(jnp.float32),
        lax.psum(shard_sums[10].astype(jnp.bfloat16), "ctx").astype(jnp.float32),
        lax.psum(shard_sums[11].astype(jnp.bfloat16), "ctx").astype(jnp.float32),
        lax.psum(shard_sums[12].astype(jnp.bfloat16), "ctx").astype(jnp.float32),
        lax.psum(shard_sums[13].astype(jnp.bfloat16), "ctx").astype(jnp.float32),
        lax.psum(shard_sums[14].astype(jnp.bfloat16), "ctx").astype(jnp.float32),
    )
    return (layer_out, input_grad) + tuple(group_sums)


def solution(mesh):
    return jax.shard_map(
        per_device,
        mesh=mesh,
        in_specs=(
            P("fsdp", "ctx", None),
            P("fsdp"),
            P("fsdp", "tp"),
            P("tp", "fsdp"),
            P("fsdp", "tp"),
            P("fsdp", "tp"),
            P("tp", "fsdp"),
            P("tp", "fsdp"),
            P("fsdp"),
            P("fsdp"),
            P("fsdp"),
            P("fsdp", "tp"),
            P("tp", "fsdp"),
            P("tp", "fsdp"),
            P("fsdp"),
            P("fsdp"),
            P("fsdp"),
            P("fsdp", "ctx", None),
        ),
        out_specs=(
            P("fsdp", "ctx", None),
            P("fsdp", "ctx", None),
            P("fsdp", "tp"),
            P("tp", "fsdp"),
            P("fsdp", "tp"),
            P("fsdp", "tp"),
            P("tp", "fsdp"),
            P("tp", "fsdp"),
            P("fsdp"),
            P("fsdp"),
            P("fsdp"),
            P("fsdp", "tp"),
            P("tp", "fsdp"),
            P("tp", "fsdp"),
            P("fsdp"),
            P("fsdp"),
            P("fsdp"),
        ),
        check_vma=False,
    )
```

profile of v0, /device:TPU:0, one launch (start us, length us, event | category | flops | bytes accessed | tf_op | source)
XLA Modules:
  0.0 1717.9 jit_solution(829029017729778975)
XLA Ops:
  8.1 9.4 all_gather.64
  18.3 4.8 convolution_convert_fusion.3
  23.2 5.2 all-gather
  28.6 7.6 all_gather.59
  37.0 3.0 add_convert_fusion.4
  40.1 5.2 all-gather.1
  45.4 7.6 all_gather.62
  53.9 3.0 add_convert_fusion.3
  59.0 8.2 all_gather.66
  67.2 72.2 %all-gather.10.cloned.1.call-done = bf16[16,512,384]{2,1,0:T(8,128)(2,1)} async-done(((bf16[16,128,384]{2,1,0:T(8,128)(2,1)}), bf16[16,512,384]{2,1,0:T(8,128)(2,1)}) %all-gather.10.cloned.1.call-update) | async-done | bytes 6291472 | tf_op jit(solution)/shard_map/all_gather | solution.py:129
  139.5 8.8 copy.68
  148.2 16.9 fusion.79
  165.1 90.0 %all-gather.8.cloned.1.call-done = bf16[16,512,384]{2,1,0:T(8,128)(2,1)} async-done(((bf16[16,128,384]{2,1,0:T(8,128)(2,1)}), bf16[16,512,384]{2,1,0:T(8,128)(2,1)}) %all-gather.8.cloned.1.call-update) | async-done | bytes 6291472 | tf_op jit(solution)/shard_map/all_gather | solution.py:130
  255.1 8.6 copy.65
  263.7 12.4 fusion.31
  278.4 4.7 fusion.29
  287.0 12.2 all-reduce.15
  299.3 5.4 all-gather.2
  304.8 130.0 %all-reduce.22.cloned.1.call-done = f32[2048,768]{1,0:T(8,128)} async-done(((f32[2048,768]{1,0:T(8,128)}), f32[2048,768]{1,0:T(8,128)}) %all-reduce.22.cloned.1.call-update) | async-done | bytes 6291472 | tf_op jit(solution)/shard_map/psum | solution.py:143
  434.8 3.7 fusion.77
  442.1 13.9 multiply_convert_fusion.1
  455.9 9.5 fusion.86
  466.4 152.5 %all-reduce.24.cloned.1.call-done = f32[2048,768]{1,0:T(8,128)} async-done(((f32[2048,768]{1,0:T(8,128)}), f32[2048,768]{1,0:T(8,128)}) %all-reduce.24.cloned.1.call-update) | async-done | bytes 6291472 | tf_op jit(solution)/shard_map/psum | solution.py:151
  618.9 5.7 fusion.76
  625.5 3.3 copy-done.5
  628.8 3.2 multiply_reduce_fusion.2
  632.1 3.3 fusion.75
  635.5 2.9 copy-done.4
  639.6 15.8 fusion.85
  658.1 7.0 fusion.87
  665.5 153.0 %all-reduce.26.cloned.1.call-done = f32[2048,768]{1,0:T(8,128)} async-done(((f32[2048,768]{1,0:T(8,128)}), f32[2048,768]{1,0:T(8,128)}) %all-reduce.26.cloned.1.call-update) | async-done | bytes 6291472 | tf_op jit(solution)/shard_map/psum | solution.py:194
  818.5 8.6 multiply_reduce_fusion.3
  827.2 4.2 fusion.74
  839.9 14.4 fusion.12
  854.3 12.6 copy.78
  866.9 22.3 %multiply_reduce_fusion = (f32[16,6,128]{2,1,0:T(8,128)S(1)}, f32[16,6,128,512]{3,2,1,0:T(8,128)}) fusion(f32[16,6,128,512]{3,2,1,0:T(8,128)} %get-tuple-element.120, f32[16,6,128]{2,1,0:T(8,128)S(1)} %get-tuple-element.119, bf16[16,512,6,64]{1,3,2,0:T(8,128)(2,1)} %bitcast.169, bf16[16,128,6,64]{1,0,3,2:T(8,128)(2,1)S(1)} %bitcast.180), kind=kOutput, calls=%fused_computation.2 | convolution fusion | flops 824168448 | bytes 58294272 | tf_op jit(solution)/shard_map/sqhd,skhd->shqk/dot_general | solution.py:214
  889.3 16.8 multiply_convert_fusion
  906.0 6.0 broadcast_multiply_fusion
  914.4 12.7 copy.76
  927.4 10.9 fusion.84
  939.3 3.3 fusion.50
  943.7 135.2 %reduce-scatter.26.cloned.1.call-done = f32[16,128,384]{2,1,0:T(8,128)} async-done(((f32[16,512,384]{2,1,0:T(8,128)}), f32[16,128,384]{2,1,0:T(8,128)}) %reduce-scatter.26.cloned.1.call-update) | async-done | bytes 3145744 | tf_op jit(solution)/shard_map/reduce_scatter | solution.py:244
  1082.5 3.3 fusion.53
  1087.0 207.3 %reduce-scatter.24.cloned.1.call-done = f32[16,128,384]{2,1,0:T(8,128)} async-done(((f32[16,512,384]{2,1,0:T(8,128)}), f32[16,128,384]{2,1,0:T(8,128)}) %reduce-scatter.24.cloned.1.call-update) | async-done | bytes 3145744 | tf_op jit(solution)/shard_map/reduce_scatter | solution.py:238
  1297.5 3.3 fusion.54
  1302.0 9.8 convolution_convert_fusion
  1312.2 12.1 convolution_convert_fusion.1
  1324.4 4.5 fusion.44
  1333.2 11.8 reduce-scatter.40.cloned.1.call-done
  1346.7 22.7 %reduce-scatter.38.cloned.1.call-done = bf16[192,384]{1,0:T(8,128)(2,1)} async-done(((bf16[768,384]{1,0:T(8,128)(2,1)}), bf16[192,384]{1,0:T(8,128)(2,1)}) %reduce-scatter.38.cloned.1.call-update) | async-done | bytes 147472
  1371.2 33.7 %reduce-scatter.32.cloned.1.call-done = bf16[1536,192]{0,1:T(8,128)(2,1)} async-done(((bf16[1536,768]{0,1:T(8,128)(2,1)}), bf16[1536,192]{0,1:T(8,128)(2,1)}) %reduce-scatter.32.cloned.1.call-update) | async-done | bytes 589840 | tf_op jit(solution)/shard_map/reduce_scatter | solution.py:300
  1404.8 35.8 %reduce-scatter.30.cloned.1.call-done = bf16[192,1536]{1,0:T(8,128)(2,1)} async-done(((bf16[768,1536]{1,0:T(8,128)(2,1)}), bf16[192,1536]{1,0:T(8,128)(2,1)}) %reduce-scatter.30.cloned.1.call-update) | async-done | bytes 589840 | tf_op jit(solution)/shard_map/reduce_scatter | solution.py:294
  1440.7 24.6 %reduce-scatter.28.cloned.1.call-done = bf16[384,192]{0,1:T(8,128)(2,1)} async-done(((bf16[384,768]{0,1:T(8,128)(2,1)}), bf16[384,192]{0,1:T(8,128)(2,1)}) %reduce-scatter.28.cloned.1.call-update) | async-done | bytes 147472 | tf_op jit(solution)/shard_map/reduce_scatter | solution.py:282
  1465.6 3.2 fusion.25
  1470.7 3.6 add_convert_fusion
  1476.0 11.6 reduce-scatter.44.cloned.1.call-done
  1488.4 10.1 all-reduce.14
  1499.1 4.7 multiply_convert_fusion.2
  1503.8 5.7 reduce-scatter.36.cloned.1.call-done
  1510.2 21.0 %reduce-scatter.42.cloned.1.call-done = bf16[16,6]{1,0:T(8,128)(2,1)} async-done(((bf16[64,6]{1,0:T(8,128)(2,1)}), bf16[16,6]{1,0:T(8,128)(2,1)}) %reduce-scatter.42.cloned.1.call-update) | async-done | bytes 208
  1532.0 19.6 %all-reduce.12 = (bf16[6,16]{1,0:T(8,128)(2,1)S(1)}, bf16[6,16]{1,0:T(8,128)(2,1)S(1)}, bf16[192]{0:T(256)(128)(2,1)S(1)}, bf16[192]{0:T(256)(128)(2,1)S(1)}, bf...) all-reduce(bf16[6,16]{1,0:T(8,128)(2,1)S(1)} %copy.89, ...), channel_id=1, replica_groups=mesh['fsdp'=4,'ctx'=4,'tp'=2] {'ctx'}, use_global_device_ids=true, to_apply=%region_21.22 | all-reduce | flops 1728 | bytes 6912 | tf_op jit(solution)/shard_map/psum | solution.py:315
  1556.8 58.7 %all-reduce.30.cloned.1.call-done = (bf16[192,384]{0,1:T(8,128)(2,1)}, bf16[192,384]{0,1:T(8,128)(2,1)}, bf16[192,384]{0,1:T(8,128)(2,1)}, bf16[384,192]{0,1:T(8...) async-done(((bf16[192,384]{0,1:T(8,128)(2,1)}, bf16[192,384]{0,1:T(8,128)(2,1)}, bf16[192,384]{0,1:T(8,128)(2,1)}, bf16[384,192]{0,1:T(8,128)(2,1)}, ...) | async-done | bytes 1769488 | tf_op jit(solution)/shard_map/psum | solution.py:314
  1627.1 76.0 %all-reduce.28.cloned.1.call-done = bf16[2048,768]{1,0:T(8,128)(2,1)} async-done(((bf16[2048,768]{1,0:T(8,128)(2,1)}), bf16[2048,768]{1,0:T(8,128)(2,1)}) %all-reduce.28.cloned.1.call-update) | async-done | bytes 3145744 | tf_op jit(solution)/shard_map/psum | solution.py:264
  1703.1 7.1 convert_add_fusion
  (263 shorter events, 73.3 us)
Async XLA Ops:
  8.0 29.0 %copy-start.17 = (bf16[16,128,768]{2,1,0:T(8,128)(2,1)S(1)}, bf16[16,128,768]{2,1,0:T(8,128)(2,1)}, u32[]{:S(2)}) copy-start(bf16[16,128,768]{2,1,0:T(8,128)(2,1)} %param.18) | copy-start | bytes 9437188
  8.0 15.2 copy-start.55
  8.0 20.5 %copy-start.30 = (bf16[192,384]{1,0:T(8,128)(2,1)S(1)}, bf16[192,384]{1,0:T(8,128)(2,1)}, u32[]{:S(2)}) copy-start(bf16[192,384]{1,0:T(8,128)(2,1)} %param.23) | copy-start | bytes 442372
  8.1 131.4 %all-gather.10.cloned.1.call-start = ((), (), s32[]{:S(2)}) async-start(), calls=%async_computation.12 | async-start | bytes 7864320 | tf_op jit(solution)/shard_map/all_gather | solution.py:129
  23.2 232.0 %all-gather.8.cloned.1.call-start = ((), (), s32[]{:S(2)}) async-start(), calls=%async_computation.11 | async-start | bytes 7864320 | tf_op jit(solution)/shard_map/all_gather | solution.py:130
  37.0 8.4 copy-start.31
  40.0 394.7 %all-reduce.22.cloned.1.call-start = ((), (), s32[]{:S(2)}) async-start(), calls=%async_computation.13 | async-start | bytes 12582912 | tf_op jit(solution)/shard_map/psum | solution.py:143
  53.9 5.1 copy-start.32
  56.8 10.3 copy-start.58
  59.0 89.3 %copy-start.11 = (bf16[48,8,16,128]{3,2,1,0:T(8,128)(2,1)}, bf16[48,8,16,128]{3,2,1,0:T(8,128)(2,1)S(1)}, u32[]{:S(2)}) copy-start(bf16[48,8,16,128]{3,2,1,0:T(8,128)(2,1)S(1)} %copy.98) | copy-start | bytes 4718596
  67.2 210.0 %copy-start.24 = (bf16[384,768]{0,1:T(8,128)(2,1)}, bf16[384,768]{0,1:T(8,128)(2,1)S(1)}, u32[]{:S(2)}) copy-start(bf16[384,768]{0,1:T(8,128)(2,1)S(1)} %all_gather.66) | copy-start | bytes 1769476
  283.1 16.2 copy-start.53
  283.1 151.6 %copy-start.18 = (bf16[16,128,768]{2,1,0:T(8,128)(2,1)S(1)}, bf16[16,128,768]{2,1,0:T(8,128)(2,1)}, u32[]{:S(2)}) copy-start(bf16[16,128,768]{2,1,0:T(8,128)(2,1)} %param.18) | copy-start | bytes 9437188
  283.2 158.9 %all-gather.12.cloned.1.call-start = ((), (), s32[]{:S(2)}) async-start(), calls=%async_computation.14 | async-start | bytes 2949120 | tf_op jit(solution)/shard_map/all_gather | solution.py:94
  283.7 172.2 %all-gather.14.cloned.1.call-start = ((), (), s32[]{:S(2)}) async-start(), calls=%async_computation.15 | async-start | bytes 2949120 | tf_op jit(solution)/shard_map/all_gather | solution.py:96
  284.3 334.6 %all-reduce.24.cloned.1.call-start = ((), (), s32[]{:S(2)}) async-start(), calls=%async_computation.16 | async-start | bytes 12582912 | tf_op jit(solution)/shard_map/psum | solution.py:151
  299.3 527.9 %copy-start.43 = (f32[768]{0:T(1024)}, f32[768]{0:T(1024)S(1)}, u32[]{:S(2)}) copy-start(f32[768]{0:T(1024)S(1)} %convert_element_type.248) | copy-start | bytes 9220
  299.3 319.6 %copy-start.46 = (f32[768]{0:T(1024)}, f32[768]{0:T(1024)S(1)}, u32[]{:S(2)}) copy-start(f32[768]{0:T(1024)S(1)} %convert_element_type.249) | copy-start | bytes 9220
  438.5 388.7 %copy-start.28 = (f32[2048]{0:T(1024)}, f32[2048]{0:T(1024)S(1)}, u32[]{:S(2)}) copy-start(f32[2048]{0:T(1024)S(1)} %broadcast_multiply_fusion.2) | copy-start | bytes 24580
  442.0 385.1 %copy-start.37 = (f32[2048]{0:T(1024)}, f32[2048]{0:T(1024)S(1)}, u32[]{:S(2)}) copy-start(f32[2048]{0:T(1024)S(1)} %fusion.63) | copy-start | bytes 24580
  465.5 353.0 %all-reduce.26.cloned.1.call-start = ((), (), s32[]{:S(2)}) async-start(), calls=%async_computation.17 | async-start | bytes 12582912 | tf_op jit(solution)/shard_map/psum | solution.py:194
  465.8 166.3 %copy-start.41 = (f32[768]{0:T(1024)}, f32[768]{0:T(1024)S(1)}, u32[]{:S(2)}) copy-start(f32[768]{0:T(1024)S(1)} %convert_element_type.253) | copy-start | bytes 9220
  466.4 165.6 %copy-start.33 = (f32[2048]{0:T(1024)}, f32[2048]{0:T(1024)S(1)}, u32[]{:S(2)}) copy-start(f32[2048]{0:T(1024)S(1)} %get-tuple-element.116) | copy-start | bytes 24580
  624.6 7.4 copy-start
  624.6 4.2 copy-start.5
  624.6 7.4 copy-start.26
  625.5 9.9 copy-start.35
  639.6 15.8 copy-start.15
  639.6 18.5 %copy-start.59 = (bf16[768,1536]{1,0:T(8,128)(2,1)S(1)}, bf16[768,1536]{1,0:T(8,128)(2,1)}, u32[]{:S(2)}) copy-start(bf16[768,1536]{1,0:T(8,128)(2,1)} %all-gather.12.cloned.1.call-done) | copy-start | bytes 7077892
  665.1 413.9 %reduce-scatter.26.cloned.1.call-start = ((), (), s32[]{:S(2)}) async-start(), calls=%async_computation.19 | async-start | bytes 15728640 | tf_op jit(solution)/shard_map/reduce_scatter | solution.py:244
  831.4 5.5 copy-start.25
  866.9 427.4 %reduce-scatter.24.cloned.1.call-start = ((), (), s32[]{:S(2)}) async-start(), calls=%async_computation.18 | async-start | bytes 15728640 | tf_op jit(solution)/shard_map/reduce_scatter | solution.py:238
  889.3 16.8 copy-start.12
  906.0 8.4 copy-start.2
  927.1 404.3 %reduce-scatter.34.cloned.1.call-start = ((), (), s32[]{:S(2)}) async-start(), calls=%async_computation.24 | async-start | bytes 737280
  943.7 401.3 %reduce-scatter.40.cloned.1.call-start = ((), (), s32[]{:S(2)}) async-start(), calls=%async_computation.27 | async-start | bytes 737280
  1086.9 282.5 %reduce-scatter.38.cloned.1.call-start = ((), (), s32[]{:S(2)}) async-start(), calls=%async_computation.26 | async-start | bytes 737280
  1301.9 10.2 copy-start.29
  1302.0 10.2 copy-start.38
  1302.0 10.2 copy-start.44
  1302.0 10.2 copy-start.47
  1302.0 102.8 %reduce-scatter.32.cloned.1.call-start = ((), (), s32[]{:S(2)}) async-start(), calls=%async_computation.23 | async-start | bytes 2949120 | tf_op jit(solution)/shard_map/reduce_scatter | solution.py:300
  1311.8 12.5 copy-start.8
  1311.8 128.8 %reduce-scatter.30.cloned.1.call-start = ((), (), s32[]{:S(2)}) async-start(), calls=%async_computation.22 | async-start | bytes 2949120 | tf_op jit(solution)/shard_map/reduce_scatter | solution.py:294
  1324.3 4.7 copy-start.54
  1324.3 140.9 %reduce-scatter.28.cloned.1.call-start = ((), (), s32[]{:S(2)}) async-start(), calls=%async_computation.21 | async-start | bytes 737280 | tf_op jit(solution)/shard_map/reduce_scatter | solution.py:282
  1329.0 158.7 %reduce-scatter.44.cloned.1.call-start = ((), (), s32[]{:S(2)}) async-start(), calls=%async_computation.29 | async-start | bytes 40960
  1329.8 179.7 %reduce-scatter.36.cloned.1.call-start = ((), (), s32[]{:S(2)}) async-start(), calls=%async_computation.25 | async-start | bytes 20480
  1330.5 200.7 %reduce-scatter.42.cloned.1.call-start = ((), (), s32[]{:S(2)}) async-start(), calls=%async_computation.28 | async-start | bytes 20480
  1331.4 284.2 %all-reduce.30.cloned.1.call-start = ((), (), s32[]{:S(2)}) async-start(), calls=%async_computation.30 | async-start | bytes 3833856 | tf_op jit(solution)/shard_map/psum | solution.py:314
  1465.3 237.8 %all-reduce.28.cloned.1.call-start = ((), (), s32[]{:S(2)}) async-start(), calls=%async_computation.20 | async-start | bytes 6291456 | tf_op jit(solution)/shard_map/psum | solution.py:264
  1470.6 4.4 copy-start.66
  1470.7 4.6 copy-start.6
  1470.7 4.6 copy-start.45
  1474.3 14.1 copy-start.48
  1474.3 14.1 copy-start.49
  1474.3 14.1 copy-start.50
  1474.3 14.1 copy-start.51
  1474.3 14.1 copy-start.52
  1474.3 24.7 %copy-start.27 = (f32[2048]{0:T(1024)S(1)}, f32[2048]{0:T(1024)}, u32[]{:S(2)}) copy-start(f32[2048]{0:T(1024)} %copy-done.26) | copy-start | bytes 24580
  1474.3 24.7 %copy-start.34 = (f32[2048]{0:T(1024)S(1)}, f32[2048]{0:T(1024)}, u32[]{:S(2)}) copy-start(f32[2048]{0:T(1024)} %copy-done.33) | copy-start | bytes 24580
  1474.3 24.7 %copy-start.36 = (f32[2048]{0:T(1024)S(1)}, f32[2048]{0:T(1024)}, u32[]{:S(2)}) copy-start(f32[2048]{0:T(1024)} %copy-done.35) | copy-start | bytes 24580
  1474.4 24.7 %copy-start.42 = (f32[768]{0:T(1024)S(1)}, f32[768]{0:T(1024)}, u32[]{:S(2)}) copy-start(f32[768]{0:T(1024)} %copy-done.41) | copy-start | bytes 9220
  1499.1 204.0 %copy-start.40 = (f32[2048]{0:T(1024)S(1)}, f32[2048]{0:T(1024)}, u32[]{:S(2)}) copy-start(f32[2048]{0:T(1024)} %copy-done.39) | copy-start | bytes 24580
  (24 other events, 57.7 us)
Sparse Core Ops, SparseCore 0:
  23.3 116.1 all-gather.9
  141.6 113.4 all-gather.7
  283.3 151.4 all-reduce.21
  465.6 153.2 all-reduce.23
  665.2 153.2 all-reduce.25
  867.0 211.8 reduce-scatter.25
  1081.3 212.8 reduce-scatter.23
  1297.3 23.0 reduce-scatter.33
  1322.9 22.0 reduce-scatter.39
  1347.4 22.0 reduce-scatter.37
  1372.0 32.8 reduce-scatter.31
  1407.8 32.8 reduce-scatter.29
  1443.2 22.0 reduce-scatter.27
  1468.1 19.5 reduce-scatter.43
  1489.9 19.5 reduce-scatter.35
  1511.7 19.4 reduce-scatter.41
  1534.5 80.9 all-reduce.29
  1618.3 84.7 all-reduce.27
Sparse Core Ops, SparseCore 1:
  285.2 22.4 all-gather.11
  309.1 23.8 all-gather.13
where the time goes:
time: 1720 us
  waiting for transfers between devices  1240 us (72%)
  matrix products  191 us (11%)
  local copies, waits for them, and re-layouts  93.4 us (5%)
  blocking collectives  90.6 us (5%)
  other arithmetic  78.8 us (5%)
  between operations  18.3 us (1%)
    reduce_scatter x1, waiting for transfers between devices, per_device(): lax.psum_scatter(key_part.reshape(seq_count, seq_total, head_cols), 'ctx'...  207 us
    psum x1, waiting for transfers between devices, per_device(): lax.psum(times_transposed(inner_grad_low, inner_back), 'tp') + second_grad  153 us
    psum x1, waiting for transfers between devices, per_device(): lax.psum(matmul(active_low, outer_full), 'tp')  152 us
    reduce_scatter x1, waiting for transfers between devices, per_device(): lax.psum_scatter(value_part.reshape(seq_count, seq_total, head_cols), 'ct...  135 us
    psum x1, waiting for transfers between devices, per_device(): lax.psum(matmul(mixed_low, output_full), 'tp')  130 us
    all_gather x1, waiting for transfers between devices, per_device(): lax.all_gather(values_local, 'ctx', axis=1, tiled=True)  90 us
    psum x1, waiting for transfers between devices, per_device(): lax.psum(input_part.astype(jnp.bfloat16), 'tp').astype(jnp.float32)  76 us
    unnamed x26, waiting for transfers between devices  74.3 us
  transfers between devices with their start and end apart: 20, of which 17 were waited for; matrix products, arithmetic and copies ran while one was open for 12% of the time, Pallas kernels for 0%

commit v1 on v0

v1 whole, which is shorter than its diff:
```python
import functools
import math

import jax
import jax.numpy as jnp
from jax import lax
from jax.experimental import pallas as pl
from jax.experimental.pallas import tpu as pltpu
from jax.sharding import PartitionSpec as P

HD = 64
BF = jnp.bfloat16
F32 = jnp.float32
ANY = pl.BlockSpec(memory_space=pl.ANY)
SMEM = pl.BlockSpec(memory_space=pltpu.SMEM)
VMEM_LIMIT = 60 * 1024 * 1024


def dot_nn(a, b):
    return lax.dot_general(a, b, (((1,), (0,)), ((), ())), preferred_element_type=F32)


def dot_nt(a, b):
    return lax.dot_general(a, b, (((1,), (1,)), ((), ())), preferred_element_type=F32)


def dot_tn(a, b):
    return lax.dot_general(a, b, (((0,), (0,)), ((), ())), preferred_element_type=F32)


def const_spec(shape):
    zeros = (0,) * len(shape)
    return pl.BlockSpec(shape, lambda *_: zeros)


def cost(flops, moved, exps=0):
    return pl.CostEstimate(flops=int(flops), bytes_accessed=int(moved), transcendentals=int(exps))


def head_columns(pair, half_cols):
    per = half_cols // 128
    return pl.multiple_of(pair // per * (3 * half_cols) + pair % per * 128, 128)


def front_kernel(dims, meta, bias, *refs):
    F, C, T, ns, span, D = dims
    xs, ws = refs[:C], refs[C : C + F * T]
    x_out, w_out, qkv, e_out, linv_out, ctx, sems = refs[C + F * T :]
    step = pl.program_id(0)
    NP = D // 128
    L = C * span
    Dl, half = D // F, D // T
    f = meta[0]
    c = meta[1]

    @pl.when(step == 0)
    def _():
        copies = [pltpu.make_async_copy(xs[k], x_out.at[k], sems.at[k]) for k in range(C)]
        for df in range(F):
            for dt in range(T):
                n = df * T + dt
                row = pl.multiple_of((f ^ df) * Dl, 16)
                copies.append(
                    pltpu.make_async_copy(
                        ws[n],
                        w_out.at[pl.ds(row, Dl), pl.ds(dt * 3 * half, 3 * half)],
                        sems.at[C + n],
                    )
                )
        for copy in copies:
            copy.start()
        for copy in copies:
            copy.wait()
        x = x_out[...].reshape(L * ns, D)

        def project(j, carry):
            cols = pl.ds(pl.multiple_of(j * 384, 128), 384)
            y = dot_nn(x_out[...].reshape(L * ns, D), w_out[:, cols]) + bias[:, cols]
            qkv[:, :, :, cols] = y.astype(BF).reshape(C, ns, span, 384)
            return carry

        lax.fori_loop(0, 3 * D // 384, project, 0)

    s = step // NP
    pair = step % NP
    q_col = head_columns(pair, half)
    q = qkv[:, s, :, pl.ds(q_col, 128)].reshape(L, 128)
    k = qkv[:, s, :, pl.ds(pl.multiple_of(q_col + half, 128), 128)].reshape(L, 128)
    v = qkv[:, s, :, pl.ds(pl.multiple_of(q_col + 2 * half, 128), 128)].reshape(L, 128)
    low = lax.broadcasted_iota(jnp.int32, (L, 128), 1) < HD
    zero = jnp.zeros((), BF)
    one = jnp.ones((L, 128), BF)
    lane = lax.broadcasted_iota(jnp.int32, (1, L), 1)
    pos = ((lane // span) ^ c) * span + lane % span
    mask = jnp.where(pos < meta[2 + s], 0.0, -1e30)
    values = []
    for h in range(2):
        mine = low if h == 0 else jnp.logical_not(low)
        scores = dot_nt(q, jnp.where(mine, k, zero)) * (math.log2(math.e) / math.sqrt(HD)) + mask
        top = jnp.max(scores, axis=-1, keepdims=True)
        e_out[0, h * L : (h + 1) * L, :] = jnp.exp2(scores - top).astype(BF)
        values.append(
            jnp.concatenate([jnp.where(mine, v, zero), jnp.where(mine, one, zero)], axis=1)
        )
    acc = dot_nn(e_out[0, :L, :], values[0]) + dot_nn(e_out[0, L:, :], values[1])
    linv = 1.0 / acc[:, 128:]
    linv_out[0] = linv
    ctx[:, s, :, pl.ds(pl.multiple_of(pair * 128, 128), 128)] = (
        (acc[:, :128] * linv).astype(BF).reshape(C, span, 128)
    )


def front_call(dims, meta, bias, xs, ws):
    F, C, T, ns, span, D = dims
    NP, L = D // 128, C * span
    rows = ns * span
    shapes = [
        jax.ShapeDtypeStruct((C, rows, D), BF),
        jax.ShapeDtypeStruct((D, 3 * D), BF),
        jax.ShapeDtypeStruct((C, ns, span, 3 * D), BF),
        jax.ShapeDtypeStruct((ns * NP, 2 * L, L), BF),
        jax.ShapeDtypeStruct((ns * NP, L, 128), F32),
        jax.ShapeDtypeStruct((C, ns, span, D), BF),
    ]
    return pl.pallas_call(
        functools.partial(front_kernel, dims),
        name="front",
        grid=(ns * NP,),
        out_shape=shapes,
        in_specs=[SMEM, const_spec((1, 3 * D))] + [ANY] * (C + F * T),
        out_specs=[
            const_spec(shapes[0].shape),
            const_spec(shapes[1].shape),
            const_spec(shapes[2].shape),
            pl.BlockSpec((1, 2 * L, L), lambda i: (i, 0, 0)),
            pl.BlockSpec((1, L, 128), lambda i: (i, 0, 0)),
            const_spec(shapes[5].shape),
        ],
        scratch_shapes=[pltpu.SemaphoreType.DMA((C + F * T,))],
        compiler_params=pltpu.CompilerParams(vmem_limit_bytes=VMEM_LIMIT),
        cost_estimate=cost(2 * L * ns * D * 3 * D, 40e6, ns * 12 * L * L),
    )(meta, bias, *xs, *ws)


def normalised(values):
    centre = values - jnp.mean(values, axis=-1, keepdims=True)
    spread = jnp.mean(centre * centre, axis=-1, keepdims=True)
    rstd = lax.rsqrt(spread + 1e-12)
    return centre * rstd, rstd


def norm_back(grad, gain, xhat, rstd):
    scaled = grad * gain
    first = jnp.mean(scaled, axis=-1, keepdims=True)
    second = jnp.mean(scaled * xhat, axis=-1, keepdims=True)
    return rstd * (scaled - first - xhat * second)


def rows_kernel(dims, FF, meta, vec, inner_bias, x_ref, ctx_ref, *refs):
    F, C, T, ns, span, D = dims
    n_w = F * T
    cots, wis, bds = refs[:C], refs[C : C + n_w], refs[C + n_w : C + 2 * n_w]
    refs = refs[C + 2 * n_w :]
    los = refs[:C]
    (
        first_out, dctx_out, nl_out, act_out, og_out, ig_out, ag_out, sums, inner_sums,
        cot_s, lo_s, wi, wo, wout, gp_s, sems, out_sems,
    ) = refs[C:]
    k = pl.program_id(0)
    R = ns * span
    Dl, half, fhalf = D // F, D // T, FF // T
    f = meta[0]
    c = meta[1]

    def weight_copies():
        copies = []
        for df in range(F):
            row = pl.multiple_of((f ^ df) * Dl, 16)
            for dt in range(T):
                n = df * T + dt
                rows = pl.ds(row, Dl)
                copies.append((
                    pltpu.make_async_copy(
                        bds[n].at[:, pl.ds(0, half)],
                        wo.at[rows, pl.ds(dt * half, half)], sems.at[n]),
                    pltpu.make_async_copy(
                        wis[n], wi.at[rows, pl.ds(dt * fhalf, fhalf)], sems.at[n_w + n]),
                    pltpu.make_async_copy(
                        bds[n].at[:, pl.ds(half, fhalf)],
                        wout.at[rows, pl.ds(dt * fhalf, fhalf)], sems.at[2 * n_w + n]),
                ))
        return copies

    def cot_copies():
        return [
            pltpu.make_async_copy(cots[i], cot_s.at[i], sems.at[3 * n_w + i]) for i in range(C)
        ]

    @pl.when(k == 0)
    def _():
        copies = weight_copies()
        for which in range(3):
            for group in copies:
                group[which].start()
        for copy in cot_copies():
            copy.start()
        sums[...] = jnp.zeros_like(sums)
        inner_sums[...] = jnp.zeros_like(inner_sums)
        for which in range(3):
            for group in copies:
                group[which].wait()
        for copy in cot_copies():
            copy.wait()

    def add_sum(row, value):
        sums[row : row + 1, :] += jnp.sum(value, axis=0, keepdims=True)

    out_bias, gain1, shift1 = vec[0:1, :], vec[1:2, :], vec[2:3, :]
    outer_bias, gain2, shift2 = vec[3:4, :], vec[4:5, :], vec[5:6, :]
    ctx_low = ctx_ref[0]
    before = x_ref[0].astype(F32) + dot_nt(ctx_low, wo[...]) + out_bias
    xhat1, rstd1 = normalised(before)
    normed = xhat1 * gain1 + shift1
    nl = normed.astype(BF)
    nl_out[0] = nl
    root = math.sqrt(2.0 / math.pi)
    chunk = 768
    for j in range(FF // chunk):
        cols = slice(j * chunk, (j + 1) * chunk)
        pre = dot_nn(nl, wi[:, cols]) + inner_bias[:, cols]
        square = pre * pre
        th = jnp.tanh(pre * (root + (root * 0.044715) * square))
        hp = 0.5 + 0.5 * th
        act_out[0, :, cols] = (pre * hp).astype(BF)
        gp_s[:, cols] = hp + (0.5 * pre) * (1.0 - th * th) * (
            root + (3.0 * root * 0.044715) * square
        )
    before2 = normed + dot_nt(act_out[0], wout[...]) + outer_bias
    xhat2, rstd2 = normalised(before2)
    row = lax.broadcasted_iota(jnp.int32, (R, 1), 0)
    position = (c ^ k) * span + row % span
    length = jnp.full((R, 1), meta[2], jnp.int32)
    for s in range(1, ns):
        length = jnp.where(row >= s * span, meta[2 + s], length)
    live = (position < length).astype(F32)
    lo_s[k] = (live * (xhat2 * gain2 + shift2)).astype(BF)
    for i in range(C):
        @pl.when(k == i)
        def _():
            pltpu.make_async_copy(lo_s.at[i], los[i], out_sems.at[i]).start()
    grad = cot_s[k].astype(F32) * live
    add_sum(4, grad * xhat2)
    add_sum(5, grad)
    second = norm_back(grad, gain2, xhat2, rstd2)
    og = second.astype(BF)
    og_out[0] = og
    add_sum(3, og.astype(F32))
    for j in range(FF // chunk):
        cols = slice(j * chunk, (j + 1) * chunk)
        ig = (dot_nn(og, wout[:, cols]) * gp_s[:, cols]).astype(BF)
        ig_out[0, :, cols] = ig
        inner_sums[:, cols] += jnp.sum(ig.astype(F32), axis=0, keepdims=True)
    ngrad = dot_nt(ig_out[0], wi[...]) + second
    add_sum(1, ngrad * xhat1)
    add_sum(2, ngrad)
    first = norm_back(ngrad, gain1, xhat1, rstd1)
    first_out[0] = first
    ag = first.astype(BF)
    ag_out[0] = ag
    add_sum(0, ag.astype(F32))
    dctx_out[0] = dot_nn(ag, wo[...]).astype(BF)

    @pl.when(k == C - 1)
    def _():
        for i in range(C):
            pltpu.make_async_copy(lo_s.at[i], los[i], out_sems.at[i]).wait()


def rows_call(dims, FF, meta, vec, inner_bias, x_all, ctx, cots, wis, bds):
    F, C, T, ns, span, D = dims
    R = ns * span
    tile = lambda n: pl.BlockSpec((1, R, n), lambda i: (i, 0, 0))
    widths = [(D, F32), (D, BF), (D, BF), (FF, BF), (D, BF), (FF, BF), (D, BF)]
    out_shape = (
        [jax.ShapeDtypeStruct((R, D), BF)] * C
        + [jax.ShapeDtypeStruct((C, R, n), kind) for n, kind in widths]
        + [jax.ShapeDtypeStruct((8, D), F32), jax.ShapeDtypeStruct((1, FF), F32)]
    )
    n_w = F * T
    outs = pl.pallas_call(
        functools.partial(rows_kernel, dims, FF),
        name="rows",
        grid=(C,),
        out_shape=out_shape,
        in_specs=[SMEM, const_spec((8, D)), const_spec((1, FF)), tile(D), tile(D)]
        + [ANY] * (C + 2 * n_w),
        out_specs=[ANY] * C
        + [tile(n) for n, _ in widths]
        + [const_spec((8, D)), const_spec((1, FF))],
        scratch_shapes=[
            pltpu.VMEM((C, R, D), BF),
            pltpu.VMEM((C, R, D), BF),
            pltpu.VMEM((D, FF), BF),
            pltpu.VMEM((D, D), BF),
            pltpu.VMEM((D, FF), BF),
            pltpu.VMEM((R, FF), F32),
            pltpu.SemaphoreType.DMA((3 * n_w + C,)),
            pltpu.SemaphoreType.DMA((C,)),
        ],
        compiler_params=pltpu.CompilerParams(vmem_limit_bytes=VMEM_LIMIT),
        cost_estimate=cost(4 * C * R * D * (2 * FF + D), 50e6, C * R * FF),
    )(meta, vec, inner_bias, x_all, ctx, *cots, *wis, *bds)
    return outs[:C], outs[C:]


def back_kernel(dims, qkv, ctx, dctx, e_ref, linv, out, ds_s):
    F, C, T, ns, span, D = dims
    step = pl.program_id(0)
    NP, L, half = D // 128, C * span, D // T
    s = step // NP
    pair = step % NP
    q_col = head_columns(pair, half)
    k_col = pl.multiple_of(q_col + half, 128)
    v_col = pl.multiple_of(q_col + 2 * half, 128)
    c_col = pl.multiple_of(pair * 128, 128)
    q = qkv[:, s, :, pl.ds(q_col, 128)].reshape(L, 128)
    k = qkv[:, s, :, pl.ds(k_col, 128)].reshape(L, 128)
    v = qkv[:, s, :, pl.ds(v_col, 128)].reshape(L, 128)
    grad = dctx[:, s, :, pl.ds(c_col, 128)].reshape(L, 128).astype(F32) * linv[0]
    grad_low = grad.astype(BF)
    product = grad_low.astype(F32) * ctx[:, s, :, pl.ds(c_col, 128)].reshape(L, 128).astype(F32)
    low = lax.broadcasted_iota(jnp.int32, (L, 128), 1) < HD
    zero = jnp.zeros((), BF)
    qs, ks, gs = [], [], []
    for h in range(2):
        mine = low if h == 0 else jnp.logical_not(low)
        row_dot = jnp.sum(jnp.where(mine, product, 0.0), axis=-1, keepdims=True)
        probs_grad = dot_nt(grad_low, jnp.where(mine, v, zero))
        e = e_ref[0, h * L : (h + 1) * L, :].astype(F32)
        ds_s[h * L : (h + 1) * L, :] = (e * (probs_grad - row_dot)).astype(BF)
        qs.append(jnp.where(mine, q, zero))
        ks.append(jnp.where(mine, k, zero))
        gs.append(jnp.where(mine, grad_low, zero))
    scale = 1.0 / math.sqrt(HD)
    dq = (dot_nn(ds_s[:L, :], ks[0]) + dot_nn(ds_s[L:, :], ks[1])) * scale
    dk = dot_tn(ds_s[...], jnp.concatenate(qs, axis=0)) * scale
    dv = dot_tn(e_ref[0], jnp.concatenate(gs, axis=0))
    out[:, s, :, pl.ds(q_col, 128)] = dq.astype(BF).reshape(C, span, 128)
    out[:, s, :, pl.ds(k_col, 128)] = dk.astype(BF).reshape(C, span, 128)
    out[:, s, :, pl.ds(v_col, 128)] = dv.astype(BF).reshape(C, span, 128)


def back_call(dims, qkv, ctx, dctx, e, linv):
    F, C, T, ns, span, D = dims
    NP, L = D // 128, C * span
    return pl.pallas_call(
        functools.partial(back_kernel, dims),
        name="back",
        grid=(ns * NP,),
        out_shape=jax.ShapeDtypeStruct(qkv.shape, BF),
        in_specs=[
            const_spec(qkv.shape),
            const_spec(ctx.shape),
            const_spec(dctx.shape),
            pl.BlockSpec((1, 2 * L, L), lambda i: (i, 0, 0)),
            pl.BlockSpec((1, L, 128), lambda i: (i, 0, 0)),
        ],
        out_specs=const_spec(qkv.shape),
        scratch_shapes=[pltpu.VMEM((2 * L, L), BF)],
        compiler_params=pltpu.CompilerParams(vmem_limit_bytes=VMEM_LIMIT),
        cost_estimate=cost(ns * NP * 16 * L * L * 128, 30e6, 0),
    )(qkv, ctx, dctx, e, linv)


def input_kernel(C, dqkv, w, first, *refs):
    outs, (sums, buf, sems) = refs[:C], refs[C:]
    k = pl.program_id(0)
    d = dqkv[0]

    @pl.when(k == 0)
    def _():
        sums[...] = jnp.zeros_like(sums)

    sums[...] += jnp.sum(d.astype(F32), axis=0, keepdims=True)
    buf[k] = (dot_nt(d, w[...]) + first[0]).astype(BF)
    for i in range(C):
        @pl.when(k == i)
        def _():
            pltpu.make_async_copy(buf.at[i], outs[i], sems.at[i]).start()

    @pl.when(k == C - 1)
    def _():
        for i in range(C):
            pltpu.make_async_copy(buf.at[i], outs[i], sems.at[i]).wait()


def input_call(dqkv, w, first):
    C, R, W = dqkv.shape
    D = w.shape[0]
    outs = pl.pallas_call(
        functools.partial(input_kernel, C),
        name="input_grad",
        grid=(C,),
        out_shape=[jax.ShapeDtypeStruct((R, D), BF)] * C + [jax.ShapeDtypeStruct((1, W), F32)],
        in_specs=[
            pl.BlockSpec((1, R, W), lambda i: (i, 0, 0)),
            const_spec(w.shape),
            pl.BlockSpec((1, R, D), lambda i: (i, 0, 0)),
        ],
        out_specs=[ANY] * C + [const_spec((1, W))],
        scratch_shapes=[pltpu.VMEM((C, R, D), BF), pltpu.SemaphoreType.DMA((C,))],
        compiler_params=pltpu.CompilerParams(vmem_limit_bytes=VMEM_LIMIT),
        cost_estimate=cost(2 * C * R * D * W, 15e6, 0),
    )(dqkv, w, first)
    return outs[:C], outs[C]


def weight_kernel(F, meta, left, right, keep, send, left_t, tile):
    D = left.shape[1]
    Dl = D // F

    @pl.when((pl.program_id(0) == 0) & (pl.program_id(1) == 0))
    def _():
        left_t[...] = left[...].T

    tile[...] = dot_nn(left_t[...], right[...]).astype(BF)
    f = meta[0]
    for high in range(F // 2):
        for bit, out in ((0, keep), (1, send)):
            row = pl.multiple_of((f ^ (2 * high + bit)) * Dl, 16)
            out[high, 0] = tile[pl.ds(row, Dl), :]


def weight_call(dims, meta, left, right):
    F, C, T, ns, span, D = dims
    rows, width = right.shape
    cols = 384
    per = width // T // cols
    out = jax.ShapeDtypeStruct((F // 2, T, D // F, width // T), BF)
    out_spec = pl.BlockSpec((F // 2, 1, D // F, cols), lambda a, b: (0, a, 0, b))
    return pl.pallas_call(
        functools.partial(weight_kernel, F),
        name="weight_grad",
        grid=(T, per),
        out_shape=[out, out],
        in_specs=[
            SMEM,
            const_spec(left.shape),
            pl.BlockSpec((rows, cols), lambda a, b: (0, a * per + b)),
        ],
        out_specs=[out_spec, out_spec],
        scratch_shapes=[pltpu.VMEM((D, rows), BF), pltpu.VMEM((D, cols), BF)],
        compiler_params=pltpu.CompilerParams(vmem_limit_bytes=VMEM_LIMIT),
        cost_estimate=cost(2 * rows * D * width, 2 * (rows * (D + width) + D * width), 0),
    )(meta, left, right)


def xor_pairs(count, mask):
    return [(i, i ^ mask) for i in range(count)]


def added(a, b):
    return (a.astype(F32) + b.astype(F32)).astype(BF)


def per_device(
    tokens_in, seq_lengths, query_weight, query_bias, key_weight, value_weight, value_bias,
    output_weight, output_bias, attn_gain, attn_shift, inner_weight, inner_bias, outer_weight,
    outer_bias, ffn_gain, ffn_shift, cotangent,
):
    F, C, T = (lax.axis_size(a) for a in ("fsdp", "ctx", "tp"))
    f, c, t = (lax.axis_index(a) for a in ("fsdp", "ctx", "tp"))
    S, span, D = tokens_in.shape
    ns = S // (C * T)
    Dl, half = D // F, D // T
    fhalf = inner_weight.shape[1]
    FF = fhalf * T
    H = query_bias.shape[0] * T
    R = ns * span
    dims = (F, C, T, ns, span, D)

    def to_sequences(array):
        out = []
        for k in range(C):
            piece = lax.dynamic_slice_in_dim(array, ((c ^ k) * T + t) * ns, ns, 0).reshape(R, D)
            out.append(lax.ppermute(piece, "ctx", xor_pairs(C, k)) if k else piece)
        return out

    def to_slots(pieces, kind):
        out = lax.full((S, span, D), 0, kind)
        for k in range(C):
            piece = lax.ppermute(pieces[k], "ctx", xor_pairs(C, k)) if k else pieces[k]
            for dt in range(T):
                got = lax.ppermute(piece, "tp", xor_pairs(T, dt)) if dt else piece
                out = lax.dynamic_update_slice_in_dim(
                    out, got.reshape(ns, span, D).astype(kind), ((c ^ k) * T + (t ^ dt)) * ns, 0
                )
        return out

    def gathered(shard):
        held = {}
        for high in range(0, F, 2):
            for dt in range(T):
                if high == 0 and dt == 0:
                    held[0, 0] = shard
                else:
                    pairs = [
                        (i * T + j, (i ^ high) * T + (j ^ dt)) for i in range(F) for j in range(T)
                    ]
                    held[high, dt] = lax.ppermute(shard, ("fsdp", "tp"), pairs)
        for high in range(0, F, 2):
            for dt in range(T):
                held[high + 1, dt] = lax.ppermute(held[high, dt], "fsdp", xor_pairs(F, 1))
        return [held[df, dt] for df in range(F) for dt in range(T)]

    def by_half(array):
        return array[jnp.arange(T) ^ t]

    x_pieces = to_sequences(tokens_in)
    qkv_pieces = gathered(jnp.concatenate([query_weight, key_weight, value_weight], axis=1))
    small = jnp.concatenate(
        [output_bias, attn_gain, attn_shift, outer_bias, ffn_gain, ffn_shift]
        + [query_bias.reshape(-1), value_bias.reshape(-1), inner_bias.reshape(-1)]
    )
    small = lax.all_gather(small, ("fsdp", "tp"), axis=0, tiled=False).reshape(F, T, -1)
    vec = small[:, 0, : 6 * Dl].reshape(F, 6, Dl).transpose(1, 0, 2).reshape(6, D).astype(F32)
    vec = jnp.concatenate([vec, jnp.zeros((2, D), F32)], axis=0)
    n_qb = query_bias.size

    def unit_rows(start, shape):
        block = small[:, :, start : start + math.prod(shape)].reshape(F, T, *shape)
        return by_half(block.transpose(1, 2, 0, 3).reshape(T, -1).astype(F32))

    q_off = unit_rows(6 * Dl, query_bias.shape)
    v_off = unit_rows(6 * Dl + n_qb, value_bias.shape)
    inner_off = unit_rows(6 * Dl + 2 * n_qb, inner_bias.shape).reshape(1, FF)
    qkv_off = jnp.stack([q_off, jnp.zeros_like(q_off), v_off], axis=1).reshape(1, 3 * D)
    inner_pieces = gathered(inner_weight)
    outer_pieces = gathered(jnp.concatenate([output_weight.T, outer_weight.T], axis=1))
    cot_pieces = to_sequences(cotangent)
    lengths = lax.dynamic_slice_in_dim(seq_lengths, (c * T + t) * ns, ns, 0)
    meta = jnp.concatenate([jnp.stack([f, c]).astype(jnp.int32), lengths])

    x_all, qkv_w, qkv, e, linv, ctx = front_call(dims, meta, qkv_off, x_pieces, qkv_pieces)
    los, (first, dctx, nl, act, og, ig, ag, sums, inner_sums) = rows_call(
        dims, FF, meta, vec, inner_off, x_all, ctx.reshape(C, R, D), cot_pieces,
        inner_pieces, outer_pieces,
    )
    layer_out = to_slots(los, BF)

    def reduced(left, right):
        left, right = left.reshape(C * R, -1), right.reshape(C * R, -1)
        keep, send = weight_call(dims, meta, left, right)
        total = added(keep, lax.ppermute(send, "fsdp", xor_pairs(F, 1)))
        while total.shape[0] > 1:
            h = total.shape[0] // 2
            total = added(total[:h], lax.ppermute(total[h:], "fsdp", xor_pairs(F, 2 * h)))
        total = total[0]
        while total.shape[0] > 1:
            h = total.shape[0] // 2
            total = added(total[:h], lax.ppermute(total[h:], "tp", xor_pairs(T, h)))
        total = total[0]
        bits = [1 << b for b in range(C.bit_length() - 1)]
        for bit in bits:
            h = total.shape[0] // 2
            mine = (c // bit) % 2
            away = lax.ppermute(
                lax.dynamic_slice_in_dim(total, (1 - mine) * h, h, 0), "ctx", xor_pairs(C, bit)
            )
            total = added(lax.dynamic_slice_in_dim(total, mine * h, h, 0), away)
        for bit in reversed(bits):
            away = lax.ppermute(total, "ctx", xor_pairs(C, bit))
            upper = (c // bit) % 2 == 1
            total = jnp.concatenate(
                [jnp.where(upper, away, total), jnp.where(upper, total, away)], axis=0
            )
        return total

    outer_t = reduced(og, act)
    inner_g = reduced(nl, ig)
    output_t = reduced(ag, ctx)
    dqkv = back_call(dims, qkv, ctx, dctx.reshape(ctx.shape), e, linv)
    ins, qkv_sums = input_call(dqkv.reshape(C, R, 3 * D), qkv_w, first)
    input_grad = to_slots(ins, F32)
    qkv_g = reduced(x_all, dqkv)

    def all_sum(array):
        for axis, count in (("fsdp", F), ("tp", T), ("ctx", C)):
            for b in range(count.bit_length() - 1):
                array = array + lax.ppermute(array, axis, xor_pairs(count, 1 << b))
        return array

    early = all_sum(jnp.concatenate([sums[:6].reshape(-1), by_half(inner_sums.reshape(T, -1)).reshape(-1)]))
    qkv_parts = by_half(qkv_sums.reshape(T, 3, half))
    late = all_sum(jnp.concatenate([qkv_parts[:, 0].reshape(-1), qkv_parts[:, 2].reshape(-1)]))
    vec_sums = lax.dynamic_slice_in_dim(early[: 6 * D].reshape(6, D), f * Dl, Dl, 1)

    def shard_of(array, shape):
        whole = array.reshape(shape[0] * T, shape[1] * F)
        return lax.dynamic_slice(whole, (t * shape[0], f * shape[1]), shape)

    return (
        layer_out,
        input_grad,
        qkv_g[:, :half].astype(F32),
        shard_of(late[:D], query_bias.shape),
        qkv_g[:, half : 2 * half].astype(F32),
        qkv_g[:, 2 * half :].astype(F32),
        shard_of(late[D:], value_bias.shape),
        output_t.T.astype(F32),
        vec_sums[0],
        vec_sums[1],
        vec_sums[2],
        inner_g.astype(F32),
        shard_of(early[6 * D :], inner_bias.shape),
        outer_t.T.astype(F32),
        vec_sums[3],
        vec_sums[4],
        vec_sums[5],
    )


def solution(mesh):
    rows3, flat = P("fsdp", "ctx", None), P("fsdp")
    wide, tall = P("fsdp", "tp"), P("tp", "fsdp")
    params = (wide, tall, wide, wide, tall, tall, flat, flat, flat, wide, tall, tall, flat, flat, flat)
    return jax.shard_map(
        per_device,
        mesh=mesh,
        in_specs=(rows3, P("fsdp")) + params + (rows3,),
        out_specs=(rows3, rows3) + params,
        check_vma=False,
    )
```

time: 1720 us -> 576 us (0.33)
  waiting for transfers between devices: 1240 us -> 248 us
  matrix products: 191 us -> 0 us
  Pallas kernels: 0 us -> 153 us
  starting transfers between devices: 2.26 us -> 86.8 us
  local copies, waits for them, and re-layouts: 93.4 us -> 25.7 us
  blocking collectives: 90.6 us -> 34 us
  other arithmetic: 78.8 us -> 24.6 us
    psum x5 -> x0, waiting for transfers between devices: 570 us -> none  [the longest x1 153 us: per_device(): lax.psum(times_transposed(inner_grad_low, inner_back), 'tp') + second_grad]
    reduce_scatter x5 -> x0, waiting for transfers between devices: 437 us -> none  [the longest x1 207 us: per_device(): lax.psum_scatter(key_part.reshape(seq_count, seq_total, head_cols), 'ctx'...]
    ppermute x0 -> x79, waiting for transfers between devices: none -> 248 us  [the longest x6 46.6 us: to_sequences(): out.append(lax.ppermute(piece, 'ctx', xor_pairs(C, k)) if k else piece)]
    dot_general x23 -> x0, matrix products: 174 us -> none  [the longest x6 38.8 us: matmul(): return jnp.dot(left_side, right_side, preferred_element_type=jnp.float32)]
    all_gather x4 -> x0, waiting for transfers between devices: 162 us -> none  [the longest x1 90 us: per_device(): lax.all_gather(values_local, 'ctx', axis=1, tiled=True)]
    pallas_call x0 -> x8, Pallas kernels: none -> 153 us  [the longest x1 46.7 us: rows_call(): pl.pallas_call(functools.partial(rows_kernel, dims, FF), name='rows', gri...]
    ppermute x0 -> x79, starting transfers between devices: none -> 86.8 us  [the longest x6 14.6 us: to_sequences(): out.append(lax.ppermute(piece, 'ctx', xor_pairs(C, k)) if k else piece)]
    unnamed x26 -> x0, waiting for transfers between devices: 74.3 us -> none
  transfers between devices with their start and end apart: 20 -> 79, of which waited for: 17 -> 34; matrix products, arithmetic and copies ran while one was open for 12% -> 7% of each run, Pallas kernels for 0% -> 18%
where the time goes in v1:
time: 576 us; the launch traced here: 574 us
  waiting for transfers between devices  248 us (43%)
  Pallas kernels  153 us (27%)
  starting transfers between devices  86.8 us (15%)
  blocking collectives  34 us (6%)
  local copies, waits for them, and re-layouts  25.7 us (4%)
  other arithmetic  24.6 us (4%)
    pallas_call x1, Pallas kernels, rows_call(): pl.pallas_call(functools.partial(rows_kernel, dims, FF), name='rows', gri...  46.7 us
    ppermute x6, waiting for transfers between devices, to_sequences(): out.append(lax.ppermute(piece, 'ctx', xor_pairs(C, k)) if k else piece)  46.6 us
    ppermute x4, waiting for transfers between devices, reduced(): lax.ppermute(total[h:], 'fsdp', xor_pairs(F, 2 * h))  42.2 us
    pallas_call x4, Pallas kernels, weight_call(): pl.pallas_call(functools.partial(weight_kernel, F), name='weight_grad', g...  40.1 us
    ppermute x8, waiting for transfers between devices, reduced(): lax.ppermute(lax.dynamic_slice_in_dim(total, (1 - mine) * h, h, 0), 'ctx'...  37.2 us
    ppermute x6, waiting for transfers between devices, to_slots(): piece = lax.ppermute(pieces[k], 'ctx', xor_pairs(C, k)) if k else pieces[k]  35.2 us
    unnamed x1, blocking collectives  34 us
    pallas_call x1, Pallas kernels, front_call(): pl.pallas_call(functools.partial(front_kernel, dims), name='front', grid=...  29.5 us
  transfers between devices with their start and end apart: 79, of which 34 were waited for; matrix products, arithmetic and copies ran while one was open for 7% of the time, Pallas kernels for 18%

profile of v1, /device:TPU:0, one launch (start us, length us, event | category | flops | bytes accessed | tf_op | source)
XLA Modules:
  0.0 574.2 jit_solution(2194246510074988790)
XLA Ops:
  0.8 3.1 constant_dynamic-slice_fusion.5
  4.0 3.1 collective-permute-start
  7.1 2.6 collective-permute-start.1
  10.6 3.5 collective-permute-start.11
  14.2 10.6 %collective-permute-done.refs_1_ = bf16[256,768]{1,0:T(8,128)(2,1)S(1)} collective-permute-done((bf16[256,768]{1,0:T(8,128)(2,1)S(1)}, bf16[256,768]{1,0:T(8,128)(2,1)S(1)}, u32[]{:S(2)}, u32[]{:S(2)}) %collective-permute-start) | collective-permute-done | bytes 393248 | tf_op jit(solution)/shard_map/ppermute | solution.py:486
  25.5 4.5 collective-permute-start.12
  30.1 6.8 %collective-permute-done.1.refs_2_ = bf16[256,768]{1,0:T(8,128)(2,1)S(1)} collective-permute-done((bf16[256,768]{1,0:T(8,128)(2,1)S(1)}, bf16[256,768]{1,0:T(8,128)(2,1)S(1)}, u32[]{:S(2)}, u32[]{:S(2)}) %collective-permute-start.1) | collective-permute-done | bytes 393248 | tf_op jit(solution)/shard_map/ppermute | solution.py:486
  39.9 2.1 collective-permute-done.10.refs_1_
  43.5 27.1 %collective-permute-done.11.refs_2_ = bf16[256,768]{1,0:T(8,128)(2,1)S(1)} collective-permute-done((bf16[256,768]{1,0:T(8,128)(2,1)S(1)}, bf16[256,768]{1,0:T(8,128)(2,1)S(1)}, u32[]{:S(2)}, u32[]{:S(2)}) %collective-permute-start.11) | collective-permute-done | bytes 393248 | tf_op jit(solution)/shard_map/ppermute | solution.py:486
  70.6 2.4 collective-permute-start.7
  75.3 9.4 %collective-permute-done.7.refs_9_ = bf16[192,1152]{1,0:T(8,128)(2,1)S(1)} collective-permute-done((bf16[192,1152]{1,0:T(8,128)(2,1)S(1)}, bf16[192,1152]{1,0:T(8,128)(2,1)S(1)}, u32[]{:S(2)}, u32[]{:S(2)}) %collective-permute-start.7) | collective-permute-done | bytes 442400 | tf_op jit(solution)/shard_map/ppermute | solution.py:510
  86.1 1.6 collective-permute-start.23
  87.7 18.5 %collective-permute-done.16.refs_8_ = bf16[192,1536]{1,0:T(8,128)(2,1)S(1)} collective-permute-done((bf16[192,1536]{1,0:T(8,128)(2,1)S(1)}, bf16[192,1536]{1,0:T(8,128)(2,1)S(1)}, u32[]{:S(2)}, u32[]{:S(2)}) %collective-permute-start.16) | collective-permute-done | bytes 589856 | tf_op jit(solution)/shard_map/ppermute | solution.py:510
  106.3 2.4 collective-permute-start.24
  111.5 34.0 %all-reduce.1 = bf16[13824]{0:T(1024)(128)(2,1)S(1)} all-reduce(bf16[13824]{0:T(1024)(128)(2,1)S(1)} %dynamic-update-slice), channel_id=2, replica_groups=mesh['fsdp'=4,'ctx'=4,'tp'=2] {'fsdp','tp'}, use_global_device_ids=true, to_apply=%add.1 | all-reduce | flops 13824 | bytes 55296
  154.8 29.5 %front.1 = (bf16[4,256,768]{2,1,0:T(8,128)(2,1)}, bf16[768,2304]{1,0:T(8,128)(2,1)}, bf16[4,2,128,2304]{3,2,1,0:T(8,128)(2,1)}, bf16[12,1024,512]{2,1,0:T(8,128)...) custom-call(s32[4]{0:T(128)} %pad_add_fusion.meta, f32[1,2304]{1,0:T(1,128)} %reshape.329.bias, ...), custom_call_target="tpu_custom_call" | custom-call | flops 3623878656 | bytes 40000000 | tf_op jit(solution)/shard_map/front/pallas_call | solution.py:125
  184.4 46.7 %rows.1 = (bf16[256,768]{1,0:T(8,128)(2,1)}, bf16[256,768]{1,0:T(8,128)(2,1)}, bf16[256,768]{1,0:T(8,128)(2,1)}, bf16[256,768]{1,0:T(8,128)(2,1)}, f32[4,256,768...) custom-call(s32[4]{0:T(128)} %pad_add_fusion.meta, ...), custom_call_target="tpu_custom_call" | custom-call | flops 21743271936 | bytes 50000000 | tf_op jit(solution)/shard_map/rows/pallas_call | solution.py:290
  234.5 5.1 weight_grad.5
  240.0 26.1 %back.1 = bf16[4,2,128,2304]{3,2,1,0:T(8,128)(2,1)} custom-call(bf16[4,2,128,2304]{3,2,1,0:T(8,128)(2,1)} %get-tuple-element.55.qkv, bf16[4,2,128,768]{3,2,1,0:T(8,128)(2,1)} %get-tuple-element.50.ctx, bf16[4,2,128,768]{3,2,1,0:T(8,128)(2,1)} %bitcast.125, bf16[12,1024,512]{2,1,0:T(8,128)(2,1)} %get-tuple-element.57.e_ref, ...), custom_call_target="tpu_custom_call" | custom-call | flops 6442450944 | bytes 30000000 | tf_op jit(solution)/shard_map/back/pallas_call | solution.py:356
  266.1 10.2 %input_grad.1 = (bf16[256,768]{1,0:T(8,128)(2,1)}, bf16[256,768]{1,0:T(8,128)(2,1)}, bf16[256,768]{1,0:T(8,128)(2,1)}, bf16[256,768]{1,0:T(8,128)(2,1)}, f32[1,2304]{1,0:T(1,128)}) custom-call(bf16[4,256,2304]{2,1,0:T(8,128)(2,1)} %bitcast.121, bf16[768,2304]{1,0:T(8,128)(2,1)} %get-tuple-element.59.w, f32[4,256,768]{2,1,0:T(8,128)} %get-tuple-element.60.first), custom_call_target="tpu_custom_call" | custom-call | flops 3623878656 | bytes 15000000 | tf_op jit(solution)/shard_map/input_grad/pallas_call | solution.py:400
  277.9 2.0 collective-permute-start.27
  279.9 12.5 %weight_grad.7 = (bf16[2,2,192,1536]{3,2,1,0:T(8,128)(2,1)}, bf16[2,2,192,1536]{3,2,1,0:T(8,128)(2,1)}) custom-call(s32[4]{0:T(128)} %pad_add_fusion.meta, bf16[1024,768]{1,0:T(8,128)(2,1)} %bitcast.167, bf16[1024,3072]{1,0:T(8,128)(2,1)} %bitcast.164), custom_call_target="tpu_custom_call" | custom-call | flops 4831838208 | bytes 12582912 | tf_op jit(solution)/shard_map/weight_grad/pallas_call | solution.py:441
  293.0 12.5 %weight_grad.6 = (bf16[2,2,192,1536]{3,2,1,0:T(8,128)(2,1)}, bf16[2,2,192,1536]{3,2,1,0:T(8,128)(2,1)}) custom-call(s32[4]{0:T(128)} %pad_add_fusion.meta, bf16[1024,768]{1,0:T(8,128)(2,1)} %bitcast.166, bf16[1024,3072]{1,0:T(8,128)(2,1)} %bitcast.163), custom_call_target="tpu_custom_call" | custom-call | flops 4831838208 | bytes 12582912 | tf_op jit(solution)/shard_map/weight_grad/pallas_call | solution.py:441
  305.6 1.6 collective-permute-start.61
  307.2 10.1 %weight_grad.4 = (bf16[2,2,192,1152]{3,2,1,0:T(8,128)(2,1)}, bf16[2,2,192,1152]{3,2,1,0:T(8,128)(2,1)}) custom-call(s32[4]{0:T(128)} %pad_add_fusion.meta, bf16[1024,768]{1,0:T(8,128)(2,1)} %bitcast.165, bf16[1024,2304]{1,0:T(8,128)(2,1)} %bitcast.122), custom_call_target="tpu_custom_call" | custom-call | flops 3623878656 | bytes 9830400 | tf_op jit(solution)/shard_map/weight_grad/pallas_call | solution.py:441
  317.2 2.7 collective-permute-start.51
  320.0 2.1 collective-permute-start.62
  322.1 3.4 broadcast_in_dim.5
  327.4 2.1 collective-permute-start.63
  332.4 2.2 collective-permute-start.64
  338.5 3.5 collective-permute-start.37
  345.4 1.7 fusion.14
  347.2 1.9 convert_dynamic-update-slice_fusion.6
  349.1 2.4 collective-permute-start.39
  351.5 2.1 convert_dynamic-update-slice_fusion.5
  354.9 14.9 %collective-permute-done.28 = bf16[256,768]{1,0:T(8,128)(2,1)S(1)} collective-permute-done((bf16[256,768]{1,0:T(8,128)(2,1)}, bf16[256,768]{1,0:T(8,128)(2,1)S(1)}, u32[]{:S(2)}, u32[]{:S(2)}) %collective-permute-start.28) | collective-permute-done | bytes 393248 | tf_op jit(solution)/shard_map/ppermute | solution.py:492
  374.8 1.9 convert_dynamic-update-slice_fusion.3
  376.7 7.3 %collective-permute-done.38 = bf16[256,768]{1,0:T(8,128)(2,1)S(1)} collective-permute-done((bf16[256,768]{1,0:T(8,128)(2,1)}, bf16[256,768]{1,0:T(8,128)(2,1)S(1)}, u32[]{:S(2)}, u32[]{:S(2)}) %collective-permute-start.38) | collective-permute-done | bytes 393248 | tf_op jit(solution)/shard_map/ppermute | solution.py:494
  386.4 5.6 collective-permute-done.54
  392.6 1.6 collective-permute-start.55
  395.1 7.6 %collective-permute-done.29 = bf16[256,768]{1,0:T(8,128)(2,1)S(1)} collective-permute-done((bf16[256,768]{1,0:T(8,128)(2,1)S(1)}, bf16[256,768]{1,0:T(8,128)(2,1)S(1)}, u32[]{:S(2)}, u32[]{:S(2)}) %collective-permute-start.29) | collective-permute-done | bytes 393248 | tf_op jit(solution)/shard_map/ppermute | solution.py:494
  404.3 3.2 collective-permute-start.32
  407.6 20.3 %collective-permute-done.30 = bf16[256,768]{1,0:T(8,128)(2,1)S(1)} collective-permute-done((bf16[256,768]{1,0:T(8,128)(2,1)S(1)}, bf16[256,768]{1,0:T(8,128)(2,1)S(1)}, u32[]{:S(2)}, u32[]{:S(2)}) %collective-permute-start.30) | collective-permute-done | bytes 393248 | tf_op jit(solution)/shard_map/ppermute | solution.py:492
  428.6 3.7 collective-permute-done.56
  433.9 6.0 %collective-permute-done.31 = bf16[256,768]{1,0:T(8,128)(2,1)S(1)} collective-permute-done((bf16[256,768]{1,0:T(8,128)(2,1)S(1)}, bf16[256,768]{1,0:T(8,128)(2,1)S(1)}, u32[]{:S(2)}, u32[]{:S(2)}) %collective-permute-start.31) | collective-permute-done | bytes 393248 | tf_op jit(solution)/shard_map/ppermute | solution.py:494
  440.0 8.3 %collective-permute-start.57 = (bf16[48,384]{1,0:T(8,128)(2,1)S(1)}, bf16[48,384]{1,0:T(8,128)(2,1)S(1)}, u32[]{:S(2)}, u32[]{:S(2)}) collective-permute-start(bf16[48,384]{1,0:T(8,128)(2,1)S(1)} %constant_dynamic-slice_fusion.3), channel_id=1, source_target_pairs={{0,4},{2,6},{4,0},{6,2},{1,5},{3,7},{5,1},{7,3},{8,12},{10,14},{12... | collective-permute-start | bytes 110600 | tf_op jit(solution)/shard_map/ppermute | solution.py:567
  448.3 1.9 collective-permute-done.57
  450.2 3.0 collective-permute-start.58
  453.3 2.0 collective-permute-done.58
  455.3 3.1 collective-permute-start.59
  461.5 5.6 collective-permute-done.43
  467.2 2.9 collective-permute-start.44
  471.4 3.1 collective-permute-done.44
  476.2 7.2 %collective-permute-done.45 = bf16[48,1152]{1,0:T(8,128)(2,1)S(1)} collective-permute-done((bf16[48,1152]{1,0:T(8,128)(2,1)S(1)}, bf16[48,1152]{1,0:T(8,128)(2,1)S(1)}, u32[]{:S(2)}, u32[]{:S(2)}) %collective-permute-start.45) | collective-permute-done | bytes 110624 | tf_op jit(solution)/shard_map/ppermute | solution.py:567
  483.5 16.3 %collective-permute-done.73 = bf16[1,2,192,1536]{3,2,1,0:T(8,128)(2,1)S(1)} collective-permute-done((bf16[1,2,192,1536]{3,2,1,0:T(8,128)(2,1)S(1)}, bf16[1,2,192,1536]{3,2,1,0:T(8,128)(2,1)S(1)}, u32[]{:S(2)}, u32[]{:S(2)}) %collective-permute-start.73) | collective-permute-done | bytes 1179680 | tf_op jit(solution)/shard_map/ppermute | solution.py:557
  500.8 20.3 %collective-permute-done.66 = bf16[1,2,192,1536]{3,2,1,0:T(8,128)(2,1)S(1)} collective-permute-done((bf16[1,2,192,1536]{3,2,1,0:T(8,128)(2,1)S(1)}, bf16[1,2,192,1536]{3,2,1,0:T(8,128)(2,1)S(1)}, u32[]{:S(2)}, u32[]{:S(2)}) %collective-permute-start.66) | collective-permute-done | bytes 1179680 | tf_op jit(solution)/shard_map/ppermute | solution.py:557
  523.4 9.4 %collective-permute-done.67 = bf16[1,192,1536]{2,1,0:T(8,128)(2,1)S(1)} collective-permute-done((bf16[1,192,1536]{2,1,0:T(8,128)(2,1)S(1)}, bf16[1,192,1536]{2,1,0:T(8,128)(2,1)S(1)}, u32[]{:S(2)}, u32[]{:S(2)}) %collective-permute-start.67) | collective-permute-done | bytes 589856 | tf_op jit(solution)/shard_map/ppermute | solution.py:561
  533.8 6.2 %collective-permute-done.68 = bf16[96,1536]{1,0:T(8,128)(2,1)S(1)} collective-permute-done((bf16[96,1536]{1,0:T(8,128)(2,1)S(1)}, bf16[96,1536]{1,0:T(8,128)(2,1)S(1)}, u32[]{:S(2)}, u32[]{:S(2)}) %collective-permute-start.68) | collective-permute-done | bytes 294944 | tf_op jit(solution)/shard_map/ppermute | solution.py:567
  540.1 8.9 %collective-permute-done.76 = bf16[48,1536]{1,0:T(8,128)(2,1)S(1)} collective-permute-done((bf16[48,1536]{1,0:T(8,128)(2,1)S(1)}, bf16[48,1536]{1,0:T(8,128)(2,1)S(1)}, u32[]{:S(2)}, u32[]{:S(2)}) %collective-permute-start.76) | collective-permute-done | bytes 147488 | tf_op jit(solution)/shard_map/ppermute | solution.py:567
  549.2 6.2 %collective-permute-done.69 = bf16[48,1536]{1,0:T(8,128)(2,1)S(1)} collective-permute-done((bf16[48,1536]{1,0:T(8,128)(2,1)S(1)}, bf16[48,1536]{1,0:T(8,128)(2,1)S(1)}, u32[]{:S(2)}, u32[]{:S(2)}) %collective-permute-start.69) | collective-permute-done | bytes 147488 | tf_op jit(solution)/shard_map/ppermute | solution.py:567
  555.5 3.0 collective-permute-done.77
  558.7 3.0 collective-permute-done.70
  561.8 6.8 %collective-permute-done.78 = bf16[96,1536]{1,0:T(8,128)(2,1)S(1)} collective-permute-done((bf16[96,1536]{1,0:T(8,128)(2,1)S(1)}, bf16[96,1536]{1,0:T(8,128)(2,1)S(1)}, u32[]{:S(2)}, u32[]{:S(2)}) %collective-permute-start.78) | collective-permute-done | bytes 294944 | tf_op jit(solution)/shard_map/ppermute | solution.py:572
  569.8 3.2 collective-permute-done.71
  (342 shorter events, 67.3 us)
Async XLA Ops:
  4.0 20.8 %collective-permute-start = (bf16[256,768]{1,0:T(8,128)(2,1)S(1)}, bf16[256,768]{1,0:T(8,128)(2,1)S(1)}, u32[]{:S(2)}, u32[]{:S(2)}) collective-permute-start(bf16[256,768]{1,0:T(8,128)(2,1)S(1)} %bitcast.134), channel_id=1, source_target_pairs={{0,2},{2,0},{4,6},{6,4},{1,3},{3,1},{5,7},{7,5},{8,10},{10,8},{12,... | collective-permute-start | bytes 1179656 | tf_op jit(solution)/shard_map/ppermute | solution.py:486
  7.1 29.8 %collective-permute-start.1 = (bf16[256,768]{1,0:T(8,128)(2,1)S(1)}, bf16[256,768]{1,0:T(8,128)(2,1)S(1)}, u32[]{:S(2)}, u32[]{:S(2)}) collective-permute-start(bf16[256,768]{1,0:T(8,128)(2,1)S(1)} %bitcast.133), channel_id=1, source_target_pairs={{0,4},{2,6},{4,0},{6,2},{1,5},{3,7},{5,1},{7,3},{8,12},{10,14},{12... | collective-permute-start | bytes 1179656 | tf_op jit(solution)/shard_map/ppermute | solution.py:486
  9.7 28.7 %collective-permute-start.2 = (bf16[256,768]{1,0:T(8,128)(2,1)S(1)}, bf16[256,768]{1,0:T(8,128)(2,1)S(1)}, u32[]{:S(2)}, u32[]{:S(2)}) collective-permute-start(bf16[256,768]{1,0:T(8,128)(2,1)S(1)} %bitcast.132), channel_id=1, source_target_pairs={{0,6},{2,4},{4,2},{6,0},{1,7},{3,5},{5,3},{7,1},{8,14},{10,12},{12... | collective-permute-start | bytes 1179656 | tf_op jit(solution)/shard_map/ppermute | solution.py:486
  9.7 32.3 %collective-permute-start.10 = (bf16[256,768]{1,0:T(8,128)(2,1)S(1)}, bf16[256,768]{1,0:T(8,128)(2,1)S(1)}, u32[]{:S(2)}, u32[]{:S(2)}) collective-permute-start(bf16[256,768]{1,0:T(8,128)(2,1)S(1)} %bitcast.131), channel_id=1, source_target_pairs={{0,2},{2,0},{4,6},{6,4},{1,3},{3,1},{5,7},{7,5},{8,10},{10,8},{12,... | collective-permute-start | bytes 1179656 | tf_op jit(solution)/shard_map/ppermute | solution.py:486
  10.6 60.0 %collective-permute-start.11 = (bf16[256,768]{1,0:T(8,128)(2,1)S(1)}, bf16[256,768]{1,0:T(8,128)(2,1)S(1)}, u32[]{:S(2)}, u32[]{:S(2)}) collective-permute-start(bf16[256,768]{1,0:T(8,128)(2,1)S(1)} %bitcast.130), channel_id=1, source_target_pairs={{0,4},{2,6},{4,0},{6,2},{1,5},{3,7},{5,1},{7,3},{8,12},{10,14},{12... | collective-permute-start | bytes 1179656 | tf_op jit(solution)/shard_map/ppermute | solution.py:486
  25.5 47.5 %collective-permute-start.12 = (bf16[256,768]{1,0:T(8,128)(2,1)S(1)}, bf16[256,768]{1,0:T(8,128)(2,1)S(1)}, u32[]{:S(2)}, u32[]{:S(2)}) collective-permute-start(bf16[256,768]{1,0:T(8,128)(2,1)S(1)} %bitcast.129), channel_id=1, source_target_pairs={{0,6},{2,4},{4,2},{6,0},{1,7},{3,5},{5,3},{7,1},{8,14},{10,12},{12... | collective-permute-start | bytes 1179656 | tf_op jit(solution)/shard_map/ppermute | solution.py:486
  36.9 36.2 %collective-permute-start.3 = (bf16[192,1152]{1,0:T(8,128)(2,1)S(1)}, bf16[192,1152]{1,0:T(8,128)(2,1)}, u32[]{:S(2)}, u32[]{:S(2)}) collective-permute-start(bf16[192,1152]{1,0:T(8,128)(2,1)S(1)} %constant_dynamic-update-slice_fusion.8.refs_4_), channel_id=1, source_target_pairs={{0,1},{1,0},{8,9},{9,8},{16,17},{17,16},{24,25},{25,24},{2,3},{3,2... | collective-permute-start | bytes 1327112 | tf_op jit(solution)/shard_map/ppermute | solution.py:510
  38.4 35.3 %collective-permute-start.6 = (bf16[192,1152]{1,0:T(8,128)(2,1)S(1)}, bf16[192,1152]{1,0:T(8,128)(2,1)}, u32[]{:S(2)}, u32[]{:S(2)}) collective-permute-start(bf16[192,1152]{1,0:T(8,128)(2,1)S(1)} %constant_dynamic-update-slice_fusion.8.refs_4_), channel_id=1, source_target_pairs={{0,16},{1,17},{8,24},{9,25},{16,0},{17,1},{24,8},{25,9},{2,18},{3,... | collective-permute-start | bytes 1327112 | tf_op jit(solution)/shard_map/ppermute | solution.py:510
  42.0 45.7 %collective-permute-start.13 = (bf16[192,1536]{1,0:T(8,128)(2,1)S(1)}, bf16[192,1536]{1,0:T(8,128)(2,1)S(1)}, u32[]{:S(2)}, u32[]{:S(2)}) collective-permute-start(bf16[192,1536]{1,0:T(8,128)(2,1)S(1)} %copy-done.27), channel_id=1, source_target_pairs={{0,1},{1,0},{8,9},{9,8},{16,17},{17,16},{24,25},{25,24},{2,3},{3,2... | collective-permute-start | bytes 1769480 | tf_op jit(solution)/shard_map/ppermute | solution.py:510
  70.6 14.0 %collective-permute-start.7 = (bf16[192,1152]{1,0:T(8,128)(2,1)S(1)}, bf16[192,1152]{1,0:T(8,128)(2,1)S(1)}, u32[]{:S(2)}, u32[]{:S(2)}) collective-permute-start(bf16[192,1152]{1,0:T(8,128)(2,1)S(1)} %constant_dynamic-update-slice_fusion.8.refs_4_), channel_id=1, source_target_pairs={{0,17},{1,16},{8,25},{9,24},{16,1},{17,0},{24,9},{25,8},{2,19},{3,... | collective-permute-start | bytes 1327112 | tf_op jit(solution)/shard_map/ppermute | solution.py:510
  73.1 13.1 %collective-permute-start.4 = (bf16[192,1152]{1,0:T(8,128)(2,1)S(1)}, bf16[192,1152]{1,0:T(8,128)(2,1)S(1)}, u32[]{:S(2)}, u32[]{:S(2)}) collective-permute-start(bf16[192,1152]{1,0:T(8,128)(2,1)S(1)} %constant_dynamic-update-slice_fusion.8.refs_4_), channel_id=1, source_target_pairs={{0,8},{8,0},{16,24},{24,16},{1,9},{9,1},{17,25},{25,17},{2,10},{10... | collective-permute-start | bytes 1327112 | tf_op jit(solution)/shard_map/ppermute | solution.py:513
  73.1 33.2 %collective-permute-start.16 = (bf16[192,1536]{1,0:T(8,128)(2,1)S(1)}, bf16[192,1536]{1,0:T(8,128)(2,1)S(1)}, u32[]{:S(2)}, u32[]{:S(2)}) collective-permute-start(bf16[192,1536]{1,0:T(8,128)(2,1)S(1)} %copy-done.27), channel_id=1, source_target_pairs={{0,16},{1,17},{8,24},{9,25},{16,0},{17,1},{24,8},{25,9},{2,18},{3,... | collective-permute-start | bytes 1769480 | tf_op jit(solution)/shard_map/ppermute | solution.py:510
  73.6 35.1 %collective-permute-start.17 = (bf16[192,1536]{1,0:T(8,128)(2,1)S(1)}, bf16[192,1536]{1,0:T(8,128)(2,1)S(1)}, u32[]{:S(2)}, u32[]{:S(2)}) collective-permute-start(bf16[192,1536]{1,0:T(8,128)(2,1)S(1)} %copy-done.27), channel_id=1, source_target_pairs={{0,17},{1,16},{8,25},{9,24},{16,1},{17,0},{24,9},{25,8},{2,19},{3,... | collective-permute-start | bytes 1769480 | tf_op jit(solution)/shard_map/ppermute | solution.py:510
  84.6 61.1 %collective-permute-start.20 = (bf16[192,1920]{1,0:T(8,128)(2,1)S(1)}, bf16[192,1920]{1,0:T(8,128)(2,1)S(1)}, u32[]{:S(2)}, u32[]{:S(2)}) collective-permute-start(bf16[192,1920]{1,0:T(8,128)(2,1)S(1)} %pad_maximum_fusion.refs_12_), channel_id=1, source_target_pairs={{0,1},{1,0},{8,9},{9,8},{16,17},{17,16},{24,25},{25,24},{2,3},{3,2... | collective-permute-start | bytes 2211848 | tf_op jit(solution)/shard_map/ppermute | solution.py:510
  86.1 60.1 %collective-permute-start.23 = (bf16[192,1920]{1,0:T(8,128)(2,1)S(1)}, bf16[192,1920]{1,0:T(8,128)(2,1)S(1)}, u32[]{:S(2)}, u32[]{:S(2)}) collective-permute-start(bf16[192,1920]{1,0:T(8,128)(2,1)S(1)} %pad_maximum_fusion.refs_12_), channel_id=1, source_target_pairs={{0,16},{1,17},{8,24},{9,25},{16,0},{17,1},{24,8},{25,9},{2,18},{3,... | collective-permute-start | bytes 2211848 | tf_op jit(solution)/shard_map/ppermute | solution.py:510
  87.7 58.0 %collective-permute-start.14 = (bf16[192,1536]{1,0:T(8,128)(2,1)S(1)}, bf16[192,1536]{1,0:T(8,128)(2,1)}, u32[]{:S(2)}, u32[]{:S(2)}) collective-permute-start(bf16[192,1536]{1,0:T(8,128)(2,1)S(1)} %copy-done.27), channel_id=1, source_target_pairs={{0,8},{8,0},{16,24},{24,16},{1,9},{9,1},{17,25},{25,17},{2,10},{10... | collective-permute-start | bytes 1769480 | tf_op jit(solution)/shard_map/ppermute | solution.py:513
  106.3 41.6 %collective-permute-start.24 = (bf16[192,1920]{1,0:T(8,128)(2,1)S(1)}, bf16[192,1920]{1,0:T(8,128)(2,1)}, u32[]{:S(2)}, u32[]{:S(2)}) collective-permute-start(bf16[192,1920]{1,0:T(8,128)(2,1)S(1)} %pad_maximum_fusion.refs_12_), channel_id=1, source_target_pairs={{0,17},{1,16},{8,25},{9,24},{16,1},{17,0},{24,9},{25,8},{2,19},{3,... | collective-permute-start | bytes 2211848 | tf_op jit(solution)/shard_map/ppermute | solution.py:510
  108.7 39.7 %collective-permute-start.21 = (bf16[192,1920]{1,0:T(8,128)(2,1)S(1)}, bf16[192,1920]{1,0:T(8,128)(2,1)}, u32[]{:S(2)}, u32[]{:S(2)}) collective-permute-start(bf16[192,1920]{1,0:T(8,128)(2,1)S(1)} %pad_maximum_fusion.refs_12_), channel_id=1, source_target_pairs={{0,8},{8,0},{16,24},{24,16},{1,9},{9,1},{17,25},{25,17},{2,10},{10... | collective-permute-start | bytes 2211848 | tf_op jit(solution)/shard_map/ppermute | solution.py:513
  148.4 35.9 %collective-permute-start.22 = (bf16[192,1920]{1,0:T(8,128)(2,1)S(1)}, bf16[192,1920]{1,0:T(8,128)(2,1)}, u32[]{:S(2)}, u32[]{:S(2)}) collective-permute-start(bf16[192,1920]{1,0:T(8,128)(2,1)S(1)} %collective-permute-done.20.refs_13_), channel_id=1, source_target_pairs={{0,8},{8,0},{16,24},{24,16},{1,9},{9,1},{17,25},{25,17},{2,10},{10... | collective-permute-start | bytes 2211848 | tf_op jit(solution)/shard_map/ppermute | solution.py:513
  148.6 35.8 %collective-permute-start.25 = (bf16[192,1920]{1,0:T(8,128)(2,1)S(1)}, bf16[192,1920]{1,0:T(8,128)(2,1)}, u32[]{:S(2)}, u32[]{:S(2)}) collective-permute-start(bf16[192,1920]{1,0:T(8,128)(2,1)S(1)} %collective-permute-done.23.refs_16_), channel_id=1, source_target_pairs={{0,8},{8,0},{16,24},{24,16},{1,9},{9,1},{17,25},{25,17},{2,10},{10... | collective-permute-start | bytes 2211848 | tf_op jit(solution)/shard_map/ppermute | solution.py:513
  149.0 35.3 %collective-permute-start.26 = (bf16[192,1920]{1,0:T(8,128)(2,1)}, bf16[192,1920]{1,0:T(8,128)(2,1)}, u32[]{:S(2)}, u32[]{:S(2)}) collective-permute-start(bf16[192,1920]{1,0:T(8,128)(2,1)} %collective-permute-done.24.refs_17_), channel_id=1, source_target_pairs={{0,8},{8,0},{16,24},{24,16},{1,9},{9,1},{17,25},{25,17},{2,10},{10... | collective-permute-start | bytes 2211848 | tf_op jit(solution)/shard_map/ppermute | solution.py:513
  150.0 34.3 %collective-permute-start.18 = (bf16[192,1536]{1,0:T(8,128)(2,1)}, bf16[192,1536]{1,0:T(8,128)(2,1)}, u32[]{:S(2)}, u32[]{:S(2)}) collective-permute-start(bf16[192,1536]{1,0:T(8,128)(2,1)} %copy-done.29), channel_id=1, source_target_pairs={{0,8},{8,0},{16,24},{24,16},{1,9},{9,1},{17,25},{25,17},{2,10},{10... | collective-permute-start | bytes 1769480 | tf_op jit(solution)/shard_map/ppermute | solution.py:513
  150.7 33.6 %collective-permute-start.19 = (bf16[192,1536]{1,0:T(8,128)(2,1)}, bf16[192,1536]{1,0:T(8,128)(2,1)}, u32[]{:S(2)}, u32[]{:S(2)}) collective-permute-start(bf16[192,1536]{1,0:T(8,128)(2,1)} %copy-done.30), channel_id=1, source_target_pairs={{0,8},{8,0},{16,24},{24,16},{1,9},{9,1},{17,25},{25,17},{2,10},{10... | collective-permute-start | bytes 1769480 | tf_op jit(solution)/shard_map/ppermute | solution.py:513
  234.3 71.3 %collective-permute-start.60 = (f32[7680]{0:T(1024)S(1)}, f32[7680]{0:T(1024)S(1)}, u32[]{:S(2)}, u32[]{:S(2)}) collective-permute-start(f32[7680]{0:T(1024)S(1)} %constant_dynamic-update-slice_fusion.14), channel_id=1, source_target_pairs={{0,8},{8,0},{16,24},{24,16},{1,9},{9,1},{17,25},{25,17},{2,10},{10... | collective-permute-start | bytes 92168 | tf_op jit(solution)/shard_map/ppermute | solution.py:590
  239.6 130.2 %collective-permute-start.53 = (bf16[2,2,192,384]{3,2,1,0:T(8,128)(2,1)}, bf16[2,2,192,384]{3,2,1,0:T(8,128)(2,1)}, u32[]{:S(2)}, u32[]{:S(2)}) collective-permute-start(bf16[2,2,192,384]{3,2,1,0:T(8,128)(2,1)} %get-tuple-element.70), channel_id=1, source_target_pairs={{0,8},{8,0},{16,24},{24,16},{1,9},{9,1},{17,25},{25,17},{2,10},{10... | collective-permute-start | bytes 1769480 | tf_op jit(solution)/shard_map/ppermute | solution.py:554
  277.7 14.8 %collective-permute-start.48 = (f32[1536]{0:T(1024)S(1)}, f32[1536]{0:T(1024)S(1)}, u32[]{:S(2)}, u32[]{:S(2)}) collective-permute-start(f32[1536]{0:T(1024)S(1)} %constant_dynamic-update-slice_fusion.13), channel_id=1, source_target_pairs={{0,8},{8,0},{16,24},{24,16},{1,9},{9,1},{17,25},{25,17},{2,10},{10... | collective-permute-start | bytes 18440 | tf_op jit(solution)/shard_map/ppermute | solution.py:590
  277.8 69.2 %collective-permute-start.34 = (bf16[256,768]{1,0:T(8,128)(2,1)}, bf16[256,768]{1,0:T(8,128)(2,1)}, u32[]{:S(2)}, u32[]{:S(2)}) collective-permute-start(bf16[256,768]{1,0:T(8,128)(2,1)} %get-tuple-element.61), channel_id=1, source_target_pairs={{0,1},{1,0},{2,3},{3,2},{4,5},{5,4},{6,7},{7,6},{8,9},{9,8},{10,11... | collective-permute-start | bytes 1179656 | tf_op jit(solution)/shard_map/ppermute | solution.py:494
  277.9 75.7 %collective-permute-start.27 = (bf16[256,768]{1,0:T(8,128)(2,1)S(1)}, bf16[256,768]{1,0:T(8,128)(2,1)}, u32[]{:S(2)}, u32[]{:S(2)}) collective-permute-start(bf16[256,768]{1,0:T(8,128)(2,1)S(1)} %copy-done.7), channel_id=1, source_target_pairs={{0,1},{1,0},{2,3},{3,2},{4,5},{5,4},{6,7},{7,6},{8,9},{9,8},{10,11... | collective-permute-start | bytes 1179656 | tf_op jit(solution)/shard_map/ppermute | solution.py:494
  292.4 13.0 %collective-permute-start.49 = (f32[1536]{0:T(1024)S(1)}, f32[1536]{0:T(1024)S(1)}, u32[]{:S(2)}, u32[]{:S(2)}) collective-permute-start(f32[1536]{0:T(1024)S(1)} %add.280), channel_id=1, source_target_pairs={{0,16},{8,24},{16,0},{24,8},{1,17},{9,25},{17,1},{25,9},{2,18},{10... | collective-permute-start | bytes 18440 | tf_op jit(solution)/shard_map/ppermute | solution.py:590
  305.5 11.8 %collective-permute-start.50 = (f32[1536]{0:T(1024)S(1)}, f32[1536]{0:T(1024)S(1)}, u32[]{:S(2)}, u32[]{:S(2)}) collective-permute-start(f32[1536]{0:T(1024)S(1)} %add.281), channel_id=1, source_target_pairs={{0,1},{1,0},{2,3},{3,2},{4,5},{5,4},{6,7},{7,6},{8,9},{9,8},{10,11... | collective-permute-start | bytes 18440 | tf_op jit(solution)/shard_map/ppermute | solution.py:590
  305.6 14.4 %collective-permute-start.61 = (f32[7680]{0:T(1024)S(1)}, f32[7680]{0:T(1024)S(1)}, u32[]{:S(2)}, u32[]{:S(2)}) collective-permute-start(f32[7680]{0:T(1024)S(1)} %add.292), channel_id=1, source_target_pairs={{0,16},{8,24},{16,0},{24,8},{1,17},{9,25},{17,1},{25,9},{2,18},{10... | collective-permute-start | bytes 92168 | tf_op jit(solution)/shard_map/ppermute | solution.py:590
  317.2 9.1 %collective-permute-start.51 = (f32[1536]{0:T(1024)S(1)}, f32[1536]{0:T(1024)S(1)}, u32[]{:S(2)}, u32[]{:S(2)}) collective-permute-start(f32[1536]{0:T(1024)S(1)} %add.282), channel_id=1, source_target_pairs={{0,2},{2,0},{4,6},{6,4},{1,3},{3,1},{5,7},{7,5},{8,10},{10,8},{12,... | collective-permute-start | bytes 18440 | tf_op jit(solution)/shard_map/ppermute | solution.py:590
  330.9 18.2 %collective-permute-start.35 = (bf16[256,768]{1,0:T(8,128)(2,1)}, bf16[256,768]{1,0:T(8,128)(2,1)}, u32[]{:S(2)}, u32[]{:S(2)}) collective-permute-start(bf16[256,768]{1,0:T(8,128)(2,1)} %get-tuple-element.62), channel_id=1, source_target_pairs={{0,2},{2,0},{4,6},{6,4},{1,3},{3,1},{5,7},{7,5},{8,10},{10,8},{12,... | collective-permute-start | bytes 1179656 | tf_op jit(solution)/shard_map/ppermute | solution.py:492
  338.5 33.2 %collective-permute-start.37 = (bf16[256,768]{1,0:T(8,128)(2,1)}, bf16[256,768]{1,0:T(8,128)(2,1)}, u32[]{:S(2)}, u32[]{:S(2)}) collective-permute-start(bf16[256,768]{1,0:T(8,128)(2,1)} %get-tuple-element.63), channel_id=1, source_target_pairs={{0,4},{2,6},{4,0},{6,2},{1,5},{3,7},{5,1},{7,3},{8,12},{10,14},{12... | collective-permute-start | bytes 1179656 | tf_op jit(solution)/shard_map/ppermute | solution.py:492
  347.1 22.7 %collective-permute-start.28 = (bf16[256,768]{1,0:T(8,128)(2,1)}, bf16[256,768]{1,0:T(8,128)(2,1)S(1)}, u32[]{:S(2)}, u32[]{:S(2)}) collective-permute-start(bf16[256,768]{1,0:T(8,128)(2,1)} %get-tuple-element.52), channel_id=1, source_target_pairs={{0,2},{2,0},{4,6},{6,4},{1,3},{3,1},{5,7},{7,5},{8,10},{10,8},{12,... | collective-permute-start | bytes 1179656 | tf_op jit(solution)/shard_map/ppermute | solution.py:492
  349.1 22.7 %collective-permute-start.39 = (bf16[256,768]{1,0:T(8,128)(2,1)}, bf16[256,768]{1,0:T(8,128)(2,1)S(1)}, u32[]{:S(2)}, u32[]{:S(2)}) collective-permute-start(bf16[256,768]{1,0:T(8,128)(2,1)} %get-tuple-element.64), channel_id=1, source_target_pairs={{0,6},{2,4},{4,2},{6,0},{1,7},{3,5},{5,3},{7,1},{8,14},{10,12},{12... | collective-permute-start | bytes 1179656 | tf_op jit(solution)/shard_map/ppermute | solution.py:492
  353.5 18.9 %collective-permute-start.36 = (bf16[256,768]{1,0:T(8,128)(2,1)}, bf16[256,768]{1,0:T(8,128)(2,1)S(1)}, u32[]{:S(2)}, u32[]{:S(2)}) collective-permute-start(bf16[256,768]{1,0:T(8,128)(2,1)} %collective-permute-done.35), channel_id=1, source_target_pairs={{0,1},{1,0},{2,3},{3,2},{4,5},{5,4},{6,7},{7,6},{8,9},{9,8},{10,11... | collective-permute-start | bytes 1179656 | tf_op jit(solution)/shard_map/ppermute | solution.py:494
  369.8 100.4 %collective-permute-start.72 = (bf16[2,2,192,1536]{3,2,1,0:T(8,128)(2,1)}, bf16[2,2,192,1536]{3,2,1,0:T(8,128)(2,1)S(1)}, u32[]{:S(2)}, u32[]{:S(2)}) collective-permute-start(bf16[2,2,192,1536]{3,2,1,0:T(8,128)(2,1)} %get-tuple-element.80), channel_id=1, source_target_pairs={{0,8},{8,0},{16,24},{24,16},{1,9},{9,1},{17,25},{25,17},{2,10},{10... | collective-permute-start | bytes 7077896 | tf_op jit(solution)/shard_map/ppermute | solution.py:554
  369.8 104.9 %collective-permute-start.65 = (bf16[2,2,192,1536]{3,2,1,0:T(8,128)(2,1)S(1)}, bf16[2,2,192,1536]{3,2,1,0:T(8,128)(2,1)S(1)}, u32[]{:S(2)}, u32[]{:S(2)}) collective-permute-start(bf16[2,2,192,1536]{3,2,1,0:T(8,128)(2,1)S(1)} %copy-done.23), channel_id=1, source_target_pairs={{0,8},{8,0},{16,24},{24,16},{1,9},{9,1},{17,25},{25,17},{2,10},{10... | collective-permute-start | bytes 7077896 | tf_op jit(solution)/shard_map/ppermute | solution.py:554
  371.7 61.1 %collective-permute-start.41 = (bf16[2,2,192,1152]{3,2,1,0:T(8,128)(2,1)S(1)}, bf16[2,2,192,1152]{3,2,1,0:T(8,128)(2,1)S(1)}, u32[]{:S(2)}, u32[]{:S(2)}) collective-permute-start(bf16[2,2,192,1152]{3,2,1,0:T(8,128)(2,1)S(1)} %copy-done.24), channel_id=1, source_target_pairs={{0,8},{8,0},{16,24},{24,16},{1,9},{9,1},{17,25},{25,17},{2,10},{10... | collective-permute-start | bytes 5308424 | tf_op jit(solution)/shard_map/ppermute | solution.py:554
  371.8 12.3 %collective-permute-start.38 = (bf16[256,768]{1,0:T(8,128)(2,1)}, bf16[256,768]{1,0:T(8,128)(2,1)S(1)}, u32[]{:S(2)}, u32[]{:S(2)}) collective-permute-start(bf16[256,768]{1,0:T(8,128)(2,1)} %collective-permute-done.37), channel_id=1, source_target_pairs={{0,1},{1,0},{2,3},{3,2},{4,5},{5,4},{6,7},{7,6},{8,9},{9,8},{10,11... | collective-permute-start | bytes 1179656 | tf_op jit(solution)/shard_map/ppermute | solution.py:494
  372.4 20.2 %collective-permute-start.40 = (bf16[256,768]{1,0:T(8,128)(2,1)S(1)}, bf16[256,768]{1,0:T(8,128)(2,1)S(1)}, u32[]{:S(2)}, u32[]{:S(2)}) collective-permute-start(bf16[256,768]{1,0:T(8,128)(2,1)S(1)} %collective-permute-done.39), channel_id=1, source_target_pairs={{0,1},{1,0},{2,3},{3,2},{4,5},{5,4},{6,7},{7,6},{8,9},{9,8},{10,11... | collective-permute-start | bytes 1179656 | tf_op jit(solution)/shard_map/ppermute | solution.py:494
  392.0 10.8 %collective-permute-start.29 = (bf16[256,768]{1,0:T(8,128)(2,1)S(1)}, bf16[256,768]{1,0:T(8,128)(2,1)S(1)}, u32[]{:S(2)}, u32[]{:S(2)}) collective-permute-start(bf16[256,768]{1,0:T(8,128)(2,1)S(1)} %collective-permute-done.28), channel_id=1, source_target_pairs={{0,1},{1,0},{2,3},{3,2},{4,5},{5,4},{6,7},{7,6},{8,9},{9,8},{10,11... | collective-permute-start | bytes 1179656 | tf_op jit(solution)/shard_map/ppermute | solution.py:494
  392.6 11.7 %collective-permute-start.55 = (bf16[1,192,384]{2,1,0:T(8,128)(2,1)S(1)}, bf16[1,192,384]{2,1,0:T(8,128)(2,1)S(1)}, u32[]{:S(2)}, u32[]{:S(2)}) collective-permute-start(bf16[1,192,384]{2,1,0:T(8,128)(2,1)S(1)} %slice_bitcast_fusion.6), channel_id=1, source_target_pairs={{0,1},{1,0},{2,3},{3,2},{4,5},{5,4},{6,7},{7,6},{8,9},{9,8},{10,11... | collective-permute-start | bytes 442376 | tf_op jit(solution)/shard_map/ppermute | solution.py:561
  402.8 25.1 %collective-permute-start.30 = (bf16[256,768]{1,0:T(8,128)(2,1)S(1)}, bf16[256,768]{1,0:T(8,128)(2,1)S(1)}, u32[]{:S(2)}, u32[]{:S(2)}) collective-permute-start(bf16[256,768]{1,0:T(8,128)(2,1)S(1)} %copy-done.42), channel_id=1, source_target_pairs={{0,4},{2,6},{4,0},{6,2},{1,5},{3,7},{5,1},{7,3},{8,12},{10,14},{12... | collective-permute-start | bytes 1179656 | tf_op jit(solution)/shard_map/ppermute | solution.py:492
  404.3 23.6 %collective-permute-start.32 = (bf16[256,768]{1,0:T(8,128)(2,1)S(1)}, bf16[256,768]{1,0:T(8,128)(2,1)S(1)}, u32[]{:S(2)}, u32[]{:S(2)}) collective-permute-start(bf16[256,768]{1,0:T(8,128)(2,1)S(1)} %copy-done.41), channel_id=1, source_target_pairs={{0,6},{2,4},{4,2},{6,0},{1,7},{3,5},{5,3},{7,1},{8,14},{10,12},{12... | collective-permute-start | bytes 1179656 | tf_op jit(solution)/shard_map/ppermute | solution.py:492
  427.9 12.1 %collective-permute-start.31 = (bf16[256,768]{1,0:T(8,128)(2,1)S(1)}, bf16[256,768]{1,0:T(8,128)(2,1)S(1)}, u32[]{:S(2)}, u32[]{:S(2)}) collective-permute-start(bf16[256,768]{1,0:T(8,128)(2,1)S(1)} %collective-permute-done.30), channel_id=1, source_target_pairs={{0,1},{1,0},{2,3},{3,2},{4,5},{5,4},{6,7},{7,6},{8,9},{9,8},{10,11... | collective-permute-start | bytes 1179656 | tf_op jit(solution)/shard_map/ppermute | solution.py:494
  432.2 27.2 %collective-permute-start.33 = (bf16[256,768]{1,0:T(8,128)(2,1)S(1)}, bf16[256,768]{1,0:T(8,128)(2,1)S(1)}, u32[]{:S(2)}, u32[]{:S(2)}) collective-permute-start(bf16[256,768]{1,0:T(8,128)(2,1)S(1)} %collective-permute-done.32), channel_id=1, source_target_pairs={{0,1},{1,0},{2,3},{3,2},{4,5},{5,4},{6,7},{7,6},{8,9},{9,8},{10,11... | collective-permute-start | bytes 1179656 | tf_op jit(solution)/shard_map/ppermute | solution.py:494
  433.4 25.0 %collective-permute-start.42 = (bf16[1,2,192,1152]{3,2,1,0:T(8,128)(2,1)S(1)}, bf16[1,2,192,1152]{3,2,1,0:T(8,128)(2,1)S(1)}, u32[]{:S(2)}, u32[]{:S(2)}) collective-permute-start(bf16[1,2,192,1152]{3,2,1,0:T(8,128)(2,1)S(1)} %slice.223), channel_id=1, source_target_pairs={{0,16},{8,24},{16,0},{24,8},{1,17},{9,25},{17,1},{25,9},{2,18},{10... | collective-permute-start | bytes 2654216 | tf_op jit(solution)/shard_map/ppermute | solution.py:557
  440.0 10.2 %collective-permute-start.57 = (bf16[48,384]{1,0:T(8,128)(2,1)S(1)}, bf16[48,384]{1,0:T(8,128)(2,1)S(1)}, u32[]{:S(2)}, u32[]{:S(2)}) collective-permute-start(bf16[48,384]{1,0:T(8,128)(2,1)S(1)} %constant_dynamic-slice_fusion.3), channel_id=1, source_target_pairs={{0,4},{2,6},{4,0},{6,2},{1,5},{3,7},{5,1},{7,3},{8,12},{10,14},{12... | collective-permute-start | bytes 110600 | tf_op jit(solution)/shard_map/ppermute | solution.py:567
  458.7 8.4 %collective-permute-start.43 = (bf16[1,192,1152]{2,1,0:T(8,128)(2,1)S(1)}, bf16[1,192,1152]{2,1,0:T(8,128)(2,1)S(1)}, u32[]{:S(2)}, u32[]{:S(2)}) collective-permute-start(bf16[1,192,1152]{2,1,0:T(8,128)(2,1)S(1)} %slice_bitcast_fusion.4), channel_id=1, source_target_pairs={{0,1},{1,0},{2,3},{3,2},{4,5},{5,4},{6,7},{7,6},{8,9},{9,8},{10,11... | collective-permute-start | bytes 1327112 | tf_op jit(solution)/shard_map/ppermute | solution.py:561
  470.9 28.9 %collective-permute-start.73 = (bf16[1,2,192,1536]{3,2,1,0:T(8,128)(2,1)S(1)}, bf16[1,2,192,1536]{3,2,1,0:T(8,128)(2,1)S(1)}, u32[]{:S(2)}, u32[]{:S(2)}) collective-permute-start(bf16[1,2,192,1536]{3,2,1,0:T(8,128)(2,1)S(1)} %slice.245), channel_id=1, source_target_pairs={{0,16},{8,24},{16,0},{24,8},{1,17},{9,25},{17,1},{25,9},{2,18},{10... | collective-permute-start | bytes 3538952 | tf_op jit(solution)/shard_map/ppermute | solution.py:557
  474.6 8.8 %collective-permute-start.45 = (bf16[48,1152]{1,0:T(8,128)(2,1)S(1)}, bf16[48,1152]{1,0:T(8,128)(2,1)S(1)}, u32[]{:S(2)}, u32[]{:S(2)}) collective-permute-start(bf16[48,1152]{1,0:T(8,128)(2,1)S(1)} %constant_dynamic-slice_fusion.4), channel_id=1, source_target_pairs={{0,4},{2,6},{4,0},{6,2},{1,5},{3,7},{5,1},{7,3},{8,12},{10,14},{12... | collective-permute-start | bytes 331784 | tf_op jit(solution)/shard_map/ppermute | solution.py:567
  475.4 45.6 %collective-permute-start.66 = (bf16[1,2,192,1536]{3,2,1,0:T(8,128)(2,1)S(1)}, bf16[1,2,192,1536]{3,2,1,0:T(8,128)(2,1)S(1)}, u32[]{:S(2)}, u32[]{:S(2)}) collective-permute-start(bf16[1,2,192,1536]{3,2,1,0:T(8,128)(2,1)S(1)} %slice.240), channel_id=1, source_target_pairs={{0,16},{8,24},{16,0},{24,8},{1,17},{9,25},{17,1},{25,9},{2,18},{10... | collective-permute-start | bytes 3538952 | tf_op jit(solution)/shard_map/ppermute | solution.py:557
  483.4 17.2 %collective-permute-start.46 = (bf16[48,1152]{1,0:T(8,128)(2,1)S(1)}, bf16[48,1152]{1,0:T(8,128)(2,1)S(1)}, u32[]{:S(2)}, u32[]{:S(2)}) collective-permute-start(bf16[48,1152]{1,0:T(8,128)(2,1)S(1)} %add_convert_fusion.10), channel_id=1, source_target_pairs={{0,4},{2,6},{4,0},{6,2},{1,5},{3,7},{5,1},{7,3},{8,12},{10,14},{12... | collective-permute-start | bytes 331784 | tf_op jit(solution)/shard_map/ppermute | solution.py:572
  500.1 22.7 %collective-permute-start.74 = (bf16[1,192,1536]{2,1,0:T(8,128)(2,1)S(1)}, bf16[1,192,1536]{2,1,0:T(8,128)(2,1)S(1)}, u32[]{:S(2)}, u32[]{:S(2)}) collective-permute-start(bf16[1,192,1536]{2,1,0:T(8,128)(2,1)S(1)} %slice_bitcast_fusion), channel_id=1, source_target_pairs={{0,1},{1,0},{2,3},{3,2},{4,5},{5,4},{6,7},{7,6},{8,9},{9,8},{10,11... | collective-permute-start | bytes 1769480 | tf_op jit(solution)/shard_map/ppermute | solution.py:561
  500.7 21.1 %collective-permute-start.47 = (bf16[96,1152]{1,0:T(8,128)(2,1)S(1)}, bf16[96,1152]{1,0:T(8,128)(2,1)S(1)}, u32[]{:S(2)}, u32[]{:S(2)}) collective-permute-start(bf16[96,1152]{1,0:T(8,128)(2,1)S(1)} %pad_maximum_fusion.3), channel_id=1, source_target_pairs={{0,2},{2,0},{4,6},{6,4},{1,3},{3,1},{5,7},{7,5},{8,10},{10,8},{12,... | collective-permute-start | bytes 663560 | tf_op jit(solution)/shard_map/ppermute | solution.py:572
  521.4 11.4 %collective-permute-start.67 = (bf16[1,192,1536]{2,1,0:T(8,128)(2,1)S(1)}, bf16[1,192,1536]{2,1,0:T(8,128)(2,1)S(1)}, u32[]{:S(2)}, u32[]{:S(2)}) collective-permute-start(bf16[1,192,1536]{2,1,0:T(8,128)(2,1)S(1)} %slice_bitcast_fusion.2), channel_id=1, source_target_pairs={{0,1},{1,0},{2,3},{3,2},{4,5},{5,4},{6,7},{7,6},{8,9},{9,8},{10,11... | collective-permute-start | bytes 1769480 | tf_op jit(solution)/shard_map/ppermute | solution.py:561
  523.0 10.6 %collective-permute-start.75 = (bf16[96,1536]{1,0:T(8,128)(2,1)S(1)}, bf16[96,1536]{1,0:T(8,128)(2,1)S(1)}, u32[]{:S(2)}, u32[]{:S(2)}) collective-permute-start(bf16[96,1536]{1,0:T(8,128)(2,1)S(1)} %dynamic-slice_bitcast_fusion), channel_id=1, source_target_pairs={{0,2},{2,0},{4,6},{6,4},{1,3},{3,1},{5,7},{7,5},{8,10},{10,8},{12,... | collective-permute-start | bytes 884744 | tf_op jit(solution)/shard_map/ppermute | solution.py:567
  533.7 15.4 %collective-permute-start.76 = (bf16[48,1536]{1,0:T(8,128)(2,1)S(1)}, bf16[48,1536]{1,0:T(8,128)(2,1)S(1)}, u32[]{:S(2)}, u32[]{:S(2)}) collective-permute-start(bf16[48,1536]{1,0:T(8,128)(2,1)S(1)} %constant_dynamic-slice_fusion.1), channel_id=1, source_target_pairs={{0,4},{2,6},{4,0},{6,2},{1,5},{3,7},{5,1},{7,3},{8,12},{10,14},{12... | collective-permute-start | bytes 442376 | tf_op jit(solution)/shard_map/ppermute | solution.py:567
  540.1 15.3 %collective-permute-start.69 = (bf16[48,1536]{1,0:T(8,128)(2,1)S(1)}, bf16[48,1536]{1,0:T(8,128)(2,1)S(1)}, u32[]{:S(2)}, u32[]{:S(2)}) collective-permute-start(bf16[48,1536]{1,0:T(8,128)(2,1)S(1)} %constant_dynamic-slice_fusion.2), channel_id=1, source_target_pairs={{0,4},{2,6},{4,0},{6,2},{1,5},{3,7},{5,1},{7,3},{8,12},{10,14},{12... | collective-permute-start | bytes 442376 | tf_op jit(solution)/shard_map/ppermute | solution.py:567
  549.1 9.4 %collective-permute-start.77 = (bf16[48,1536]{1,0:T(8,128)(2,1)S(1)}, bf16[48,1536]{1,0:T(8,128)(2,1)S(1)}, u32[]{:S(2)}, u32[]{:S(2)}) collective-permute-start(bf16[48,1536]{1,0:T(8,128)(2,1)S(1)} %add_convert_fusion.8), channel_id=1, source_target_pairs={{0,4},{2,6},{4,0},{6,2},{1,5},{3,7},{5,1},{7,3},{8,12},{10,14},{12... | collective-permute-start | bytes 442376 | tf_op jit(solution)/shard_map/ppermute | solution.py:572
  558.6 9.9 %collective-permute-start.78 = (bf16[96,1536]{1,0:T(8,128)(2,1)S(1)}, bf16[96,1536]{1,0:T(8,128)(2,1)S(1)}, u32[]{:S(2)}, u32[]{:S(2)}) collective-permute-start(bf16[96,1536]{1,0:T(8,128)(2,1)S(1)} %pad_maximum_fusion.2), channel_id=1, source_target_pairs={{0,2},{2,0},{4,6},{6,4},{1,3},{3,1},{5,7},{7,5},{8,10},{10,8},{12,... | collective-permute-start | bytes 884744 | tf_op jit(solution)/shard_map/ppermute | solution.py:572
  561.7 11.3 %collective-permute-start.71 = (bf16[96,1536]{1,0:T(8,128)(2,1)S(1)}, bf16[96,1536]{1,0:T(8,128)(2,1)S(1)}, u32[]{:S(2)}, u32[]{:S(2)}) collective-permute-start(bf16[96,1536]{1,0:T(8,128)(2,1)S(1)} %pad_maximum_fusion.1), channel_id=1, source_target_pairs={{0,2},{2,0},{4,6},{6,4},{1,3},{3,1},{5,7},{7,5},{8,10},{10,8},{12,... | collective-permute-start | bytes 884744 | tf_op jit(solution)/shard_map/ppermute | solution.py:572
  (60 other events, 2210.3 us)

commit v2 on v1

--- a/solution.py
+++ b/solution.py
@@ -13,6 +13,7 @@
 F32 = jnp.float32
 ANY = pl.BlockSpec(memory_space=pl.ANY)
 SMEM = pl.BlockSpec(memory_space=pltpu.SMEM)
+EXTRA = 16
 VMEM_LIMIT = 60 * 1024 * 1024
 
 
@@ -42,10 +43,35 @@
     return pl.multiple_of(pair // per * (3 * half_cols) + pair % per * 128, 128)
 
 
-def front_kernel(dims, meta, bias, *refs):
+def order_of(F, T, across):
+    chip = [("fsdp", 1 << b) for b in range(1, F.bit_length() - 1)]
+    pair = [("tp", 1 << b) for b in range(T.bit_length() - 1)]
+    return chip + pair if across else pair + chip
+
+
+def stacks(F, T, across):
+    held, out = [(0, 0)], []
+    steps = order_of(F, T, across)
+    for n, (axis, bit) in enumerate(steps):
+        got = [(df ^ bit, dt) if axis == "fsdp" else (df, dt ^ bit) for df, dt in held]
+        if n == len(steps) - 1:
+            out += [held, got]
+        held = held + got
+    return out + [[(df ^ 1, dt) for df, dt in part] for part in out]
+
+
+def pieces_of(refs, F, T, across):
+    return {
+        at: ref.at[i] for ref, part in zip(refs, stacks(F, T, across)) for i, at in enumerate(part)
+    }
+
+
+def front_kernel(dims, meta, *refs):
     F, C, T, ns, span, D = dims
-    xs, ws = refs[:C], refs[C : C + F * T]
-    x_out, w_out, qkv, e_out, linv_out, ctx, sems = refs[C + F * T :]
+    n_w = F * T
+    n_a = len(stacks(F, T, False))
+    xs, low_refs, high_refs = refs[:C], refs[C : C + n_a], refs[C + n_a : C + 2 * n_a]
+    x_out, w_out, qkv, e_out, linv_out, ctx, small, bias, sems = refs[C + 2 * n_a :]
     step = pl.program_id(0)
     NP = D // 128
     L = C * span
@@ -56,22 +82,33 @@
     @pl.when(step == 0)
     def _():
         copies = [pltpu.make_async_copy(xs[k], x_out.at[k], sems.at[k]) for k in range(C)]
+        qk = pieces_of(low_refs, F, T, False)
+        vo = pieces_of(high_refs, F, T, True)
         for df in range(F):
             for dt in range(T):
                 n = df * T + dt
-                row = pl.multiple_of((f ^ df) * Dl, 16)
-                copies.append(
+                rows = pl.ds(pl.multiple_of((f ^ df) * Dl, 16), Dl)
+                start = dt * 3 * half
+                copies += [
                     pltpu.make_async_copy(
-                        ws[n],
-                        w_out.at[pl.ds(row, Dl), pl.ds(dt * 3 * half, 3 * half)],
-                        sems.at[C + n],
-                    )
-                )
+                        qk[df, dt].at[pl.ds(0, Dl)], w_out.at[rows, pl.ds(start, 2 * half)],
+                        sems.at[C + n]),
+                    pltpu.make_async_copy(
+                        vo[df, dt].at[pl.ds(0, Dl), pl.ds(0, half)],
+                        w_out.at[rows, pl.ds(start + 2 * half, half)], sems.at[C + n_w + n]),
+                    pltpu.make_async_copy(
+                        qk[df, dt].at[pl.ds(Dl, EXTRA), pl.ds(0, half)], small.at[n],
+                        sems.at[C + 2 * n_w + n]),
+                ]
         for copy in copies:
             copy.start()
         for copy in copies:
             copy.wait()
-        x = x_out[...].reshape(L * ns, D)
+        bias[...] = jnp.zeros_like(bias)
+        for dt in range(T):
+            part = sum(small[df * T + dt, :2, :].astype(F32) for df in range(F))
+            bias[:, dt * 3 * half : dt * 3 * half + half] = part[0:1]
+            bias[:, (dt * 3 + 2) * half : (dt * 3 + 3) * half] = part[1:2]
 
         def project(j, carry):
             cols = pl.ds(pl.multiple_of(j * 384, 128), 384)
@@ -110,7 +147,7 @@
     )
 
 
-def front_call(dims, meta, bias, xs, ws):
+def front_call(dims, meta, xs, lows, highs):
     F, C, T, ns, span, D = dims
     NP, L = D // 128, C * span
     rows = ns * span
@@ -127,7 +164,7 @@
         name="front",
         grid=(ns * NP,),
         out_shape=shapes,
-        in_specs=[SMEM, const_spec((1, 3 * D))] + [ANY] * (C + F * T),
+        in_specs=[SMEM] + [ANY] * (C + len(lows) + len(highs)),
         out_specs=[
             const_spec(shapes[0].shape),
             const_spec(shapes[1].shape),
@@ -136,10 +173,14 @@
             pl.BlockSpec((1, L, 128), lambda i: (i, 0, 0)),
             const_spec(shapes[5].shape),
         ],
-        scratch_shapes=[pltpu.SemaphoreType.DMA((C + F * T,))],
+        scratch_shapes=[
+            pltpu.VMEM((F * T, EXTRA, D // T), BF),
+            pltpu.VMEM((1, 3 * D), F32),
+            pltpu.SemaphoreType.DMA((C + 3 * F * T,)),
+        ],
         compiler_params=pltpu.CompilerParams(vmem_limit_bytes=VMEM_LIMIT),
         cost_estimate=cost(2 * L * ns * D * 3 * D, 40e6, ns * 12 * L * L),
-    )(meta, bias, *xs, *ws)
+    )(meta, *xs, *lows, *highs)
 
 
 def normalised(values):
@@ -156,15 +197,19 @@
     return rstd * (scaled - first - xhat * second)
 
 
-def rows_kernel(dims, FF, meta, vec, inner_bias, x_ref, ctx_ref, *refs):
+def rows_kernel(dims, FF, meta, x_ref, ctx_ref, *refs):
     F, C, T, ns, span, D = dims
     n_w = F * T
-    cots, wis, bds = refs[:C], refs[C : C + n_w], refs[C + n_w : C + 2 * n_w]
-    refs = refs[C + 2 * n_w :]
+    n_a = len(stacks(F, T, False))
+    cots = refs[:C]
+    qk, vo, inner, outer = (
+        pieces_of(refs[C + i * n_a : C + (i + 1) * n_a], F, T, i % 2 == 1) for i in range(4)
+    )
+    refs = refs[C + 4 * n_a :]
     los = refs[:C]
     (
-        first_out, dctx_out, nl_out, act_out, og_out, ig_out, ag_out, sums, inner_sums,
-        cot_s, lo_s, wi, wo, wout, gp_s, sems, out_sems,
+        first_out, dctx_out, nl_out, act_out, og_out, ig_out, ag_out, sums,
+        cot_s, lo_s, wi, wo, wout, gp_s, small, vec, inner_bias, sems, out_sems,
     ) = refs[C:]
     k = pl.program_id(0)
     R = ns * span
@@ -181,36 +226,46 @@
                 rows = pl.ds(row, Dl)
                 copies.append((
                     pltpu.make_async_copy(
-                        bds[n].at[:, pl.ds(0, half)],
+                        vo[df, dt].at[pl.ds(0, Dl), pl.ds(half, half)],
                         wo.at[rows, pl.ds(dt * half, half)], sems.at[n]),
                     pltpu.make_async_copy(
-                        wis[n], wi.at[rows, pl.ds(dt * fhalf, fhalf)], sems.at[n_w + n]),
+                        inner[df, dt],
+                        wi.at[rows, pl.ds(dt * fhalf, fhalf)], sems.at[n_w + n]),
                     pltpu.make_async_copy(
-                        bds[n].at[:, pl.ds(half, fhalf)],
+                        outer[df, dt],
                         wout.at[rows, pl.ds(dt * fhalf, fhalf)], sems.at[2 * n_w + n]),
+                ) + tuple(
+                    pltpu.make_async_copy(
+                        (qk if part == 0 else vo)[df, dt].at[pl.ds(Dl, EXTRA)],
+                        small.at[n, :, pl.ds(part * D, D)], sems.at[(3 + part) * n_w + n])
+                    for part in range(2)
                 ))
         return copies
 
     def cot_copies():
         return [
-            pltpu.make_async_copy(cots[i], cot_s.at[i], sems.at[3 * n_w + i]) for i in range(C)
+            pltpu.make_async_copy(cots[i], cot_s.at[i], sems.at[5 * n_w + i]) for i in range(C)
         ]
 
     @pl.when(k == 0)
     def _():
         copies = weight_copies()
-        for which in range(3):
+        for which in range(5):
             for group in copies:
                 group[which].start()
         for copy in cot_copies():
             copy.start()
         sums[...] = jnp.zeros_like(sums)
-        inner_sums[...] = jnp.zeros_like(inner_sums)
-        for which in range(3):
+        for which in range(5):
             for group in copies:
                 group[which].wait()
         for copy in cot_copies():
             copy.wait()
+        for dt in range(T):
+            part = sum(small[df * T + dt, :EXTRA, :].astype(F32) for df in range(F))
+            inner_bias[:, dt * fhalf : (dt + 1) * fhalf] = part[2:3]
+            if dt == 0:
+                vec[...] = part[3:9, :D]
 
     def add_sum(row, value):
         sums[row : row + 1, :] += jnp.sum(value, axis=0, keepdims=True)
@@ -259,7 +314,6 @@
         cols = slice(j * chunk, (j + 1) * chunk)
         ig = (dot_nn(og, wout[:, cols]) * gp_s[:, cols]).astype(BF)
         ig_out[0, :, cols] = ig
-        inner_sums[:, cols] += jnp.sum(ig.astype(F32), axis=0, keepdims=True)
     ngrad = dot_nt(ig_out[0], wi[...]) + second
     add_sum(1, ngrad * xhat1)
     add_sum(2, ngrad)
@@ -276,7 +330,7 @@
             pltpu.make_async_copy(lo_s.at[i], los[i], out_sems.at[i]).wait()
 
 
-def rows_call(dims, FF, meta, vec, inner_bias, x_all, ctx, cots, wis, bds):
+def rows_call(dims, FF, meta, x_all, ctx, cots, weights):
     F, C, T, ns, span, D = dims
     R = ns * span
     tile = lambda n: pl.BlockSpec((1, R, n), lambda i: (i, 0, 0))
@@ -284,7 +338,7 @@
     out_shape = (
         [jax.ShapeDtypeStruct((R, D), BF)] * C
         + [jax.ShapeDtypeStruct((C, R, n), kind) for n, kind in widths]
-        + [jax.ShapeDtypeStruct((8, D), F32), jax.ShapeDtypeStruct((1, FF), F32)]
+        + [jax.ShapeDtypeStruct((EXTRA, D), F32)]
     )
     n_w = F * T
     outs = pl.pallas_call(
@@ -292,11 +346,11 @@
         name="rows",
         grid=(C,),
         out_shape=out_shape,
-        in_specs=[SMEM, const_spec((8, D)), const_spec((1, FF)), tile(D), tile(D)]
-        + [ANY] * (C + 2 * n_w),
+        in_specs=[SMEM, tile(D), tile(D)]
+        + [ANY] * (C + len(weights)),
         out_specs=[ANY] * C
         + [tile(n) for n, _ in widths]
-        + [const_spec((8, D)), const_spec((1, FF))],
+        + [const_spec((EXTRA, D))],
         scratch_shapes=[
             pltpu.VMEM((C, R, D), BF),
             pltpu.VMEM((C, R, D), BF),
@@ -304,12 +358,15 @@
             pltpu.VMEM((D, D), BF),
             pltpu.VMEM((D, FF), BF),
             pltpu.VMEM((R, FF), F32),
-            pltpu.SemaphoreType.DMA((3 * n_w + C,)),
+            pltpu.VMEM((n_w, EXTRA, FF // T), BF),
+            pltpu.VMEM((6, D), F32),
+            pltpu.VMEM((1, FF), F32),
+            pltpu.SemaphoreType.DMA((5 * n_w + C,)),
             pltpu.SemaphoreType.DMA((C,)),
         ],
         compiler_params=pltpu.CompilerParams(vmem_limit_bytes=VMEM_LIMIT),
         cost_estimate=cost(4 * C * R * D * (2 * FF + D), 50e6, C * R * FF),
-    )(meta, vec, inner_bias, x_all, ctx, *cots, *wis, *bds)
+    )(meta, x_all, ctx, *cots, *weights)
     return outs[:C], outs[C:]
 
 
@@ -373,16 +430,9 @@
 
 
 def input_kernel(C, dqkv, w, first, *refs):
-    outs, (sums, buf, sems) = refs[:C], refs[C:]
+    outs, (buf, sems) = refs[:C], refs[C:]
     k = pl.program_id(0)
-    d = dqkv[0]
-
-    @pl.when(k == 0)
-    def _():
-        sums[...] = jnp.zeros_like(sums)
-
-    sums[...] += jnp.sum(d.astype(F32), axis=0, keepdims=True)
-    buf[k] = (dot_nt(d, w[...]) + first[0]).astype(BF)
+    buf[k] = (dot_nt(dqkv[0], w[...]) + first[0]).astype(BF)
     for i in range(C):
         @pl.when(k == i)
         def _():
@@ -397,66 +447,109 @@
 def input_call(dqkv, w, first):
     C, R, W = dqkv.shape
     D = w.shape[0]
-    outs = pl.pallas_call(
+    return pl.pallas_call(
         functools.partial(input_kernel, C),
         name="input_grad",
         grid=(C,),
-        out_shape=[jax.ShapeDtypeStruct((R, D), BF)] * C + [jax.ShapeDtypeStruct((1, W), F32)],
+        out_shape=[jax.ShapeDtypeStruct((R, D), BF)] * C,
         in_specs=[
             pl.BlockSpec((1, R, W), lambda i: (i, 0, 0)),
             const_spec(w.shape),
             pl.BlockSpec((1, R, D), lambda i: (i, 0, 0)),
         ],
-        out_specs=[ANY] * C + [const_spec((1, W))],
+        out_specs=[ANY] * C,
         scratch_shapes=[pltpu.VMEM((C, R, D), BF), pltpu.SemaphoreType.DMA((C,))],
         compiler_params=pltpu.CompilerParams(vmem_limit_bytes=VMEM_LIMIT),
         cost_estimate=cost(2 * C * R * D * W, 15e6, 0),
     )(dqkv, w, first)
-    return outs[:C], outs[C]
-
-
-def weight_kernel(F, meta, left, right, keep, send, left_t, tile):
-    D = left.shape[1]
+
+
+COLS = 384
+
+
+def weight_kernel(F, pers, with_sums, meta, *refs):
+    n = len(pers)
+    lefts, rights = refs[:n], refs[n : 2 * n]
+    refs = refs[2 * n :]
+    sums, refs = (refs[0], refs[1:]) if with_sums else (None, refs)
+    keep, send, tile = refs[:3]
+    turned = refs[3:]
+    D = lefts[0].shape[1]
     Dl = D // F
-
-    @pl.when((pl.program_id(0) == 0) & (pl.program_id(1) == 0))
+    b = pl.program_id(1)
+
+    @pl.when((pl.program_id(0) == 0) & (b == 0))
     def _():
-        left_t[...] = left[...].T
-
-    tile[...] = dot_nn(left_t[...], right[...]).astype(BF)
+        for left, left_t in zip(lefts, turned):
+            left_t[:D, :] = left[...].T
+            left_t[D:, :] = jnp.ones((EXTRA, left.shape[0]), BF)
+
+    start = 0
+    for right, left_t, per in zip(rights, turned, pers):
+        @pl.when((b >= start) & (b < start + per))
+        def _():
+            tile[...] = dot_nn(left_t[...], right[...]).astype(BF)
+        start += per
+    if with_sums:
+        for j in range(D // COLS):
+            @pl.when(b == j)
+            def _():
+                tile[D:, :] = sums[:, j * COLS : (j + 1) * COLS].astype(BF)
     f = meta[0]
     for high in range(F // 2):
         for bit, out in ((0, keep), (1, send)):
             row = pl.multiple_of((f ^ (2 * high + bit)) * Dl, 16)
-            out[high, 0] = tile[pl.ds(row, Dl), :]
-
-
-def weight_call(dims, meta, left, right):
+            out[high, 0, :Dl] = tile[pl.ds(row, Dl), :]
+            out[high, 0, Dl:] = tile[D:, :]
+
+
+def weight_call(dims, meta, pairs, sums=None):
     F, C, T, ns, span, D = dims
-    rows, width = right.shape
-    cols = 384
-    per = width // T // cols
-    out = jax.ShapeDtypeStruct((F // 2, T, D // F, width // T), BF)
-    out_spec = pl.BlockSpec((F // 2, 1, D // F, cols), lambda a, b: (0, a, 0, b))
+    rows = C * ns * span
+    pairs = [(left.reshape(rows, -1), right.reshape(rows, -1)) for left, right in pairs]
+    pers = [right.shape[1] // T // COLS for _, right in pairs]
+    width = sum(pers) * COLS
+    out = jax.ShapeDtypeStruct((F // 2, T, D // F + EXTRA, width), BF)
+    out_spec = pl.BlockSpec((F // 2, 1, D // F + EXTRA, COLS), lambda a, b: (0, a, 0, b))
+    right_specs, start = [], 0
+    for per in pers:
+        right_specs.append(
+            pl.BlockSpec(
+                (rows, COLS),
+                lambda a, b, per=per, start=start: (0, a * per + jnp.clip(b - start, 0, per - 1)),
+            )
+        )
+        start += per
     return pl.pallas_call(
-        functools.partial(weight_kernel, F),
+        functools.partial(weight_kernel, F, pers, sums is not None),
         name="weight_grad",
-        grid=(T, per),
+        grid=(T, sum(pers)),
         out_shape=[out, out],
-        in_specs=[
-            SMEM,
-            const_spec(left.shape),
-            pl.BlockSpec((rows, cols), lambda a, b: (0, a * per + b)),
-        ],
+        in_specs=[SMEM]
+        + [const_spec(left.shape) for left, _ in pairs]
+        + right_specs
+        + ([] if sums is None else [const_spec(sums.shape)]),
         out_specs=[out_spec, out_spec],
-        scratch_shapes=[pltpu.VMEM((D, rows), BF), pltpu.VMEM((D, cols), BF)],
+        scratch_shapes=[pltpu.VMEM((D + EXTRA, COLS), BF)]
+        + [pltpu.VMEM((D + EXTRA, rows), BF) for _ in pairs],
         compiler_params=pltpu.CompilerParams(vmem_limit_bytes=VMEM_LIMIT),
-        cost_estimate=cost(2 * rows * D * width, 2 * (rows * (D + width) + D * width), 0),
-    )(meta, left, right)
+        cost_estimate=cost(
+            2 * rows * D * width * T, 2 * (rows * (D + width * T) + D * width * T), 0
+        ),
+    )(
+        meta,
+        *[left for left, _ in pairs],
+        *[right for _, right in pairs],
+        *([] if sums is None else [sums]),
+    )
 
 
 def xor_pairs(count, mask):
     return [(i, i ^ mask) for i in range(count)]
+
+
+def after(value, others):
+    return lax.optimization_barrier((value, *others))[0]
 
 
 def added(a, b):
@@ -475,7 +568,6 @@
     Dl, half = D // F, D // T
     fhalf = inner_weight.shape[1]
     FF = fhalf * T
-    H = query_bias.shape[0] * T
     R = ns * span
     dims = (F, C, T, ns, span, D)
 
@@ -486,134 +578,150 @@
             out.append(lax.ppermute(piece, "ctx", xor_pairs(C, k)) if k else piece)
         return out
 
+    def ctx_moved(piece, k):
+        return lax.ppermute(piece, "ctx", xor_pairs(C, k)) if k else piece
+
+    def tp_moved(piece):
+        return [piece] + [lax.ppermute(piece, "tp", xor_pairs(T, dt)) for dt in range(1, T)]
+
     def to_slots(pieces, kind):
         out = lax.full((S, span, D), 0, kind)
         for k in range(C):
-            piece = lax.ppermute(pieces[k], "ctx", xor_pairs(C, k)) if k else pieces[k]
-            for dt in range(T):
-                got = lax.ppermute(piece, "tp", xor_pairs(T, dt)) if dt else piece
+            for dt, got in enumerate(pieces[k]):
                 out = lax.dynamic_update_slice_in_dim(
                     out, got.reshape(ns, span, D).astype(kind), ((c ^ k) * T + (t ^ dt)) * ns, 0
                 )
         return out
 
-    def gathered(shard):
-        held = {}
-        for high in range(0, F, 2):
-            for dt in range(T):
-                if high == 0 and dt == 0:
-                    held[0, 0] = shard
-                else:
-                    pairs = [
-                        (i * T + j, (i ^ high) * T + (j ^ dt)) for i in range(F) for j in range(T)
-                    ]
-                    held[high, dt] = lax.ppermute(shard, ("fsdp", "tp"), pairs)
-        for high in range(0, F, 2):
-            for dt in range(T):
-                held[high + 1, dt] = lax.ppermute(held[high, dt], "fsdp", xor_pairs(F, 1))
-        return [held[df, dt] for df in range(F) for dt in range(T)]
-
-    def by_half(array):
-        return array[jnp.arange(T) ^ t]
+    def swapped(array, axis, bit):
+        return lax.ppermute(array, axis, xor_pairs(lax.axis_size(axis), bit))
+
+    def chip_start(shard, across):
+        held = shard[None]
+        for axis, bit in order_of(F, T, across)[:-1]:
+            held = jnp.concatenate([held, swapped(held, axis, bit)], axis=0)
+        return held
+
+    def chip_end(held, across):
+        axis, bit = order_of(F, T, across)[-1]
+        return swapped(held, axis, bit)
+
+    def both_cores(held, got):
+        return [held, got, swapped(held, "fsdp", 1), swapped(got, "fsdp", 1)]
+
+    def spread(array, width):
+        rows, part = array.shape
+        owner = lax.broadcasted_iota(jnp.int32, (rows, part * F), 1) // part
+        return jnp.where(owner == f, jnp.tile(array, (1, F)), jnp.zeros((), BF)).reshape(-1, width)
 
     x_pieces = to_sequences(tokens_in)
-    qkv_pieces = gathered(jnp.concatenate([query_weight, key_weight, value_weight], axis=1))
-    small = jnp.concatenate(
-        [output_bias, attn_gain, attn_shift, outer_bias, ffn_gain, ffn_shift]
-        + [query_bias.reshape(-1), value_bias.reshape(-1), inner_bias.reshape(-1)]
-    )
-    small = lax.all_gather(small, ("fsdp", "tp"), axis=0, tiled=False).reshape(F, T, -1)
-    vec = small[:, 0, : 6 * Dl].reshape(F, 6, Dl).transpose(1, 0, 2).reshape(6, D).astype(F32)
-    vec = jnp.concatenate([vec, jnp.zeros((2, D), F32)], axis=0)
-    n_qb = query_bias.size
-
-    def unit_rows(start, shape):
-        block = small[:, :, start : start + math.prod(shape)].reshape(F, T, *shape)
-        return by_half(block.transpose(1, 2, 0, 3).reshape(T, -1).astype(F32))
-
-    q_off = unit_rows(6 * Dl, query_bias.shape)
-    v_off = unit_rows(6 * Dl + n_qb, value_bias.shape)
-    inner_off = unit_rows(6 * Dl + 2 * n_qb, inner_bias.shape).reshape(1, FF)
-    qkv_off = jnp.stack([q_off, jnp.zeros_like(q_off), v_off], axis=1).reshape(1, 3 * D)
-    inner_pieces = gathered(inner_weight)
-    outer_pieces = gathered(jnp.concatenate([output_weight.T, outer_weight.T], axis=1))
-    cot_pieces = to_sequences(cotangent)
+    vectors = jnp.stack([output_bias, attn_gain, attn_shift, outer_bias, ffn_gain, ffn_shift])
+    small = [
+        spread(query_bias, half), spread(value_bias, half), spread(inner_bias, fhalf),
+        spread(vectors, D),
+    ]
+    small = jnp.concatenate([jnp.pad(a, ((0, 0), (0, fhalf - a.shape[1]))) for a in small])
+    small = jnp.pad(small, ((0, EXTRA - small.shape[0]), (0, 0)))
+    low = jnp.concatenate([query_weight, key_weight], axis=1)
+    high = jnp.concatenate([value_weight, output_weight.T], axis=1)
+    low = chip_start(jnp.concatenate([low, small[:, :D]], axis=0), False)
+    high = chip_start(jnp.concatenate([high, small[:, D:]], axis=0), True)
+    low = after(low, [x_pieces[k] for k in range(1, C, 2)])
+    lows = both_cores(low, chip_end(low, False))
+    highs = both_cores(high, chip_end(high, True))
+    inner = chip_start(after(inner_weight, [lows[1], highs[1]]), False)
+    outer = chip_start(after(outer_weight.T, [lows[1], highs[1]]), True)
+    inner_got, outer_got = chip_end(inner, False), chip_end(outer, True)
+    cot_pieces = to_sequences(after(cotangent, [*x_pieces, *lows, *highs]))
     lengths = lax.dynamic_slice_in_dim(seq_lengths, (c * T + t) * ns, ns, 0)
     meta = jnp.concatenate([jnp.stack([f, c]).astype(jnp.int32), lengths])
 
-    x_all, qkv_w, qkv, e, linv, ctx = front_call(dims, meta, qkv_off, x_pieces, qkv_pieces)
-    los, (first, dctx, nl, act, og, ig, ag, sums, inner_sums) = rows_call(
-        dims, FF, meta, vec, inner_off, x_all, ctx.reshape(C, R, D), cot_pieces,
-        inner_pieces, outer_pieces,
+    x_all, qkv_w, qkv, e, linv, ctx = front_call(
+        dims, after(meta, [inner, outer]), x_pieces, lows, highs
     )
-    layer_out = to_slots(los, BF)
-
-    def reduced(left, right):
-        left, right = left.reshape(C * R, -1), right.reshape(C * R, -1)
-        keep, send = weight_call(dims, meta, left, right)
-        total = added(keep, lax.ppermute(send, "fsdp", xor_pairs(F, 1)))
+    inners = both_cores(after(inner, [ctx]), inner_got)
+    outers = both_cores(after(outer, [ctx]), outer_got)
+    los, (first, dctx, nl, act, og, ig, ag, sums) = rows_call(
+        dims, FF, meta, x_all, ctx.reshape(C, R, D), cot_pieces, lows + highs + inners + outers,
+    )
+
+    def core_sum(keep, send):
+        return added(keep, lax.ppermute(send, "fsdp", xor_pairs(F, 1)))
+
+    def y_sum(total):
         while total.shape[0] > 1:
             h = total.shape[0] // 2
             total = added(total[:h], lax.ppermute(total[h:], "fsdp", xor_pairs(F, 2 * h)))
-        total = total[0]
+        return total[0]
+
+    def x_sum(total):
         while total.shape[0] > 1:
             h = total.shape[0] // 2
             total = added(total[:h], lax.ppermute(total[h:], "tp", xor_pairs(T, h)))
-        total = total[0]
-        bits = [1 << b for b in range(C.bit_length() - 1)]
-        for bit in bits:
-            h = total.shape[0] // 2
-            mine = (c // bit) % 2
-            away = lax.ppermute(
-                lax.dynamic_slice_in_dim(total, (1 - mine) * h, h, 0), "ctx", xor_pairs(C, bit)
-            )
-            total = added(lax.dynamic_slice_in_dim(total, mine * h, h, 0), away)
-        for bit in reversed(bits):
-            away = lax.ppermute(total, "ctx", xor_pairs(C, bit))
-            upper = (c // bit) % 2 == 1
-            total = jnp.concatenate(
-                [jnp.where(upper, away, total), jnp.where(upper, total, away)], axis=0
-            )
-        return total
-
-    outer_t = reduced(og, act)
-    inner_g = reduced(nl, ig)
-    output_t = reduced(ag, ctx)
+        return total[0]
+
+    def ctx_scatter(total):
+        part = total.shape[1] // C
+        mine = 0.0
+        for k in range(C):
+            block = lax.dynamic_slice_in_dim(total, (c ^ k) * part, part, 1)
+            mine += ctx_moved(block, k).astype(F32)
+        return mine.astype(BF)
+
+    def ctx_gather(mine, like):
+        part = mine.shape[1]
+        out = like
+        for k in range(C):
+            out = lax.dynamic_update_slice_in_dim(out, ctx_moved(mine, k), (c ^ k) * part, 1)
+        return out.astype(F32)
+
+    lo = {k: ctx_moved(los[k], k) for k in range(C)}
+    lo_both = [tp_moved(lo[k]) for k in range(C)]
+    outer_parts = weight_call(dims, meta, [(og, act)], sums)
+    nl = after(nl, [lo[1], *lo_both[0]])
+    inner_parts = weight_call(dims, meta, [(nl, ig)])
+    outer_core = core_sum(*outer_parts)
+    dctx = after(dctx, [outer_core, lo[3], *lo_both[1], *inner_parts])
     dqkv = back_call(dims, qkv, ctx, dctx.reshape(ctx.shape), e, linv)
-    ins, qkv_sums = input_call(dqkv.reshape(C, R, 3 * D), qkv_w, first)
-    input_grad = to_slots(ins, F32)
-    qkv_g = reduced(x_all, dqkv)
-
-    def all_sum(array):
-        for axis, count in (("fsdp", F), ("tp", T), ("ctx", C)):
-            for b in range(count.bit_length() - 1):
-                array = array + lax.ppermute(array, axis, xor_pairs(count, 1 << b))
-        return array
-
-    early = all_sum(jnp.concatenate([sums[:6].reshape(-1), by_half(inner_sums.reshape(T, -1)).reshape(-1)]))
-    qkv_parts = by_half(qkv_sums.reshape(T, 3, half))
-    late = all_sum(jnp.concatenate([qkv_parts[:, 0].reshape(-1), qkv_parts[:, 2].reshape(-1)]))
-    vec_sums = lax.dynamic_slice_in_dim(early[: 6 * D].reshape(6, D), f * Dl, Dl, 1)
-
-    def shard_of(array, shape):
-        whole = array.reshape(shape[0] * T, shape[1] * F)
-        return lax.dynamic_slice(whole, (t * shape[0], f * shape[1]), shape)
+    inner_core = core_sum(*inner_parts)
+    outer_y = y_sum(outer_core)
+    ag = after(ag, [inner_core, outer_y, lo[2], *lo_both[3], dqkv])
+    qkv_parts = weight_call(dims, meta, [(x_all, dqkv), (ag, ctx)])
+    outer_x = x_sum(outer_y)
+    inner_y = y_sum(inner_core)
+    first = after(first, [outer_x, *lo_both[2], *qkv_parts])
+    ins = input_call(dqkv.reshape(C, R, 3 * D), qkv_w, first)
+    qkv_core = core_sum(*qkv_parts)
+    outer_part = ctx_scatter(outer_x)
+    layer_out = to_slots(lo_both, BF)
+    input_grad = to_slots([tp_moved(ctx_moved(ins[k], k)) for k in range(C)], F32)
+    inner_x = x_sum(inner_y)
+    qkv_x = x_sum(y_sum(qkv_core))
+    outer_g = ctx_gather(outer_part, outer_x)
+    inner_g = ctx_gather(ctx_scatter(inner_x), inner_x)
+    qkv_g = ctx_gather(ctx_scatter(qkv_x), qkv_x)
+
+    def own(row, shape):
+        whole = row.reshape(shape[0], shape[1] * F)
+        return lax.dynamic_slice_in_dim(whole, f * shape[1], shape[1], 1)
+
+    vec_sums = lax.dynamic_slice_in_dim(outer_g[Dl : Dl + 6, :D], f * Dl, Dl, 1)
 
     return (
         layer_out,
         input_grad,
-        qkv_g[:, :half].astype(F32),
-        shard_of(late[:D], query_bias.shape),
-        qkv_g[:, half : 2 * half].astype(F32),
-        qkv_g[:, 2 * half :].astype(F32),
-        shard_of(late[D:], value_bias.shape),
-        output_t.T.astype(F32),
+        qkv_g[:Dl, :half],
+        own(qkv_g[Dl, :half], query_bias.shape),
+        qkv_g[:Dl, half : 2 * half],
+        qkv_g[:Dl, 2 * half : 3 * half],
+        own(qkv_g[Dl, 2 * half : 3 * half], value_bias.shape),
+        qkv_g[:Dl, 3 * half :].T,
         vec_sums[0],
         vec_sums[1],
         vec_sums[2],
-        inner_g.astype(F32),
-        shard_of(early[6 * D :], inner_bias.shape),
-        outer_t.T.astype(F32),
+        inner_g[:Dl],
+        own(inner_g[Dl], inner_bias.shape),
+        outer_g[:Dl].T,
         vec_sums[3],
         vec_sums[4],
         vec_sums[5],

time: 576 us -> 510 us (0.89)
  blocking collectives: 34 us -> 0 us
  waiting for transfers between devices: 248 us -> 232 us
  starting transfers between devices: 86.8 us -> 72.9 us
  local copies, waits for them, and re-layouts: 25.7 us -> 34.5 us
  other arithmetic: 24.6 us -> 16.5 us
    unnamed x1 -> x0, blocking collectives: 34 us -> none
    ppermute x73 -> x57, waiting for transfers between devices: 201 us -> 169 us  [the longest x24 93.7 us: ctx_moved(): return lax.ppermute(piece, 'ctx', xor_pairs(C, k)) if k else piece]
    ppermute x6, waiting for transfers between devices: 46.6 us -> 63.6 us  [to_sequences(): out.append(lax.ppermute(piece, 'ctx', xor_pairs(C, k)) if k else piece)]
    dynamic_update_slice x8, other arithmetic: 10.6 us -> 0.44 us  [to_slots(): lax.dynamic_update_slice_in_dim(out, got.reshape(ns, span, D).astype(kind...]
    convert_element_type x20 -> x9, other arithmetic: 4.52 us -> 12.2 us  [added(): return (a.astype(F32) + b.astype(F32)).astype(BF)]
    ppermute x73 -> x57, starting transfers between devices: 72.2 us -> 64.9 us  [the longest x24 39.1 us: ctx_moved(): return lax.ppermute(piece, 'ctx', xor_pairs(C, k)) if k else piece]
    ppermute x6, starting transfers between devices: 14.6 us -> 8.05 us  [to_sequences(): out.append(lax.ppermute(piece, 'ctx', xor_pairs(C, k)) if k else piece)]
    another operation x4 -> x17, local copies, waits for them, and re-layouts: 0.1 us -> 6.56 us  [the longest x7 3.98 us: per_device(): jnp.stack([output_bias, attn_gain, attn_shift, outer_bias, ffn_gain, ffn_...]
  transfers between devices with their start and end apart: 79 -> 63, of which waited for: 34 -> 34; matrix products, arithmetic and copies ran while one was open for 7% -> 6% of each run, Pallas kernels for 18% -> 18%
where the time goes in v2:
time: 510 us; the launch traced here: 509 us
  waiting for transfers between devices  232 us (45%)
  Pallas kernels  151 us (30%)
  starting transfers between devices  72.9 us (14%)
  local copies, waits for them, and re-layouts  34.5 us (7%)
  other arithmetic  16.5 us (3%)
    ppermute x24, waiting for transfers between devices, ctx_moved(): return lax.ppermute(piece, 'ctx', xor_pairs(C, k)) if k else piece  93.7 us
    ppermute x6, waiting for transfers between devices, to_sequences(): out.append(lax.ppermute(piece, 'ctx', xor_pairs(C, k)) if k else piece)  63.6 us
    pallas_call x1, Pallas kernels, rows_call(): pl.pallas_call(functools.partial(rows_kernel, dims, FF), name='rows', gri...  46.8 us
    pallas_call x3, Pallas kernels, weight_call(): pl.pallas_call(functools.partial(weight_kernel, F, pers, sums is not None...  39.7 us
    ppermute x24, starting transfers between devices, ctx_moved(): return lax.ppermute(piece, 'ctx', xor_pairs(C, k)) if k else piece  39.1 us
    pallas_call x1, Pallas kernels, front_call(): pl.pallas_call(functools.partial(front_kernel, dims), name='front', grid=...  29.9 us
    pallas_call x1, Pallas kernels, back_call(): pl.pallas_call(functools.partial(back_kernel, dims), name='back', grid=(n...  26.2 us
    ppermute x16, waiting for transfers between devices, swapped(): return lax.ppermute(array, axis, xor_pairs(lax.axis_size(axis), bit))  25.2 us
  transfers between devices with their start and end apart: 63, of which 34 were waited for; matrix products, arithmetic and copies ran while one was open for 6% of the time, Pallas kernels for 18%

profile of v2, /device:TPU:0, one launch (start us, length us, event | category | flops | bytes accessed | tf_op | source)
XLA Modules:
  0.0 508.6 jit_solution(18061573785908021651)
XLA Ops:
  8.4 3.1 collective-permute-start.4
  12.5 1.6 collective-permute-start
  14.0 2.3 constant_dynamic-slice_fusion.8
  16.3 1.6 collective-permute-start.1
  17.9 2.5 collective-permute-start.2
  21.6 5.8 %collective-permute-done.1.refs_1_ = bf16[256,768]{1,0:T(8,128)(2,1)S(1)} collective-permute-done((bf16[256,768]{1,0:T(8,128)(2,1)S(1)}, bf16[256,768]{1,0:T(8,128)(2,1)S(1)}, u32[]{:S(2)}, u32[]{:S(2)}) %collective-permute-start.1) | collective-permute-done | bytes 393248 | tf_op jit(solution)/shard_map/ppermute | solution.py:578
  27.4 9.8 %collective-permute-done.2.refs_3_ = bf16[256,768]{1,0:T(8,128)(2,1)S(1)} collective-permute-done((bf16[256,768]{1,0:T(8,128)(2,1)S(1)}, bf16[256,768]{1,0:T(8,128)(2,1)S(1)}, u32[]{:S(2)}, u32[]{:S(2)}) %collective-permute-start.2) | collective-permute-done | bytes 393248 | tf_op jit(solution)/shard_map/ppermute | solution.py:578
  37.7 14.1 %collective-permute-done.3.refs_5_ = bf16[2,208,768]{2,1,0:T(8,128)(2,1)S(1)} collective-permute-done((bf16[2,208,768]{2,1,0:T(8,128)(2,1)S(1)}, bf16[2,208,768]{2,1,0:T(8,128)(2,1)S(1)}, u32[]{:S(2)}, u32[]{:S(2)}) %collective-permute-start.3) | collective-permute-done | bytes 639008 | tf_op jit(solution)/shard_map/ppermute | solution.py:597
  53.0 3.3 collective-permute-start.8
  56.3 8.5 %collective-permute-done.7 = bf16[1,192,1536]{2,1,0:T(8,128)(2,1)S(1)} collective-permute-done((bf16[1,192,1536]{2,1,0:T(8,128)(2,1)S(1)}, bf16[1,192,1536]{2,1,0:T(8,128)(2,1)S(1)}, u32[]{:S(2)}, u32[]{:S(2)}) %collective-permute-start.7) | collective-permute-done | bytes 589856 | tf_op jit(solution)/shard_map/ppermute | solution.py:597
  65.8 2.6 collective-permute-start.16
  68.4 6.1 %collective-permute-done.8.refs_2_ = bf16[256,768]{1,0:T(8,128)(2,1)S(1)} collective-permute-done((bf16[256,768]{1,0:T(8,128)(2,1)S(1)}, bf16[256,768]{1,0:T(8,128)(2,1)S(1)}, u32[]{:S(2)}, u32[]{:S(2)}) %collective-permute-start.8) | collective-permute-done | bytes 393248 | tf_op jit(solution)/shard_map/ppermute | solution.py:578
  78.3 29.9 %front.1 = (bf16[4,256,768]{2,1,0:T(8,128)(2,1)}, bf16[768,2304]{1,0:T(8,128)(2,1)}, bf16[4,2,128,2304]{3,2,1,0:T(8,128)(2,1)}, bf16[12,1024,512]{2,1,0:T(8,128)...) custom-call(s32[4]{0:T(128)} %pad_add_fusion.meta, bf16[256,768]{1,0:T(8,128)(2,1)} %bitcast.148, ...), custom_call_target="tpu_custom_call" | custom-call | flops 3623878656 | bytes 40000000 | tf_op jit(solution)/shard_map/front/pallas_call | solution.py:162
  108.3 2.2 constant_dynamic-slice_fusion.4
  111.5 10.1 %collective-permute-done.13.refs_1_ = bf16[256,768]{1,0:T(8,128)(2,1)S(1)} collective-permute-done((bf16[256,768]{1,0:T(8,128)(2,1)S(1)}, bf16[256,768]{1,0:T(8,128)(2,1)S(1)}, u32[]{:S(2)}, u32[]{:S(2)}) %collective-permute-start.13) | collective-permute-done | bytes 393248 | tf_op jit(solution)/shard_map/ppermute | solution.py:578
  121.7 19.6 %collective-permute-done.14.refs_2_ = bf16[256,768]{1,0:T(8,128)(2,1)S(1)} collective-permute-done((bf16[256,768]{1,0:T(8,128)(2,1)S(1)}, bf16[256,768]{1,0:T(8,128)(2,1)S(1)}, u32[]{:S(2)}, u32[]{:S(2)}) %collective-permute-start.14) | collective-permute-done | bytes 393248 | tf_op jit(solution)/shard_map/ppermute | solution.py:578
  142.0 12.2 %collective-permute-done.15.refs_3_ = bf16[256,768]{1,0:T(8,128)(2,1)S(1)} collective-permute-done((bf16[256,768]{1,0:T(8,128)(2,1)S(1)}, bf16[256,768]{1,0:T(8,128)(2,1)S(1)}, u32[]{:S(2)}, u32[]{:S(2)}) %collective-permute-start.15) | collective-permute-done | bytes 393248 | tf_op jit(solution)/shard_map/ppermute | solution.py:578
  157.3 46.8 %rows.1 = (bf16[256,768]{1,0:T(8,128)(2,1)}, bf16[256,768]{1,0:T(8,128)(2,1)}, bf16[256,768]{1,0:T(8,128)(2,1)}, bf16[256,768]{1,0:T(8,128)(2,1)}, f32[4,256,768...) custom-call(s32[4]{0:T(128)} %pad_add_fusion.meta, ...), custom_call_target="tpu_custom_call" | custom-call | flops 21743271936 | bytes 50000000 | tf_op jit(solution)/shard_map/rows/pallas_call | solution.py:344
  204.2 12.8 %weight_grad.3 = (bf16[2,2,208,1536]{3,2,1,0:T(8,128)(2,1)}, bf16[2,2,208,1536]{3,2,1,0:T(8,128)(2,1)}) custom-call(s32[4]{0:T(128)} %pad_add_fusion.meta, bf16[1024,768]{1,0:T(8,128)(2,1)} %bitcast.169, bf16[1024,3072]{1,0:T(8,128)(2,1)} %bitcast.165, f32[16,768]{1,0:T(8,128)} %get-tuple-element.73.refs_2_), custom_call_target="tpu_custom_call" | custom-call | flops 4831838208 | bytes 12582912 | tf_op jit(solution)/shard_map/weight_grad/pallas_call | solution.py:523
  218.3 4.9 collective-permute-start.23
  224.4 4.1 collective-permute-done.22
  229.3 11.8 %collective-permute-done.23 = bf16[256,768]{1,0:T(8,128)(2,1)} collective-permute-done((bf16[256,768]{1,0:T(8,128)(2,1)S(1)}, bf16[256,768]{1,0:T(8,128)(2,1)}, u32[]{:S(2)}, u32[]{:S(2)}) %collective-permute-start.23) | collective-permute-done | bytes 393248 | tf_op jit(solution)/shard_map/ppermute | solution.py:582
  241.0 12.8 %weight_grad.4 = (bf16[2,2,208,1536]{3,2,1,0:T(8,128)(2,1)}, bf16[2,2,208,1536]{3,2,1,0:T(8,128)(2,1)}) custom-call(s32[4]{0:T(128)} %pad_add_fusion.meta, bf16[1024,768]{1,0:T(8,128)(2,1)} %bitcast.168, bf16[1024,3072]{1,0:T(8,128)(2,1)} %bitcast.164), custom_call_target="tpu_custom_call" | custom-call | flops 4831838208 | bytes 12582912 | tf_op jit(solution)/shard_map/weight_grad/pallas_call | solution.py:523
  257.5 10.1 %collective-permute-done.27 = bf16[256,768]{1,0:T(8,128)(2,1)} collective-permute-done((bf16[256,768]{1,0:T(8,128)(2,1)}, bf16[256,768]{1,0:T(8,128)(2,1)}, u32[]{:S(2)}, u32[]{:S(2)}) %collective-permute-start.27) | collective-permute-done | bytes 393248 | tf_op jit(solution)/shard_map/ppermute | solution.py:582
  270.4 5.2 %collective-permute-done.26 = bf16[256,768]{1,0:T(8,128)(2,1)S(1)} collective-permute-done((bf16[256,768]{1,0:T(8,128)(2,1)S(1)}, bf16[256,768]{1,0:T(8,128)(2,1)S(1)}, u32[]{:S(2)}, u32[]{:S(2)}) %collective-permute-start.26) | collective-permute-done | bytes 393248 | tf_op jit(solution)/shard_map/ppermute | solution.py:585
  276.7 6.6 %collective-permute-done.28 = bf16[256,768]{1,0:T(8,128)(2,1)S(1)} collective-permute-done((bf16[256,768]{1,0:T(8,128)(2,1)}, bf16[256,768]{1,0:T(8,128)(2,1)S(1)}, u32[]{:S(2)}, u32[]{:S(2)}) %collective-permute-start.28) | collective-permute-done | bytes 393248 | tf_op jit(solution)/shard_map/ppermute | solution.py:585
  283.3 1.6 copy-done.3
  285.0 1.5 copy-done.5
  286.5 2.4 add_convert_fusion.2
  289.0 1.6 collective-permute-start.30
  290.6 26.2 %back.1 = bf16[4,2,128,2304]{3,2,1,0:T(8,128)(2,1)} custom-call(bf16[4,2,128,2304]{3,2,1,0:T(8,128)(2,1)} %get-tuple-element.69.qkv, bf16[4,2,128,768]{3,2,1,0:T(8,128)(2,1)} %get-tuple-element.61.ctx, bf16[4,2,128,768]{3,2,1,0:T(8,128)(2,1)} %bitcast.130, bf16[12,1024,512]{2,1,0:T(8,128)(2,1)} %get-tuple-element.82.e_ref, ...), custom_call_target="tpu_custom_call" | custom-call | flops 6442450944 | bytes 30000000 | tf_op jit(solution)/shard_map/back/pallas_call | solution.py:413
  316.8 3.2 add_convert_fusion.1
  319.9 1.5 copy-done
  323.1 14.1 %weight_grad.5 = (bf16[2,2,208,1536]{3,2,1,0:T(8,128)(2,1)}, bf16[2,2,208,1536]{3,2,1,0:T(8,128)(2,1)}) custom-call(s32[4]{0:T(128)} %pad_add_fusion.meta, bf16[1024,768]{1,0:T(8,128)(2,1)} %bitcast.166, bf16[1024,768]{1,0:T(8,128)(2,1)} %bitcast.167, bf16[1024,2304]{1,0:T(8,128)(2,1)} %bitcast.126, bf16[1024,768]{1,0:T(8,128)(2,1)} %bitcast.129), custom_call_target="tpu_custom_call" | custom-call | flops 4831838208 | bytes 12582912 | tf_op jit(solution)/shard_map/weight_grad/pallas_call | solution.py:523
  337.3 1.8 add_convert_fusion.5
  339.9 12.0 %collective-permute-done.55 = bf16[1,2,208,1536]{3,2,1,0:T(8,128)(2,1)} collective-permute-done((bf16[1,2,208,1536]{3,2,1,0:T(8,128)(2,1)}, bf16[1,2,208,1536]{3,2,1,0:T(8,128)(2,1)}, u32[]{:S(2)}, u32[]{:S(2)}) %collective-permute-start.55) | collective-permute-done | bytes 1277984 | tf_op jit(solution)/shard_map/ppermute | solution.py:654
  352.0 1.6 add_convert_fusion.3
  354.2 2.2 collective-permute-done.31
  358.4 2.1 collective-permute-start.50
  361.7 8.5 %input_grad.1 = (bf16[256,768]{1,0:T(8,128)(2,1)}, bf16[256,768]{1,0:T(8,128)(2,1)}, bf16[256,768]{1,0:T(8,128)(2,1)}, bf16[256,768]{1,0:T(8,128)(2,1)}) custom-call(bf16[4,256,2304]{2,1,0:T(8,128)(2,1)} %bitcast.127, bf16[768,2304]{1,0:T(8,128)(2,1)} %get-tuple-element.84.w, f32[4,256,768]{2,1,0:T(8,128)} %get-tuple-element.90.first), custom_call_target="tpu_custom_call" | custom-call | flops 3623878656 | bytes 15000000 | tf_op jit(solution)/shard_map/input_grad/pallas_call | solution.py:450
  372.5 2.4 collective-permute-start.52
  376.4 3.6 collective-permute-done.52
  381.5 6.7 %collective-permute-done.53 = bf16[208,384]{1,0:T(8,128)(2,1)S(1)} collective-permute-done((bf16[208,384]{1,0:T(8,128)(2,1)S(1)}, bf16[208,384]{1,0:T(8,128)(2,1)S(1)}, u32[]{:S(2)}, u32[]{:S(2)}) %collective-permute-start.53) | collective-permute-done | bytes 159776 | tf_op jit(solution)/shard_map/ppermute | solution.py:582
  391.0 2.1 collective-permute-start.57
  393.8 1.9 collective-permute-start.59
  395.7 2.4 add_convert_fusion
  398.3 1.6 collective-permute-start.41
  399.9 3.4 collective-permute-done.57
  403.3 16.7 %collective-permute-done.58 = bf16[208,384]{1,0:T(8,128)(2,1)S(1)} collective-permute-done((bf16[208,384]{1,0:T(8,128)(2,1)S(1)}, bf16[208,384]{1,0:T(8,128)(2,1)S(1)}, u32[]{:S(2)}, u32[]{:S(2)}) %collective-permute-start.58) | collective-permute-done | bytes 159776 | tf_op jit(solution)/shard_map/ppermute | solution.py:582
  420.0 2.4 collective-permute-start.38
  422.5 2.2 collective-permute-start.60
  424.8 2.1 collective-permute-start.61
  427.0 8.3 %collective-permute-done.60 = bf16[208,384]{1,0:T(8,128)(2,1)S(1)} collective-permute-done((bf16[208,384]{1,0:T(8,128)(2,1)S(1)}, bf16[208,384]{1,0:T(8,128)(2,1)S(1)}, u32[]{:S(2)}, u32[]{:S(2)}) %collective-permute-start.60) | collective-permute-done | bytes 159776 | tf_op jit(solution)/shard_map/ppermute | solution.py:582
  435.2 2.0 collective-permute-start.62
  437.3 5.6 %collective-permute-done.36 = bf16[256,768]{1,0:T(8,128)(2,1)S(1)} collective-permute-done((bf16[256,768]{1,0:T(8,128)(2,1)S(1)}, bf16[256,768]{1,0:T(8,128)(2,1)S(1)}, u32[]{:S(2)}, u32[]{:S(2)}) %collective-permute-start.36) | collective-permute-done | bytes 393248 | tf_op jit(solution)/shard_map/ppermute | solution.py:582
  444.9 9.4 %collective-permute-done.61 = bf16[208,384]{1,0:T(8,128)(2,1)S(1)} collective-permute-done((bf16[208,384]{1,0:T(8,128)(2,1)S(1)}, bf16[208,384]{1,0:T(8,128)(2,1)S(1)}, u32[]{:S(2)}, u32[]{:S(2)}) %collective-permute-start.61) | collective-permute-done | bytes 159776 | tf_op jit(solution)/shard_map/ppermute | solution.py:582
  460.0 18.5 %collective-permute-done.42 = bf16[1,208,1536]{2,1,0:T(8,128)(2,1)S(1)} collective-permute-done((bf16[1,208,1536]{2,1,0:T(8,128)(2,1)S(1)}, bf16[1,208,1536]{2,1,0:T(8,128)(2,1)S(1)}, u32[]{:S(2)}, u32[]{:S(2)}) %collective-permute-start.42) | collective-permute-done | bytes 639008 | tf_op jit(solution)/shard_map/ppermute | solution.py:660
  478.7 2.4 collective-permute-start.43
  481.9 1.7 collective-permute-start.45
  483.7 3.0 collective-permute-done.43
  486.8 4.7 collective-permute-done.44
  491.6 2.3 collective-permute-start.46
  496.5 4.5 collective-permute-done.46
  501.1 4.1 collective-permute-done.47
  (251 shorter events, 62.5 us)
Async XLA Ops:
  8.4 12.0 %collective-permute-start.4 = (bf16[1,208,768]{2,1,0:T(8,128)(2,1)S(1)}, bf16[1,208,768]{2,1,0:T(8,128)(2,1)S(1)}, u32[]{:S(2)}, u32[]{:S(2)}) collective-permute-start(bf16[1,208,768]{2,1,0:T(8,128)(2,1)S(1)} %maximum_bitcast_fusion.1), channel_id=1, source_target_pairs={{0,16},{8,24},{16,0},{24,8},{1,17},{9,25},{17,1},{25,9},{2,18},{10... | collective-permute-start | bytes 958472 | tf_op jit(solution)/shard_map/ppermute | solution.py:597
  12.5 9.1 %collective-permute-start = (bf16[1,208,768]{2,1,0:T(8,128)(2,1)S(1)}, bf16[1,208,768]{2,1,0:T(8,128)(2,1)S(1)}, u32[]{:S(2)}, u32[]{:S(2)}) collective-permute-start(bf16[1,208,768]{2,1,0:T(8,128)(2,1)S(1)} %maximum_bitcast_fusion), channel_id=1, source_target_pairs={{0,1},{1,0},{2,3},{3,2},{4,5},{5,4},{6,7},{7,6},{8,9},{9,8},{10,11... | collective-permute-start | bytes 958472 | tf_op jit(solution)/shard_map/ppermute | solution.py:597
  16.3 11.1 %collective-permute-start.1 = (bf16[256,768]{1,0:T(8,128)(2,1)S(1)}, bf16[256,768]{1,0:T(8,128)(2,1)S(1)}, u32[]{:S(2)}, u32[]{:S(2)}) collective-permute-start(bf16[256,768]{1,0:T(8,128)(2,1)S(1)} %bitcast.155), channel_id=1, source_target_pairs={{0,2},{2,0},{4,6},{6,4},{1,3},{3,1},{5,7},{7,5},{8,10},{10,8},{12,... | collective-permute-start | bytes 1179656 | tf_op jit(solution)/shard_map/ppermute | solution.py:578
  17.9 19.3 %collective-permute-start.2 = (bf16[256,768]{1,0:T(8,128)(2,1)S(1)}, bf16[256,768]{1,0:T(8,128)(2,1)S(1)}, u32[]{:S(2)}, u32[]{:S(2)}) collective-permute-start(bf16[256,768]{1,0:T(8,128)(2,1)S(1)} %bitcast.153), channel_id=1, source_target_pairs={{0,6},{2,4},{4,2},{6,0},{1,7},{3,5},{5,3},{7,1},{8,14},{10,12},{12... | collective-permute-start | bytes 1179656 | tf_op jit(solution)/shard_map/ppermute | solution.py:578
  20.5 17.2 %collective-permute-start.5 = (bf16[2,208,768]{2,1,0:T(8,128)(2,1)S(1)}, bf16[2,208,768]{2,1,0:T(8,128)(2,1)S(1)}, u32[]{:S(2)}, u32[]{:S(2)}) collective-permute-start(bf16[2,208,768]{2,1,0:T(8,128)(2,1)S(1)} %pad_maximum_fusion.3.refs_8_), channel_id=1, source_target_pairs={{0,1},{1,0},{2,3},{3,2},{4,5},{5,4},{6,7},{7,6},{8,9},{9,8},{10,11... | collective-permute-start | bytes 1916936 | tf_op jit(solution)/shard_map/ppermute | solution.py:597
  21.6 56.7 %copy-start.10 = (bf16[2,208,768]{2,1,0:T(8,128)(2,1)}, bf16[2,208,768]{2,1,0:T(8,128)(2,1)S(1)}, u32[]{:S(2)}) copy-start(bf16[2,208,768]{2,1,0:T(8,128)(2,1)S(1)} %pad_maximum_fusion.2.refs_4_) | copy-start | bytes 1916932
  37.2 14.6 %collective-permute-start.3 = (bf16[2,208,768]{2,1,0:T(8,128)(2,1)S(1)}, bf16[2,208,768]{2,1,0:T(8,128)(2,1)S(1)}, u32[]{:S(2)}, u32[]{:S(2)}) collective-permute-start(bf16[2,208,768]{2,1,0:T(8,128)(2,1)S(1)} %pad_maximum_fusion.2.refs_4_), channel_id=1, source_target_pairs={{0,16},{8,24},{16,0},{24,8},{1,17},{9,25},{17,1},{25,9},{2,18},{10... | collective-permute-start | bytes 1916936 | tf_op jit(solution)/shard_map/ppermute | solution.py:597
  51.8 12.9 %collective-permute-start.7 = (bf16[1,192,1536]{2,1,0:T(8,128)(2,1)S(1)}, bf16[1,192,1536]{2,1,0:T(8,128)(2,1)S(1)}, u32[]{:S(2)}, u32[]{:S(2)}) collective-permute-start(bf16[1,192,1536]{2,1,0:T(8,128)(2,1)S(1)} %bitcast.131), channel_id=1, source_target_pairs={{0,16},{8,24},{16,0},{24,8},{1,17},{9,25},{17,1},{25,9},{2,18},{10... | collective-permute-start | bytes 1769480 | tf_op jit(solution)/shard_map/ppermute | solution.py:597
  52.4 13.3 %collective-permute-start.6 = (bf16[1,192,1536]{2,1,0:T(8,128)(2,1)S(1)}, bf16[1,192,1536]{2,1,0:T(8,128)(2,1)S(1)}, u32[]{:S(2)}, u32[]{:S(2)}) collective-permute-start(bf16[1,192,1536]{2,1,0:T(8,128)(2,1)S(1)} %bitcast.133), channel_id=1, source_target_pairs={{0,1},{1,0},{2,3},{3,2},{4,5},{5,4},{6,7},{7,6},{8,9},{9,8},{10,11... | collective-permute-start | bytes 1769480 | tf_op jit(solution)/shard_map/ppermute | solution.py:597
  53.0 21.5 %collective-permute-start.11 = (bf16[2,208,768]{2,1,0:T(8,128)(2,1)S(1)}, bf16[2,208,768]{2,1,0:T(8,128)(2,1)S(1)}, u32[]{:S(2)}, u32[]{:S(2)}) collective-permute-start(bf16[2,208,768]{2,1,0:T(8,128)(2,1)S(1)} %pad_maximum_fusion.3.refs_8_), channel_id=1, source_target_pairs={{0,8},{8,0},{16,24},{24,16},{1,9},{9,1},{17,25},{25,17},{2,10},{10... | collective-permute-start | bytes 1916936 | tf_op jit(solution)/shard_map/ppermute | solution.py:597
  53.0 21.5 %collective-permute-start.8 = (bf16[256,768]{1,0:T(8,128)(2,1)S(1)}, bf16[256,768]{1,0:T(8,128)(2,1)S(1)}, u32[]{:S(2)}, u32[]{:S(2)}) collective-permute-start(bf16[256,768]{1,0:T(8,128)(2,1)S(1)} %bitcast.150), channel_id=1, source_target_pairs={{0,4},{2,6},{4,0},{6,2},{1,5},{3,7},{5,1},{7,3},{8,12},{10,14},{12... | collective-permute-start | bytes 1179656 | tf_op jit(solution)/shard_map/ppermute | solution.py:578
  64.9 46.1 %collective-permute-start.19 = (bf16[2,192,1536]{2,1,0:T(8,128)(2,1)S(1)}, bf16[2,192,1536]{2,1,0:T(8,128)(2,1)}, u32[]{:S(2)}, u32[]{:S(2)}) collective-permute-start(bf16[2,192,1536]{2,1,0:T(8,128)(2,1)S(1)} %pad_maximum_fusion.1.refs_16_), channel_id=1, source_target_pairs={{0,1},{1,0},{2,3},{3,2},{4,5},{5,4},{6,7},{7,6},{8,9},{9,8},{10,11... | collective-permute-start | bytes 3538952 | tf_op jit(solution)/shard_map/ppermute | solution.py:597
  65.8 45.4 %collective-permute-start.16 = (bf16[2,192,1536]{2,1,0:T(8,128)(2,1)S(1)}, bf16[2,192,1536]{2,1,0:T(8,128)(2,1)}, u32[]{:S(2)}, u32[]{:S(2)}) collective-permute-start(bf16[2,192,1536]{2,1,0:T(8,128)(2,1)S(1)} %pad_maximum_fusion.refs_12_), channel_id=1, source_target_pairs={{0,16},{8,24},{16,0},{24,8},{1,17},{9,25},{17,1},{25,9},{2,18},{10... | collective-permute-start | bytes 3538952 | tf_op jit(solution)/shard_map/ppermute | solution.py:597
  68.4 7.3 %collective-permute-start.9 = (bf16[2,208,768]{2,1,0:T(8,128)(2,1)S(1)}, bf16[2,208,768]{2,1,0:T(8,128)(2,1)S(1)}, u32[]{:S(2)}, u32[]{:S(2)}) collective-permute-start(bf16[2,208,768]{2,1,0:T(8,128)(2,1)S(1)} %pad_maximum_fusion.2.refs_4_), channel_id=1, source_target_pairs={{0,8},{8,0},{16,24},{24,16},{1,9},{9,1},{17,25},{25,17},{2,10},{10... | collective-permute-start | bytes 1916936 | tf_op jit(solution)/shard_map/ppermute | solution.py:597
  74.5 2.1 collective-permute-start.12
  74.5 3.0 collective-permute-start.10
  110.5 11.2 %collective-permute-start.13 = (bf16[256,768]{1,0:T(8,128)(2,1)S(1)}, bf16[256,768]{1,0:T(8,128)(2,1)S(1)}, u32[]{:S(2)}, u32[]{:S(2)}) collective-permute-start(bf16[256,768]{1,0:T(8,128)(2,1)S(1)} %bitcast.154), channel_id=1, source_target_pairs={{0,2},{2,0},{4,6},{6,4},{1,3},{3,1},{5,7},{7,5},{8,10},{10,8},{12,... | collective-permute-start | bytes 1179656 | tf_op jit(solution)/shard_map/ppermute | solution.py:578
  110.5 43.7 %collective-permute-start.20 = (bf16[2,192,1536]{2,1,0:T(8,128)(2,1)S(1)}, bf16[2,192,1536]{2,1,0:T(8,128)(2,1)S(1)}, u32[]{:S(2)}, u32[]{:S(2)}) collective-permute-start(bf16[2,192,1536]{2,1,0:T(8,128)(2,1)S(1)} %pad_maximum_fusion.1.refs_16_), channel_id=1, source_target_pairs={{0,8},{8,0},{16,24},{24,16},{1,9},{9,1},{17,25},{25,17},{2,10},{10... | collective-permute-start | bytes 3538952 | tf_op jit(solution)/shard_map/ppermute | solution.py:597
  110.6 43.6 %collective-permute-start.17 = (bf16[2,192,1536]{2,1,0:T(8,128)(2,1)S(1)}, bf16[2,192,1536]{2,1,0:T(8,128)(2,1)S(1)}, u32[]{:S(2)}, u32[]{:S(2)}) collective-permute-start(bf16[2,192,1536]{2,1,0:T(8,128)(2,1)S(1)} %pad_maximum_fusion.refs_12_), channel_id=1, source_target_pairs={{0,8},{8,0},{16,24},{24,16},{1,9},{9,1},{17,25},{25,17},{2,10},{10... | collective-permute-start | bytes 3538952 | tf_op jit(solution)/shard_map/ppermute | solution.py:597
  111.0 44.3 %collective-permute-start.21 = (bf16[2,192,1536]{2,1,0:T(8,128)(2,1)}, bf16[2,192,1536]{2,1,0:T(8,128)(2,1)S(1)}, u32[]{:S(2)}, u32[]{:S(2)}) collective-permute-start(bf16[2,192,1536]{2,1,0:T(8,128)(2,1)} %collective-permute-done.19.refs_17_), channel_id=1, source_target_pairs={{0,8},{8,0},{16,24},{24,16},{1,9},{9,1},{17,25},{25,17},{2,10},{10... | collective-permute-start | bytes 3538952 | tf_op jit(solution)/shard_map/ppermute | solution.py:597
  111.2 45.1 %collective-permute-start.18 = (bf16[2,192,1536]{2,1,0:T(8,128)(2,1)}, bf16[2,192,1536]{2,1,0:T(8,128)(2,1)S(1)}, u32[]{:S(2)}, u32[]{:S(2)}) collective-permute-start(bf16[2,192,1536]{2,1,0:T(8,128)(2,1)} %collective-permute-done.16.refs_13_), channel_id=1, source_target_pairs={{0,8},{8,0},{16,24},{24,16},{1,9},{9,1},{17,25},{25,17},{2,10},{10... | collective-permute-start | bytes 3538952 | tf_op jit(solution)/shard_map/ppermute | solution.py:597
  121.7 19.6 %collective-permute-start.14 = (bf16[256,768]{1,0:T(8,128)(2,1)S(1)}, bf16[256,768]{1,0:T(8,128)(2,1)S(1)}, u32[]{:S(2)}, u32[]{:S(2)}) collective-permute-start(bf16[256,768]{1,0:T(8,128)(2,1)S(1)} %bitcast.152), channel_id=1, source_target_pairs={{0,4},{2,6},{4,0},{6,2},{1,5},{3,7},{5,1},{7,3},{8,12},{10,14},{12... | collective-permute-start | bytes 1179656 | tf_op jit(solution)/shard_map/ppermute | solution.py:578
  141.3 12.9 %collective-permute-start.15 = (bf16[256,768]{1,0:T(8,128)(2,1)S(1)}, bf16[256,768]{1,0:T(8,128)(2,1)S(1)}, u32[]{:S(2)}, u32[]{:S(2)}) collective-permute-start(bf16[256,768]{1,0:T(8,128)(2,1)S(1)} %bitcast.151), channel_id=1, source_target_pairs={{0,6},{2,4},{4,2},{6,0},{1,7},{3,5},{5,3},{7,1},{8,14},{10,12},{12... | collective-permute-start | bytes 1179656 | tf_op jit(solution)/shard_map/ppermute | solution.py:578
  217.0 66.3 %collective-permute-start.29 = (bf16[2,2,208,1536]{3,2,1,0:T(8,128)(2,1)}, bf16[2,2,208,1536]{3,2,1,0:T(8,128)(2,1)S(1)}, u32[]{:S(2)}, u32[]{:S(2)}) collective-permute-start(bf16[2,2,208,1536]{3,2,1,0:T(8,128)(2,1)} %get-tuple-element.75), channel_id=1, source_target_pairs={{0,8},{8,0},{16,24},{24,16},{1,9},{9,1},{17,25},{25,17},{2,10},{10... | collective-permute-start | bytes 7667720 | tf_op jit(solution)/shard_map/ppermute | solution.py:649
  217.0 11.5 %collective-permute-start.22 = (bf16[256,768]{1,0:T(8,128)(2,1)S(1)}, bf16[256,768]{1,0:T(8,128)(2,1)S(1)}, u32[]{:S(2)}, u32[]{:S(2)}) collective-permute-start(bf16[256,768]{1,0:T(8,128)(2,1)S(1)} %copy-done.13), channel_id=1, source_target_pairs={{0,1},{1,0},{2,3},{3,2},{4,5},{5,4},{6,7},{7,6},{8,9},{9,8},{10,11... | collective-permute-start | bytes 1179656 | tf_op jit(solution)/shard_map/ppermute | solution.py:585
  218.3 22.7 %collective-permute-start.23 = (bf16[256,768]{1,0:T(8,128)(2,1)S(1)}, bf16[256,768]{1,0:T(8,128)(2,1)}, u32[]{:S(2)}, u32[]{:S(2)}) collective-permute-start(bf16[256,768]{1,0:T(8,128)(2,1)S(1)} %copy-done.35), channel_id=1, source_target_pairs={{0,2},{2,0},{4,6},{6,4},{1,3},{3,1},{5,7},{7,5},{8,10},{10,8},{12,... | collective-permute-start | bytes 1179656 | tf_op jit(solution)/shard_map/ppermute | solution.py:582
  223.2 32.9 %collective-permute-start.25 = (bf16[256,768]{1,0:T(8,128)(2,1)}, bf16[256,768]{1,0:T(8,128)(2,1)S(1)}, u32[]{:S(2)}, u32[]{:S(2)}) collective-permute-start(bf16[256,768]{1,0:T(8,128)(2,1)} %get-tuple-element.67), channel_id=1, source_target_pairs={{0,4},{2,6},{4,0},{6,2},{1,5},{3,7},{5,1},{7,3},{8,12},{10,14},{12... | collective-permute-start | bytes 1179656 | tf_op jit(solution)/shard_map/ppermute | solution.py:582
  253.8 63.0 %collective-permute-start.32 = (bf16[2,2,208,1536]{3,2,1,0:T(8,128)(2,1)}, bf16[2,2,208,1536]{3,2,1,0:T(8,128)(2,1)}, u32[]{:S(2)}, u32[]{:S(2)}) collective-permute-start(bf16[2,2,208,1536]{3,2,1,0:T(8,128)(2,1)} %get-tuple-element.80), channel_id=1, source_target_pairs={{0,8},{8,0},{16,24},{24,16},{1,9},{9,1},{17,25},{25,17},{2,10},{10... | collective-permute-start | bytes 7667720 | tf_op jit(solution)/shard_map/ppermute | solution.py:649
  253.8 13.7 %collective-permute-start.27 = (bf16[256,768]{1,0:T(8,128)(2,1)}, bf16[256,768]{1,0:T(8,128)(2,1)}, u32[]{:S(2)}, u32[]{:S(2)}) collective-permute-start(bf16[256,768]{1,0:T(8,128)(2,1)} %get-tuple-element.68), channel_id=1, source_target_pairs={{0,6},{2,4},{4,2},{6,0},{1,7},{3,5},{5,3},{7,1},{8,14},{10,12},{12... | collective-permute-start | bytes 1179656 | tf_op jit(solution)/shard_map/ppermute | solution.py:582
  255.0 14.4 %collective-permute-start.24 = (bf16[256,768]{1,0:T(8,128)(2,1)}, bf16[256,768]{1,0:T(8,128)(2,1)}, u32[]{:S(2)}, u32[]{:S(2)}) collective-permute-start(bf16[256,768]{1,0:T(8,128)(2,1)} %collective-permute-done.23), channel_id=1, source_target_pairs={{0,1},{1,0},{2,3},{3,2},{4,5},{5,4},{6,7},{7,6},{8,9},{9,8},{10,11... | collective-permute-start | bytes 1179656 | tf_op jit(solution)/shard_map/ppermute | solution.py:585
  256.1 19.5 %collective-permute-start.26 = (bf16[256,768]{1,0:T(8,128)(2,1)S(1)}, bf16[256,768]{1,0:T(8,128)(2,1)S(1)}, u32[]{:S(2)}, u32[]{:S(2)}) collective-permute-start(bf16[256,768]{1,0:T(8,128)(2,1)S(1)} %collective-permute-done.25), channel_id=1, source_target_pairs={{0,1},{1,0},{2,3},{3,2},{4,5},{5,4},{6,7},{7,6},{8,9},{9,8},{10,11... | collective-permute-start | bytes 1179656 | tf_op jit(solution)/shard_map/ppermute | solution.py:585
  267.5 15.7 %collective-permute-start.28 = (bf16[256,768]{1,0:T(8,128)(2,1)}, bf16[256,768]{1,0:T(8,128)(2,1)S(1)}, u32[]{:S(2)}, u32[]{:S(2)}) collective-permute-start(bf16[256,768]{1,0:T(8,128)(2,1)} %collective-permute-done.27), channel_id=1, source_target_pairs={{0,1},{1,0},{2,3},{3,2},{4,5},{5,4},{6,7},{7,6},{8,9},{9,8},{10,11... | collective-permute-start | bytes 1179656 | tf_op jit(solution)/shard_map/ppermute | solution.py:585
  289.0 48.3 %collective-permute-start.30 = (bf16[1,2,208,1536]{3,2,1,0:T(8,128)(2,1)S(1)}, bf16[1,2,208,1536]{3,2,1,0:T(8,128)(2,1)}, u32[]{:S(2)}, u32[]{:S(2)}) collective-permute-start(bf16[1,2,208,1536]{3,2,1,0:T(8,128)(2,1)S(1)} %slice.136), channel_id=1, source_target_pairs={{0,16},{8,24},{16,0},{24,8},{1,17},{9,25},{17,1},{25,9},{2,18},{10... | collective-permute-start | bytes 3833864 | tf_op jit(solution)/shard_map/ppermute | solution.py:654
  322.6 29.4 %collective-permute-start.55 = (bf16[1,2,208,1536]{3,2,1,0:T(8,128)(2,1)}, bf16[1,2,208,1536]{3,2,1,0:T(8,128)(2,1)}, u32[]{:S(2)}, u32[]{:S(2)}) collective-permute-start(bf16[1,2,208,1536]{3,2,1,0:T(8,128)(2,1)} %slice.151), channel_id=1, source_target_pairs={{0,16},{8,24},{16,0},{24,8},{1,17},{9,25},{17,1},{25,9},{2,18},{10... | collective-permute-start | bytes 3833864 | tf_op jit(solution)/shard_map/ppermute | solution.py:654
  337.2 56.6 %collective-permute-start.40 = (bf16[2,2,208,1536]{3,2,1,0:T(8,128)(2,1)}, bf16[2,2,208,1536]{3,2,1,0:T(8,128)(2,1)}, u32[]{:S(2)}, u32[]{:S(2)}) collective-permute-start(bf16[2,2,208,1536]{3,2,1,0:T(8,128)(2,1)} %get-tuple-element.89), channel_id=1, source_target_pairs={{0,8},{8,0},{16,24},{24,16},{1,9},{9,1},{17,25},{25,17},{2,10},{10... | collective-permute-start | bytes 7667720 | tf_op jit(solution)/shard_map/ppermute | solution.py:649
  339.1 17.3 %collective-permute-start.31 = (bf16[1,208,1536]{2,1,0:T(8,128)(2,1)S(1)}, bf16[1,208,1536]{2,1,0:T(8,128)(2,1)S(1)}, u32[]{:S(2)}, u32[]{:S(2)}) collective-permute-start(bf16[1,208,1536]{2,1,0:T(8,128)(2,1)S(1)} %slice_bitcast_fusion.5), channel_id=1, source_target_pairs={{0,1},{1,0},{2,3},{3,2},{4,5},{5,4},{6,7},{7,6},{8,9},{9,8},{10,11... | collective-permute-start | bytes 1916936 | tf_op jit(solution)/shard_map/ppermute | solution.py:660
  353.6 37.2 %collective-permute-start.56 = (bf16[1,208,1536]{2,1,0:T(8,128)(2,1)S(1)}, bf16[1,208,1536]{2,1,0:T(8,128)(2,1)S(1)}, u32[]{:S(2)}, u32[]{:S(2)}) collective-permute-start(bf16[1,208,1536]{2,1,0:T(8,128)(2,1)S(1)} %slice_bitcast_fusion.1), channel_id=1, source_target_pairs={{0,1},{1,0},{2,3},{3,2},{4,5},{5,4},{6,7},{7,6},{8,9},{9,8},{10,11... | collective-permute-start | bytes 1916936 | tf_op jit(solution)/shard_map/ppermute | solution.py:660
  357.3 13.0 %collective-permute-start.49 = (bf16[208,384]{1,0:T(8,128)(2,1)}, bf16[208,384]{1,0:T(8,128)(2,1)S(1)}, u32[]{:S(2)}, u32[]{:S(2)}) collective-permute-start(bf16[208,384]{1,0:T(8,128)(2,1)} %get-tuple-element.114), channel_id=1, source_target_pairs={{0,2},{2,0},{4,6},{6,4},{1,3},{3,1},{5,7},{7,5},{8,10},{10,8},{12,... | collective-permute-start | bytes 479240 | tf_op jit(solution)/shard_map/ppermute | solution.py:582
  358.4 14.0 %collective-permute-start.50 = (bf16[208,384]{1,0:T(8,128)(2,1)S(1)}, bf16[208,384]{1,0:T(8,128)(2,1)S(1)}, u32[]{:S(2)}, u32[]{:S(2)}) collective-permute-start(bf16[208,384]{1,0:T(8,128)(2,1)S(1)} %get-tuple-element.116), channel_id=1, source_target_pairs={{0,4},{2,6},{4,0},{6,2},{1,5},{3,7},{5,1},{7,3},{8,12},{10,14},{12... | collective-permute-start | bytes 479240 | tf_op jit(solution)/shard_map/ppermute | solution.py:582
  360.5 11.9 %collective-permute-start.51 = (bf16[208,384]{1,0:T(8,128)(2,1)S(1)}, bf16[208,384]{1,0:T(8,128)(2,1)S(1)}, u32[]{:S(2)}, u32[]{:S(2)}) collective-permute-start(bf16[208,384]{1,0:T(8,128)(2,1)S(1)} %get-tuple-element.115), channel_id=1, source_target_pairs={{0,6},{2,4},{4,2},{6,0},{1,7},{3,5},{5,3},{7,1},{8,14},{10,12},{12... | collective-permute-start | bytes 479240 | tf_op jit(solution)/shard_map/ppermute | solution.py:582
  370.3 28.0 %collective-permute-start.33 = (bf16[256,768]{1,0:T(8,128)(2,1)}, bf16[256,768]{1,0:T(8,128)(2,1)S(1)}, u32[]{:S(2)}, u32[]{:S(2)}) collective-permute-start(bf16[256,768]{1,0:T(8,128)(2,1)} %get-tuple-element.91), channel_id=1, source_target_pairs={{0,1},{1,0},{2,3},{3,2},{4,5},{5,4},{6,7},{7,6},{8,9},{9,8},{10,11... | collective-permute-start | bytes 1179656 | tf_op jit(solution)/shard_map/ppermute | solution.py:585
  372.5 7.5 %collective-permute-start.52 = (bf16[208,384]{1,0:T(8,128)(2,1)S(1)}, bf16[208,384]{1,0:T(8,128)(2,1)S(1)}, u32[]{:S(2)}, u32[]{:S(2)}) collective-permute-start(bf16[208,384]{1,0:T(8,128)(2,1)S(1)} %get-tuple-element.100), channel_id=1, source_target_pairs={{0,2},{2,0},{4,6},{6,4},{1,3},{3,1},{5,7},{7,5},{8,10},{10,8},{12,... | collective-permute-start | bytes 479240 | tf_op jit(solution)/shard_map/ppermute | solution.py:582
  374.9 13.3 %collective-permute-start.53 = (bf16[208,384]{1,0:T(8,128)(2,1)S(1)}, bf16[208,384]{1,0:T(8,128)(2,1)S(1)}, u32[]{:S(2)}, u32[]{:S(2)}) collective-permute-start(bf16[208,384]{1,0:T(8,128)(2,1)S(1)} %get-tuple-element.100), channel_id=1, source_target_pairs={{0,4},{2,6},{4,0},{6,2},{1,5},{3,7},{5,1},{7,3},{8,12},{10,14},{12... | collective-permute-start | bytes 479240 | tf_op jit(solution)/shard_map/ppermute | solution.py:582
  380.1 8.8 %collective-permute-start.54 = (bf16[208,384]{1,0:T(8,128)(2,1)S(1)}, bf16[208,384]{1,0:T(8,128)(2,1)S(1)}, u32[]{:S(2)}, u32[]{:S(2)}) collective-permute-start(bf16[208,384]{1,0:T(8,128)(2,1)S(1)} %get-tuple-element.100), channel_id=1, source_target_pairs={{0,6},{2,4},{4,2},{6,0},{1,7},{3,5},{5,3},{7,1},{8,14},{10,12},{12... | collective-permute-start | bytes 479240 | tf_op jit(solution)/shard_map/ppermute | solution.py:582
  388.2 36.6 %collective-permute-start.34 = (bf16[256,768]{1,0:T(8,128)(2,1)S(1)}, bf16[256,768]{1,0:T(8,128)(2,1)S(1)}, u32[]{:S(2)}, u32[]{:S(2)}) collective-permute-start(bf16[256,768]{1,0:T(8,128)(2,1)S(1)} %copy-done.29), channel_id=1, source_target_pairs={{0,2},{2,0},{4,6},{6,4},{1,3},{3,1},{5,7},{7,5},{8,10},{10,8},{12,... | collective-permute-start | bytes 1179656 | tf_op jit(solution)/shard_map/ppermute | solution.py:582
  391.0 12.2 %collective-permute-start.57 = (bf16[208,384]{1,0:T(8,128)(2,1)S(1)}, bf16[208,384]{1,0:T(8,128)(2,1)S(1)}, u32[]{:S(2)}, u32[]{:S(2)}) collective-permute-start(bf16[208,384]{1,0:T(8,128)(2,1)S(1)} %get-tuple-element.111), channel_id=1, source_target_pairs={{0,2},{2,0},{4,6},{6,4},{1,3},{3,1},{5,7},{7,5},{8,10},{10,8},{12,... | collective-permute-start | bytes 479240 | tf_op jit(solution)/shard_map/ppermute | solution.py:582
  393.2 26.8 %collective-permute-start.58 = (bf16[208,384]{1,0:T(8,128)(2,1)S(1)}, bf16[208,384]{1,0:T(8,128)(2,1)S(1)}, u32[]{:S(2)}, u32[]{:S(2)}) collective-permute-start(bf16[208,384]{1,0:T(8,128)(2,1)S(1)} %get-tuple-element.113), channel_id=1, source_target_pairs={{0,4},{2,6},{4,0},{6,2},{1,5},{3,7},{5,1},{7,3},{8,12},{10,14},{12... | collective-permute-start | bytes 479240 | tf_op jit(solution)/shard_map/ppermute | solution.py:582
  393.8 28.6 %collective-permute-start.59 = (bf16[208,384]{1,0:T(8,128)(2,1)S(1)}, bf16[208,384]{1,0:T(8,128)(2,1)S(1)}, u32[]{:S(2)}, u32[]{:S(2)}) collective-permute-start(bf16[208,384]{1,0:T(8,128)(2,1)S(1)} %get-tuple-element.112), channel_id=1, source_target_pairs={{0,6},{2,4},{4,2},{6,0},{1,7},{3,5},{5,3},{7,1},{8,14},{10,12},{12... | collective-permute-start | bytes 479240 | tf_op jit(solution)/shard_map/ppermute | solution.py:582
  398.3 58.8 %collective-permute-start.41 = (bf16[1,2,208,1536]{3,2,1,0:T(8,128)(2,1)S(1)}, bf16[1,2,208,1536]{3,2,1,0:T(8,128)(2,1)S(1)}, u32[]{:S(2)}, u32[]{:S(2)}) collective-permute-start(bf16[1,2,208,1536]{3,2,1,0:T(8,128)(2,1)S(1)} %slice.140), channel_id=1, source_target_pairs={{0,16},{8,24},{16,0},{24,8},{1,17},{9,25},{17,1},{25,9},{2,18},{10... | collective-permute-start | bytes 3833864 | tf_op jit(solution)/shard_map/ppermute | solution.py:654
  403.3 39.6 %collective-permute-start.36 = (bf16[256,768]{1,0:T(8,128)(2,1)S(1)}, bf16[256,768]{1,0:T(8,128)(2,1)S(1)}, u32[]{:S(2)}, u32[]{:S(2)}) collective-permute-start(bf16[256,768]{1,0:T(8,128)(2,1)S(1)} %copy-done.28), channel_id=1, source_target_pairs={{0,4},{2,6},{4,0},{6,2},{1,5},{3,7},{5,1},{7,3},{8,12},{10,14},{12... | collective-permute-start | bytes 1179656 | tf_op jit(solution)/shard_map/ppermute | solution.py:582
  420.0 23.7 %collective-permute-start.38 = (bf16[256,768]{1,0:T(8,128)(2,1)S(1)}, bf16[256,768]{1,0:T(8,128)(2,1)S(1)}, u32[]{:S(2)}, u32[]{:S(2)}) collective-permute-start(bf16[256,768]{1,0:T(8,128)(2,1)S(1)} %copy-done.27), channel_id=1, source_target_pairs={{0,6},{2,4},{4,2},{6,0},{1,7},{3,5},{5,3},{7,1},{8,14},{10,12},{12... | collective-permute-start | bytes 1179656 | tf_op jit(solution)/shard_map/ppermute | solution.py:582
  422.5 12.7 %collective-permute-start.60 = (bf16[208,384]{1,0:T(8,128)(2,1)S(1)}, bf16[208,384]{1,0:T(8,128)(2,1)S(1)}, u32[]{:S(2)}, u32[]{:S(2)}) collective-permute-start(bf16[208,384]{1,0:T(8,128)(2,1)S(1)} %get-tuple-element.98), channel_id=1, source_target_pairs={{0,2},{2,0},{4,6},{6,4},{1,3},{3,1},{5,7},{7,5},{8,10},{10,8},{12,... | collective-permute-start | bytes 479240 | tf_op jit(solution)/shard_map/ppermute | solution.py:582
  424.8 29.5 %collective-permute-start.61 = (bf16[208,384]{1,0:T(8,128)(2,1)S(1)}, bf16[208,384]{1,0:T(8,128)(2,1)S(1)}, u32[]{:S(2)}, u32[]{:S(2)}) collective-permute-start(bf16[208,384]{1,0:T(8,128)(2,1)S(1)} %get-tuple-element.98), channel_id=1, source_target_pairs={{0,4},{2,6},{4,0},{6,2},{1,5},{3,7},{5,1},{7,3},{8,12},{10,14},{12... | collective-permute-start | bytes 479240 | tf_op jit(solution)/shard_map/ppermute | solution.py:582
  435.2 19.8 %collective-permute-start.62 = (bf16[208,384]{1,0:T(8,128)(2,1)S(1)}, bf16[208,384]{1,0:T(8,128)(2,1)S(1)}, u32[]{:S(2)}, u32[]{:S(2)}) collective-permute-start(bf16[208,384]{1,0:T(8,128)(2,1)S(1)} %get-tuple-element.98), channel_id=1, source_target_pairs={{0,6},{2,4},{4,2},{6,0},{1,7},{3,5},{5,3},{7,1},{8,14},{10,12},{12... | collective-permute-start | bytes 479240 | tf_op jit(solution)/shard_map/ppermute | solution.py:582
  442.9 15.9 %collective-permute-start.35 = (bf16[256,768]{1,0:T(8,128)(2,1)S(1)}, bf16[256,768]{1,0:T(8,128)(2,1)S(1)}, u32[]{:S(2)}, u32[]{:S(2)}) collective-permute-start(bf16[256,768]{1,0:T(8,128)(2,1)S(1)} %collective-permute-done.34), channel_id=1, source_target_pairs={{0,1},{1,0},{2,3},{3,2},{4,5},{5,4},{6,7},{7,6},{8,9},{9,8},{10,11... | collective-permute-start | bytes 1179656 | tf_op jit(solution)/shard_map/ppermute | solution.py:585
  443.6 16.3 %collective-permute-start.37 = (bf16[256,768]{1,0:T(8,128)(2,1)S(1)}, bf16[256,768]{1,0:T(8,128)(2,1)S(1)}, u32[]{:S(2)}, u32[]{:S(2)}) collective-permute-start(bf16[256,768]{1,0:T(8,128)(2,1)S(1)} %collective-permute-done.36), channel_id=1, source_target_pairs={{0,1},{1,0},{2,3},{3,2},{4,5},{5,4},{6,7},{7,6},{8,9},{9,8},{10,11... | collective-permute-start | bytes 1179656 | tf_op jit(solution)/shard_map/ppermute | solution.py:585
  454.2 40.8 %collective-permute-start.39 = (bf16[256,768]{1,0:T(8,128)(2,1)S(1)}, bf16[256,768]{1,0:T(8,128)(2,1)S(1)}, u32[]{:S(2)}, u32[]{:S(2)}) collective-permute-start(bf16[256,768]{1,0:T(8,128)(2,1)S(1)} %collective-permute-done.38), channel_id=1, source_target_pairs={{0,1},{1,0},{2,3},{3,2},{4,5},{5,4},{6,7},{7,6},{8,9},{9,8},{10,11... | collective-permute-start | bytes 1179656 | tf_op jit(solution)/shard_map/ppermute | solution.py:585
  457.5 21.0 %collective-permute-start.42 = (bf16[1,208,1536]{2,1,0:T(8,128)(2,1)S(1)}, bf16[1,208,1536]{2,1,0:T(8,128)(2,1)S(1)}, u32[]{:S(2)}, u32[]{:S(2)}) collective-permute-start(bf16[1,208,1536]{2,1,0:T(8,128)(2,1)S(1)} %slice_bitcast_fusion.3), channel_id=1, source_target_pairs={{0,1},{1,0},{2,3},{3,2},{4,5},{5,4},{6,7},{7,6},{8,9},{9,8},{10,11... | collective-permute-start | bytes 1916936 | tf_op jit(solution)/shard_map/ppermute | solution.py:660
  478.7 8.0 %collective-permute-start.43 = (bf16[208,384]{1,0:T(8,128)(2,1)S(1)}, bf16[208,384]{1,0:T(8,128)(2,1)S(1)}, u32[]{:S(2)}, u32[]{:S(2)}) collective-permute-start(bf16[208,384]{1,0:T(8,128)(2,1)S(1)} %get-tuple-element.120), channel_id=1, source_target_pairs={{0,2},{2,0},{4,6},{6,4},{1,3},{3,1},{5,7},{7,5},{8,10},{10,8},{12,... | collective-permute-start | bytes 479240 | tf_op jit(solution)/shard_map/ppermute | solution.py:582
  481.2 10.2 %collective-permute-start.44 = (bf16[208,384]{1,0:T(8,128)(2,1)S(1)}, bf16[208,384]{1,0:T(8,128)(2,1)S(1)}, u32[]{:S(2)}, u32[]{:S(2)}) collective-permute-start(bf16[208,384]{1,0:T(8,128)(2,1)S(1)} %get-tuple-element.122), channel_id=1, source_target_pairs={{0,4},{2,6},{4,0},{6,2},{1,5},{3,7},{5,1},{7,3},{8,12},{10,14},{12... | collective-permute-start | bytes 479240 | tf_op jit(solution)/shard_map/ppermute | solution.py:582
  481.9 9.5 %collective-permute-start.45 = (bf16[208,384]{1,0:T(8,128)(2,1)S(1)}, bf16[208,384]{1,0:T(8,128)(2,1)S(1)}, u32[]{:S(2)}, u32[]{:S(2)}) collective-permute-start(bf16[208,384]{1,0:T(8,128)(2,1)S(1)} %get-tuple-element.121), channel_id=1, source_target_pairs={{0,6},{2,4},{4,2},{6,0},{1,7},{3,5},{5,3},{7,1},{8,14},{10,12},{12... | collective-permute-start | bytes 479240 | tf_op jit(solution)/shard_map/ppermute | solution.py:582
  491.6 9.5 %collective-permute-start.46 = (bf16[208,384]{1,0:T(8,128)(2,1)S(1)}, bf16[208,384]{1,0:T(8,128)(2,1)S(1)}, u32[]{:S(2)}, u32[]{:S(2)}) collective-permute-start(bf16[208,384]{1,0:T(8,128)(2,1)S(1)} %get-tuple-element.102), channel_id=1, source_target_pairs={{0,2},{2,0},{4,6},{6,4},{1,3},{3,1},{5,7},{7,5},{8,10},{10,8},{12,... | collective-permute-start | bytes 479240 | tf_op jit(solution)/shard_map/ppermute | solution.py:582
  493.9 11.3 %collective-permute-start.47 = (bf16[208,384]{1,0:T(8,128)(2,1)S(1)}, bf16[208,384]{1,0:T(8,128)(2,1)S(1)}, u32[]{:S(2)}, u32[]{:S(2)}) collective-permute-start(bf16[208,384]{1,0:T(8,128)(2,1)S(1)} %get-tuple-element.102), channel_id=1, source_target_pairs={{0,4},{2,6},{4,0},{6,2},{1,5},{3,7},{5,1},{7,3},{8,12},{10,14},{12... | collective-permute-start | bytes 479240 | tf_op jit(solution)/shard_map/ppermute | solution.py:582
  495.1 10.2 %collective-permute-start.48 = (bf16[208,384]{1,0:T(8,128)(2,1)S(1)}, bf16[208,384]{1,0:T(8,128)(2,1)S(1)}, u32[]{:S(2)}, u32[]{:S(2)}) collective-permute-start(bf16[208,384]{1,0:T(8,128)(2,1)S(1)} %get-tuple-element.102), channel_id=1, source_target_pairs={{0,6},{2,4},{4,2},{6,0},{1,7},{3,5},{5,3},{7,1},{8,14},{10,12},{12... | collective-permute-start | bytes 479240 | tf_op jit(solution)/shard_map/ppermute | solution.py:582
  (37 other events, 574.2 us)

commit v3 on v2

--- a/solution.py
+++ b/solution.py
@@ -571,12 +571,15 @@
     R = ns * span
     dims = (F, C, T, ns, span, D)
 
-    def to_sequences(array):
-        out = []
-        for k in range(C):
+    def to_sequences(array, chained):
+        out, before = {}, []
+        for k in sorted(range(C), key=lambda k: (k > 0, k % 2 == 0, k)):
             piece = lax.dynamic_slice_in_dim(array, ((c ^ k) * T + t) * ns, ns, 0).reshape(R, D)
-            out.append(lax.ppermute(piece, "ctx", xor_pairs(C, k)) if k else piece)
-        return out
+            if k:
+                piece = lax.ppermute(after(piece, before), "ctx", xor_pairs(C, k))
+                before = [piece] if chained else []
+            out[k] = piece
+        return [out[k] for k in range(C)]
 
     def ctx_moved(piece, k):
         return lax.ppermute(piece, "ctx", xor_pairs(C, k)) if k else piece
@@ -606,15 +609,16 @@
         axis, bit = order_of(F, T, across)[-1]
         return swapped(held, axis, bit)
 
-    def both_cores(held, got):
-        return [held, got, swapped(held, "fsdp", 1), swapped(got, "fsdp", 1)]
+    def both_cores(held, got, others=()):
+        near = swapped(after(held, others), "fsdp", 1)
+        return [held, got, near, swapped(got, "fsdp", 1)]
 
     def spread(array, width):
         rows, part = array.shape
         owner = lax.broadcasted_iota(jnp.int32, (rows, part * F), 1) // part
         return jnp.where(owner == f, jnp.tile(array, (1, F)), jnp.zeros((), BF)).reshape(-1, width)
 
-    x_pieces = to_sequences(tokens_in)
+    x_pieces = to_sequences(tokens_in, True)
     vectors = jnp.stack([output_bias, attn_gain, attn_shift, outer_bias, ffn_gain, ffn_shift])
     small = [
         spread(query_bias, half), spread(value_bias, half), spread(inner_bias, fhalf),
@@ -626,39 +630,41 @@
     high = jnp.concatenate([value_weight, output_weight.T], axis=1)
     low = chip_start(jnp.concatenate([low, small[:, :D]], axis=0), False)
     high = chip_start(jnp.concatenate([high, small[:, D:]], axis=0), True)
-    low = after(low, [x_pieces[k] for k in range(1, C, 2)])
-    lows = both_cores(low, chip_end(low, False))
-    highs = both_cores(high, chip_end(high, True))
-    inner = chip_start(after(inner_weight, [lows[1], highs[1]]), False)
-    outer = chip_start(after(outer_weight.T, [lows[1], highs[1]]), True)
-    inner_got, outer_got = chip_end(inner, False), chip_end(outer, True)
-    cot_pieces = to_sequences(after(cotangent, [*x_pieces, *lows, *highs]))
+    lows = both_cores(low, chip_end(after(low, x_pieces[1:2]), False))
+    highs = both_cores(high, chip_end(after(high, x_pieces[1:2]), True))
+    halfway = [lows[1], highs[1], *x_pieces[3:4]]
+    inner = chip_start(after(inner_weight, halfway), False)
+    outer = chip_start(after(outer_weight.T, halfway), True)
+    inner_got = chip_end(after(inner, x_pieces[2:3]), False)
+    outer_got = chip_end(after(outer, x_pieces[2:3]), True)
+    cot_pieces = to_sequences(after(cotangent, [*x_pieces, *lows, *highs]), False)
     lengths = lax.dynamic_slice_in_dim(seq_lengths, (c * T + t) * ns, ns, 0)
     meta = jnp.concatenate([jnp.stack([f, c]).astype(jnp.int32), lengths])
 
     x_all, qkv_w, qkv, e, linv, ctx = front_call(
         dims, after(meta, [inner, outer]), x_pieces, lows, highs
     )
-    inners = both_cores(after(inner, [ctx]), inner_got)
-    outers = both_cores(after(outer, [ctx]), outer_got)
-    los, (first, dctx, nl, act, og, ig, ag, sums) = rows_call(
+    inners = both_cores(inner, inner_got, [ctx, *cot_pieces])
+    outers = both_cores(outer, outer_got, [ctx, *cot_pieces])
+    los, (first, dctx, nl, act, og, inner_low, ag, sums) = rows_call(
         dims, FF, meta, x_all, ctx.reshape(C, R, D), cot_pieces, lows + highs + inners + outers,
     )
 
     def core_sum(keep, send):
         return added(keep, lax.ppermute(send, "fsdp", xor_pairs(F, 1)))
 
+    def chip_sum(total, axis, dim):
+        while total.shape[dim] > 1:
+            h = total.shape[dim] // 2
+            stay, go = jnp.split(total, 2, axis=dim)
+            total = added(stay, swapped(go, axis, 2 * h if axis == "fsdp" else h))
+        return total
+
     def y_sum(total):
-        while total.shape[0] > 1:
-            h = total.shape[0] // 2
-            total = added(total[:h], lax.ppermute(total[h:], "fsdp", xor_pairs(F, 2 * h)))
-        return total[0]
+        return chip_sum(total, "fsdp", 0)
 
     def x_sum(total):
-        while total.shape[0] > 1:
-            h = total.shape[0] // 2
-            total = added(total[:h], lax.ppermute(total[h:], "tp", xor_pairs(T, h)))
-        return total[0]
+        return chip_sum(total, "tp", 1)
 
     def ctx_scatter(total):
         part = total.shape[1] // C
@@ -677,26 +683,29 @@
 
     lo = {k: ctx_moved(los[k], k) for k in range(C)}
     lo_both = [tp_moved(lo[k]) for k in range(C)]
+    dqkv = back_call(dims, qkv, ctx, dctx.reshape(ctx.shape), e, linv)
+    first = after(first, [lo[1], lo[3], *lo_both[0]])
+    ins = input_call(dqkv.reshape(C, R, 3 * D), qkv_w, first)
+    ig = {k: ctx_moved(ins[k], k) for k in range(C)}
+    ig_both = [tp_moved(ig[k]) for k in range(C)]
+    og = after(og, [lo[2], *lo_both[1], *ins])
     outer_parts = weight_call(dims, meta, [(og, act)], sums)
-    nl = after(nl, [lo[1], *lo_both[0]])
-    inner_parts = weight_call(dims, meta, [(nl, ig)])
+    nl = after(nl, [ig[1], ig[3], *lo_both[3], *outer_parts])
+    inner_parts = weight_call(dims, meta, [(nl, inner_low)])
     outer_core = core_sum(*outer_parts)
-    dctx = after(dctx, [outer_core, lo[3], *lo_both[1], *inner_parts])
-    dqkv = back_call(dims, qkv, ctx, dctx.reshape(ctx.shape), e, linv)
+    ag = after(ag, [outer_core, *lo_both[2], *ig_both[0], *inner_parts])
+    qkv_parts = weight_call(dims, meta, [(x_all, dqkv), (ag, ctx)])
     inner_core = core_sum(*inner_parts)
     outer_y = y_sum(outer_core)
-    ag = after(ag, [inner_core, outer_y, lo[2], *lo_both[3], dqkv])
-    qkv_parts = weight_call(dims, meta, [(x_all, dqkv), (ag, ctx)])
-    outer_x = x_sum(outer_y)
-    inner_y = y_sum(inner_core)
-    first = after(first, [outer_x, *lo_both[2], *qkv_parts])
-    ins = input_call(dqkv.reshape(C, R, 3 * D), qkv_w, first)
-    qkv_core = core_sum(*qkv_parts)
+    inner_half = x_sum(inner_core)
+    keep, send = qkv_parts
+    qkv_core = core_sum(after(keep, [inner_half, ig[2], *ig_both[1]]), send)
+    layer_out = to_slots(lo_both, BF)
+    input_grad = to_slots(ig_both, F32)
+    inner_x = y_sum(inner_half)[0, 0]
+    qkv_x = x_sum(y_sum(qkv_core))[0, 0]
+    outer_x = x_sum(outer_y)[0, 0]
     outer_part = ctx_scatter(outer_x)
-    layer_out = to_slots(lo_both, BF)
-    input_grad = to_slots([tp_moved(ctx_moved(ins[k], k)) for k in range(C)], F32)
-    inner_x = x_sum(inner_y)
-    qkv_x = x_sum(y_sum(qkv_core))
     outer_g = ctx_gather(outer_part, outer_x)
     inner_g = ctx_gather(ctx_scatter(inner_x), inner_x)
     qkv_g = ctx_gather(ctx_scatter(qkv_x), qkv_x)

time: 510 us -> 427 us (0.84)
  waiting for transfers between devices: 232 us -> 122 us
  starting transfers between devices: 72.9 us -> 97.6 us
  other arithmetic: 16.5 us -> 25.4 us
  local copies, waits for them, and re-layouts: 34.5 us -> 28.2 us
    ppermute x12 -> x6, waiting for transfers between devices: 96.3 us -> 24.6 us  [to_sequences(): piece = lax.ppermute(after(piece, before), 'ctx', xor_pairs(C, k))]
    ppermute x24, waiting for transfers between devices: 93.7 us -> 33.5 us  [ctx_moved(): return lax.ppermute(piece, 'ctx', xor_pairs(C, k)) if k else piece]
    ppermute x16 -> x22, waiting for transfers between devices: 25.2 us -> 59 us  [swapped(): return lax.ppermute(array, axis, xor_pairs(lax.axis_size(axis), bit))]
    ppermute x24, starting transfers between devices: 39.1 us -> 55.6 us  [ctx_moved(): return lax.ppermute(piece, 'ctx', xor_pairs(C, k)) if k else piece]
    ppermute x8, waiting for transfers between devices: 17 us -> 4.75 us  [tp_moved(): lax.ppermute(piece, 'tp', xor_pairs(T, dt))]
    dynamic_update_slice x8, other arithmetic: 0.44 us -> 12.5 us  [to_slots(): lax.dynamic_update_slice_in_dim(out, got.reshape(ns, span, D).astype(kind...]
    unnamed x79 -> x53, local copies, waits for them, and re-layouts: 9.89 us -> 0.93 us
    ppermute x16 -> x22, starting transfers between devices: 11.5 us -> 15.7 us  [swapped(): return lax.ppermute(array, axis, xor_pairs(lax.axis_size(axis), bit))]
  transfers between devices with their start and end apart: 63 -> 63, of which waited for: 34 -> 26; matrix products, arithmetic and copies ran while one was open for 6% -> 10% of each run, Pallas kernels for 18% -> 24%
where the time goes in v3:
time: 427 us; the launch traced here: 425 us
  Pallas kernels  151 us (35%)
  waiting for transfers between devices  122 us (29%)
  starting transfers between devices  97.6 us (23%)
  local copies, waits for them, and re-layouts  28.2 us (7%)
  other arithmetic  25.4 us (6%)
    ppermute x22, waiting for transfers between devices, swapped(): return lax.ppermute(array, axis, xor_pairs(lax.axis_size(axis), bit))  59 us
    ppermute x24, starting transfers between devices, ctx_moved(): return lax.ppermute(piece, 'ctx', xor_pairs(C, k)) if k else piece  55.6 us
    pallas_call x1, Pallas kernels, rows_call(): pl.pallas_call(functools.partial(rows_kernel, dims, FF), name='rows', gri...  46.7 us
    pallas_call x3, Pallas kernels, weight_call(): pl.pallas_call(functools.partial(weight_kernel, F, pers, sums is not None...  39.6 us
    ppermute x24, waiting for transfers between devices, ctx_moved(): return lax.ppermute(piece, 'ctx', xor_pairs(C, k)) if k else piece  33.5 us
    pallas_call x1, Pallas kernels, front_call(): pl.pallas_call(functools.partial(front_kernel, dims), name='front', grid=...  29.6 us
    pallas_call x1, Pallas kernels, back_call(): pl.pallas_call(functools.partial(back_kernel, dims), name='back', grid=(n...  26.1 us
    ppermute x6, waiting for transfers between devices, to_sequences(): piece = lax.ppermute(after(piece, before), 'ctx', xor_pairs(C, k))  24.6 us
  transfers between devices with their start and end apart: 63, of which 26 were waited for; matrix products, arithmetic and copies ran while one was open for 10% of the time, Pallas kernels for 24%

profile of v3, /device:TPU:0, one launch (start us, length us, event | category | flops | bytes accessed | tf_op | source)
XLA Modules:
  0.0 425.1 jit_solution(18065482132289249186)
XLA Ops:
  8.4 3.0 collective-permute-start
  12.4 1.6 collective-permute-start.3
  14.0 2.3 constant_dynamic-slice_fusion.8
  16.3 1.6 collective-permute-start.1
  19.0 2.5 collective-permute-done.3
  21.6 5.0 %collective-permute-done.1.refs_1_ = bf16[256,768]{1,0:T(8,128)(2,1)S(1)} collective-permute-done((bf16[256,768]{1,0:T(8,128)(2,1)S(1)}, bf16[256,768]{1,0:T(8,128)(2,1)S(1)}, u32[]{:S(2)}, u32[]{:S(2)}) %collective-permute-start.1) | collective-permute-done | bytes 393248 | tf_op jit(solution)/shard_map/ppermute | solution.py:579
  27.5 3.8 collective-permute-start.5
  31.3 7.3 %collective-permute-done.5.refs_3_ = bf16[256,768]{1,0:T(8,128)(2,1)S(1)} collective-permute-done((bf16[256,768]{1,0:T(8,128)(2,1)S(1)}, bf16[256,768]{1,0:T(8,128)(2,1)S(1)}, u32[]{:S(2)}, u32[]{:S(2)}) %collective-permute-start.5) | collective-permute-done | bytes 393248 | tf_op jit(solution)/shard_map/ppermute | solution.py:579
  38.6 2.7 collective-permute-done.2.refs_5_
  41.6 1.6 collective-permute-start.7
  43.7 7.6 %collective-permute-start.8 = (bf16[256,768]{1,0:T(8,128)(2,1)S(1)}, bf16[256,768]{1,0:T(8,128)(2,1)S(1)}, u32[]{:S(2)}, u32[]{:S(2)}) collective-permute-start(bf16[256,768]{1,0:T(8,128)(2,1)S(1)} %bitcast.122), channel_id=1, source_target_pairs={{0,4},{2,6},{4,0},{6,2},{1,5},{3,7},{5,1},{7,3},{8,12},{10,14},{12... | collective-permute-start | bytes 1179656 | tf_op jit(solution)/shard_map/ppermute | solution.py:579
  51.8 2.4 collective-permute-done.7
  54.4 12.2 %collective-permute-done.8.refs_2_ = bf16[256,768]{1,0:T(8,128)(2,1)S(1)} collective-permute-done((bf16[256,768]{1,0:T(8,128)(2,1)S(1)}, bf16[256,768]{1,0:T(8,128)(2,1)S(1)}, u32[]{:S(2)}, u32[]{:S(2)}) %collective-permute-start.8) | collective-permute-done | bytes 393248 | tf_op jit(solution)/shard_map/ppermute | solution.py:579
  69.7 3.0 collective-permute-start.14
  72.7 1.4 collective-permute-start.15
  74.7 29.6 %front.1 = (bf16[4,256,768]{2,1,0:T(8,128)(2,1)}, bf16[768,2304]{1,0:T(8,128)(2,1)}, bf16[4,2,128,2304]{3,2,1,0:T(8,128)(2,1)}, bf16[12,1024,512]{2,1,0:T(8,128)...) custom-call(s32[4]{0:T(128)} %pad_add_fusion.meta, bf16[256,768]{1,0:T(8,128)(2,1)} %bitcast.121, ...), custom_call_target="tpu_custom_call" | custom-call | flops 3623878656 | bytes 40000000 | tf_op jit(solution)/shard_map/front/pallas_call | solution.py:162
  106.1 1.8 collective-permute-done.20.refs_18_
  107.9 1.8 collective-permute-done.17.refs_14_
  109.7 1.7 collective-permute-done.21.refs_19_
  111.4 1.7 collective-permute-done.18.refs_15_
  113.1 46.7 %rows.1 = (bf16[256,768]{1,0:T(8,128)(2,1)}, bf16[256,768]{1,0:T(8,128)(2,1)}, bf16[256,768]{1,0:T(8,128)(2,1)}, bf16[256,768]{1,0:T(8,128)(2,1)}, f32[4,256,768...) custom-call(s32[4]{0:T(128)} %pad_add_fusion.meta, ...), custom_call_target="tpu_custom_call" | custom-call | flops 21743271936 | bytes 50000000 | tf_op jit(solution)/shard_map/rows/pallas_call | solution.py:344
  160.9 2.7 collective-permute-start.23
  163.6 2.4 collective-permute-start.27
  166.0 26.1 %back.1 = bf16[4,2,128,2304]{3,2,1,0:T(8,128)(2,1)} custom-call(bf16[4,2,128,2304]{3,2,1,0:T(8,128)(2,1)} %get-tuple-element.80.qkv, bf16[4,2,128,768]{3,2,1,0:T(8,128)(2,1)} %get-tuple-element.70.ctx, bf16[4,2,128,768]{3,2,1,0:T(8,128)(2,1)} %bitcast.109, bf16[12,1024,512]{2,1,0:T(8,128)(2,1)} %get-tuple-element.82.e_ref, ...), custom_call_target="tpu_custom_call" | custom-call | flops 6442450944 | bytes 30000000 | tf_op jit(solution)/shard_map/back/pallas_call | solution.py:413
  193.7 8.7 %input_grad.1 = (bf16[256,768]{1,0:T(8,128)(2,1)}, bf16[256,768]{1,0:T(8,128)(2,1)}, bf16[256,768]{1,0:T(8,128)(2,1)}, bf16[256,768]{1,0:T(8,128)(2,1)}) custom-call(bf16[4,256,2304]{2,1,0:T(8,128)(2,1)} %bitcast.105, bf16[768,2304]{1,0:T(8,128)(2,1)} %get-tuple-element.84.w, f32[4,256,768]{2,1,0:T(8,128)} %get-tuple-element.86.first), custom_call_target="tpu_custom_call" | custom-call | flops 3623878656 | bytes 15000000 | tf_op jit(solution)/shard_map/input_grad/pallas_call | solution.py:450
  202.4 2.0 collective-permute-start.30
  204.4 2.4 collective-permute-start.34
  208.9 12.8 %weight_grad.3 = (bf16[2,2,208,1536]{3,2,1,0:T(8,128)(2,1)}, bf16[2,2,208,1536]{3,2,1,0:T(8,128)(2,1)}) custom-call(s32[4]{0:T(128)} %pad_add_fusion.meta, bf16[1024,768]{1,0:T(8,128)(2,1)} %bitcast.141, bf16[1024,3072]{1,0:T(8,128)(2,1)} %bitcast.137, f32[16,768]{1,0:T(8,128)} %get-tuple-element.95.refs_2_), custom_call_target="tpu_custom_call" | custom-call | flops 4831838208 | bytes 12582912 | tf_op jit(solution)/shard_map/weight_grad/pallas_call | solution.py:523
  223.8 3.4 broadcast_in_dim.39
  229.0 12.8 %weight_grad.4 = (bf16[2,2,208,1536]{3,2,1,0:T(8,128)(2,1)}, bf16[2,2,208,1536]{3,2,1,0:T(8,128)(2,1)}) custom-call(s32[4]{0:T(128)} %pad_add_fusion.meta, bf16[1024,768]{1,0:T(8,128)(2,1)} %bitcast.140, bf16[1024,3072]{1,0:T(8,128)(2,1)} %bitcast.136), custom_call_target="tpu_custom_call" | custom-call | flops 4831838208 | bytes 12582912 | tf_op jit(solution)/shard_map/weight_grad/pallas_call | solution.py:523
  246.3 1.9 convert_dynamic-update-slice_fusion.6
  252.4 4.7 %collective-permute-done.31 = bf16[256,768]{1,0:T(8,128)(2,1)S(1)} collective-permute-done((bf16[256,768]{1,0:T(8,128)(2,1)S(1)}, bf16[256,768]{1,0:T(8,128)(2,1)S(1)}, u32[]{:S(2)}, u32[]{:S(2)}) %collective-permute-start.31) | collective-permute-done | bytes 393248 | tf_op jit(solution)/shard_map/ppermute | solution.py:588
  258.1 1.9 convert_dynamic-update-slice_fusion.3
  260.0 2.4 add_convert_fusion.2
  262.6 1.4 collective-permute-start.48
  264.0 14.1 %weight_grad.5 = (bf16[2,2,208,1536]{3,2,1,0:T(8,128)(2,1)}, bf16[2,2,208,1536]{3,2,1,0:T(8,128)(2,1)}) custom-call(s32[4]{0:T(128)} %pad_add_fusion.meta, bf16[1024,768]{1,0:T(8,128)(2,1)} %bitcast.138, bf16[1024,768]{1,0:T(8,128)(2,1)} %bitcast.139, bf16[1024,2304]{1,0:T(8,128)(2,1)} %bitcast.106, bf16[1024,768]{1,0:T(8,128)(2,1)} %bitcast.108), custom_call_target="tpu_custom_call" | custom-call | flops 4831838208 | bytes 12582912 | tf_op jit(solution)/shard_map/weight_grad/pallas_call | solution.py:523
  278.1 3.2 add_convert_fusion.1
  282.0 1.9 convert_dynamic-update-slice_fusion.2
  283.9 1.9 convert_dynamic-update-slice_fusion.1
  285.9 5.6 %collective-permute-done.48 = bf16[1,2,208,1536]{3,2,1,0:T(8,128)(2,1)} collective-permute-done((bf16[1,2,208,1536]{3,2,1,0:T(8,128)(2,1)S(1)}, bf16[1,2,208,1536]{3,2,1,0:T(8,128)(2,1)}, u32[]{:S(2)}, u32[]{:S(2)}) %collective-permute-start.48) | collective-permute-done | bytes 1277984 | tf_op jit(solution)/shard_map/ppermute | solution.py:600
  291.5 1.6 add_convert_fusion.3
  294.3 1.9 convert_dynamic-update-slice_fusion
  296.3 16.1 %collective-permute-done.38 = bf16[2,1,208,1536]{3,2,1,0:T(8,128)(2,1)S(1)} collective-permute-done((bf16[2,1,208,1536]{3,2,1,0:T(8,128)(2,1)S(1)}, bf16[2,1,208,1536]{3,2,1,0:T(8,128)(2,1)S(1)}, u32[]{:S(2)}, u32[]{:S(2)}) %collective-permute-start.38) | collective-permute-done | bytes 1277984 | tf_op jit(solution)/shard_map/ppermute | solution.py:600
  313.5 12.1 %collective-permute-done.49 = bf16[1,1,208,1536]{3,2,1,0:T(8,128)(2,1)S(1)} collective-permute-done((bf16[1,1,208,1536]{3,2,1,0:T(8,128)(2,1)S(1)}, bf16[1,1,208,1536]{3,2,1,0:T(8,128)(2,1)S(1)}, u32[]{:S(2)}, u32[]{:S(2)}) %collective-permute-start.49) | collective-permute-done | bytes 639008 | tf_op jit(solution)/shard_map/ppermute | solution.py:600
  325.8 1.8 collective-permute-start.50
  328.6 1.7 collective-permute-start.52
  334.2 1.3 collective-permute-start.58
  335.5 6.8 %collective-permute-done.51 = bf16[208,384]{1,0:T(8,128)(2,1)S(1)} collective-permute-done((bf16[208,384]{1,0:T(8,128)(2,1)S(1)}, bf16[208,384]{1,0:T(8,128)(2,1)S(1)}, u32[]{:S(2)}, u32[]{:S(2)}) %collective-permute-start.51) | collective-permute-done | bytes 159776 | tf_op jit(solution)/shard_map/ppermute | solution.py:585
  342.3 2.4 collective-permute-start.59
  344.8 10.2 %collective-permute-start.53 = (bf16[208,384]{1,0:T(8,128)(2,1)S(1)}, bf16[208,384]{1,0:T(8,128)(2,1)S(1)}, u32[]{:S(2)}, u32[]{:S(2)}) collective-permute-start(bf16[208,384]{1,0:T(8,128)(2,1)S(1)} %get-tuple-element.112), channel_id=1, source_target_pairs={{0,2},{2,0},{4,6},{6,4},{1,3},{3,1},{5,7},{7,5},{8,10},{10,8},{12,... | collective-permute-start | bytes 479240 | tf_op jit(solution)/shard_map/ppermute | solution.py:585
  355.7 2.0 collective-permute-done.58
  357.8 5.8 %collective-permute-start.60 = (bf16[208,384]{1,0:T(8,128)(2,1)S(1)}, bf16[208,384]{1,0:T(8,128)(2,1)S(1)}, u32[]{:S(2)}, u32[]{:S(2)}) collective-permute-start(bf16[208,384]{1,0:T(8,128)(2,1)S(1)} %get-tuple-element.110), channel_id=1, source_target_pairs={{0,2},{2,0},{4,6},{6,4},{1,3},{3,1},{5,7},{7,5},{8,10},{10,8},{12,... | collective-permute-start | bytes 479240 | tf_op jit(solution)/shard_map/ppermute | solution.py:585
  364.2 1.8 collective-permute-start.55
  366.0 8.8 %collective-permute-done.54 = bf16[208,384]{1,0:T(8,128)(2,1)S(1)} collective-permute-done((bf16[208,384]{1,0:T(8,128)(2,1)S(1)}, bf16[208,384]{1,0:T(8,128)(2,1)S(1)}, u32[]{:S(2)}, u32[]{:S(2)}) %collective-permute-start.54) | collective-permute-done | bytes 159776 | tf_op jit(solution)/shard_map/ppermute | solution.py:585
  374.8 2.0 collective-permute-start.62
  379.4 8.6 %collective-permute-done.41 = bf16[1,1,208,1536]{3,2,1,0:T(8,128)(2,1)S(1)} collective-permute-done((bf16[1,1,208,1536]{3,2,1,0:T(8,128)(2,1)S(1)}, bf16[1,1,208,1536]{3,2,1,0:T(8,128)(2,1)S(1)}, u32[]{:S(2)}, u32[]{:S(2)}) %collective-permute-start.41) | collective-permute-done | bytes 639008 | tf_op jit(solution)/shard_map/ppermute | solution.py:600
  388.2 8.2 %collective-permute-start.42 = (bf16[208,384]{1,0:T(8,128)(2,1)S(1)}, bf16[208,384]{1,0:T(8,128)(2,1)S(1)}, u32[]{:S(2)}, u32[]{:S(2)}) collective-permute-start(bf16[208,384]{1,0:T(8,128)(2,1)S(1)} %get-tuple-element.132), channel_id=1, source_target_pairs={{0,2},{2,0},{4,6},{6,4},{1,3},{3,1},{5,7},{7,5},{8,10},{10,8},{12,... | collective-permute-start | bytes 479240 | tf_op jit(solution)/shard_map/ppermute | solution.py:585
  396.5 1.3 collective-permute-start.43
  397.8 1.4 collective-permute-start.44
  399.4 2.5 collective-permute-done.42
  401.9 4.6 %collective-permute-done.43 = bf16[208,384]{1,0:T(8,128)(2,1)S(1)} collective-permute-done((bf16[208,384]{1,0:T(8,128)(2,1)S(1)}, bf16[208,384]{1,0:T(8,128)(2,1)S(1)}, u32[]{:S(2)}, u32[]{:S(2)}) %collective-permute-start.43) | collective-permute-done | bytes 159776 | tf_op jit(solution)/shard_map/ppermute | solution.py:585
  406.7 2.3 collective-permute-start.45
  412.8 1.4 collective-permute-start.47
  414.2 7.4 %collective-permute-done.46 = bf16[208,384]{1,0:T(8,128)(2,1)S(1)} collective-permute-done((bf16[208,384]{1,0:T(8,128)(2,1)S(1)}, bf16[208,384]{1,0:T(8,128)(2,1)S(1)}, u32[]{:S(2)}, u32[]{:S(2)}) %collective-permute-start.46) | collective-permute-done | bytes 159776 | tf_op jit(solution)/shard_map/ppermute | solution.py:585
  (225 shorter events, 55.8 us)
Async XLA Ops:
  8.4 10.6 %collective-permute-start = (bf16[1,208,768]{2,1,0:T(8,128)(2,1)S(1)}, bf16[1,208,768]{2,1,0:T(8,128)(2,1)S(1)}, u32[]{:S(2)}, u32[]{:S(2)}) collective-permute-start(bf16[1,208,768]{2,1,0:T(8,128)(2,1)S(1)} %maximum_bitcast_fusion), channel_id=1, source_target_pairs={{0,1},{1,0},{2,3},{3,2},{4,5},{5,4},{6,7},{7,6},{8,9},{9,8},{10,11... | collective-permute-start | bytes 958472 | tf_op jit(solution)/shard_map/ppermute | solution.py:600
  12.4 9.1 %collective-permute-start.3 = (bf16[1,208,768]{2,1,0:T(8,128)(2,1)S(1)}, bf16[1,208,768]{2,1,0:T(8,128)(2,1)S(1)}, u32[]{:S(2)}, u32[]{:S(2)}) collective-permute-start(bf16[1,208,768]{2,1,0:T(8,128)(2,1)S(1)} %maximum_bitcast_fusion.1), channel_id=1, source_target_pairs={{0,16},{8,24},{16,0},{24,8},{1,17},{9,25},{17,1},{25,9},{2,18},{10... | collective-permute-start | bytes 958472 | tf_op jit(solution)/shard_map/ppermute | solution.py:600
  16.3 10.3 %collective-permute-start.1 = (bf16[256,768]{1,0:T(8,128)(2,1)S(1)}, bf16[256,768]{1,0:T(8,128)(2,1)S(1)}, u32[]{:S(2)}, u32[]{:S(2)}) collective-permute-start(bf16[256,768]{1,0:T(8,128)(2,1)S(1)} %bitcast.127), channel_id=1, source_target_pairs={{0,2},{2,0},{4,6},{6,4},{1,3},{3,1},{5,7},{7,5},{8,10},{10,8},{12,... | collective-permute-start | bytes 1179656 | tf_op jit(solution)/shard_map/ppermute | solution.py:579
  26.6 14.7 %collective-permute-start.2 = (bf16[2,208,768]{2,1,0:T(8,128)(2,1)S(1)}, bf16[2,208,768]{2,1,0:T(8,128)(2,1)S(1)}, u32[]{:S(2)}, u32[]{:S(2)}) collective-permute-start(bf16[2,208,768]{2,1,0:T(8,128)(2,1)S(1)} %pad_maximum_fusion.2.refs_4_), channel_id=1, source_target_pairs={{0,16},{8,24},{16,0},{24,8},{1,17},{9,25},{17,1},{25,9},{2,18},{10... | collective-permute-start | bytes 1916936 | tf_op jit(solution)/shard_map/ppermute | solution.py:600
  27.1 14.4 %collective-permute-start.4 = (bf16[2,208,768]{2,1,0:T(8,128)(2,1)S(1)}, bf16[2,208,768]{2,1,0:T(8,128)(2,1)S(1)}, u32[]{:S(2)}, u32[]{:S(2)}) collective-permute-start(bf16[2,208,768]{2,1,0:T(8,128)(2,1)S(1)} %pad_maximum_fusion.3.refs_8_), channel_id=1, source_target_pairs={{0,1},{1,0},{2,3},{3,2},{4,5},{5,4},{6,7},{7,6},{8,9},{9,8},{10,11... | collective-permute-start | bytes 1916936 | tf_op jit(solution)/shard_map/ppermute | solution.py:600
  27.5 11.1 %collective-permute-start.5 = (bf16[256,768]{1,0:T(8,128)(2,1)S(1)}, bf16[256,768]{1,0:T(8,128)(2,1)S(1)}, u32[]{:S(2)}, u32[]{:S(2)}) collective-permute-start(bf16[256,768]{1,0:T(8,128)(2,1)S(1)} %bitcast.123), channel_id=1, source_target_pairs={{0,6},{2,4},{4,2},{6,0},{1,7},{3,5},{5,3},{7,1},{8,14},{10,12},{12... | collective-permute-start | bytes 1179656 | tf_op jit(solution)/shard_map/ppermute | solution.py:579
  41.6 12.7 %collective-permute-start.7 = (bf16[1,192,1536]{2,1,0:T(8,128)(2,1)S(1)}, bf16[1,192,1536]{2,1,0:T(8,128)(2,1)S(1)}, u32[]{:S(2)}, u32[]{:S(2)}) collective-permute-start(bf16[1,192,1536]{2,1,0:T(8,128)(2,1)S(1)} %bitcast.110), channel_id=1, source_target_pairs={{0,16},{8,24},{16,0},{24,8},{1,17},{9,25},{17,1},{25,9},{2,18},{10... | collective-permute-start | bytes 1769480 | tf_op jit(solution)/shard_map/ppermute | solution.py:600
  43.2 23.4 %collective-permute-start.6 = (bf16[1,192,1536]{2,1,0:T(8,128)(2,1)S(1)}, bf16[1,192,1536]{2,1,0:T(8,128)(2,1)S(1)}, u32[]{:S(2)}, u32[]{:S(2)}) collective-permute-start(bf16[1,192,1536]{2,1,0:T(8,128)(2,1)S(1)} %bitcast.112), channel_id=1, source_target_pairs={{0,1},{1,0},{2,3},{3,2},{4,5},{5,4},{6,7},{7,6},{8,9},{9,8},{10,11... | collective-permute-start | bytes 1769480 | tf_op jit(solution)/shard_map/ppermute | solution.py:600
  43.7 22.9 %collective-permute-start.8 = (bf16[256,768]{1,0:T(8,128)(2,1)S(1)}, bf16[256,768]{1,0:T(8,128)(2,1)S(1)}, u32[]{:S(2)}, u32[]{:S(2)}) collective-permute-start(bf16[256,768]{1,0:T(8,128)(2,1)S(1)} %bitcast.122), channel_id=1, source_target_pairs={{0,4},{2,6},{4,0},{6,2},{1,5},{3,7},{5,1},{7,3},{8,12},{10,14},{12... | collective-permute-start | bytes 1179656 | tf_op jit(solution)/shard_map/ppermute | solution.py:579
  51.3 16.0 %collective-permute-start.11 = (bf16[2,208,768]{2,1,0:T(8,128)(2,1)S(1)}, bf16[2,208,768]{2,1,0:T(8,128)(2,1)S(1)}, u32[]{:S(2)}, u32[]{:S(2)}) collective-permute-start(bf16[2,208,768]{2,1,0:T(8,128)(2,1)S(1)} %pad_maximum_fusion.3.refs_8_), channel_id=1, source_target_pairs={{0,8},{8,0},{16,24},{24,16},{1,9},{9,1},{17,25},{25,17},{2,10},{10... | collective-permute-start | bytes 1916936 | tf_op jit(solution)/shard_map/ppermute | solution.py:600
  51.3 16.7 %collective-permute-start.9 = (bf16[2,208,768]{2,1,0:T(8,128)(2,1)S(1)}, bf16[2,208,768]{2,1,0:T(8,128)(2,1)S(1)}, u32[]{:S(2)}, u32[]{:S(2)}) collective-permute-start(bf16[2,208,768]{2,1,0:T(8,128)(2,1)S(1)} %pad_maximum_fusion.2.refs_4_), channel_id=1, source_target_pairs={{0,8},{8,0},{16,24},{24,16},{1,9},{9,1},{17,25},{25,17},{2,10},{10... | collective-permute-start | bytes 1916936 | tf_op jit(solution)/shard_map/ppermute | solution.py:600
  54.2 13.8 %collective-permute-start.10 = (bf16[2,208,768]{2,1,0:T(8,128)(2,1)S(1)}, bf16[2,208,768]{2,1,0:T(8,128)(2,1)S(1)}, u32[]{:S(2)}, u32[]{:S(2)}) collective-permute-start(bf16[2,208,768]{2,1,0:T(8,128)(2,1)S(1)} %collective-permute-done.2.refs_5_), channel_id=1, source_target_pairs={{0,8},{8,0},{16,24},{24,16},{1,9},{9,1},{17,25},{25,17},{2,10},{10... | collective-permute-start | bytes 1916936 | tf_op jit(solution)/shard_map/ppermute | solution.py:600
  54.3 50.7 %copy-start.3 = (bf16[2,192,1536]{2,1,0:T(8,128)(2,1)}, bf16[2,192,1536]{2,1,0:T(8,128)(2,1)S(1)}, u32[]{:S(2)}) copy-start(bf16[2,192,1536]{2,1,0:T(8,128)(2,1)S(1)} %pad_maximum_fusion.1.refs_16_) | copy-start | bytes 3538948
  66.6 2.1 collective-permute-start.12
  66.6 39.0 %collective-permute-start.19 = (bf16[2,192,1536]{2,1,0:T(8,128)(2,1)S(1)}, bf16[2,192,1536]{2,1,0:T(8,128)(2,1)}, u32[]{:S(2)}, u32[]{:S(2)}) collective-permute-start(bf16[2,192,1536]{2,1,0:T(8,128)(2,1)S(1)} %pad_maximum_fusion.1.refs_16_), channel_id=1, source_target_pairs={{0,1},{1,0},{2,3},{3,2},{4,5},{5,4},{6,7},{7,6},{8,9},{9,8},{10,11... | collective-permute-start | bytes 3538952 | tf_op jit(solution)/shard_map/ppermute | solution.py:600
  67.3 38.3 %collective-permute-start.16 = (bf16[2,192,1536]{2,1,0:T(8,128)(2,1)S(1)}, bf16[2,192,1536]{2,1,0:T(8,128)(2,1)}, u32[]{:S(2)}, u32[]{:S(2)}) collective-permute-start(bf16[2,192,1536]{2,1,0:T(8,128)(2,1)S(1)} %pad_maximum_fusion.refs_12_), channel_id=1, source_target_pairs={{0,16},{8,24},{16,0},{24,8},{1,17},{9,25},{17,1},{25,9},{2,18},{10... | collective-permute-start | bytes 3538952 | tf_op jit(solution)/shard_map/ppermute | solution.py:600
  69.6 34.7 %collective-permute-start.13 = (bf16[256,768]{1,0:T(8,128)(2,1)S(1)}, bf16[256,768]{1,0:T(8,128)(2,1)S(1)}, u32[]{:S(2)}, u32[]{:S(2)}) collective-permute-start(bf16[256,768]{1,0:T(8,128)(2,1)S(1)} %bitcast.126), channel_id=1, source_target_pairs={{0,2},{2,0},{4,6},{6,4},{1,3},{3,1},{5,7},{7,5},{8,10},{10,8},{12,... | collective-permute-start | bytes 1179656 | tf_op jit(solution)/shard_map/ppermute | solution.py:579
  69.7 34.6 %collective-permute-start.14 = (bf16[256,768]{1,0:T(8,128)(2,1)S(1)}, bf16[256,768]{1,0:T(8,128)(2,1)}, u32[]{:S(2)}, u32[]{:S(2)}) collective-permute-start(bf16[256,768]{1,0:T(8,128)(2,1)S(1)} %bitcast.125), channel_id=1, source_target_pairs={{0,4},{2,6},{4,0},{6,2},{1,5},{3,7},{5,1},{7,3},{8,12},{10,14},{12... | collective-permute-start | bytes 1179656 | tf_op jit(solution)/shard_map/ppermute | solution.py:579
  72.7 31.7 %collective-permute-start.15 = (bf16[256,768]{1,0:T(8,128)(2,1)S(1)}, bf16[256,768]{1,0:T(8,128)(2,1)}, u32[]{:S(2)}, u32[]{:S(2)}) collective-permute-start(bf16[256,768]{1,0:T(8,128)(2,1)S(1)} %bitcast.124), channel_id=1, source_target_pairs={{0,6},{2,4},{4,2},{6,0},{1,7},{3,5},{5,3},{7,1},{8,14},{10,12},{12... | collective-permute-start | bytes 1179656 | tf_op jit(solution)/shard_map/ppermute | solution.py:579
  105.1 2.8 collective-permute-start.20
  105.1 4.7 %collective-permute-start.17 = (bf16[2,192,1536]{2,1,0:T(8,128)(2,1)S(1)}, bf16[2,192,1536]{2,1,0:T(8,128)(2,1)}, u32[]{:S(2)}, u32[]{:S(2)}) collective-permute-start(bf16[2,192,1536]{2,1,0:T(8,128)(2,1)S(1)} %pad_maximum_fusion.refs_12_), channel_id=1, source_target_pairs={{0,8},{8,0},{16,24},{24,16},{1,9},{9,1},{17,25},{25,17},{2,10},{10... | collective-permute-start | bytes 3538952 | tf_op jit(solution)/shard_map/ppermute | solution.py:600
  105.6 5.8 %collective-permute-start.21 = (bf16[2,192,1536]{2,1,0:T(8,128)(2,1)}, bf16[2,192,1536]{2,1,0:T(8,128)(2,1)}, u32[]{:S(2)}, u32[]{:S(2)}) collective-permute-start(bf16[2,192,1536]{2,1,0:T(8,128)(2,1)} %collective-permute-done.19.refs_17_), channel_id=1, source_target_pairs={{0,8},{8,0},{16,24},{24,16},{1,9},{9,1},{17,25},{25,17},{2,10},{10... | collective-permute-start | bytes 3538952 | tf_op jit(solution)/shard_map/ppermute | solution.py:600
  105.7 7.4 %collective-permute-start.18 = (bf16[2,192,1536]{2,1,0:T(8,128)(2,1)}, bf16[2,192,1536]{2,1,0:T(8,128)(2,1)}, u32[]{:S(2)}, u32[]{:S(2)}) collective-permute-start(bf16[2,192,1536]{2,1,0:T(8,128)(2,1)} %collective-permute-done.16.refs_13_), channel_id=1, source_target_pairs={{0,8},{8,0},{16,24},{24,16},{1,9},{9,1},{17,25},{25,17},{2,10},{10... | collective-permute-start | bytes 3538952 | tf_op jit(solution)/shard_map/ppermute | solution.py:600
  159.8 33.9 %collective-permute-start.22 = (bf16[256,768]{1,0:T(8,128)(2,1)}, bf16[256,768]{1,0:T(8,128)(2,1)S(1)}, u32[]{:S(2)}, u32[]{:S(2)}) collective-permute-start(bf16[256,768]{1,0:T(8,128)(2,1)} %get-tuple-element.76), channel_id=1, source_target_pairs={{0,1},{1,0},{2,3},{3,2},{4,5},{5,4},{6,7},{7,6},{8,9},{9,8},{10,11... | collective-permute-start | bytes 1179656 | tf_op jit(solution)/shard_map/ppermute | solution.py:588
  160.9 31.2 %collective-permute-start.23 = (bf16[256,768]{1,0:T(8,128)(2,1)}, bf16[256,768]{1,0:T(8,128)(2,1)}, u32[]{:S(2)}, u32[]{:S(2)}) collective-permute-start(bf16[256,768]{1,0:T(8,128)(2,1)} %get-tuple-element.77), channel_id=1, source_target_pairs={{0,2},{2,0},{4,6},{6,4},{1,3},{3,1},{5,7},{7,5},{8,10},{10,8},{12,... | collective-permute-start | bytes 1179656 | tf_op jit(solution)/shard_map/ppermute | solution.py:585
  163.6 30.2 %collective-permute-start.27 = (bf16[256,768]{1,0:T(8,128)(2,1)}, bf16[256,768]{1,0:T(8,128)(2,1)S(1)}, u32[]{:S(2)}, u32[]{:S(2)}) collective-permute-start(bf16[256,768]{1,0:T(8,128)(2,1)} %get-tuple-element.79), channel_id=1, source_target_pairs={{0,6},{2,4},{4,2},{6,0},{1,7},{3,5},{5,3},{7,1},{8,14},{10,12},{12... | collective-permute-start | bytes 1179656 | tf_op jit(solution)/shard_map/ppermute | solution.py:585
  166.0 41.8 %collective-permute-start.25 = (bf16[256,768]{1,0:T(8,128)(2,1)}, bf16[256,768]{1,0:T(8,128)(2,1)}, u32[]{:S(2)}, u32[]{:S(2)}) collective-permute-start(bf16[256,768]{1,0:T(8,128)(2,1)} %get-tuple-element.78), channel_id=1, source_target_pairs={{0,4},{2,6},{4,0},{6,2},{1,5},{3,7},{5,1},{7,3},{8,12},{10,14},{12... | collective-permute-start | bytes 1179656 | tf_op jit(solution)/shard_map/ppermute | solution.py:585
  192.1 16.8 %collective-permute-start.24 = (bf16[256,768]{1,0:T(8,128)(2,1)}, bf16[256,768]{1,0:T(8,128)(2,1)}, u32[]{:S(2)}, u32[]{:S(2)}) collective-permute-start(bf16[256,768]{1,0:T(8,128)(2,1)} %collective-permute-done.23), channel_id=1, source_target_pairs={{0,1},{1,0},{2,3},{3,2},{4,5},{5,4},{6,7},{7,6},{8,9},{9,8},{10,11... | collective-permute-start | bytes 1179656 | tf_op jit(solution)/shard_map/ppermute | solution.py:588
  202.4 25.7 %collective-permute-start.30 = (bf16[256,768]{1,0:T(8,128)(2,1)}, bf16[256,768]{1,0:T(8,128)(2,1)S(1)}, u32[]{:S(2)}, u32[]{:S(2)}) collective-permute-start(bf16[256,768]{1,0:T(8,128)(2,1)} %get-tuple-element.88), channel_id=1, source_target_pairs={{0,2},{2,0},{4,6},{6,4},{1,3},{3,1},{5,7},{7,5},{8,10},{10,8},{12,... | collective-permute-start | bytes 1179656 | tf_op jit(solution)/shard_map/ppermute | solution.py:585
  204.4 23.6 %collective-permute-start.34 = (bf16[256,768]{1,0:T(8,128)(2,1)}, bf16[256,768]{1,0:T(8,128)(2,1)}, u32[]{:S(2)}, u32[]{:S(2)}) collective-permute-start(bf16[256,768]{1,0:T(8,128)(2,1)} %get-tuple-element.90), channel_id=1, source_target_pairs={{0,6},{2,4},{4,2},{6,0},{1,7},{3,5},{5,3},{7,1},{8,14},{10,12},{12... | collective-permute-start | bytes 1179656 | tf_op jit(solution)/shard_map/ppermute | solution.py:585
  206.9 39.5 %collective-permute-start.29 = (bf16[256,768]{1,0:T(8,128)(2,1)}, bf16[256,768]{1,0:T(8,128)(2,1)}, u32[]{:S(2)}, u32[]{:S(2)}) collective-permute-start(bf16[256,768]{1,0:T(8,128)(2,1)} %get-tuple-element.87), channel_id=1, source_target_pairs={{0,1},{1,0},{2,3},{3,2},{4,5},{5,4},{6,7},{7,6},{8,9},{9,8},{10,11... | collective-permute-start | bytes 1179656 | tf_op jit(solution)/shard_map/ppermute | solution.py:588
  207.7 21.3 %collective-permute-start.28 = (bf16[256,768]{1,0:T(8,128)(2,1)S(1)}, bf16[256,768]{1,0:T(8,128)(2,1)}, u32[]{:S(2)}, u32[]{:S(2)}) collective-permute-start(bf16[256,768]{1,0:T(8,128)(2,1)S(1)} %collective-permute-done.27), channel_id=1, source_target_pairs={{0,1},{1,0},{2,3},{3,2},{4,5},{5,4},{6,7},{7,6},{8,9},{9,8},{10,11... | collective-permute-start | bytes 1179656 | tf_op jit(solution)/shard_map/ppermute | solution.py:588
  221.7 38.3 %collective-permute-start.36 = (bf16[2,2,208,1536]{3,2,1,0:T(8,128)(2,1)}, bf16[2,2,208,1536]{3,2,1,0:T(8,128)(2,1)}, u32[]{:S(2)}, u32[]{:S(2)}) collective-permute-start(bf16[2,2,208,1536]{3,2,1,0:T(8,128)(2,1)} %get-tuple-element.97), channel_id=1, source_target_pairs={{0,8},{8,0},{16,24},{24,16},{1,9},{9,1},{17,25},{25,17},{2,10},{10... | collective-permute-start | bytes 7667720 | tf_op jit(solution)/shard_map/ppermute | solution.py:654
  228.1 21.2 %collective-permute-start.32 = (bf16[256,768]{1,0:T(8,128)(2,1)}, bf16[256,768]{1,0:T(8,128)(2,1)}, u32[]{:S(2)}, u32[]{:S(2)}) collective-permute-start(bf16[256,768]{1,0:T(8,128)(2,1)} %get-tuple-element.89), channel_id=1, source_target_pairs={{0,4},{2,6},{4,0},{6,2},{1,5},{3,7},{5,1},{7,3},{8,12},{10,14},{12... | collective-permute-start | bytes 1179656 | tf_op jit(solution)/shard_map/ppermute | solution.py:585
  228.1 16.0 %collective-permute-start.26 = (bf16[256,768]{1,0:T(8,128)(2,1)}, bf16[256,768]{1,0:T(8,128)(2,1)}, u32[]{:S(2)}, u32[]{:S(2)}) collective-permute-start(bf16[256,768]{1,0:T(8,128)(2,1)} %collective-permute-done.25), channel_id=1, source_target_pairs={{0,1},{1,0},{2,3},{3,2},{4,5},{5,4},{6,7},{7,6},{8,9},{9,8},{10,11... | collective-permute-start | bytes 1179656 | tf_op jit(solution)/shard_map/ppermute | solution.py:588
  241.8 36.3 %collective-permute-start.37 = (bf16[2,2,208,1536]{3,2,1,0:T(8,128)(2,1)}, bf16[2,2,208,1536]{3,2,1,0:T(8,128)(2,1)}, u32[]{:S(2)}, u32[]{:S(2)}) collective-permute-start(bf16[2,2,208,1536]{3,2,1,0:T(8,128)(2,1)} %get-tuple-element.102), channel_id=1, source_target_pairs={{0,8},{8,0},{16,24},{24,16},{1,9},{9,1},{17,25},{25,17},{2,10},{10... | collective-permute-start | bytes 7667720 | tf_op jit(solution)/shard_map/ppermute | solution.py:654
  245.1 12.1 %collective-permute-start.31 = (bf16[256,768]{1,0:T(8,128)(2,1)S(1)}, bf16[256,768]{1,0:T(8,128)(2,1)S(1)}, u32[]{:S(2)}, u32[]{:S(2)}) collective-permute-start(bf16[256,768]{1,0:T(8,128)(2,1)S(1)} %collective-permute-done.30), channel_id=1, source_target_pairs={{0,1},{1,0},{2,3},{3,2},{4,5},{5,4},{6,7},{7,6},{8,9},{9,8},{10,11... | collective-permute-start | bytes 1179656 | tf_op jit(solution)/shard_map/ppermute | solution.py:588
  248.3 46.0 %collective-permute-start.35 = (bf16[256,768]{1,0:T(8,128)(2,1)}, bf16[256,768]{1,0:T(8,128)(2,1)}, u32[]{:S(2)}, u32[]{:S(2)}) collective-permute-start(bf16[256,768]{1,0:T(8,128)(2,1)} %collective-permute-done.34), channel_id=1, source_target_pairs={{0,1},{1,0},{2,3},{3,2},{4,5},{5,4},{6,7},{7,6},{8,9},{9,8},{10,11... | collective-permute-start | bytes 1179656 | tf_op jit(solution)/shard_map/ppermute | solution.py:588
  249.3 32.7 %collective-permute-start.33 = (bf16[256,768]{1,0:T(8,128)(2,1)}, bf16[256,768]{1,0:T(8,128)(2,1)}, u32[]{:S(2)}, u32[]{:S(2)}) collective-permute-start(bf16[256,768]{1,0:T(8,128)(2,1)} %collective-permute-done.32), channel_id=1, source_target_pairs={{0,1},{1,0},{2,3},{3,2},{4,5},{5,4},{6,7},{7,6},{8,9},{9,8},{10,11... | collective-permute-start | bytes 1179656 | tf_op jit(solution)/shard_map/ppermute | solution.py:588
  262.6 28.9 %collective-permute-start.48 = (bf16[1,2,208,1536]{3,2,1,0:T(8,128)(2,1)S(1)}, bf16[1,2,208,1536]{3,2,1,0:T(8,128)(2,1)}, u32[]{:S(2)}, u32[]{:S(2)}) collective-permute-start(bf16[1,2,208,1536]{3,2,1,0:T(8,128)(2,1)S(1)} %split.55), channel_id=1, source_target_pairs={{0,16},{8,24},{16,0},{24,8},{1,17},{9,25},{17,1},{25,9},{2,18},{10... | collective-permute-start | bytes 3833864 | tf_op jit(solution)/shard_map/ppermute | solution.py:600
  278.1 52.2 %collective-permute-start.39 = (bf16[2,2,208,1536]{3,2,1,0:T(8,128)(2,1)}, bf16[2,2,208,1536]{3,2,1,0:T(8,128)(2,1)S(1)}, u32[]{:S(2)}, u32[]{:S(2)}) collective-permute-start(bf16[2,2,208,1536]{3,2,1,0:T(8,128)(2,1)} %get-tuple-element.106), channel_id=1, source_target_pairs={{0,8},{8,0},{16,24},{24,16},{1,9},{9,1},{17,25},{25,17},{2,10},{10... | collective-permute-start | bytes 7667720 | tf_op jit(solution)/shard_map/ppermute | solution.py:654
  281.3 31.0 %collective-permute-start.38 = (bf16[2,1,208,1536]{3,2,1,0:T(8,128)(2,1)S(1)}, bf16[2,1,208,1536]{3,2,1,0:T(8,128)(2,1)S(1)}, u32[]{:S(2)}, u32[]{:S(2)}) collective-permute-start(bf16[2,1,208,1536]{3,2,1,0:T(8,128)(2,1)S(1)} %split.49), channel_id=1, source_target_pairs={{0,1},{1,0},{2,3},{3,2},{4,5},{5,4},{6,7},{7,6},{8,9},{9,8},{10,11... | collective-permute-start | bytes 3833864 | tf_op jit(solution)/shard_map/ppermute | solution.py:600
  293.1 32.5 %collective-permute-start.49 = (bf16[1,1,208,1536]{3,2,1,0:T(8,128)(2,1)S(1)}, bf16[1,1,208,1536]{3,2,1,0:T(8,128)(2,1)S(1)}, u32[]{:S(2)}, u32[]{:S(2)}) collective-permute-start(bf16[1,1,208,1536]{3,2,1,0:T(8,128)(2,1)S(1)} %split.57), channel_id=1, source_target_pairs={{0,1},{1,0},{2,3},{3,2},{4,5},{5,4},{6,7},{7,6},{8,9},{9,8},{10,11... | collective-permute-start | bytes 1916936 | tf_op jit(solution)/shard_map/ppermute | solution.py:600
  312.7 19.1 %collective-permute-start.56 = (bf16[1,1,208,1536]{3,2,1,0:T(8,128)(2,1)S(1)}, bf16[1,1,208,1536]{3,2,1,0:T(8,128)(2,1)S(1)}, u32[]{:S(2)}, u32[]{:S(2)}) collective-permute-start(bf16[1,1,208,1536]{3,2,1,0:T(8,128)(2,1)S(1)} %split.59), channel_id=1, source_target_pairs={{0,16},{8,24},{16,0},{24,8},{1,17},{9,25},{17,1},{25,9},{2,18},{10... | collective-permute-start | bytes 1916936 | tf_op jit(solution)/shard_map/ppermute | solution.py:600
  325.8 8.4 %collective-permute-start.50 = (bf16[208,384]{1,0:T(8,128)(2,1)S(1)}, bf16[208,384]{1,0:T(8,128)(2,1)S(1)}, u32[]{:S(2)}, u32[]{:S(2)}) collective-permute-start(bf16[208,384]{1,0:T(8,128)(2,1)S(1)} %get-tuple-element.126), channel_id=1, source_target_pairs={{0,2},{2,0},{4,6},{6,4},{1,3},{3,1},{5,7},{7,5},{8,10},{10,8},{12,... | collective-permute-start | bytes 479240 | tf_op jit(solution)/shard_map/ppermute | solution.py:585
  327.5 14.7 %collective-permute-start.51 = (bf16[208,384]{1,0:T(8,128)(2,1)S(1)}, bf16[208,384]{1,0:T(8,128)(2,1)S(1)}, u32[]{:S(2)}, u32[]{:S(2)}) collective-permute-start(bf16[208,384]{1,0:T(8,128)(2,1)S(1)} %get-tuple-element.128), channel_id=1, source_target_pairs={{0,4},{2,6},{4,0},{6,2},{1,5},{3,7},{5,1},{7,3},{8,12},{10,14},{12... | collective-permute-start | bytes 479240 | tf_op jit(solution)/shard_map/ppermute | solution.py:585
  328.6 16.1 %collective-permute-start.52 = (bf16[208,384]{1,0:T(8,128)(2,1)S(1)}, bf16[208,384]{1,0:T(8,128)(2,1)S(1)}, u32[]{:S(2)}, u32[]{:S(2)}) collective-permute-start(bf16[208,384]{1,0:T(8,128)(2,1)S(1)} %get-tuple-element.127), channel_id=1, source_target_pairs={{0,6},{2,4},{4,2},{6,0},{1,7},{3,5},{5,3},{7,1},{8,14},{10,12},{12... | collective-permute-start | bytes 479240 | tf_op jit(solution)/shard_map/ppermute | solution.py:585
  331.1 46.1 %collective-permute-start.40 = (bf16[1,2,208,1536]{3,2,1,0:T(8,128)(2,1)S(1)}, bf16[1,2,208,1536]{3,2,1,0:T(8,128)(2,1)S(1)}, u32[]{:S(2)}, u32[]{:S(2)}) collective-permute-start(bf16[1,2,208,1536]{3,2,1,0:T(8,128)(2,1)S(1)} %split.51), channel_id=1, source_target_pairs={{0,16},{8,24},{16,0},{24,8},{1,17},{9,25},{17,1},{25,9},{2,18},{10... | collective-permute-start | bytes 3833864 | tf_op jit(solution)/shard_map/ppermute | solution.py:600
  332.1 22.9 %collective-permute-start.57 = (bf16[208,384]{1,0:T(8,128)(2,1)S(1)}, bf16[208,384]{1,0:T(8,128)(2,1)S(1)}, u32[]{:S(2)}, u32[]{:S(2)}) collective-permute-start(bf16[208,384]{1,0:T(8,128)(2,1)S(1)} %get-tuple-element.123), channel_id=1, source_target_pairs={{0,2},{2,0},{4,6},{6,4},{1,3},{3,1},{5,7},{7,5},{8,10},{10,8},{12,... | collective-permute-start | bytes 479240 | tf_op jit(solution)/shard_map/ppermute | solution.py:585
  334.2 23.5 %collective-permute-start.58 = (bf16[208,384]{1,0:T(8,128)(2,1)S(1)}, bf16[208,384]{1,0:T(8,128)(2,1)S(1)}, u32[]{:S(2)}, u32[]{:S(2)}) collective-permute-start(bf16[208,384]{1,0:T(8,128)(2,1)S(1)} %get-tuple-element.125), channel_id=1, source_target_pairs={{0,4},{2,6},{4,0},{6,2},{1,5},{3,7},{5,1},{7,3},{8,12},{10,14},{12... | collective-permute-start | bytes 479240 | tf_op jit(solution)/shard_map/ppermute | solution.py:585
  342.3 15.4 %collective-permute-start.59 = (bf16[208,384]{1,0:T(8,128)(2,1)S(1)}, bf16[208,384]{1,0:T(8,128)(2,1)S(1)}, u32[]{:S(2)}, u32[]{:S(2)}) collective-permute-start(bf16[208,384]{1,0:T(8,128)(2,1)S(1)} %get-tuple-element.124), channel_id=1, source_target_pairs={{0,6},{2,4},{4,2},{6,0},{1,7},{3,5},{5,3},{7,1},{8,14},{10,12},{12... | collective-permute-start | bytes 479240 | tf_op jit(solution)/shard_map/ppermute | solution.py:585
  344.8 19.5 %collective-permute-start.53 = (bf16[208,384]{1,0:T(8,128)(2,1)S(1)}, bf16[208,384]{1,0:T(8,128)(2,1)S(1)}, u32[]{:S(2)}, u32[]{:S(2)}) collective-permute-start(bf16[208,384]{1,0:T(8,128)(2,1)S(1)} %get-tuple-element.112), channel_id=1, source_target_pairs={{0,2},{2,0},{4,6},{6,4},{1,3},{3,1},{5,7},{7,5},{8,10},{10,8},{12,... | collective-permute-start | bytes 479240 | tf_op jit(solution)/shard_map/ppermute | solution.py:585
  355.0 19.8 %collective-permute-start.54 = (bf16[208,384]{1,0:T(8,128)(2,1)S(1)}, bf16[208,384]{1,0:T(8,128)(2,1)S(1)}, u32[]{:S(2)}, u32[]{:S(2)}) collective-permute-start(bf16[208,384]{1,0:T(8,128)(2,1)S(1)} %get-tuple-element.112), channel_id=1, source_target_pairs={{0,4},{2,6},{4,0},{6,2},{1,5},{3,7},{5,1},{7,3},{8,12},{10,14},{12... | collective-permute-start | bytes 479240 | tf_op jit(solution)/shard_map/ppermute | solution.py:585
  357.8 19.3 %collective-permute-start.60 = (bf16[208,384]{1,0:T(8,128)(2,1)S(1)}, bf16[208,384]{1,0:T(8,128)(2,1)S(1)}, u32[]{:S(2)}, u32[]{:S(2)}) collective-permute-start(bf16[208,384]{1,0:T(8,128)(2,1)S(1)} %get-tuple-element.110), channel_id=1, source_target_pairs={{0,2},{2,0},{4,6},{6,4},{1,3},{3,1},{5,7},{7,5},{8,10},{10,8},{12,... | collective-permute-start | bytes 479240 | tf_op jit(solution)/shard_map/ppermute | solution.py:585
  363.6 14.7 %collective-permute-start.61 = (bf16[208,384]{1,0:T(8,128)(2,1)S(1)}, bf16[208,384]{1,0:T(8,128)(2,1)S(1)}, u32[]{:S(2)}, u32[]{:S(2)}) collective-permute-start(bf16[208,384]{1,0:T(8,128)(2,1)S(1)} %get-tuple-element.110), channel_id=1, source_target_pairs={{0,4},{2,6},{4,0},{6,2},{1,5},{3,7},{5,1},{7,3},{8,12},{10,14},{12... | collective-permute-start | bytes 479240 | tf_op jit(solution)/shard_map/ppermute | solution.py:585
  364.2 12.7 %collective-permute-start.55 = (bf16[208,384]{1,0:T(8,128)(2,1)S(1)}, bf16[208,384]{1,0:T(8,128)(2,1)S(1)}, u32[]{:S(2)}, u32[]{:S(2)}) collective-permute-start(bf16[208,384]{1,0:T(8,128)(2,1)S(1)} %get-tuple-element.112), channel_id=1, source_target_pairs={{0,6},{2,4},{4,2},{6,0},{1,7},{3,5},{5,3},{7,1},{8,14},{10,12},{12... | collective-permute-start | bytes 479240 | tf_op jit(solution)/shard_map/ppermute | solution.py:585
  374.8 24.3 %collective-permute-start.62 = (bf16[208,384]{1,0:T(8,128)(2,1)S(1)}, bf16[208,384]{1,0:T(8,128)(2,1)S(1)}, u32[]{:S(2)}, u32[]{:S(2)}) collective-permute-start(bf16[208,384]{1,0:T(8,128)(2,1)S(1)} %get-tuple-element.110), channel_id=1, source_target_pairs={{0,6},{2,4},{4,2},{6,0},{1,7},{3,5},{5,3},{7,1},{8,14},{10,12},{12... | collective-permute-start | bytes 479240 | tf_op jit(solution)/shard_map/ppermute | solution.py:585
  377.5 10.5 %collective-permute-start.41 = (bf16[1,1,208,1536]{3,2,1,0:T(8,128)(2,1)S(1)}, bf16[1,1,208,1536]{3,2,1,0:T(8,128)(2,1)S(1)}, u32[]{:S(2)}, u32[]{:S(2)}) collective-permute-start(bf16[1,1,208,1536]{3,2,1,0:T(8,128)(2,1)S(1)} %split.53), channel_id=1, source_target_pairs={{0,1},{1,0},{2,3},{3,2},{4,5},{5,4},{6,7},{7,6},{8,9},{9,8},{10,11... | collective-permute-start | bytes 1916936 | tf_op jit(solution)/shard_map/ppermute | solution.py:600
  388.2 13.7 %collective-permute-start.42 = (bf16[208,384]{1,0:T(8,128)(2,1)S(1)}, bf16[208,384]{1,0:T(8,128)(2,1)S(1)}, u32[]{:S(2)}, u32[]{:S(2)}) collective-permute-start(bf16[208,384]{1,0:T(8,128)(2,1)S(1)} %get-tuple-element.132), channel_id=1, source_target_pairs={{0,2},{2,0},{4,6},{6,4},{1,3},{3,1},{5,7},{7,5},{8,10},{10,8},{12,... | collective-permute-start | bytes 479240 | tf_op jit(solution)/shard_map/ppermute | solution.py:585
  396.5 10.1 %collective-permute-start.43 = (bf16[208,384]{1,0:T(8,128)(2,1)S(1)}, bf16[208,384]{1,0:T(8,128)(2,1)S(1)}, u32[]{:S(2)}, u32[]{:S(2)}) collective-permute-start(bf16[208,384]{1,0:T(8,128)(2,1)S(1)} %get-tuple-element.134), channel_id=1, source_target_pairs={{0,4},{2,6},{4,0},{6,2},{1,5},{3,7},{5,1},{7,3},{8,12},{10,14},{12... | collective-permute-start | bytes 479240 | tf_op jit(solution)/shard_map/ppermute | solution.py:585
  397.8 8.8 %collective-permute-start.44 = (bf16[208,384]{1,0:T(8,128)(2,1)S(1)}, bf16[208,384]{1,0:T(8,128)(2,1)S(1)}, u32[]{:S(2)}, u32[]{:S(2)}) collective-permute-start(bf16[208,384]{1,0:T(8,128)(2,1)S(1)} %get-tuple-element.133), channel_id=1, source_target_pairs={{0,6},{2,4},{4,2},{6,0},{1,7},{3,5},{5,3},{7,1},{8,14},{10,12},{12... | collective-permute-start | bytes 479240 | tf_op jit(solution)/shard_map/ppermute | solution.py:585
  406.7 7.5 %collective-permute-start.45 = (bf16[208,384]{1,0:T(8,128)(2,1)S(1)}, bf16[208,384]{1,0:T(8,128)(2,1)S(1)}, u32[]{:S(2)}, u32[]{:S(2)}) collective-permute-start(bf16[208,384]{1,0:T(8,128)(2,1)S(1)} %get-tuple-element.114), channel_id=1, source_target_pairs={{0,2},{2,0},{4,6},{6,4},{1,3},{3,1},{5,7},{7,5},{8,10},{10,8},{12,... | collective-permute-start | bytes 479240 | tf_op jit(solution)/shard_map/ppermute | solution.py:585
  409.7 12.0 %collective-permute-start.46 = (bf16[208,384]{1,0:T(8,128)(2,1)S(1)}, bf16[208,384]{1,0:T(8,128)(2,1)S(1)}, u32[]{:S(2)}, u32[]{:S(2)}) collective-permute-start(bf16[208,384]{1,0:T(8,128)(2,1)S(1)} %get-tuple-element.114), channel_id=1, source_target_pairs={{0,4},{2,6},{4,0},{6,2},{1,5},{3,7},{5,1},{7,3},{8,12},{10,14},{12... | collective-permute-start | bytes 479240 | tf_op jit(solution)/shard_map/ppermute | solution.py:585
  412.8 9.0 %collective-permute-start.47 = (bf16[208,384]{1,0:T(8,128)(2,1)S(1)}, bf16[208,384]{1,0:T(8,128)(2,1)S(1)}, u32[]{:S(2)}, u32[]{:S(2)}) collective-permute-start(bf16[208,384]{1,0:T(8,128)(2,1)S(1)} %get-tuple-element.114), channel_id=1, source_target_pairs={{0,6},{2,4},{4,2},{6,0},{1,7},{3,5},{5,3},{7,1},{8,14},{10,12},{12... | collective-permute-start | bytes 479240 | tf_op jit(solution)/shard_map/ppermute | solution.py:585
  (24 other events, 443.4 us)

commit v4 on v3

--- a/solution.py
+++ b/solution.py
@@ -571,26 +571,44 @@
     R = ns * span
     dims = (F, C, T, ns, span, D)
 
-    def to_sequences(array, chained):
-        out, before = {}, []
-        for k in sorted(range(C), key=lambda k: (k > 0, k % 2 == 0, k)):
-            piece = lax.dynamic_slice_in_dim(array, ((c ^ k) * T + t) * ns, ns, 0).reshape(R, D)
-            if k:
-                piece = lax.ppermute(after(piece, before), "ctx", xor_pairs(C, k))
-                before = [piece] if chained else []
-            out[k] = piece
-        return [out[k] for k in range(C)]
+    def sequence_pieces(array):
+        return [
+            lax.dynamic_slice_in_dim(array, ((c ^ k) * T + t) * ns, ns, 0).reshape(R, D)
+            for k in range(C)
+        ]
+
+    def ctx_first(pieces):
+        if C != 4:
+            return [ctx_moved(piece, k) for k, piece in enumerate(pieces)][1:]
+        h = R // 2
+        up = jnp.concatenate([pieces[1], pieces[2][:h]], axis=0)
+        down = jnp.concatenate([pieces[3], pieces[2][h:]], axis=0)
+        return [ctx_moved(up, 1), ctx_moved(down, 3)]
+
+    def ctx_second(own, got):
+        if C != 4:
+            return [own, *got], list(got)
+        up, down = got
+        raw = [ctx_moved(up[R:], 3), ctx_moved(down[R:], 1)]
+        return [own, up[:R], jnp.concatenate(raw, axis=0), down[:R]], raw
 
     def ctx_moved(piece, k):
         return lax.ppermute(piece, "ctx", xor_pairs(C, k)) if k else piece
 
-    def tp_moved(piece):
-        return [piece] + [lax.ppermute(piece, "tp", xor_pairs(T, dt)) for dt in range(1, T)]
-
-    def to_slots(pieces, kind):
+    def tp_moved(pieces):
+        both = jnp.concatenate(pieces, axis=0)
+        return [both] + [lax.ppermute(both, "tp", xor_pairs(T, dt)) for dt in range(1, T)]
+
+    def to_slots(groups, kind):
         out = lax.full((S, span, D), 0, kind)
+        pieces = {}
+        for ks, group in groups:
+            for dt, merged in enumerate(group):
+                for i, k in enumerate(ks):
+                    pieces[k, dt] = merged[i * R : (i + 1) * R]
         for k in range(C):
-            for dt, got in enumerate(pieces[k]):
+            for dt in range(T):
+                got = pieces[k, dt]
                 out = lax.dynamic_update_slice_in_dim(
                     out, got.reshape(ns, span, D).astype(kind), ((c ^ k) * T + (t ^ dt)) * ns, 0
                 )
@@ -618,7 +636,8 @@
         owner = lax.broadcasted_iota(jnp.int32, (rows, part * F), 1) // part
         return jnp.where(owner == f, jnp.tile(array, (1, F)), jnp.zeros((), BF)).reshape(-1, width)
 
-    x_pieces = to_sequences(tokens_in, True)
+    x_pieces = sequence_pieces(tokens_in)
+    x_got = ctx_first(x_pieces)
     vectors = jnp.stack([output_bias, attn_gain, attn_shift, outer_bias, ffn_gain, ffn_shift])
     small = [
         spread(query_bias, half), spread(value_bias, half), spread(inner_bias, fhalf),
@@ -630,22 +649,25 @@
     high = jnp.concatenate([value_weight, output_weight.T], axis=1)
     low = chip_start(jnp.concatenate([low, small[:, :D]], axis=0), False)
     high = chip_start(jnp.concatenate([high, small[:, D:]], axis=0), True)
-    lows = both_cores(low, chip_end(after(low, x_pieces[1:2]), False))
-    highs = both_cores(high, chip_end(after(high, x_pieces[1:2]), True))
-    halfway = [lows[1], highs[1], *x_pieces[3:4]]
+    lows = both_cores(low, chip_end(low, False))
+    highs = both_cores(high, chip_end(high, True))
+    halfway = [lows[1], highs[1], *x_got]
+    x_pieces, x_raw = ctx_second(x_pieces[0], x_got)
     inner = chip_start(after(inner_weight, halfway), False)
     outer = chip_start(after(outer_weight.T, halfway), True)
-    inner_got = chip_end(after(inner, x_pieces[2:3]), False)
-    outer_got = chip_end(after(outer, x_pieces[2:3]), True)
-    cot_pieces = to_sequences(after(cotangent, [*x_pieces, *lows, *highs]), False)
+    inner_got = chip_end(after(inner, x_raw), False)
+    outer_got = chip_end(after(outer, x_raw), True)
+    cot_pieces = sequence_pieces(after(cotangent, [*x_raw, *lows, *highs]))
+    cot_got = ctx_first(cot_pieces)
     lengths = lax.dynamic_slice_in_dim(seq_lengths, (c * T + t) * ns, ns, 0)
     meta = jnp.concatenate([jnp.stack([f, c]).astype(jnp.int32), lengths])
 
     x_all, qkv_w, qkv, e, linv, ctx = front_call(
         dims, after(meta, [inner, outer]), x_pieces, lows, highs
     )
-    inners = both_cores(inner, inner_got, [ctx, *cot_pieces])
-    outers = both_cores(outer, outer_got, [ctx, *cot_pieces])
+    inners = both_cores(inner, inner_got, [ctx, *cot_got])
+    outers = both_cores(outer, outer_got, [ctx, *cot_got])
+    cot_pieces, _ = ctx_second(cot_pieces[0], cot_got)
     los, (first, dctx, nl, act, og, inner_low, ag, sums) = rows_call(
         dims, FF, meta, x_all, ctx.reshape(C, R, D), cot_pieces, lows + highs + inners + outers,
     )
@@ -681,33 +703,39 @@
             out = lax.dynamic_update_slice_in_dim(out, ctx_moved(mine, k), (c ^ k) * part, 1)
         return out.astype(F32)
 
-    lo = {k: ctx_moved(los[k], k) for k in range(C)}
-    lo_both = [tp_moved(lo[k]) for k in range(C)]
+    outer_parts = weight_call(dims, meta, [(og, act)], sums)
+    inner_parts = weight_call(dims, meta, [(after(nl, outer_parts), inner_low)])
+    outer_core = core_sum(*outer_parts)
+    dctx = after(dctx, [outer_core, *inner_parts])
     dqkv = back_call(dims, qkv, ctx, dctx.reshape(ctx.shape), e, linv)
-    first = after(first, [lo[1], lo[3], *lo_both[0]])
-    ins = input_call(dqkv.reshape(C, R, 3 * D), qkv_w, first)
-    ig = {k: ctx_moved(ins[k], k) for k in range(C)}
-    ig_both = [tp_moved(ig[k]) for k in range(C)]
-    og = after(og, [lo[2], *lo_both[1], *ins])
-    outer_parts = weight_call(dims, meta, [(og, act)], sums)
-    nl = after(nl, [ig[1], ig[3], *lo_both[3], *outer_parts])
-    inner_parts = weight_call(dims, meta, [(nl, inner_low)])
-    outer_core = core_sum(*outer_parts)
-    ag = after(ag, [outer_core, *lo_both[2], *ig_both[0], *inner_parts])
-    qkv_parts = weight_call(dims, meta, [(x_all, dqkv), (ag, ctx)])
+    lo_got = ctx_first(los)
+    own_lo = tp_moved(los[:1])
     inner_core = core_sum(*inner_parts)
     outer_y = y_sum(outer_core)
-    inner_half = x_sum(inner_core)
+    first = after(first, [inner_core, outer_y, *lo_got, *own_lo])
+    ins = input_call(dqkv.reshape(C, R, 3 * D), qkv_w, first)
+    los, lo_raw = ctx_second(los[0], [after(got, [dqkv]) for got in lo_got])
+    outer_x = x_sum(outer_y)
+    inner_y = y_sum(after(inner_core, [outer_y]))
+    ag = after(ag, [*lo_raw, *ins])
+    qkv_parts = weight_call(dims, meta, [(x_all, dqkv), (ag, ctx)])
+    ig_got = ctx_first(ins)
+    far_lo = tp_moved(los[1:])
     keep, send = qkv_parts
-    qkv_core = core_sum(after(keep, [inner_half, ig[2], *ig_both[1]]), send)
-    layer_out = to_slots(lo_both, BF)
-    input_grad = to_slots(ig_both, F32)
-    inner_x = y_sum(inner_half)[0, 0]
-    qkv_x = x_sum(y_sum(qkv_core))[0, 0]
-    outer_x = x_sum(outer_y)[0, 0]
+    qkv_core = core_sum(keep, after(send, [outer_x, inner_y, *ig_got]))
+    ig, ig_raw = ctx_second(ins[0], ig_got)
+    outer_x = after(outer_x[0, 0], [qkv_core, *ig_raw])
     outer_part = ctx_scatter(outer_x)
-    outer_g = ctx_gather(outer_part, outer_x)
-    inner_g = ctx_gather(ctx_scatter(inner_x), inner_x)
+    qkv_y = after(y_sum(qkv_core), [outer_part, *ig_raw])
+    ig_both = tp_moved(after(tuple(ig[:2]), [outer_part]) + tuple(ig[2:]))
+    inner_x = after(x_sum(after(inner_y, [outer_part]))[0, 0], [qkv_y])
+    inner_part = ctx_scatter(inner_x)
+    outer_g = ctx_gather(after(outer_part, [qkv_y]), outer_x)
+    qkv_x = after(x_sum(qkv_y)[0, 0], [outer_g, inner_part])
+    own_lo, far_lo = (after(tuple(part), [qkv_core]) for part in (own_lo, far_lo))
+    layer_out = to_slots([([0], own_lo), (list(range(1, C)), far_lo)], BF)
+    input_grad = to_slots([(list(range(C)), after(tuple(ig_both), [qkv_x]))], F32)
+    inner_g = ctx_gather(inner_part, inner_x)
     qkv_g = ctx_gather(ctx_scatter(qkv_x), qkv_x)
 
     def own(row, shape):

time: 427 us -> 423 us (level)
  starting transfers between devices: 97.6 us -> 80.5 us
  local copies, waits for them, and re-layouts: 28.2 us -> 42.1 us
    ppermute x24 -> x34, waiting for transfers between devices: 33.5 us -> 85.4 us  [ctx_moved(): return lax.ppermute(piece, 'ctx', xor_pairs(C, k)) if k else piece]
    ppermute x22, waiting for transfers between devices: 59 us -> 25.8 us  [swapped(): return lax.ppermute(array, axis, xor_pairs(lax.axis_size(axis), bit))]
    ppermute x14 -> x3, starting transfers between devices: 25.9 us -> 2.38 us  [tp_moved(): lax.ppermute(both, 'tp', xor_pairs(T, dt))]
    ppermute x14 -> x3, waiting for transfers between devices: 29.3 us -> 8.63 us  [tp_moved(): lax.ppermute(both, 'tp', xor_pairs(T, dt))]
    dynamic_update_slice x8, other arithmetic: 12.5 us -> 0.46 us  [to_slots(): lax.dynamic_update_slice_in_dim(out, got.reshape(ns, span, D).astype(kind...]
    slice x0 -> x25, local copies, waits for them, and re-layouts: none -> 10.2 us  [the longest x9 4.17 us: ctx_second(): return ([own, up[:R], jnp.concatenate(raw, axis=0), down[:R]], raw)]
    concatenate x0 -> x11, other arithmetic: none -> 7.98 us  [the longest x4 2.8 us: ctx_first(): down = jnp.concatenate([pieces[3], pieces[2][h:]], axis=0)]
    unnamed x53 -> x66, local copies, waits for them, and re-layouts: 0.93 us -> 7.31 us
  transfers between devices with their start and end apart: 63 -> 62, of which waited for: 26 -> 23; matrix products, arithmetic and copies ran while one was open for 10% -> 12% of each run, Pallas kernels for 24% -> 22%
where the time goes in v4:
time: 423 us; the launch traced here: 422 us
  Pallas kernels  151 us (36%)
  waiting for transfers between devices  120 us (28%)
  starting transfers between devices  80.5 us (19%)
  local copies, waits for them, and re-layouts  42.1 us (10%)
  other arithmetic  26.8 us (6%)
    ppermute x34, waiting for transfers between devices, ctx_moved(): return lax.ppermute(piece, 'ctx', xor_pairs(C, k)) if k else piece  85.4 us
    ppermute x34, starting transfers between devices, ctx_moved(): return lax.ppermute(piece, 'ctx', xor_pairs(C, k)) if k else piece  60.5 us
    pallas_call x1, Pallas kernels, rows_call(): pl.pallas_call(functools.partial(rows_kernel, dims, FF), name='rows', gri...  46.6 us
    pallas_call x3, Pallas kernels, weight_call(): pl.pallas_call(functools.partial(weight_kernel, F, pers, sums is not None...  40 us
    pallas_call x1, Pallas kernels, front_call(): pl.pallas_call(functools.partial(front_kernel, dims), name='front', grid=...  29.6 us
    pallas_call x1, Pallas kernels, back_call(): pl.pallas_call(functools.partial(back_kernel, dims), name='back', grid=(n...  26.2 us
    ppermute x22, waiting for transfers between devices, swapped(): return lax.ppermute(array, axis, xor_pairs(lax.axis_size(axis), bit))  25.8 us
    ppermute x22, starting transfers between devices, swapped(): return lax.ppermute(array, axis, xor_pairs(lax.axis_size(axis), bit))  17.2 us
  transfers between devices with their start and end apart: 62, of which 23 were waited for; matrix products, arithmetic and copies ran while one was open for 12% of the time, Pallas kernels for 22%

profile of v4, /device:TPU:0, one launch (start us, length us, event | category | flops | bytes accessed | tf_op | source)
XLA Modules:
  0.0 422.0 jit_solution(10213582573314347347)
XLA Ops:
  8.4 3.0 collective-permute-start
  12.4 1.6 collective-permute-start.2
  14.0 2.1 constant_dynamic-slice_fusion.16
  17.2 1.6 collective-permute-start.4
  19.0 1.8 collective-permute-start.1
  20.9 1.2 collective-permute-done.2
  22.6 3.7 collective-permute-start.5
  26.2 6.3 %collective-permute-done.4 = bf16[384,768]{1,0:T(8,128)(2,1)S(1)} collective-permute-done((bf16[384,768]{1,0:T(8,128)(2,1)S(1)}, bf16[384,768]{1,0:T(8,128)(2,1)S(1)}, u32[]{:S(2)}, u32[]{:S(2)}) %collective-permute-start.4) | collective-permute-done | bytes 589856 | tf_op jit(solution)/shard_map/ppermute | solution.py:596
  32.6 14.0 %collective-permute-done.5 = bf16[384,768]{1,0:T(8,128)(2,1)S(1)} collective-permute-done((bf16[384,768]{1,0:T(8,128)(2,1)S(1)}, bf16[384,768]{1,0:T(8,128)(2,1)S(1)}, u32[]{:S(2)}, u32[]{:S(2)}) %collective-permute-start.5) | collective-permute-done | bytes 589856 | tf_op jit(solution)/shard_map/ppermute | solution.py:596
  47.7 1.5 collective-permute-start.8
  49.3 8.7 %collective-permute-start.9 = (bf16[128,768]{1,0:T(8,128)(2,1)S(1)}, bf16[128,768]{1,0:T(8,128)(2,1)S(1)}, u32[]{:S(2)}, u32[]{:S(2)}) collective-permute-start(bf16[128,768]{1,0:T(8,128)(2,1)S(1)} %slice.242), channel_id=1, source_target_pairs={{0,2},{2,0},{4,6},{6,4},{1,3},{3,1},{5,7},{7,5},{8,10},{10,8},{12,... | collective-permute-start | bytes 589832 | tf_op jit(solution)/shard_map/ppermute | solution.py:596
  58.5 3.1 collective-permute-done.9
  67.5 3.0 collective-permute-start.14
  73.5 29.6 %front.1 = (bf16[4,256,768]{2,1,0:T(8,128)(2,1)}, bf16[768,2304]{1,0:T(8,128)(2,1)}, bf16[4,2,128,2304]{3,2,1,0:T(8,128)(2,1)}, bf16[12,1024,512]{2,1,0:T(8,128)...) custom-call(s32[4]{0:T(128)} %pad_add_fusion.meta, bf16[256,768]{1,0:T(8,128)(2,1)} %bitcast.110, ...), custom_call_target="tpu_custom_call" | custom-call | flops 3623878656 | bytes 40000000 | tf_op jit(solution)/shard_map/front/pallas_call | solution.py:162
  104.4 6.9 %collective-permute-done.17 = bf16[128,768]{1,0:T(8,128)(2,1)S(1)} collective-permute-done((bf16[128,768]{1,0:T(8,128)(2,1)S(1)}, bf16[128,768]{1,0:T(8,128)(2,1)S(1)}, u32[]{:S(2)}, u32[]{:S(2)}) %collective-permute-start.17) | collective-permute-done | bytes 196640 | tf_op jit(solution)/shard_map/ppermute | solution.py:596
  113.9 5.3 %collective-permute-done.15 = bf16[128,768]{1,0:T(8,128)(2,1)S(1)} collective-permute-done((bf16[128,768]{1,0:T(8,128)(2,1)S(1)}, bf16[128,768]{1,0:T(8,128)(2,1)S(1)}, u32[]{:S(2)}, u32[]{:S(2)}) %collective-permute-start.15) | collective-permute-done | bytes 196640 | tf_op jit(solution)/shard_map/ppermute | solution.py:596
  124.1 46.6 %rows.1 = (bf16[256,768]{1,0:T(8,128)(2,1)}, bf16[256,768]{1,0:T(8,128)(2,1)}, bf16[256,768]{1,0:T(8,128)(2,1)}, bf16[256,768]{1,0:T(8,128)(2,1)}, f32[4,256,768...) custom-call(s32[4]{0:T(128)} %pad_add_fusion.meta, ...), custom_call_target="tpu_custom_call" | custom-call | flops 21743271936 | bytes 50000000 | tf_op jit(solution)/shard_map/rows/pallas_call | solution.py:344
  170.7 12.9 %weight_grad.3 = (bf16[2,2,208,1536]{3,2,1,0:T(8,128)(2,1)}, bf16[2,2,208,1536]{3,2,1,0:T(8,128)(2,1)}) custom-call(s32[4]{0:T(128)} %pad_add_fusion.meta, bf16[1024,768]{1,0:T(8,128)(2,1)} %bitcast.125, bf16[1024,3072]{1,0:T(8,128)(2,1)} %bitcast.121, f32[16,768]{1,0:T(8,128)} %get-tuple-element.93.refs_2_), custom_call_target="tpu_custom_call" | custom-call | flops 4831838208 | bytes 12582912 | tf_op jit(solution)/shard_map/weight_grad/pallas_call | solution.py:523
  183.6 13.1 %weight_grad.4 = (bf16[2,2,208,1536]{3,2,1,0:T(8,128)(2,1)}, bf16[2,2,208,1536]{3,2,1,0:T(8,128)(2,1)}) custom-call(s32[4]{0:T(128)} %pad_add_fusion.meta, bf16[1024,768]{1,0:T(8,128)(2,1)} %bitcast.124, bf16[1024,3072]{1,0:T(8,128)(2,1)} %bitcast.120), custom_call_target="tpu_custom_call" | custom-call | flops 4831838208 | bytes 12582912 | tf_op jit(solution)/shard_map/weight_grad/pallas_call | solution.py:523
  200.0 2.3 collective-permute-start.25
  204.0 1.5 copy-done
  205.5 1.1 split.49
  206.6 1.3 collective-permute-start.31
  207.9 26.2 %back.1 = bf16[4,2,128,2304]{3,2,1,0:T(8,128)(2,1)} custom-call(bf16[4,2,128,2304]{3,2,1,0:T(8,128)(2,1)} %get-tuple-element.89.qkv, bf16[4,2,128,768]{3,2,1,0:T(8,128)(2,1)} %get-tuple-element.79.ctx, bf16[4,2,128,768]{3,2,1,0:T(8,128)(2,1)} %bitcast.87, bf16[12,1024,512]{2,1,0:T(8,128)(2,1)} %get-tuple-element.102.e_ref, ...), custom_call_target="tpu_custom_call" | custom-call | flops 6442450944 | bytes 30000000 | tf_op jit(solution)/shard_map/back/pallas_call | solution.py:413
  235.6 2.4 collective-permute-start.27
  238.0 3.2 add_convert_fusion.1
  241.2 2.7 add_convert_fusion.5
  243.9 1.1 split.41
  245.6 8.6 %input_grad.1 = (bf16[256,768]{1,0:T(8,128)(2,1)}, bf16[256,768]{1,0:T(8,128)(2,1)}, bf16[256,768]{1,0:T(8,128)(2,1)}, bf16[256,768]{1,0:T(8,128)(2,1)}) custom-call(bf16[4,256,2304]{2,1,0:T(8,128)(2,1)} %bitcast.83, bf16[768,2304]{1,0:T(8,128)(2,1)} %get-tuple-element.107.w, f32[4,256,768]{2,1,0:T(8,128)} %get-tuple-element.109.first), custom_call_target="tpu_custom_call" | custom-call | flops 3623878656 | bytes 15000000 | tf_op jit(solution)/shard_map/input_grad/pallas_call | solution.py:450
  256.4 1.4 collective-permute-start.32
  257.8 1.9 pad_maximum_fusion.12
  259.7 1.4 collective-permute-start.35
  262.4 14.1 %weight_grad.5 = (bf16[2,2,208,1536]{3,2,1,0:T(8,128)(2,1)}, bf16[2,2,208,1536]{3,2,1,0:T(8,128)(2,1)}) custom-call(s32[4]{0:T(128)} %pad_add_fusion.meta, bf16[1024,768]{1,0:T(8,128)(2,1)} %bitcast.122, bf16[1024,768]{1,0:T(8,128)(2,1)} %bitcast.123, bf16[1024,2304]{1,0:T(8,128)(2,1)} %bitcast.84, bf16[1024,768]{1,0:T(8,128)(2,1)} %bitcast.86), custom_call_target="tpu_custom_call" | custom-call | flops 4831838208 | bytes 12582912 | tf_op jit(solution)/shard_map/weight_grad/pallas_call | solution.py:523
  276.4 1.4 add_convert_fusion.8
  277.9 2.7 add_convert_fusion.4
  280.6 7.1 %collective-permute-done.34 = bf16[384,768]{1,0:T(8,128)(2,1)} collective-permute-done((bf16[384,768]{1,0:T(8,128)(2,1)}, bf16[384,768]{1,0:T(8,128)(2,1)}, u32[]{:S(2)}, u32[]{:S(2)}) %collective-permute-start.34) | collective-permute-done | bytes 589856 | tf_op jit(solution)/shard_map/ppermute | solution.py:596
  291.5 2.1 collective-permute-start.38
  294.6 3.2 add_convert_fusion
  298.3 3.5 collective-permute-done.38
  301.9 2.7 collective-permute-start.40
  304.9 2.1 collective-permute-start.42
  307.1 1.5 collective-permute-start.44
  308.6 8.6 %collective-permute-done.37 = bf16[768,768]{1,0:T(8,128)(2,1)S(1)} collective-permute-done((bf16[768,768]{1,0:T(8,128)(2,1)S(1)}, bf16[768,768]{1,0:T(8,128)(2,1)S(1)}, u32[]{:S(2)}, u32[]{:S(2)}) %collective-permute-start.37) | collective-permute-done | bytes 1179680 | tf_op jit(solution)/shard_map/ppermute | solution.py:600
  318.7 1.1 constant_dynamic-update-slice_fusion.18
  321.2 1.5 copy-done.4
  322.7 13.5 %collective-permute-done.49 = bf16[1,1,208,1536]{3,2,1,0:T(8,128)(2,1)S(1)} collective-permute-done((bf16[1,1,208,1536]{3,2,1,0:T(8,128)(2,1)S(1)}, bf16[1,1,208,1536]{3,2,1,0:T(8,128)(2,1)S(1)}, u32[]{:S(2)}, u32[]{:S(2)}) %collective-permute-start.49) | collective-permute-done | bytes 639008 | tf_op jit(solution)/shard_map/ppermute | solution.py:618
  337.1 1.8 collective-permute-start.51
  338.9 2.4 collective-permute-start.52
  343.3 1.9 collective-permute-done.50
  345.5 6.3 %collective-permute-done.51 = bf16[208,384]{1,0:T(8,128)(2,1)S(1)} collective-permute-done((bf16[208,384]{1,0:T(8,128)(2,1)S(1)}, bf16[208,384]{1,0:T(8,128)(2,1)S(1)}, u32[]{:S(2)}, u32[]{:S(2)}) %collective-permute-start.51) | collective-permute-done | bytes 159776 | tf_op jit(solution)/shard_map/ppermute | solution.py:596
  351.8 1.8 collective-permute-start.48
  354.5 8.7 %collective-permute-start.59 = (bf16[208,384]{1,0:T(8,128)(2,1)S(1)}, bf16[208,384]{1,0:T(8,128)(2,1)S(1)}, u32[]{:S(2)}, u32[]{:S(2)}) collective-permute-start(bf16[208,384]{1,0:T(8,128)(2,1)S(1)} %get-tuple-element.136), channel_id=1, source_target_pairs={{0,2},{2,0},{4,6},{6,4},{1,3},{3,1},{5,7},{7,5},{8,10},{10,8},{12,... | collective-permute-start | bytes 479240 | tf_op jit(solution)/shard_map/ppermute | solution.py:596
  363.3 3.6 collective-permute-done.47
  368.9 9.6 %collective-permute-done.60 = bf16[208,384]{1,0:T(8,128)(2,1)S(1)} collective-permute-done((bf16[208,384]{1,0:T(8,128)(2,1)S(1)}, bf16[208,384]{1,0:T(8,128)(2,1)S(1)}, u32[]{:S(2)}, u32[]{:S(2)}) %collective-permute-start.60) | collective-permute-done | bytes 159776 | tf_op jit(solution)/shard_map/ppermute | solution.py:596
  378.8 1.1 slice.259
  380.6 9.7 %collective-permute-done.45 = bf16[1,1,208,1536]{3,2,1,0:T(8,128)(2,1)S(1)} collective-permute-done((bf16[1,1,208,1536]{3,2,1,0:T(8,128)(2,1)S(1)}, bf16[1,1,208,1536]{3,2,1,0:T(8,128)(2,1)S(1)}, u32[]{:S(2)}, u32[]{:S(2)}) %collective-permute-start.45) | collective-permute-done | bytes 639008 | tf_op jit(solution)/shard_map/ppermute | solution.py:618
  390.6 2.0 collective-permute-start.54
  392.6 2.4 collective-permute-start.55
  396.3 2.1 collective-permute-done.53
  398.4 4.9 %collective-permute-done.54 = bf16[208,384]{1,0:T(8,128)(2,1)S(1)} collective-permute-done((bf16[208,384]{1,0:T(8,128)(2,1)S(1)}, bf16[208,384]{1,0:T(8,128)(2,1)S(1)}, u32[]{:S(2)}, u32[]{:S(2)}) %collective-permute-start.54) | collective-permute-done | bytes 159776 | tf_op jit(solution)/shard_map/ppermute | solution.py:596
  403.4 2.3 collective-permute-start.56
  405.9 2.5 collective-permute-start.58
  408.3 1.9 collective-permute-done.56
  410.3 8.3 %collective-permute-done.57 = bf16[208,384]{1,0:T(8,128)(2,1)S(1)} collective-permute-done((bf16[208,384]{1,0:T(8,128)(2,1)S(1)}, bf16[208,384]{1,0:T(8,128)(2,1)S(1)}, u32[]{:S(2)}, u32[]{:S(2)}) %collective-permute-start.57) | collective-permute-done | bytes 159776 | tf_op jit(solution)/shard_map/ppermute | solution.py:596
  (274 shorter events, 60.5 us)
Async XLA Ops:
  8.4 10.6 %collective-permute-start = (bf16[1,208,768]{2,1,0:T(8,128)(2,1)S(1)}, bf16[1,208,768]{2,1,0:T(8,128)(2,1)S(1)}, u32[]{:S(2)}, u32[]{:S(2)}) collective-permute-start(bf16[1,208,768]{2,1,0:T(8,128)(2,1)S(1)} %maximum_bitcast_fusion), channel_id=1, source_target_pairs={{0,1},{1,0},{2,3},{3,2},{4,5},{5,4},{6,7},{7,6},{8,9},{9,8},{10,11... | collective-permute-start | bytes 958472 | tf_op jit(solution)/shard_map/ppermute | solution.py:618
  12.4 9.6 %collective-permute-start.2 = (bf16[1,208,768]{2,1,0:T(8,128)(2,1)S(1)}, bf16[1,208,768]{2,1,0:T(8,128)(2,1)S(1)}, u32[]{:S(2)}, u32[]{:S(2)}) collective-permute-start(bf16[1,208,768]{2,1,0:T(8,128)(2,1)S(1)} %maximum_bitcast_fusion.1), channel_id=1, source_target_pairs={{0,16},{8,24},{16,0},{24,8},{1,17},{9,25},{17,1},{25,9},{2,18},{10... | collective-permute-start | bytes 958472 | tf_op jit(solution)/shard_map/ppermute | solution.py:618
  17.2 15.4 %collective-permute-start.4 = (bf16[384,768]{1,0:T(8,128)(2,1)S(1)}, bf16[384,768]{1,0:T(8,128)(2,1)S(1)}, u32[]{:S(2)}, u32[]{:S(2)}) collective-permute-start(bf16[384,768]{1,0:T(8,128)(2,1)S(1)} %pad_maximum_fusion.5), channel_id=1, source_target_pairs={{0,2},{2,0},{4,6},{6,4},{1,3},{3,1},{5,7},{7,5},{8,10},{10,8},{12,... | collective-permute-start | bytes 1769480 | tf_op jit(solution)/shard_map/ppermute | solution.py:596
  19.0 43.2 %copy-start.11 = (bf16[2,208,768]{2,1,0:T(8,128)(2,1)}, bf16[2,208,768]{2,1,0:T(8,128)(2,1)S(1)}, u32[]{:S(2)}) copy-start(bf16[2,208,768]{2,1,0:T(8,128)(2,1)S(1)} %pad_maximum_fusion.3.refs_4_) | copy-start | bytes 1916932
  19.0 27.5 %collective-permute-start.1 = (bf16[2,208,768]{2,1,0:T(8,128)(2,1)S(1)}, bf16[2,208,768]{2,1,0:T(8,128)(2,1)S(1)}, u32[]{:S(2)}, u32[]{:S(2)}) collective-permute-start(bf16[2,208,768]{2,1,0:T(8,128)(2,1)S(1)} %pad_maximum_fusion.3.refs_4_), channel_id=1, source_target_pairs={{0,16},{8,24},{16,0},{24,8},{1,17},{9,25},{17,1},{25,9},{2,18},{10... | collective-permute-start | bytes 1916936 | tf_op jit(solution)/shard_map/ppermute | solution.py:618
  22.1 40.9 %copy-start.12 = (bf16[2,208,768]{2,1,0:T(8,128)(2,1)}, bf16[2,208,768]{2,1,0:T(8,128)(2,1)S(1)}, u32[]{:S(2)}) copy-start(bf16[2,208,768]{2,1,0:T(8,128)(2,1)S(1)} %pad_maximum_fusion.4.refs_8_) | copy-start | bytes 1916932
  22.1 24.4 %collective-permute-start.3 = (bf16[2,208,768]{2,1,0:T(8,128)(2,1)S(1)}, bf16[2,208,768]{2,1,0:T(8,128)(2,1)S(1)}, u32[]{:S(2)}, u32[]{:S(2)}) collective-permute-start(bf16[2,208,768]{2,1,0:T(8,128)(2,1)S(1)} %pad_maximum_fusion.4.refs_8_), channel_id=1, source_target_pairs={{0,1},{1,0},{2,3},{3,2},{4,5},{5,4},{6,7},{7,6},{8,9},{9,8},{10,11... | collective-permute-start | bytes 1916936 | tf_op jit(solution)/shard_map/ppermute | solution.py:618
  22.6 24.0 %collective-permute-start.5 = (bf16[384,768]{1,0:T(8,128)(2,1)S(1)}, bf16[384,768]{1,0:T(8,128)(2,1)S(1)}, u32[]{:S(2)}, u32[]{:S(2)}) collective-permute-start(bf16[384,768]{1,0:T(8,128)(2,1)S(1)} %pad_maximum_fusion.6), channel_id=1, source_target_pairs={{0,6},{2,4},{4,2},{6,0},{1,7},{3,5},{5,3},{7,1},{8,14},{10,12},{12... | collective-permute-start | bytes 1769480 | tf_op jit(solution)/shard_map/ppermute | solution.py:596
  46.6 15.1 %collective-permute-start.7 = (bf16[1,192,1536]{2,1,0:T(8,128)(2,1)S(1)}, bf16[1,192,1536]{2,1,0:T(8,128)(2,1)S(1)}, u32[]{:S(2)}, u32[]{:S(2)}) collective-permute-start(bf16[1,192,1536]{2,1,0:T(8,128)(2,1)S(1)} %bitcast.106), channel_id=1, source_target_pairs={{0,16},{8,24},{16,0},{24,8},{1,17},{9,25},{17,1},{25,9},{2,18},{10... | collective-permute-start | bytes 1769480 | tf_op jit(solution)/shard_map/ppermute | solution.py:618
  47.2 15.1 %collective-permute-start.6 = (bf16[1,192,1536]{2,1,0:T(8,128)(2,1)S(1)}, bf16[1,192,1536]{2,1,0:T(8,128)(2,1)S(1)}, u32[]{:S(2)}, u32[]{:S(2)}) collective-permute-start(bf16[1,192,1536]{2,1,0:T(8,128)(2,1)S(1)} %bitcast.108), channel_id=1, source_target_pairs={{0,1},{1,0},{2,3},{3,2},{4,5},{5,4},{6,7},{7,6},{8,9},{9,8},{10,11... | collective-permute-start | bytes 1769480 | tf_op jit(solution)/shard_map/ppermute | solution.py:618
  47.7 10.3 %collective-permute-start.8 = (bf16[128,768]{1,0:T(8,128)(2,1)S(1)}, bf16[128,768]{1,0:T(8,128)(2,1)S(1)}, u32[]{:S(2)}, u32[]{:S(2)}) collective-permute-start(bf16[128,768]{1,0:T(8,128)(2,1)S(1)} %slice.241), channel_id=1, source_target_pairs={{0,6},{2,4},{4,2},{6,0},{1,7},{3,5},{5,3},{7,1},{8,14},{10,12},{12... | collective-permute-start | bytes 589832 | tf_op jit(solution)/shard_map/ppermute | solution.py:596
  49.3 12.4 %collective-permute-start.9 = (bf16[128,768]{1,0:T(8,128)(2,1)S(1)}, bf16[128,768]{1,0:T(8,128)(2,1)S(1)}, u32[]{:S(2)}, u32[]{:S(2)}) collective-permute-start(bf16[128,768]{1,0:T(8,128)(2,1)S(1)} %slice.242), channel_id=1, source_target_pairs={{0,2},{2,0},{4,6},{6,4},{1,3},{3,1},{5,7},{7,5},{8,10},{10,8},{12,... | collective-permute-start | bytes 589832 | tf_op jit(solution)/shard_map/ppermute | solution.py:596
  58.0 5.1 %collective-permute-start.10 = (bf16[2,208,768]{2,1,0:T(8,128)(2,1)S(1)}, bf16[2,208,768]{2,1,0:T(8,128)(2,1)S(1)}, u32[]{:S(2)}, u32[]{:S(2)}) collective-permute-start(bf16[2,208,768]{2,1,0:T(8,128)(2,1)S(1)} %pad_maximum_fusion.3.refs_4_), channel_id=1, source_target_pairs={{0,8},{8,0},{16,24},{24,16},{1,9},{9,1},{17,25},{25,17},{2,10},{10... | collective-permute-start | bytes 1916936 | tf_op jit(solution)/shard_map/ppermute | solution.py:618
  58.0 5.3 %collective-permute-start.12 = (bf16[2,208,768]{2,1,0:T(8,128)(2,1)S(1)}, bf16[2,208,768]{2,1,0:T(8,128)(2,1)S(1)}, u32[]{:S(2)}, u32[]{:S(2)}) collective-permute-start(bf16[2,208,768]{2,1,0:T(8,128)(2,1)S(1)} %pad_maximum_fusion.4.refs_8_), channel_id=1, source_target_pairs={{0,8},{8,0},{16,24},{24,16},{1,9},{9,1},{17,25},{25,17},{2,10},{10... | collective-permute-start | bytes 1916936 | tf_op jit(solution)/shard_map/ppermute | solution.py:618
  61.7 2.1 collective-permute-start.11
  61.7 3.0 collective-permute-start.13
  62.3 41.5 %collective-permute-start.21 = (bf16[2,192,1536]{2,1,0:T(8,128)(2,1)S(1)}, bf16[2,192,1536]{2,1,0:T(8,128)(2,1)}, u32[]{:S(2)}, u32[]{:S(2)}) collective-permute-start(bf16[2,192,1536]{2,1,0:T(8,128)(2,1)S(1)} %pad_maximum_fusion.1.refs_16_), channel_id=1, source_target_pairs={{0,1},{1,0},{2,3},{3,2},{4,5},{5,4},{6,7},{7,6},{8,9},{9,8},{10,11... | collective-permute-start | bytes 3538952 | tf_op jit(solution)/shard_map/ppermute | solution.py:618
  63.1 40.8 %collective-permute-start.18 = (bf16[2,192,1536]{2,1,0:T(8,128)(2,1)S(1)}, bf16[2,192,1536]{2,1,0:T(8,128)(2,1)}, u32[]{:S(2)}, u32[]{:S(2)}) collective-permute-start(bf16[2,192,1536]{2,1,0:T(8,128)(2,1)S(1)} %pad_maximum_fusion.refs_12_), channel_id=1, source_target_pairs={{0,16},{8,24},{16,0},{24,8},{1,17},{9,25},{17,1},{25,9},{2,18},{10... | collective-permute-start | bytes 3538952 | tf_op jit(solution)/shard_map/ppermute | solution.py:618
  65.6 37.5 %collective-permute-start.16 = (bf16[384,768]{1,0:T(8,128)(2,1)S(1)}, bf16[384,768]{1,0:T(8,128)(2,1)S(1)}, u32[]{:S(2)}, u32[]{:S(2)}) collective-permute-start(bf16[384,768]{1,0:T(8,128)(2,1)S(1)} %pad_maximum_fusion.8), channel_id=1, source_target_pairs={{0,6},{2,4},{4,2},{6,0},{1,7},{3,5},{5,3},{7,1},{8,14},{10,12},{12... | collective-permute-start | bytes 1769480 | tf_op jit(solution)/shard_map/ppermute | solution.py:596
  67.5 35.7 %collective-permute-start.14 = (bf16[384,768]{1,0:T(8,128)(2,1)}, bf16[384,768]{1,0:T(8,128)(2,1)S(1)}, u32[]{:S(2)}, u32[]{:S(2)}) collective-permute-start(bf16[384,768]{1,0:T(8,128)(2,1)} %pad_maximum_fusion.7), channel_id=1, source_target_pairs={{0,2},{2,0},{4,6},{6,4},{1,3},{3,1},{5,7},{7,5},{8,10},{10,8},{12,... | collective-permute-start | bytes 1769480 | tf_op jit(solution)/shard_map/ppermute | solution.py:596
  103.2 16.8 %collective-permute-start.22 = (bf16[2,192,1536]{2,1,0:T(8,128)(2,1)S(1)}, bf16[2,192,1536]{2,1,0:T(8,128)(2,1)S(1)}, u32[]{:S(2)}, u32[]{:S(2)}) collective-permute-start(bf16[2,192,1536]{2,1,0:T(8,128)(2,1)S(1)} %pad_maximum_fusion.1.refs_16_), channel_id=1, source_target_pairs={{0,8},{8,0},{16,24},{24,16},{1,9},{9,1},{17,25},{25,17},{2,10},{10... | collective-permute-start | bytes 3538952 | tf_op jit(solution)/shard_map/ppermute | solution.py:618
  103.3 16.7 %collective-permute-start.19 = (bf16[2,192,1536]{2,1,0:T(8,128)(2,1)S(1)}, bf16[2,192,1536]{2,1,0:T(8,128)(2,1)S(1)}, u32[]{:S(2)}, u32[]{:S(2)}) collective-permute-start(bf16[2,192,1536]{2,1,0:T(8,128)(2,1)S(1)} %pad_maximum_fusion.refs_12_), channel_id=1, source_target_pairs={{0,8},{8,0},{16,24},{24,16},{1,9},{9,1},{17,25},{25,17},{2,10},{10... | collective-permute-start | bytes 3538952 | tf_op jit(solution)/shard_map/ppermute | solution.py:618
  103.8 17.2 %collective-permute-start.23 = (bf16[2,192,1536]{2,1,0:T(8,128)(2,1)}, bf16[2,192,1536]{2,1,0:T(8,128)(2,1)S(1)}, u32[]{:S(2)}, u32[]{:S(2)}) collective-permute-start(bf16[2,192,1536]{2,1,0:T(8,128)(2,1)} %collective-permute-done.21.refs_17_), channel_id=1, source_target_pairs={{0,8},{8,0},{16,24},{24,16},{1,9},{9,1},{17,25},{25,17},{2,10},{10... | collective-permute-start | bytes 3538952 | tf_op jit(solution)/shard_map/ppermute | solution.py:618
  103.9 18.2 %collective-permute-start.20 = (bf16[2,192,1536]{2,1,0:T(8,128)(2,1)}, bf16[2,192,1536]{2,1,0:T(8,128)(2,1)S(1)}, u32[]{:S(2)}, u32[]{:S(2)}) collective-permute-start(bf16[2,192,1536]{2,1,0:T(8,128)(2,1)} %collective-permute-done.18.refs_13_), channel_id=1, source_target_pairs={{0,8},{8,0},{16,24},{24,16},{1,9},{9,1},{17,25},{25,17},{2,10},{10... | collective-permute-start | bytes 3538952 | tf_op jit(solution)/shard_map/ppermute | solution.py:618
  104.3 7.0 %collective-permute-start.17 = (bf16[128,768]{1,0:T(8,128)(2,1)S(1)}, bf16[128,768]{1,0:T(8,128)(2,1)S(1)}, u32[]{:S(2)}, u32[]{:S(2)}) collective-permute-start(bf16[128,768]{1,0:T(8,128)(2,1)S(1)} %slice.246), channel_id=1, source_target_pairs={{0,2},{2,0},{4,6},{6,4},{1,3},{3,1},{5,7},{7,5},{8,10},{10,8},{12,... | collective-permute-start | bytes 589832 | tf_op jit(solution)/shard_map/ppermute | solution.py:596
  111.3 7.9 %collective-permute-start.15 = (bf16[128,768]{1,0:T(8,128)(2,1)S(1)}, bf16[128,768]{1,0:T(8,128)(2,1)S(1)}, u32[]{:S(2)}, u32[]{:S(2)}) collective-permute-start(bf16[128,768]{1,0:T(8,128)(2,1)S(1)} %slice.245), channel_id=1, source_target_pairs={{0,6},{2,4},{4,2},{6,0},{1,7},{3,5},{5,3},{7,1},{8,14},{10,12},{12... | collective-permute-start | bytes 589832 | tf_op jit(solution)/shard_map/ppermute | solution.py:596
  183.6 19.7 %collective-permute-start.26 = (bf16[2,2,208,1536]{3,2,1,0:T(8,128)(2,1)}, bf16[2,2,208,1536]{3,2,1,0:T(8,128)(2,1)S(1)}, u32[]{:S(2)}, u32[]{:S(2)}) collective-permute-start(bf16[2,2,208,1536]{3,2,1,0:T(8,128)(2,1)} %get-tuple-element.95), channel_id=1, source_target_pairs={{0,8},{8,0},{16,24},{24,16},{1,9},{9,1},{17,25},{25,17},{2,10},{10... | collective-permute-start | bytes 7667720 | tf_op jit(solution)/shard_map/ppermute | solution.py:676
  196.7 41.4 %collective-permute-start.30 = (bf16[2,2,208,1536]{3,2,1,0:T(8,128)(2,1)}, bf16[2,2,208,1536]{3,2,1,0:T(8,128)(2,1)}, u32[]{:S(2)}, u32[]{:S(2)}) collective-permute-start(bf16[2,2,208,1536]{3,2,1,0:T(8,128)(2,1)} %get-tuple-element.100), channel_id=1, source_target_pairs={{0,8},{8,0},{16,24},{24,16},{1,9},{9,1},{17,25},{25,17},{2,10},{10... | collective-permute-start | bytes 7667720 | tf_op jit(solution)/shard_map/ppermute | solution.py:676
  198.1 36.0 %collective-permute-start.28 = (bf16[384,768]{1,0:T(8,128)(2,1)}, bf16[384,768]{1,0:T(8,128)(2,1)S(1)}, u32[]{:S(2)}, u32[]{:S(2)}) collective-permute-start(bf16[384,768]{1,0:T(8,128)(2,1)} %pad_maximum_fusion.10), channel_id=1, source_target_pairs={{0,6},{2,4},{4,2},{6,0},{1,7},{3,5},{5,3},{7,1},{8,14},{10,12},{12... | collective-permute-start | bytes 1769480 | tf_op jit(solution)/shard_map/ppermute | solution.py:596
  200.0 34.9 %collective-permute-start.25 = (bf16[384,768]{1,0:T(8,128)(2,1)}, bf16[384,768]{1,0:T(8,128)(2,1)S(1)}, u32[]{:S(2)}, u32[]{:S(2)}) collective-permute-start(bf16[384,768]{1,0:T(8,128)(2,1)} %pad_maximum_fusion.9), channel_id=1, source_target_pairs={{0,2},{2,0},{4,6},{6,4},{1,3},{3,1},{5,7},{7,5},{8,10},{10,8},{12,... | collective-permute-start | bytes 1769480 | tf_op jit(solution)/shard_map/ppermute | solution.py:596
  202.3 41.6 %collective-permute-start.24 = (bf16[256,768]{1,0:T(8,128)(2,1)}, bf16[256,768]{1,0:T(8,128)(2,1)}, u32[]{:S(2)}, u32[]{:S(2)}) collective-permute-start(bf16[256,768]{1,0:T(8,128)(2,1)} %get-tuple-element.119), channel_id=1, source_target_pairs={{0,1},{1,0},{2,3},{3,2},{4,5},{5,4},{6,7},{7,6},{8,9},{9,8},{10,11... | collective-permute-start | bytes 1179656 | tf_op jit(solution)/shard_map/ppermute | solution.py:600
  206.6 34.6 %collective-permute-start.31 = (bf16[1,2,208,1536]{3,2,1,0:T(8,128)(2,1)}, bf16[1,2,208,1536]{3,2,1,0:T(8,128)(2,1)}, u32[]{:S(2)}, u32[]{:S(2)}) collective-permute-start(bf16[1,2,208,1536]{3,2,1,0:T(8,128)(2,1)} %split.49), channel_id=1, source_target_pairs={{0,16},{8,24},{16,0},{24,8},{1,17},{9,25},{17,1},{25,9},{2,18},{10... | collective-permute-start | bytes 3833864 | tf_op jit(solution)/shard_map/ppermute | solution.py:618
  234.9 27.0 %collective-permute-start.29 = (bf16[128,768]{1,0:T(8,128)(2,1)}, bf16[128,768]{1,0:T(8,128)(2,1)S(1)}, u32[]{:S(2)}, u32[]{:S(2)}) collective-permute-start(bf16[128,768]{1,0:T(8,128)(2,1)} %slice.201), channel_id=1, source_target_pairs={{0,2},{2,0},{4,6},{6,4},{1,3},{3,1},{5,7},{7,5},{8,10},{10,8},{12,... | collective-permute-start | bytes 589832 | tf_op jit(solution)/shard_map/ppermute | solution.py:596
  235.6 26.7 %collective-permute-start.27 = (bf16[128,768]{1,0:T(8,128)(2,1)}, bf16[128,768]{1,0:T(8,128)(2,1)}, u32[]{:S(2)}, u32[]{:S(2)}) collective-permute-start(bf16[128,768]{1,0:T(8,128)(2,1)} %slice.199), channel_id=1, source_target_pairs={{0,6},{2,4},{4,2},{6,0},{1,7},{3,5},{5,3},{7,1},{8,14},{10,12},{12... | collective-permute-start | bytes 589832 | tf_op jit(solution)/shard_map/ppermute | solution.py:596
  245.1 32.8 %collective-permute-start.33 = (bf16[1,2,208,1536]{3,2,1,0:T(8,128)(2,1)}, bf16[1,2,208,1536]{3,2,1,0:T(8,128)(2,1)}, u32[]{:S(2)}, u32[]{:S(2)}) collective-permute-start(bf16[1,2,208,1536]{3,2,1,0:T(8,128)(2,1)} %split.41), channel_id=1, source_target_pairs={{0,16},{8,24},{16,0},{24,8},{1,17},{9,25},{17,1},{25,9},{2,18},{10... | collective-permute-start | bytes 3833864 | tf_op jit(solution)/shard_map/ppermute | solution.py:618
  256.4 20.1 %collective-permute-start.32 = (bf16[1,1,208,1536]{3,2,1,0:T(8,128)(2,1)S(1)}, bf16[1,1,208,1536]{3,2,1,0:T(8,128)(2,1)}, u32[]{:S(2)}, u32[]{:S(2)}) collective-permute-start(bf16[1,1,208,1536]{3,2,1,0:T(8,128)(2,1)S(1)} %split.51), channel_id=1, source_target_pairs={{0,1},{1,0},{2,3},{3,2},{4,5},{5,4},{6,7},{7,6},{8,9},{9,8},{10,11... | collective-permute-start | bytes 1916936 | tf_op jit(solution)/shard_map/ppermute | solution.py:618
  259.7 21.0 %collective-permute-start.35 = (bf16[384,768]{1,0:T(8,128)(2,1)}, bf16[384,768]{1,0:T(8,128)(2,1)}, u32[]{:S(2)}, u32[]{:S(2)}) collective-permute-start(bf16[384,768]{1,0:T(8,128)(2,1)} %pad_maximum_fusion.12), channel_id=1, source_target_pairs={{0,6},{2,4},{4,2},{6,0},{1,7},{3,5},{5,3},{7,1},{8,14},{10,12},{12... | collective-permute-start | bytes 1769480 | tf_op jit(solution)/shard_map/ppermute | solution.py:596
  261.9 25.8 %collective-permute-start.34 = (bf16[384,768]{1,0:T(8,128)(2,1)}, bf16[384,768]{1,0:T(8,128)(2,1)}, u32[]{:S(2)}, u32[]{:S(2)}) collective-permute-start(bf16[384,768]{1,0:T(8,128)(2,1)} %pad_maximum_fusion.11), channel_id=1, source_target_pairs={{0,2},{2,0},{4,6},{6,4},{1,3},{3,1},{5,7},{7,5},{8,10},{10,8},{12,... | collective-permute-start | bytes 1769480 | tf_op jit(solution)/shard_map/ppermute | solution.py:596
  287.7 6.8 %collective-permute-start.36 = (bf16[2,2,208,1536]{3,2,1,0:T(8,128)(2,1)}, bf16[2,2,208,1536]{3,2,1,0:T(8,128)(2,1)}, u32[]{:S(2)}, u32[]{:S(2)}) collective-permute-start(bf16[2,2,208,1536]{3,2,1,0:T(8,128)(2,1)} %get-tuple-element.118), channel_id=1, source_target_pairs={{0,8},{8,0},{16,24},{24,16},{1,9},{9,1},{17,25},{25,17},{2,10},{10... | collective-permute-start | bytes 7667720 | tf_op jit(solution)/shard_map/ppermute | solution.py:676
  288.8 28.4 %collective-permute-start.37 = (bf16[768,768]{1,0:T(8,128)(2,1)S(1)}, bf16[768,768]{1,0:T(8,128)(2,1)S(1)}, u32[]{:S(2)}, u32[]{:S(2)}) collective-permute-start(bf16[768,768]{1,0:T(8,128)(2,1)S(1)} %pad_maximum_fusion.2), channel_id=1, source_target_pairs={{0,1},{1,0},{2,3},{3,2},{4,5},{5,4},{6,7},{7,6},{8,9},{9,8},{10,11... | collective-permute-start | bytes 3538952 | tf_op jit(solution)/shard_map/ppermute | solution.py:600
  290.4 7.8 %collective-permute-start.39 = (bf16[128,768]{1,0:T(8,128)(2,1)S(1)}, bf16[128,768]{1,0:T(8,128)(2,1)S(1)}, u32[]{:S(2)}, u32[]{:S(2)}) collective-permute-start(bf16[128,768]{1,0:T(8,128)(2,1)S(1)} %slice.250), channel_id=1, source_target_pairs={{0,2},{2,0},{4,6},{6,4},{1,3},{3,1},{5,7},{7,5},{8,10},{10,8},{12,... | collective-permute-start | bytes 589832 | tf_op jit(solution)/shard_map/ppermute | solution.py:596
  291.5 10.4 %collective-permute-start.38 = (bf16[128,768]{1,0:T(8,128)(2,1)S(1)}, bf16[128,768]{1,0:T(8,128)(2,1)S(1)}, u32[]{:S(2)}, u32[]{:S(2)}) collective-permute-start(bf16[128,768]{1,0:T(8,128)(2,1)S(1)} %slice.249), channel_id=1, source_target_pairs={{0,6},{2,4},{4,2},{6,0},{1,7},{3,5},{5,3},{7,1},{8,14},{10,12},{12... | collective-permute-start | bytes 589832 | tf_op jit(solution)/shard_map/ppermute | solution.py:596
  301.9 18.2 %collective-permute-start.40 = (bf16[208,384]{1,0:T(8,128)(2,1)S(1)}, bf16[208,384]{1,0:T(8,128)(2,1)S(1)}, u32[]{:S(2)}, u32[]{:S(2)}) collective-permute-start(bf16[208,384]{1,0:T(8,128)(2,1)S(1)} %get-tuple-element.172), channel_id=1, source_target_pairs={{0,2},{2,0},{4,6},{6,4},{1,3},{3,1},{5,7},{7,5},{8,10},{10,8},{12,... | collective-permute-start | bytes 479240 | tf_op jit(solution)/shard_map/ppermute | solution.py:596
  304.6 15.4 %collective-permute-start.41 = (bf16[208,384]{1,0:T(8,128)(2,1)S(1)}, bf16[208,384]{1,0:T(8,128)(2,1)S(1)}, u32[]{:S(2)}, u32[]{:S(2)}) collective-permute-start(bf16[208,384]{1,0:T(8,128)(2,1)S(1)} %get-tuple-element.174), channel_id=1, source_target_pairs={{0,4},{2,6},{4,0},{6,2},{1,5},{3,7},{5,1},{7,3},{8,12},{10,14},{12... | collective-permute-start | bytes 479240 | tf_op jit(solution)/shard_map/ppermute | solution.py:596
  304.9 15.1 %collective-permute-start.42 = (bf16[208,384]{1,0:T(8,128)(2,1)S(1)}, bf16[208,384]{1,0:T(8,128)(2,1)S(1)}, u32[]{:S(2)}, u32[]{:S(2)}) collective-permute-start(bf16[208,384]{1,0:T(8,128)(2,1)S(1)} %get-tuple-element.173), channel_id=1, source_target_pairs={{0,6},{2,4},{4,2},{6,0},{1,7},{3,5},{5,3},{7,1},{8,14},{10,12},{12... | collective-permute-start | bytes 479240 | tf_op jit(solution)/shard_map/ppermute | solution.py:596
  307.1 29.4 %collective-permute-start.44 = (bf16[1,2,208,1536]{3,2,1,0:T(8,128)(2,1)S(1)}, bf16[1,2,208,1536]{3,2,1,0:T(8,128)(2,1)S(1)}, u32[]{:S(2)}, u32[]{:S(2)}) collective-permute-start(bf16[1,2,208,1536]{3,2,1,0:T(8,128)(2,1)S(1)} %split.53), channel_id=1, source_target_pairs={{0,16},{8,24},{16,0},{24,8},{1,17},{9,25},{17,1},{25,9},{2,18},{10... | collective-permute-start | bytes 3833864 | tf_op jit(solution)/shard_map/ppermute | solution.py:618
  320.2 16.0 %collective-permute-start.49 = (bf16[1,1,208,1536]{3,2,1,0:T(8,128)(2,1)S(1)}, bf16[1,1,208,1536]{3,2,1,0:T(8,128)(2,1)S(1)}, u32[]{:S(2)}, u32[]{:S(2)}) collective-permute-start(bf16[1,1,208,1536]{3,2,1,0:T(8,128)(2,1)S(1)} %split.47), channel_id=1, source_target_pairs={{0,1},{1,0},{2,3},{3,2},{4,5},{5,4},{6,7},{7,6},{8,9},{9,8},{10,11... | collective-permute-start | bytes 1916936 | tf_op jit(solution)/shard_map/ppermute | solution.py:618
  336.8 8.4 %collective-permute-start.50 = (bf16[208,384]{1,0:T(8,128)(2,1)S(1)}, bf16[208,384]{1,0:T(8,128)(2,1)S(1)}, u32[]{:S(2)}, u32[]{:S(2)}) collective-permute-start(bf16[208,384]{1,0:T(8,128)(2,1)S(1)} %get-tuple-element.169), channel_id=1, source_target_pairs={{0,2},{2,0},{4,6},{6,4},{1,3},{3,1},{5,7},{7,5},{8,10},{10,8},{12,... | collective-permute-start | bytes 479240 | tf_op jit(solution)/shard_map/ppermute | solution.py:596
  337.1 14.7 %collective-permute-start.51 = (bf16[208,384]{1,0:T(8,128)(2,1)S(1)}, bf16[208,384]{1,0:T(8,128)(2,1)S(1)}, u32[]{:S(2)}, u32[]{:S(2)}) collective-permute-start(bf16[208,384]{1,0:T(8,128)(2,1)S(1)} %get-tuple-element.171), channel_id=1, source_target_pairs={{0,4},{2,6},{4,0},{6,2},{1,5},{3,7},{5,1},{7,3},{8,12},{10,14},{12... | collective-permute-start | bytes 479240 | tf_op jit(solution)/shard_map/ppermute | solution.py:596
  338.9 14.8 %collective-permute-start.52 = (bf16[208,384]{1,0:T(8,128)(2,1)S(1)}, bf16[208,384]{1,0:T(8,128)(2,1)S(1)}, u32[]{:S(2)}, u32[]{:S(2)}) collective-permute-start(bf16[208,384]{1,0:T(8,128)(2,1)S(1)} %get-tuple-element.170), channel_id=1, source_target_pairs={{0,6},{2,4},{4,2},{6,0},{1,7},{3,5},{5,3},{7,1},{8,14},{10,12},{12... | collective-permute-start | bytes 479240 | tf_op jit(solution)/shard_map/ppermute | solution.py:596
  342.3 52.7 %collective-permute-start.43 = (bf16[1024,768]{1,0:T(8,128)(2,1)S(1)}, bf16[1024,768]{1,0:T(8,128)(2,1)S(1)}, u32[]{:S(2)}, u32[]{:S(2)}) collective-permute-start(bf16[1024,768]{1,0:T(8,128)(2,1)S(1)} %slice_dynamic-update-slice_fusion), channel_id=1, source_target_pairs={{0,1},{1,0},{2,3},{3,2},{4,5},{5,4},{6,7},{7,6},{8,9},{9,8},{10,11... | collective-permute-start | bytes 4718600 | tf_op jit(solution)/shard_map/ppermute | solution.py:600
  343.1 11.5 %collective-permute-start.46 = (bf16[208,384]{1,0:T(8,128)(2,1)S(1)}, bf16[208,384]{1,0:T(8,128)(2,1)S(1)}, u32[]{:S(2)}, u32[]{:S(2)}) collective-permute-start(bf16[208,384]{1,0:T(8,128)(2,1)S(1)} %add_convert_fusion.11), channel_id=1, source_target_pairs={{0,2},{2,0},{4,6},{6,4},{1,3},{3,1},{5,7},{7,5},{8,10},{10,8},{12,... | collective-permute-start | bytes 479240 | tf_op jit(solution)/shard_map/ppermute | solution.py:596
  345.2 21.6 %collective-permute-start.47 = (bf16[208,384]{1,0:T(8,128)(2,1)S(1)}, bf16[208,384]{1,0:T(8,128)(2,1)S(1)}, u32[]{:S(2)}, u32[]{:S(2)}) collective-permute-start(bf16[208,384]{1,0:T(8,128)(2,1)S(1)} %add_convert_fusion.11), channel_id=1, source_target_pairs={{0,4},{2,6},{4,0},{6,2},{1,5},{3,7},{5,1},{7,3},{8,12},{10,14},{12... | collective-permute-start | bytes 479240 | tf_op jit(solution)/shard_map/ppermute | solution.py:596
  351.8 15.1 %collective-permute-start.48 = (bf16[208,384]{1,0:T(8,128)(2,1)S(1)}, bf16[208,384]{1,0:T(8,128)(2,1)S(1)}, u32[]{:S(2)}, u32[]{:S(2)}) collective-permute-start(bf16[208,384]{1,0:T(8,128)(2,1)S(1)} %add_convert_fusion.11), channel_id=1, source_target_pairs={{0,6},{2,4},{4,2},{6,0},{1,7},{3,5},{5,3},{7,1},{8,14},{10,12},{12... | collective-permute-start | bytes 479240 | tf_op jit(solution)/shard_map/ppermute | solution.py:596
  353.6 36.7 %collective-permute-start.45 = (bf16[1,1,208,1536]{3,2,1,0:T(8,128)(2,1)S(1)}, bf16[1,1,208,1536]{3,2,1,0:T(8,128)(2,1)S(1)}, u32[]{:S(2)}, u32[]{:S(2)}) collective-permute-start(bf16[1,1,208,1536]{3,2,1,0:T(8,128)(2,1)S(1)} %split.45), channel_id=1, source_target_pairs={{0,1},{1,0},{2,3},{3,2},{4,5},{5,4},{6,7},{7,6},{8,9},{9,8},{10,11... | collective-permute-start | bytes 1916936 | tf_op jit(solution)/shard_map/ppermute | solution.py:618
  354.5 14.4 %collective-permute-start.59 = (bf16[208,384]{1,0:T(8,128)(2,1)S(1)}, bf16[208,384]{1,0:T(8,128)(2,1)S(1)}, u32[]{:S(2)}, u32[]{:S(2)}) collective-permute-start(bf16[208,384]{1,0:T(8,128)(2,1)S(1)} %get-tuple-element.136), channel_id=1, source_target_pairs={{0,2},{2,0},{4,6},{6,4},{1,3},{3,1},{5,7},{7,5},{8,10},{10,8},{12,... | collective-permute-start | bytes 479240 | tf_op jit(solution)/shard_map/ppermute | solution.py:596
  366.8 11.7 %collective-permute-start.60 = (bf16[208,384]{1,0:T(8,128)(2,1)S(1)}, bf16[208,384]{1,0:T(8,128)(2,1)S(1)}, u32[]{:S(2)}, u32[]{:S(2)}) collective-permute-start(bf16[208,384]{1,0:T(8,128)(2,1)S(1)} %get-tuple-element.136), channel_id=1, source_target_pairs={{0,4},{2,6},{4,0},{6,2},{1,5},{3,7},{5,1},{7,3},{8,12},{10,14},{12... | collective-permute-start | bytes 479240 | tf_op jit(solution)/shard_map/ppermute | solution.py:596
  366.9 11.7 %collective-permute-start.61 = (bf16[208,384]{1,0:T(8,128)(2,1)S(1)}, bf16[208,384]{1,0:T(8,128)(2,1)S(1)}, u32[]{:S(2)}, u32[]{:S(2)}) collective-permute-start(bf16[208,384]{1,0:T(8,128)(2,1)S(1)} %get-tuple-element.136), channel_id=1, source_target_pairs={{0,6},{2,4},{4,2},{6,0},{1,7},{3,5},{5,3},{7,1},{8,14},{10,12},{12... | collective-permute-start | bytes 479240 | tf_op jit(solution)/shard_map/ppermute | solution.py:596
  390.6 7.8 %collective-permute-start.53 = (bf16[208,384]{1,0:T(8,128)(2,1)S(1)}, bf16[208,384]{1,0:T(8,128)(2,1)S(1)}, u32[]{:S(2)}, u32[]{:S(2)}) collective-permute-start(bf16[208,384]{1,0:T(8,128)(2,1)S(1)} %get-tuple-element.166), channel_id=1, source_target_pairs={{0,2},{2,0},{4,6},{6,4},{1,3},{3,1},{5,7},{7,5},{8,10},{10,8},{12,... | collective-permute-start | bytes 479240 | tf_op jit(solution)/shard_map/ppermute | solution.py:596
  390.6 12.7 %collective-permute-start.54 = (bf16[208,384]{1,0:T(8,128)(2,1)S(1)}, bf16[208,384]{1,0:T(8,128)(2,1)S(1)}, u32[]{:S(2)}, u32[]{:S(2)}) collective-permute-start(bf16[208,384]{1,0:T(8,128)(2,1)S(1)} %get-tuple-element.168), channel_id=1, source_target_pairs={{0,4},{2,6},{4,0},{6,2},{1,5},{3,7},{5,1},{7,3},{8,12},{10,14},{12... | collective-permute-start | bytes 479240 | tf_op jit(solution)/shard_map/ppermute | solution.py:596
  392.6 10.7 %collective-permute-start.55 = (bf16[208,384]{1,0:T(8,128)(2,1)S(1)}, bf16[208,384]{1,0:T(8,128)(2,1)S(1)}, u32[]{:S(2)}, u32[]{:S(2)}) collective-permute-start(bf16[208,384]{1,0:T(8,128)(2,1)S(1)} %get-tuple-element.167), channel_id=1, source_target_pairs={{0,6},{2,4},{4,2},{6,0},{1,7},{3,5},{5,3},{7,1},{8,14},{10,12},{12... | collective-permute-start | bytes 479240 | tf_op jit(solution)/shard_map/ppermute | solution.py:596
  403.4 6.8 %collective-permute-start.56 = (bf16[208,384]{1,0:T(8,128)(2,1)S(1)}, bf16[208,384]{1,0:T(8,128)(2,1)S(1)}, u32[]{:S(2)}, u32[]{:S(2)}) collective-permute-start(bf16[208,384]{1,0:T(8,128)(2,1)S(1)} %get-tuple-element.138), channel_id=1, source_target_pairs={{0,2},{2,0},{4,6},{6,4},{1,3},{3,1},{5,7},{7,5},{8,10},{10,8},{12,... | collective-permute-start | bytes 479240 | tf_op jit(solution)/shard_map/ppermute | solution.py:596
  405.8 12.8 %collective-permute-start.57 = (bf16[208,384]{1,0:T(8,128)(2,1)S(1)}, bf16[208,384]{1,0:T(8,128)(2,1)S(1)}, u32[]{:S(2)}, u32[]{:S(2)}) collective-permute-start(bf16[208,384]{1,0:T(8,128)(2,1)S(1)} %get-tuple-element.138), channel_id=1, source_target_pairs={{0,4},{2,6},{4,0},{6,2},{1,5},{3,7},{5,1},{7,3},{8,12},{10,14},{12... | collective-permute-start | bytes 479240 | tf_op jit(solution)/shard_map/ppermute | solution.py:596
  405.9 12.7 %collective-permute-start.58 = (bf16[208,384]{1,0:T(8,128)(2,1)S(1)}, bf16[208,384]{1,0:T(8,128)(2,1)S(1)}, u32[]{:S(2)}, u32[]{:S(2)}) collective-permute-start(bf16[208,384]{1,0:T(8,128)(2,1)S(1)} %get-tuple-element.138), channel_id=1, source_target_pairs={{0,6},{2,4},{4,2},{6,0},{1,7},{3,5},{5,3},{7,1},{8,14},{10,12},{12... | collective-permute-start | bytes 479240 | tf_op jit(solution)/shard_map/ppermute | solution.py:596
  (31 other events, 323.0 us)

commit v5 on v4

--- a/solution.py
+++ b/solution.py
@@ -577,26 +577,11 @@
             for k in range(C)
         ]
 
-    def ctx_first(pieces):
-        if C != 4:
-            return [ctx_moved(piece, k) for k, piece in enumerate(pieces)][1:]
-        h = R // 2
-        up = jnp.concatenate([pieces[1], pieces[2][:h]], axis=0)
-        down = jnp.concatenate([pieces[3], pieces[2][h:]], axis=0)
-        return [ctx_moved(up, 1), ctx_moved(down, 3)]
-
-    def ctx_second(own, got):
-        if C != 4:
-            return [own, *got], list(got)
-        up, down = got
-        raw = [ctx_moved(up[R:], 3), ctx_moved(down[R:], 1)]
-        return [own, up[:R], jnp.concatenate(raw, axis=0), down[:R]], raw
-
     def ctx_moved(piece, k):
         return lax.ppermute(piece, "ctx", xor_pairs(C, k)) if k else piece
 
     def tp_moved(pieces):
-        both = jnp.concatenate(pieces, axis=0)
+        both = jnp.concatenate(pieces, axis=0) if len(pieces) > 1 else pieces[0]
         return [both] + [lax.ppermute(both, "tp", xor_pairs(T, dt)) for dt in range(1, T)]
 
     def to_slots(groups, kind):
@@ -637,7 +622,10 @@
         return jnp.where(owner == f, jnp.tile(array, (1, F)), jnp.zeros((), BF)).reshape(-1, width)
 
     x_pieces = sequence_pieces(tokens_in)
-    x_got = ctx_first(x_pieces)
+    near_x = ctx_moved(x_pieces[1], 1)
+    x_pieces = x_pieces[:1] + [near_x] + [
+        ctx_moved(after(x_pieces[k], [near_x]), k) for k in range(2, C)
+    ]
     vectors = jnp.stack([output_bias, attn_gain, attn_shift, outer_bias, ffn_gain, ffn_shift])
     small = [
         spread(query_bias, half), spread(value_bias, half), spread(inner_bias, fhalf),
@@ -649,25 +637,23 @@
     high = jnp.concatenate([value_weight, output_weight.T], axis=1)
     low = chip_start(jnp.concatenate([low, small[:, :D]], axis=0), False)
     high = chip_start(jnp.concatenate([high, small[:, D:]], axis=0), True)
-    lows = both_cores(low, chip_end(low, False))
-    highs = both_cores(high, chip_end(high, True))
-    halfway = [lows[1], highs[1], *x_got]
-    x_pieces, x_raw = ctx_second(x_pieces[0], x_got)
+    lows = both_cores(low, chip_end(after(low, [near_x]), False))
+    highs = both_cores(high, chip_end(after(high, [near_x]), True))
+    halfway = [lows[1], highs[1], *x_pieces[2:]]
     inner = chip_start(after(inner_weight, halfway), False)
     outer = chip_start(after(outer_weight.T, halfway), True)
-    inner_got = chip_end(after(inner, x_raw), False)
-    outer_got = chip_end(after(outer, x_raw), True)
-    cot_pieces = sequence_pieces(after(cotangent, [*x_raw, *lows, *highs]))
-    cot_got = ctx_first(cot_pieces)
+    inner_got = chip_end(inner, False)
+    outer_got = chip_end(outer, True)
+    cot_pieces = sequence_pieces(after(cotangent, [*x_pieces[1:], *lows, *highs]))
+    cot_pieces = [ctx_moved(piece, k) for k, piece in enumerate(cot_pieces)]
     lengths = lax.dynamic_slice_in_dim(seq_lengths, (c * T + t) * ns, ns, 0)
     meta = jnp.concatenate([jnp.stack([f, c]).astype(jnp.int32), lengths])
 
     x_all, qkv_w, qkv, e, linv, ctx = front_call(
         dims, after(meta, [inner, outer]), x_pieces, lows, highs
     )
-    inners = both_cores(inner, inner_got, [ctx, *cot_got])
-    outers = both_cores(outer, outer_got, [ctx, *cot_got])
-    cot_pieces, _ = ctx_second(cot_pieces[0], cot_got)
+    inners = both_cores(inner, inner_got, [ctx, *cot_pieces[1:]])
+    outers = both_cores(outer, outer_got, [ctx, *cot_pieces[1:]])
     los, (first, dctx, nl, act, og, inner_low, ag, sums) = rows_call(
         dims, FF, meta, x_all, ctx.reshape(C, R, D), cot_pieces, lows + highs + inners + outers,
     )
@@ -676,11 +662,13 @@
         return added(keep, lax.ppermute(send, "fsdp", xor_pairs(F, 1)))
 
     def chip_sum(total, axis, dim):
+        got = total
         while total.shape[dim] > 1:
             h = total.shape[dim] // 2
             stay, go = jnp.split(total, 2, axis=dim)
-            total = added(stay, swapped(go, axis, 2 * h if axis == "fsdp" else h))
-        return total
+            got = swapped(go, axis, 2 * h if axis == "fsdp" else h)
+            total = added(stay, got)
+        return total, got
 
     def y_sum(total):
         return chip_sum(total, "fsdp", 0)
@@ -705,36 +693,45 @@
 
     outer_parts = weight_call(dims, meta, [(og, act)], sums)
     inner_parts = weight_call(dims, meta, [(after(nl, outer_parts), inner_low)])
-    outer_core = core_sum(*outer_parts)
+    los = [ctx_moved(piece, k) for k, piece in enumerate(los)]
+    keep, send = outer_parts
+    outer_core = core_sum(keep, after(send, los[1:2]))
+    keep, send = inner_parts
+    inner_parts = keep, after(send, los[3:4])
     dctx = after(dctx, [outer_core, *inner_parts])
     dqkv = back_call(dims, qkv, ctx, dctx.reshape(ctx.shape), e, linv)
-    lo_got = ctx_first(los)
-    own_lo = tp_moved(los[:1])
     inner_core = core_sum(*inner_parts)
-    outer_y = y_sum(outer_core)
-    first = after(first, [inner_core, outer_y, *lo_got, *own_lo])
+    outer_y, outer_raw = y_sum(outer_core)
+    even = range(2, C, 2)
+    early = [0] + list(range(1, C, 2))
+    early_lo = tp_moved([los[k] for k in early])
+    first = after(first, [inner_core, outer_y, *los[1:], *early_lo[1:]])
     ins = input_call(dqkv.reshape(C, R, 3 * D), qkv_w, first)
-    los, lo_raw = ctx_second(los[0], [after(got, [dqkv]) for got in lo_got])
-    outer_x = x_sum(outer_y)
-    inner_y = y_sum(after(inner_core, [outer_y]))
-    ag = after(ag, [*lo_raw, *ins])
-    qkv_parts = weight_call(dims, meta, [(x_all, dqkv), (ag, ctx)])
-    ig_got = ctx_first(ins)
-    far_lo = tp_moved(los[1:])
-    keep, send = qkv_parts
-    qkv_core = core_sum(keep, after(send, [outer_x, inner_y, *ig_got]))
-    ig, ig_raw = ctx_second(ins[0], ig_got)
-    outer_x = after(outer_x[0, 0], [qkv_core, *ig_raw])
+    late_lo = tp_moved([after(los[k], [dqkv]) for k in even])
+    outer_x, outer_raw = x_sum(outer_y)
+    inner_y, inner_raw = y_sum(inner_core)
+    ag = after(ag, ins)
+    keep, send = weight_call(dims, meta, [(x_all, dqkv), (ag, ctx)])
+    ig = [ctx_moved(piece, k) if k % 2 else piece for k, piece in enumerate(ins)]
+    send = after(send, [outer_raw, inner_raw] + ig[1::2] + late_lo[1:])
+    qkv_core = core_sum(keep, send)
+    for k in even:
+        ig[k] = ctx_moved(after(ins[k], ig[1::2]), k)
+    outer_x = after(outer_x[0, 0], [qkv_core])
     outer_part = ctx_scatter(outer_x)
-    qkv_y = after(y_sum(qkv_core), [outer_part, *ig_raw])
-    ig_both = tp_moved(after(tuple(ig[:2]), [outer_part]) + tuple(ig[2:]))
-    inner_x = after(x_sum(after(inner_y, [outer_part]))[0, 0], [qkv_y])
+    early_ig = tp_moved(after(tuple(ig[k] for k in early), [qkv_core]))
+    qkv_y, _ = y_sum(qkv_core)
+    inner_x, _ = x_sum(after(inner_y, [outer_part]))
+    outer_g = ctx_gather(after(outer_part, [qkv_y]), outer_x)
+    inner_x = after(inner_x[0, 0], [ig[k] for k in even])
     inner_part = ctx_scatter(inner_x)
-    outer_g = ctx_gather(after(outer_part, [qkv_y]), outer_x)
-    qkv_x = after(x_sum(qkv_y)[0, 0], [outer_g, inner_part])
-    own_lo, far_lo = (after(tuple(part), [qkv_core]) for part in (own_lo, far_lo))
-    layer_out = to_slots([([0], own_lo), (list(range(1, C)), far_lo)], BF)
-    input_grad = to_slots([(list(range(C)), after(tuple(ig_both), [qkv_x]))], F32)
+    qkv_x, _ = x_sum(qkv_y)
+    qkv_x = qkv_x[0, 0]
+    late_ig = tp_moved([after(ig[k], [qkv_x]) for k in even])
+    early_lo, late_lo = (after(tuple(part), [qkv_core]) for part in (early_lo, late_lo))
+    early_ig = after(tuple(early_ig), [qkv_x])
+    layer_out = to_slots([(early, early_lo), (list(even), late_lo)], BF)
+    input_grad = to_slots([(early, early_ig), (list(even), late_ig)], F32)
     inner_g = ctx_gather(inner_part, inner_x)
     qkv_g = ctx_gather(ctx_scatter(qkv_x), qkv_x)
 

time: 423 us -> 437 us (1.033)
  waiting for transfers between devices: 120 us -> 141 us
  other arithmetic: 26.8 us -> 20.2 us
  local copies, waits for them, and re-layouts: 42.1 us -> 36.4 us
  starting transfers between devices: 80.5 us -> 85.5 us
    ppermute x22, waiting for transfers between devices: 25.8 us -> 41.7 us  [swapped(): return lax.ppermute(array, axis, xor_pairs(lax.axis_size(axis), bit))]
    ppermute x34 -> x30, waiting for transfers between devices: 85.4 us -> 97.8 us  [ctx_moved(): return lax.ppermute(piece, 'ctx', xor_pairs(C, k)) if k else piece]
    slice x21 -> x0, local copies, waits for them, and re-layouts: 9.83 us -> none  [the longest x9 4.17 us: ctx_second(): return ([own, up[:R], jnp.concatenate(raw, axis=0), down[:R]], raw)]
    ppermute x3 -> x4, waiting for transfers between devices: 8.63 us -> 0.01 us  [tp_moved(): lax.ppermute(both, 'tp', xor_pairs(T, dt))]
    concatenate x11 -> x0, other arithmetic: 7.98 us -> none  [the longest x4 2.8 us: ctx_first(): down = jnp.concatenate([pieces[3], pieces[2][h:]], axis=0)]
    ppermute x34 -> x30, starting transfers between devices: 60.5 us -> 62.7 us  [ctx_moved(): return lax.ppermute(piece, 'ctx', xor_pairs(C, k)) if k else piece]
    unnamed x66 -> x77, local copies, waits for them, and re-layouts: 7.31 us -> 8.9 us
  transfers between devices with their start and end apart: 62 -> 59, of which waited for: 23 -> 25; matrix products, arithmetic and copies ran while one was open for 12% -> 9% of each run, Pallas kernels for 22% -> 24%
where the time goes in v5:
time: 437 us; the launch traced here: 436 us
  Pallas kernels  151 us (35%)
  waiting for transfers between devices  141 us (32%)
  starting transfers between devices  85.5 us (20%)
  local copies, waits for them, and re-layouts  36.4 us (8%)
  other arithmetic  20.2 us (5%)
    ppermute x30, waiting for transfers between devices, ctx_moved(): return lax.ppermute(piece, 'ctx', xor_pairs(C, k)) if k else piece  97.8 us
    ppermute x30, starting transfers between devices, ctx_moved(): return lax.ppermute(piece, 'ctx', xor_pairs(C, k)) if k else piece  62.7 us
    pallas_call x1, Pallas kernels, rows_call(): pl.pallas_call(functools.partial(rows_kernel, dims, FF), name='rows', gri...  46.7 us
    ppermute x22, waiting for transfers between devices, swapped(): return lax.ppermute(array, axis, xor_pairs(lax.axis_size(axis), bit))  41.7 us
    pallas_call x3, Pallas kernels, weight_call(): pl.pallas_call(functools.partial(weight_kernel, F, pers, sums is not None...  40.1 us
    pallas_call x1, Pallas kernels, front_call(): pl.pallas_call(functools.partial(front_kernel, dims), name='front', grid=...  29.9 us
    pallas_call x1, Pallas kernels, back_call(): pl.pallas_call(functools.partial(back_kernel, dims), name='back', grid=(n...  26.2 us
    ppermute x22, starting transfers between devices, swapped(): return lax.ppermute(array, axis, xor_pairs(lax.axis_size(axis), bit))  18.8 us
  transfers between devices with their start and end apart: 59, of which 25 were waited for; matrix products, arithmetic and copies ran while one was open for 9% of the time, Pallas kernels for 24%

profile of v5, /device:TPU:0, one launch (start us, length us, event | category | flops | bytes accessed | tf_op | source)
XLA Modules:
  0.0 435.6 jit_solution(15840269561020394618)
XLA Ops:
  8.4 3.0 collective-permute-start
  12.4 1.6 collective-permute-start.3
  14.0 2.3 constant_dynamic-slice_fusion.14
  16.3 1.6 collective-permute-start.1
  19.0 2.5 collective-permute-done.3
  21.6 5.0 %collective-permute-done.1.refs_1_ = bf16[256,768]{1,0:T(8,128)(2,1)S(1)} collective-permute-done((bf16[256,768]{1,0:T(8,128)(2,1)S(1)}, bf16[256,768]{1,0:T(8,128)(2,1)S(1)}, u32[]{:S(2)}, u32[]{:S(2)}) %collective-permute-start.1) | collective-permute-done | bytes 393248 | tf_op jit(solution)/shard_map/ppermute | solution.py:581
  27.5 2.7 collective-permute-start.5
  30.3 1.3 collective-permute-start.6
  31.6 23.8 %collective-permute-done.5.refs_2_ = bf16[256,768]{1,0:T(8,128)(2,1)S(1)} collective-permute-done((bf16[256,768]{1,0:T(8,128)(2,1)S(1)}, bf16[256,768]{1,0:T(8,128)(2,1)S(1)}, u32[]{:S(2)}, u32[]{:S(2)}) %collective-permute-start.5) | collective-permute-done | bytes 393248 | tf_op jit(solution)/shard_map/ppermute | solution.py:581
  55.5 1.6 collective-permute-start.8
  57.0 1.5 collective-permute-start.7
  59.1 9.9 %collective-permute-done.8 = bf16[1,192,1536]{2,1,0:T(8,128)(2,1)S(1)} collective-permute-done((bf16[1,192,1536]{2,1,0:T(8,128)(2,1)S(1)}, bf16[1,192,1536]{2,1,0:T(8,128)(2,1)S(1)}, u32[]{:S(2)}, u32[]{:S(2)}) %collective-permute-start.8) | collective-permute-done | bytes 589856 | tf_op jit(solution)/shard_map/ppermute | solution.py:603
  69.9 1.5 collective-permute-start.19
  73.5 10.1 %collective-permute-start.13 = (bf16[256,768]{1,0:T(8,128)(2,1)}, bf16[256,768]{1,0:T(8,128)(2,1)S(1)}, u32[]{:S(2)}, u32[]{:S(2)}) collective-permute-start(bf16[256,768]{1,0:T(8,128)(2,1)} %bitcast.14), channel_id=1, source_target_pairs={{0,2},{2,0},{4,6},{6,4},{1,3},{3,1},{5,7},{7,5},{8,10},{10,8},{12,... | collective-permute-start | bytes 1179656 | tf_op jit(solution)/shard_map/ppermute | solution.py:581
  83.5 2.0 collective-permute-start.14
  85.5 1.4 collective-permute-start.15
  87.5 29.9 %front.1 = (bf16[4,256,768]{2,1,0:T(8,128)(2,1)}, bf16[768,2304]{1,0:T(8,128)(2,1)}, bf16[4,2,128,2304]{3,2,1,0:T(8,128)(2,1)}, bf16[12,1024,512]{2,1,0:T(8,128)...) custom-call(s32[4]{0:T(128)} %pad_add_fusion.meta, bf16[256,768]{1,0:T(8,128)(2,1)} %bitcast.108, ...), custom_call_target="tpu_custom_call" | custom-call | flops 3623878656 | bytes 40000000 | tf_op jit(solution)/shard_map/front/pallas_call | solution.py:162
  119.3 1.8 collective-permute-done.20.refs_18_
  121.1 1.7 collective-permute-done.17.refs_14_
  127.2 46.7 %rows.1 = (bf16[256,768]{1,0:T(8,128)(2,1)}, bf16[256,768]{1,0:T(8,128)(2,1)}, bf16[256,768]{1,0:T(8,128)(2,1)}, bf16[256,768]{1,0:T(8,128)(2,1)}, f32[4,256,768...) custom-call(s32[4]{0:T(128)} %pad_add_fusion.meta, ...), custom_call_target="tpu_custom_call" | custom-call | flops 21743271936 | bytes 50000000 | tf_op jit(solution)/shard_map/rows/pallas_call | solution.py:344
  173.9 2.9 collective-permute-start.22
  176.8 12.8 %weight_grad.3 = (bf16[2,2,208,1536]{3,2,1,0:T(8,128)(2,1)}, bf16[2,2,208,1536]{3,2,1,0:T(8,128)(2,1)}) custom-call(s32[4]{0:T(128)} %pad_add_fusion.meta, bf16[1024,768]{1,0:T(8,128)(2,1)} %bitcast.128, bf16[1024,3072]{1,0:T(8,128)(2,1)} %bitcast.124, f32[16,768]{1,0:T(8,128)} %get-tuple-element.98.refs_2_), custom_call_target="tpu_custom_call" | custom-call | flops 4831838208 | bytes 12582912 | tf_op jit(solution)/shard_map/weight_grad/pallas_call | solution.py:523
  189.7 3.4 collective-permute-start.23
  193.1 13.2 %weight_grad.4 = (bf16[2,2,208,1536]{3,2,1,0:T(8,128)(2,1)}, bf16[2,2,208,1536]{3,2,1,0:T(8,128)(2,1)}) custom-call(s32[4]{0:T(128)} %pad_add_fusion.meta, bf16[1024,768]{1,0:T(8,128)(2,1)} %bitcast.127, bf16[1024,3072]{1,0:T(8,128)(2,1)} %bitcast.123), custom_call_target="tpu_custom_call" | custom-call | flops 4831838208 | bytes 12582912 | tf_op jit(solution)/shard_map/weight_grad/pallas_call | solution.py:523
  206.4 5.4 %collective-permute-start.28 = (bf16[256,768]{1,0:T(8,128)(2,1)S(1)}, bf16[256,768]{1,0:T(8,128)(2,1)}, u32[]{:S(2)}, u32[]{:S(2)}) collective-permute-start(bf16[256,768]{1,0:T(8,128)(2,1)S(1)} %copy-done.33), channel_id=1, source_target_pairs={{0,4},{2,6},{4,0},{6,2},{1,5},{3,7},{5,1},{7,3},{8,12},{10,14},{12... | collective-permute-start | bytes 1179656 | tf_op jit(solution)/shard_map/ppermute | solution.py:581
  214.7 2.4 add_convert_fusion.2
  217.1 1.5 copy-done
  220.8 26.2 %back.1 = bf16[4,2,128,2304]{3,2,1,0:T(8,128)(2,1)} custom-call(bf16[4,2,128,2304]{3,2,1,0:T(8,128)(2,1)} %get-tuple-element.94.qkv, bf16[4,2,128,768]{3,2,1,0:T(8,128)(2,1)} %get-tuple-element.86.ctx, bf16[4,2,128,768]{3,2,1,0:T(8,128)(2,1)} %bitcast.89, bf16[12,1024,512]{2,1,0:T(8,128)(2,1)} %get-tuple-element.109.e_ref, ...), custom_call_target="tpu_custom_call" | custom-call | flops 6442450944 | bytes 30000000 | tf_op jit(solution)/shard_map/back/pallas_call | solution.py:413
  248.0 3.2 add_convert_fusion.1
  252.4 1.4 collective-permute-start.30
  253.8 1.6 add_convert_fusion.5
  257.2 8.5 %input_grad.1 = (bf16[256,768]{1,0:T(8,128)(2,1)}, bf16[256,768]{1,0:T(8,128)(2,1)}, bf16[256,768]{1,0:T(8,128)(2,1)}, bf16[256,768]{1,0:T(8,128)(2,1)}) custom-call(bf16[4,256,2304]{2,1,0:T(8,128)(2,1)} %bitcast.85, bf16[768,2304]{1,0:T(8,128)(2,1)} %get-tuple-element.111.w, f32[4,256,768]{2,1,0:T(8,128)} %get-tuple-element.114.first), custom_call_target="tpu_custom_call" | custom-call | flops 3623878656 | bytes 15000000 | tf_op jit(solution)/shard_map/input_grad/pallas_call | solution.py:450
  265.8 1.5 collective-permute-start.32
  267.3 14.0 %weight_grad.5 = (bf16[2,2,208,1536]{3,2,1,0:T(8,128)(2,1)}, bf16[2,2,208,1536]{3,2,1,0:T(8,128)(2,1)}) custom-call(s32[4]{0:T(128)} %pad_add_fusion.meta, bf16[1024,768]{1,0:T(8,128)(2,1)} %bitcast.125, bf16[1024,768]{1,0:T(8,128)(2,1)} %bitcast.126, bf16[1024,2304]{1,0:T(8,128)(2,1)} %bitcast.86, bf16[1024,768]{1,0:T(8,128)(2,1)} %bitcast.88), custom_call_target="tpu_custom_call" | custom-call | flops 4831838208 | bytes 12582912 | tf_op jit(solution)/shard_map/weight_grad/pallas_call | solution.py:523
  282.1 2.5 collective-permute-done.31
  285.3 1.8 add_convert_fusion.3
  288.1 1.2 fusion
  290.5 2.4 add_convert_fusion
  295.3 2.3 collective-permute-start.48
  298.5 1.3 fusion.21
  302.5 16.5 %collective-permute-done.47 = bf16[208,384]{1,0:T(8,128)(2,1)S(1)} collective-permute-done((bf16[208,384]{1,0:T(8,128)(2,1)S(1)}, bf16[208,384]{1,0:T(8,128)(2,1)S(1)}, u32[]{:S(2)}, u32[]{:S(2)}) %collective-permute-start.47) | collective-permute-done | bytes 159776 | tf_op jit(solution)/shard_map/ppermute | solution.py:581
  320.6 1.3 fusion.20
  322.1 19.8 %collective-permute-done.52 = bf16[1,1,208,1536]{3,2,1,0:T(8,128)(2,1)S(1)} collective-permute-done((bf16[1,1,208,1536]{3,2,1,0:T(8,128)(2,1)S(1)}, bf16[1,1,208,1536]{3,2,1,0:T(8,128)(2,1)S(1)}, u32[]{:S(2)}, u32[]{:S(2)}) %collective-permute-start.52) | collective-permute-done | bytes 639008 | tf_op jit(solution)/shard_map/ppermute | solution.py:603
  342.1 2.5 collective-permute-start.53
  344.7 1.3 collective-permute-start.54
  345.9 1.4 collective-permute-start.55
  349.6 8.4 %collective-permute-done.54 = bf16[208,384]{1,0:T(8,128)(2,1)S(1)} collective-permute-done((bf16[208,384]{1,0:T(8,128)(2,1)S(1)}, bf16[208,384]{1,0:T(8,128)(2,1)S(1)}, u32[]{:S(2)}, u32[]{:S(2)}) %collective-permute-start.54) | collective-permute-done | bytes 159776 | tf_op jit(solution)/shard_map/ppermute | solution.py:581
  358.2 2.3 collective-permute-start.56
  360.5 1.3 collective-permute-start.57
  361.9 1.5 collective-permute-start.58
  363.4 2.2 collective-permute-done.56
  365.6 9.0 %collective-permute-done.57 = bf16[208,384]{1,0:T(8,128)(2,1)S(1)} collective-permute-done((bf16[208,384]{1,0:T(8,128)(2,1)S(1)}, bf16[208,384]{1,0:T(8,128)(2,1)S(1)}, u32[]{:S(2)}, u32[]{:S(2)}) %collective-permute-start.57) | collective-permute-done | bytes 159776 | tf_op jit(solution)/shard_map/ppermute | solution.py:581
  375.2 2.3 collective-permute-start.49
  380.4 1.5 collective-permute-start.51
  383.2 9.6 %collective-permute-done.50 = bf16[208,384]{1,0:T(8,128)(2,1)S(1)} collective-permute-done((bf16[208,384]{1,0:T(8,128)(2,1)S(1)}, bf16[208,384]{1,0:T(8,128)(2,1)S(1)}, u32[]{:S(2)}, u32[]{:S(2)}) %collective-permute-start.50) | collective-permute-done | bytes 159776 | tf_op jit(solution)/shard_map/ppermute | solution.py:581
  394.8 2.1 collective-permute-done.37
  397.8 2.4 collective-permute-start.41
  400.2 1.4 collective-permute-start.42
  403.9 8.5 %collective-permute-done.41 = bf16[208,384]{1,0:T(8,128)(2,1)S(1)} collective-permute-done((bf16[208,384]{1,0:T(8,128)(2,1)S(1)}, bf16[208,384]{1,0:T(8,128)(2,1)S(1)}, u32[]{:S(2)}, u32[]{:S(2)}) %collective-permute-start.41) | collective-permute-done | bytes 159776 | tf_op jit(solution)/shard_map/ppermute | solution.py:581
  412.6 2.3 collective-permute-start.43
  414.9 1.4 collective-permute-start.44
  416.4 1.5 collective-permute-start.45
  417.8 2.2 collective-permute-done.43
  420.1 9.3 %collective-permute-done.44 = bf16[208,384]{1,0:T(8,128)(2,1)S(1)} collective-permute-done((bf16[208,384]{1,0:T(8,128)(2,1)S(1)}, bf16[208,384]{1,0:T(8,128)(2,1)S(1)}, u32[]{:S(2)}, u32[]{:S(2)}) %collective-permute-start.44) | collective-permute-done | bytes 159776 | tf_op jit(solution)/shard_map/ppermute | solution.py:581
  (248 shorter events, 60.6 us)
Async XLA Ops:
  8.4 10.6 %collective-permute-start = (bf16[1,208,768]{2,1,0:T(8,128)(2,1)S(1)}, bf16[1,208,768]{2,1,0:T(8,128)(2,1)S(1)}, u32[]{:S(2)}, u32[]{:S(2)}) collective-permute-start(bf16[1,208,768]{2,1,0:T(8,128)(2,1)S(1)} %maximum_bitcast_fusion), channel_id=1, source_target_pairs={{0,1},{1,0},{2,3},{3,2},{4,5},{5,4},{6,7},{7,6},{8,9},{9,8},{10,11... | collective-permute-start | bytes 958472 | tf_op jit(solution)/shard_map/ppermute | solution.py:603
  12.4 9.1 %collective-permute-start.3 = (bf16[1,208,768]{2,1,0:T(8,128)(2,1)S(1)}, bf16[1,208,768]{2,1,0:T(8,128)(2,1)S(1)}, u32[]{:S(2)}, u32[]{:S(2)}) collective-permute-start(bf16[1,208,768]{2,1,0:T(8,128)(2,1)S(1)} %maximum_bitcast_fusion.1), channel_id=1, source_target_pairs={{0,16},{8,24},{16,0},{24,8},{1,17},{9,25},{17,1},{25,9},{2,18},{10... | collective-permute-start | bytes 958472 | tf_op jit(solution)/shard_map/ppermute | solution.py:603
  16.3 10.3 %collective-permute-start.1 = (bf16[256,768]{1,0:T(8,128)(2,1)S(1)}, bf16[256,768]{1,0:T(8,128)(2,1)S(1)}, u32[]{:S(2)}, u32[]{:S(2)}) collective-permute-start(bf16[256,768]{1,0:T(8,128)(2,1)S(1)} %bitcast.114), channel_id=1, source_target_pairs={{0,2},{2,0},{4,6},{6,4},{1,3},{3,1},{5,7},{7,5},{8,10},{10,8},{12,... | collective-permute-start | bytes 1179656 | tf_op jit(solution)/shard_map/ppermute | solution.py:581
  19.0 52.5 %copy-start.11 = (bf16[2,208,768]{2,1,0:T(8,128)(2,1)}, bf16[2,208,768]{2,1,0:T(8,128)(2,1)S(1)}, u32[]{:S(2)}) copy-start(bf16[2,208,768]{2,1,0:T(8,128)(2,1)S(1)} %pad_maximum_fusion.2.refs_4_) | copy-start | bytes 1916932
  21.6 51.9 %copy-start.12 = (bf16[2,208,768]{2,1,0:T(8,128)(2,1)}, bf16[2,208,768]{2,1,0:T(8,128)(2,1)S(1)}, u32[]{:S(2)}) copy-start(bf16[2,208,768]{2,1,0:T(8,128)(2,1)S(1)} %pad_maximum_fusion.3.refs_8_) | copy-start | bytes 1916932
  21.6 50.6 %copy-start.35 = (s32[16]{0:T(128)S(1)}, s32[16]{0:T(128)}, u32[]{:S(2)}) copy-start(s32[16]{0:T(128)} %param.19) | copy-start | bytes 196
  21.6 50.7 %copy-start.10 = (bf16[16,128,768]{2,1,0:T(8,128)(2,1)S(1)}, bf16[16,128,768]{2,1,0:T(8,128)(2,1)}, u32[]{:S(2)}) copy-start(bf16[16,128,768]{2,1,0:T(8,128)(2,1)} %param.35) | copy-start | bytes 9437188
  26.6 28.8 %collective-permute-start.2 = (bf16[2,208,768]{2,1,0:T(8,128)(2,1)S(1)}, bf16[2,208,768]{2,1,0:T(8,128)(2,1)S(1)}, u32[]{:S(2)}, u32[]{:S(2)}) collective-permute-start(bf16[2,208,768]{2,1,0:T(8,128)(2,1)S(1)} %pad_maximum_fusion.2.refs_4_), channel_id=1, source_target_pairs={{0,16},{8,24},{16,0},{24,8},{1,17},{9,25},{17,1},{25,9},{2,18},{10... | collective-permute-start | bytes 1916936 | tf_op jit(solution)/shard_map/ppermute | solution.py:603
  27.1 28.3 %collective-permute-start.4 = (bf16[2,208,768]{2,1,0:T(8,128)(2,1)S(1)}, bf16[2,208,768]{2,1,0:T(8,128)(2,1)S(1)}, u32[]{:S(2)}, u32[]{:S(2)}) collective-permute-start(bf16[2,208,768]{2,1,0:T(8,128)(2,1)S(1)} %pad_maximum_fusion.3.refs_8_), channel_id=1, source_target_pairs={{0,1},{1,0},{2,3},{3,2},{4,5},{5,4},{6,7},{7,6},{8,9},{9,8},{10,11... | collective-permute-start | bytes 1916936 | tf_op jit(solution)/shard_map/ppermute | solution.py:603
  27.5 27.9 %collective-permute-start.5 = (bf16[256,768]{1,0:T(8,128)(2,1)S(1)}, bf16[256,768]{1,0:T(8,128)(2,1)S(1)}, u32[]{:S(2)}, u32[]{:S(2)}) collective-permute-start(bf16[256,768]{1,0:T(8,128)(2,1)S(1)} %bitcast.111), channel_id=1, source_target_pairs={{0,4},{2,6},{4,0},{6,2},{1,5},{3,7},{5,1},{7,3},{8,12},{10,14},{12... | collective-permute-start | bytes 1179656 | tf_op jit(solution)/shard_map/ppermute | solution.py:581
  30.3 25.2 %collective-permute-start.6 = (bf16[256,768]{1,0:T(8,128)(2,1)S(1)}, bf16[256,768]{1,0:T(8,128)(2,1)S(1)}, u32[]{:S(2)}, u32[]{:S(2)}) collective-permute-start(bf16[256,768]{1,0:T(8,128)(2,1)S(1)} %bitcast.110), channel_id=1, source_target_pairs={{0,6},{2,4},{4,2},{6,0},{1,7},{3,5},{5,3},{7,1},{8,14},{10,12},{12... | collective-permute-start | bytes 1179656 | tf_op jit(solution)/shard_map/ppermute | solution.py:581
  55.5 13.5 %collective-permute-start.8 = (bf16[1,192,1536]{2,1,0:T(8,128)(2,1)S(1)}, bf16[1,192,1536]{2,1,0:T(8,128)(2,1)S(1)}, u32[]{:S(2)}, u32[]{:S(2)}) collective-permute-start(bf16[1,192,1536]{2,1,0:T(8,128)(2,1)S(1)} %bitcast.102), channel_id=1, source_target_pairs={{0,16},{8,24},{16,0},{24,8},{1,17},{9,25},{17,1},{25,9},{2,18},{10... | collective-permute-start | bytes 1769480 | tf_op jit(solution)/shard_map/ppermute | solution.py:603
  57.0 12.8 %collective-permute-start.7 = (bf16[1,192,1536]{2,1,0:T(8,128)(2,1)S(1)}, bf16[1,192,1536]{2,1,0:T(8,128)(2,1)S(1)}, u32[]{:S(2)}, u32[]{:S(2)}) collective-permute-start(bf16[1,192,1536]{2,1,0:T(8,128)(2,1)S(1)} %bitcast.104), channel_id=1, source_target_pairs={{0,1},{1,0},{2,3},{3,2},{4,5},{5,4},{6,7},{7,6},{8,9},{9,8},{10,11... | collective-permute-start | bytes 1769480 | tf_op jit(solution)/shard_map/ppermute | solution.py:603
  58.5 13.0 %collective-permute-start.11 = (bf16[2,208,768]{2,1,0:T(8,128)(2,1)S(1)}, bf16[2,208,768]{2,1,0:T(8,128)(2,1)S(1)}, u32[]{:S(2)}, u32[]{:S(2)}) collective-permute-start(bf16[2,208,768]{2,1,0:T(8,128)(2,1)S(1)} %pad_maximum_fusion.3.refs_8_), channel_id=1, source_target_pairs={{0,8},{8,0},{16,24},{24,16},{1,9},{9,1},{17,25},{25,17},{2,10},{10... | collective-permute-start | bytes 1916936 | tf_op jit(solution)/shard_map/ppermute | solution.py:603
  58.5 13.7 %collective-permute-start.9 = (bf16[2,208,768]{2,1,0:T(8,128)(2,1)S(1)}, bf16[2,208,768]{2,1,0:T(8,128)(2,1)S(1)}, u32[]{:S(2)}, u32[]{:S(2)}) collective-permute-start(bf16[2,208,768]{2,1,0:T(8,128)(2,1)S(1)} %pad_maximum_fusion.2.refs_4_), channel_id=1, source_target_pairs={{0,8},{8,0},{16,24},{24,16},{1,9},{9,1},{17,25},{25,17},{2,10},{10... | collective-permute-start | bytes 1916936 | tf_op jit(solution)/shard_map/ppermute | solution.py:603
  59.1 13.2 %collective-permute-start.10 = (bf16[2,208,768]{2,1,0:T(8,128)(2,1)S(1)}, bf16[2,208,768]{2,1,0:T(8,128)(2,1)S(1)}, u32[]{:S(2)}, u32[]{:S(2)}) collective-permute-start(bf16[2,208,768]{2,1,0:T(8,128)(2,1)S(1)} %collective-permute-done.2.refs_5_), channel_id=1, source_target_pairs={{0,8},{8,0},{16,24},{24,16},{1,9},{9,1},{17,25},{25,17},{2,10},{10... | collective-permute-start | bytes 1916936 | tf_op jit(solution)/shard_map/ppermute | solution.py:603
  68.9 3.4 collective-permute-start.12
  69.1 49.1 %copy-start.8 = (bf16[2,192,1536]{2,1,0:T(8,128)(2,1)}, bf16[2,192,1536]{2,1,0:T(8,128)(2,1)S(1)}, u32[]{:S(2)}) copy-start(bf16[2,192,1536]{2,1,0:T(8,128)(2,1)S(1)} %pad_maximum_fusion.1.refs_16_) | copy-start | bytes 3538948
  69.9 48.9 %collective-permute-start.19 = (bf16[2,192,1536]{2,1,0:T(8,128)(2,1)S(1)}, bf16[2,192,1536]{2,1,0:T(8,128)(2,1)}, u32[]{:S(2)}, u32[]{:S(2)}) collective-permute-start(bf16[2,192,1536]{2,1,0:T(8,128)(2,1)S(1)} %pad_maximum_fusion.1.refs_16_), channel_id=1, source_target_pairs={{0,1},{1,0},{2,3},{3,2},{4,5},{5,4},{6,7},{7,6},{8,9},{9,8},{10,11... | collective-permute-start | bytes 3538952 | tf_op jit(solution)/shard_map/ppermute | solution.py:603
  71.5 47.3 %collective-permute-start.16 = (bf16[2,192,1536]{2,1,0:T(8,128)(2,1)S(1)}, bf16[2,192,1536]{2,1,0:T(8,128)(2,1)}, u32[]{:S(2)}, u32[]{:S(2)}) collective-permute-start(bf16[2,192,1536]{2,1,0:T(8,128)(2,1)S(1)} %pad_maximum_fusion.refs_12_), channel_id=1, source_target_pairs={{0,16},{8,24},{16,0},{24,8},{1,17},{9,25},{17,1},{25,9},{2,18},{10... | collective-permute-start | bytes 3538952 | tf_op jit(solution)/shard_map/ppermute | solution.py:603
  73.5 44.0 %collective-permute-start.13 = (bf16[256,768]{1,0:T(8,128)(2,1)}, bf16[256,768]{1,0:T(8,128)(2,1)S(1)}, u32[]{:S(2)}, u32[]{:S(2)}) collective-permute-start(bf16[256,768]{1,0:T(8,128)(2,1)} %bitcast.14), channel_id=1, source_target_pairs={{0,2},{2,0},{4,6},{6,4},{1,3},{3,1},{5,7},{7,5},{8,10},{10,8},{12,... | collective-permute-start | bytes 1179656 | tf_op jit(solution)/shard_map/ppermute | solution.py:581
  83.5 33.9 %collective-permute-start.14 = (bf16[256,768]{1,0:T(8,128)(2,1)S(1)}, bf16[256,768]{1,0:T(8,128)(2,1)S(1)}, u32[]{:S(2)}, u32[]{:S(2)}) collective-permute-start(bf16[256,768]{1,0:T(8,128)(2,1)S(1)} %bitcast.113), channel_id=1, source_target_pairs={{0,4},{2,6},{4,0},{6,2},{1,5},{3,7},{5,1},{7,3},{8,12},{10,14},{12... | collective-permute-start | bytes 1179656 | tf_op jit(solution)/shard_map/ppermute | solution.py:581
  85.5 31.9 %collective-permute-start.15 = (bf16[256,768]{1,0:T(8,128)(2,1)S(1)}, bf16[256,768]{1,0:T(8,128)(2,1)}, u32[]{:S(2)}, u32[]{:S(2)}) collective-permute-start(bf16[256,768]{1,0:T(8,128)(2,1)S(1)} %bitcast.112), channel_id=1, source_target_pairs={{0,6},{2,4},{4,2},{6,0},{1,7},{3,5},{5,3},{7,1},{8,14},{10,12},{12... | collective-permute-start | bytes 1179656 | tf_op jit(solution)/shard_map/ppermute | solution.py:581
  118.3 2.8 collective-permute-start.20
  118.3 4.5 %collective-permute-start.17 = (bf16[2,192,1536]{2,1,0:T(8,128)(2,1)S(1)}, bf16[2,192,1536]{2,1,0:T(8,128)(2,1)S(1)}, u32[]{:S(2)}, u32[]{:S(2)}) collective-permute-start(bf16[2,192,1536]{2,1,0:T(8,128)(2,1)S(1)} %pad_maximum_fusion.refs_12_), channel_id=1, source_target_pairs={{0,8},{8,0},{16,24},{24,16},{1,9},{9,1},{17,25},{25,17},{2,10},{10... | collective-permute-start | bytes 3538952 | tf_op jit(solution)/shard_map/ppermute | solution.py:603
  118.8 5.7 %collective-permute-start.21 = (bf16[2,192,1536]{2,1,0:T(8,128)(2,1)}, bf16[2,192,1536]{2,1,0:T(8,128)(2,1)S(1)}, u32[]{:S(2)}, u32[]{:S(2)}) collective-permute-start(bf16[2,192,1536]{2,1,0:T(8,128)(2,1)} %collective-permute-done.19.refs_17_), channel_id=1, source_target_pairs={{0,8},{8,0},{16,24},{24,16},{1,9},{9,1},{17,25},{25,17},{2,10},{10... | collective-permute-start | bytes 3538952 | tf_op jit(solution)/shard_map/ppermute | solution.py:603
  118.9 7.3 %collective-permute-start.18 = (bf16[2,192,1536]{2,1,0:T(8,128)(2,1)}, bf16[2,192,1536]{2,1,0:T(8,128)(2,1)S(1)}, u32[]{:S(2)}, u32[]{:S(2)}) collective-permute-start(bf16[2,192,1536]{2,1,0:T(8,128)(2,1)} %collective-permute-done.16.refs_13_), channel_id=1, source_target_pairs={{0,8},{8,0},{16,24},{24,16},{1,9},{9,1},{17,25},{25,17},{2,10},{10... | collective-permute-start | bytes 3538952 | tf_op jit(solution)/shard_map/ppermute | solution.py:603
  173.9 15.8 %collective-permute-start.22 = (bf16[256,768]{1,0:T(8,128)(2,1)}, bf16[256,768]{1,0:T(8,128)(2,1)S(1)}, u32[]{:S(2)}, u32[]{:S(2)}) collective-permute-start(bf16[256,768]{1,0:T(8,128)(2,1)} %get-tuple-element.91), channel_id=1, source_target_pairs={{0,2},{2,0},{4,6},{6,4},{1,3},{3,1},{5,7},{7,5},{8,10},{10,8},{12,... | collective-permute-start | bytes 1179656 | tf_op jit(solution)/shard_map/ppermute | solution.py:581
  189.6 25.0 %collective-permute-start.25 = (bf16[2,2,208,1536]{3,2,1,0:T(8,128)(2,1)}, bf16[2,2,208,1536]{3,2,1,0:T(8,128)(2,1)}, u32[]{:S(2)}, u32[]{:S(2)}) collective-permute-start(bf16[2,2,208,1536]{3,2,1,0:T(8,128)(2,1)} %get-tuple-element.101), channel_id=1, source_target_pairs={{0,8},{8,0},{16,24},{24,16},{1,9},{9,1},{17,25},{25,17},{2,10},{10... | collective-permute-start | bytes 7667720 | tf_op jit(solution)/shard_map/ppermute | solution.py:662
  189.7 16.6 %collective-permute-start.23 = (bf16[256,768]{1,0:T(8,128)(2,1)}, bf16[256,768]{1,0:T(8,128)(2,1)S(1)}, u32[]{:S(2)}, u32[]{:S(2)}) collective-permute-start(bf16[256,768]{1,0:T(8,128)(2,1)} %get-tuple-element.92), channel_id=1, source_target_pairs={{0,6},{2,4},{4,2},{6,0},{1,7},{3,5},{5,3},{7,1},{8,14},{10,12},{12... | collective-permute-start | bytes 1179656 | tf_op jit(solution)/shard_map/ppermute | solution.py:581
  206.3 41.8 %collective-permute-start.26 = (bf16[2,2,208,1536]{3,2,1,0:T(8,128)(2,1)}, bf16[2,2,208,1536]{3,2,1,0:T(8,128)(2,1)}, u32[]{:S(2)}, u32[]{:S(2)}) collective-permute-start(bf16[2,2,208,1536]{3,2,1,0:T(8,128)(2,1)} %get-tuple-element.107), channel_id=1, source_target_pairs={{0,8},{8,0},{16,24},{24,16},{1,9},{9,1},{17,25},{25,17},{2,10},{10... | collective-permute-start | bytes 7667720 | tf_op jit(solution)/shard_map/ppermute | solution.py:662
  206.4 40.6 %collective-permute-start.28 = (bf16[256,768]{1,0:T(8,128)(2,1)S(1)}, bf16[256,768]{1,0:T(8,128)(2,1)}, u32[]{:S(2)}, u32[]{:S(2)}) collective-permute-start(bf16[256,768]{1,0:T(8,128)(2,1)S(1)} %copy-done.33), channel_id=1, source_target_pairs={{0,4},{2,6},{4,0},{6,2},{1,5},{3,7},{5,1},{7,3},{8,12},{10,14},{12... | collective-permute-start | bytes 1179656 | tf_op jit(solution)/shard_map/ppermute | solution.py:581
  214.1 43.1 %collective-permute-start.24 = (bf16[768,768]{1,0:T(8,128)(2,1)}, bf16[768,768]{1,0:T(8,128)(2,1)}, u32[]{:S(2)}, u32[]{:S(2)}) collective-permute-start(bf16[768,768]{1,0:T(8,128)(2,1)} %constant_dynamic-update-slice_fusion), channel_id=1, source_target_pairs={{0,1},{1,0},{2,3},{3,2},{4,5},{5,4},{6,7},{7,6},{8,9},{9,8},{10,11... | collective-permute-start | bytes 3538952 | tf_op jit(solution)/shard_map/ppermute | solution.py:585
  219.7 34.1 %collective-permute-start.27 = (bf16[1,2,208,1536]{3,2,1,0:T(8,128)(2,1)}, bf16[1,2,208,1536]{3,2,1,0:T(8,128)(2,1)}, u32[]{:S(2)}, u32[]{:S(2)}) collective-permute-start(bf16[1,2,208,1536]{3,2,1,0:T(8,128)(2,1)} %split.49), channel_id=1, source_target_pairs={{0,16},{8,24},{16,0},{24,8},{1,17},{9,25},{17,1},{25,9},{2,18},{10... | collective-permute-start | bytes 3833864 | tf_op jit(solution)/shard_map/ppermute | solution.py:603
  247.0 34.4 %collective-permute-start.33 = (bf16[256,768]{1,0:T(8,128)(2,1)}, bf16[256,768]{1,0:T(8,128)(2,1)}, u32[]{:S(2)}, u32[]{:S(2)}) collective-permute-start(bf16[256,768]{1,0:T(8,128)(2,1)} %collective-permute-done.28), channel_id=1, source_target_pairs={{0,1},{1,0},{2,3},{3,2},{4,5},{5,4},{6,7},{7,6},{8,9},{9,8},{10,11... | collective-permute-start | bytes 1179656 | tf_op jit(solution)/shard_map/ppermute | solution.py:585
  252.4 29.7 %collective-permute-start.30 = (bf16[1,2,208,1536]{3,2,1,0:T(8,128)(2,1)}, bf16[1,2,208,1536]{3,2,1,0:T(8,128)(2,1)}, u32[]{:S(2)}, u32[]{:S(2)}) collective-permute-start(bf16[1,2,208,1536]{3,2,1,0:T(8,128)(2,1)} %split.51), channel_id=1, source_target_pairs={{0,16},{8,24},{16,0},{24,8},{1,17},{9,25},{17,1},{25,9},{2,18},{10... | collective-permute-start | bytes 3833864 | tf_op jit(solution)/shard_map/ppermute | solution.py:603
  256.5 28.1 %collective-permute-start.29 = (bf16[1,1,208,1536]{3,2,1,0:T(8,128)(2,1)S(1)}, bf16[1,1,208,1536]{3,2,1,0:T(8,128)(2,1)}, u32[]{:S(2)}, u32[]{:S(2)}) collective-permute-start(bf16[1,1,208,1536]{3,2,1,0:T(8,128)(2,1)S(1)} %split.50), channel_id=1, source_target_pairs={{0,1},{1,0},{2,3},{3,2},{4,5},{5,4},{6,7},{7,6},{8,9},{9,8},{10,11... | collective-permute-start | bytes 1916936 | tf_op jit(solution)/shard_map/ppermute | solution.py:603
  265.8 18.8 %collective-permute-start.31 = (bf16[256,768]{1,0:T(8,128)(2,1)}, bf16[256,768]{1,0:T(8,128)(2,1)S(1)}, u32[]{:S(2)}, u32[]{:S(2)}) collective-permute-start(bf16[256,768]{1,0:T(8,128)(2,1)} %get-tuple-element.116), channel_id=1, source_target_pairs={{0,2},{2,0},{4,6},{6,4},{1,3},{3,1},{5,7},{7,5},{8,10},{10,8},{12,... | collective-permute-start | bytes 1179656 | tf_op jit(solution)/shard_map/ppermute | solution.py:581
  265.8 18.8 %collective-permute-start.32 = (bf16[256,768]{1,0:T(8,128)(2,1)}, bf16[256,768]{1,0:T(8,128)(2,1)}, u32[]{:S(2)}, u32[]{:S(2)}) collective-permute-start(bf16[256,768]{1,0:T(8,128)(2,1)} %get-tuple-element.118), channel_id=1, source_target_pairs={{0,6},{2,4},{4,2},{6,0},{1,7},{3,5},{5,3},{7,1},{8,14},{10,12},{12... | collective-permute-start | bytes 1179656 | tf_op jit(solution)/shard_map/ppermute | solution.py:581
  285.3 5.2 %collective-permute-start.34 = (bf16[2,2,208,1536]{3,2,1,0:T(8,128)(2,1)}, bf16[2,2,208,1536]{3,2,1,0:T(8,128)(2,1)}, u32[]{:S(2)}, u32[]{:S(2)}) collective-permute-start(bf16[2,2,208,1536]{3,2,1,0:T(8,128)(2,1)} %get-tuple-element.123), channel_id=1, source_target_pairs={{0,8},{8,0},{16,24},{24,16},{1,9},{9,1},{17,25},{25,17},{2,10},{10... | collective-permute-start | bytes 7667720 | tf_op jit(solution)/shard_map/ppermute | solution.py:662
  287.1 55.0 %collective-permute-start.38 = (bf16[256,768]{1,0:T(8,128)(2,1)}, bf16[256,768]{1,0:T(8,128)(2,1)S(1)}, u32[]{:S(2)}, u32[]{:S(2)}) collective-permute-start(bf16[256,768]{1,0:T(8,128)(2,1)} %get-tuple-element.133), channel_id=1, source_target_pairs={{0,4},{2,6},{4,0},{6,2},{1,5},{3,7},{5,1},{7,3},{8,12},{10,14},{12... | collective-permute-start | bytes 1179656 | tf_op jit(solution)/shard_map/ppermute | solution.py:581
  293.1 8.2 %collective-permute-start.46 = (bf16[208,384]{1,0:T(8,128)(2,1)S(1)}, bf16[208,384]{1,0:T(8,128)(2,1)S(1)}, u32[]{:S(2)}, u32[]{:S(2)}) collective-permute-start(bf16[208,384]{1,0:T(8,128)(2,1)S(1)} %get-tuple-element.168), channel_id=1, source_target_pairs={{0,2},{2,0},{4,6},{6,4},{1,3},{3,1},{5,7},{7,5},{8,10},{10,8},{12,... | collective-permute-start | bytes 479240 | tf_op jit(solution)/shard_map/ppermute | solution.py:581
  294.3 24.7 %collective-permute-start.47 = (bf16[208,384]{1,0:T(8,128)(2,1)S(1)}, bf16[208,384]{1,0:T(8,128)(2,1)S(1)}, u32[]{:S(2)}, u32[]{:S(2)}) collective-permute-start(bf16[208,384]{1,0:T(8,128)(2,1)S(1)} %get-tuple-element.170), channel_id=1, source_target_pairs={{0,4},{2,6},{4,0},{6,2},{1,5},{3,7},{5,1},{7,3},{8,12},{10,14},{12... | collective-permute-start | bytes 479240 | tf_op jit(solution)/shard_map/ppermute | solution.py:581
  295.3 23.7 %collective-permute-start.48 = (bf16[208,384]{1,0:T(8,128)(2,1)S(1)}, bf16[208,384]{1,0:T(8,128)(2,1)S(1)}, u32[]{:S(2)}, u32[]{:S(2)}) collective-permute-start(bf16[208,384]{1,0:T(8,128)(2,1)S(1)} %get-tuple-element.169), channel_id=1, source_target_pairs={{0,6},{2,4},{4,2},{6,0},{1,7},{3,5},{5,3},{7,1},{8,14},{10,12},{12... | collective-permute-start | bytes 479240 | tf_op jit(solution)/shard_map/ppermute | solution.py:581
  297.6 77.3 %collective-permute-start.36 = (bf16[1,2,208,1536]{3,2,1,0:T(8,128)(2,1)S(1)}, bf16[1,2,208,1536]{3,2,1,0:T(8,128)(2,1)S(1)}, u32[]{:S(2)}, u32[]{:S(2)}) collective-permute-start(bf16[1,2,208,1536]{3,2,1,0:T(8,128)(2,1)S(1)} %split.53), channel_id=1, source_target_pairs={{0,16},{8,24},{16,0},{24,8},{1,17},{9,25},{17,1},{25,9},{2,18},{10... | collective-permute-start | bytes 3833864 | tf_op jit(solution)/shard_map/ppermute | solution.py:603
  301.3 100.4 %collective-permute-start.35 = (bf16[768,768]{1,0:T(8,128)(2,1)S(1)}, bf16[768,768]{1,0:T(8,128)(2,1)S(1)}, u32[]{:S(2)}, u32[]{:S(2)}) collective-permute-start(bf16[768,768]{1,0:T(8,128)(2,1)S(1)} %constant_dynamic-update-slice_fusion.3), channel_id=1, source_target_pairs={{0,1},{1,0},{2,3},{3,2},{4,5},{5,4},{6,7},{7,6},{8,9},{9,8},{10,11... | collective-permute-start | bytes 3538952 | tf_op jit(solution)/shard_map/ppermute | solution.py:585
  319.1 22.8 %collective-permute-start.52 = (bf16[1,1,208,1536]{3,2,1,0:T(8,128)(2,1)S(1)}, bf16[1,1,208,1536]{3,2,1,0:T(8,128)(2,1)S(1)}, u32[]{:S(2)}, u32[]{:S(2)}) collective-permute-start(bf16[1,1,208,1536]{3,2,1,0:T(8,128)(2,1)S(1)} %split.47), channel_id=1, source_target_pairs={{0,1},{1,0},{2,3},{3,2},{4,5},{5,4},{6,7},{7,6},{8,9},{9,8},{10,11... | collective-permute-start | bytes 1916936 | tf_op jit(solution)/shard_map/ppermute | solution.py:603
  342.1 7.5 %collective-permute-start.53 = (bf16[208,384]{1,0:T(8,128)(2,1)S(1)}, bf16[208,384]{1,0:T(8,128)(2,1)S(1)}, u32[]{:S(2)}, u32[]{:S(2)}) collective-permute-start(bf16[208,384]{1,0:T(8,128)(2,1)S(1)} %get-tuple-element.165), channel_id=1, source_target_pairs={{0,2},{2,0},{4,6},{6,4},{1,3},{3,1},{5,7},{7,5},{8,10},{10,8},{12,... | collective-permute-start | bytes 479240 | tf_op jit(solution)/shard_map/ppermute | solution.py:581
  344.7 13.4 %collective-permute-start.54 = (bf16[208,384]{1,0:T(8,128)(2,1)S(1)}, bf16[208,384]{1,0:T(8,128)(2,1)S(1)}, u32[]{:S(2)}, u32[]{:S(2)}) collective-permute-start(bf16[208,384]{1,0:T(8,128)(2,1)S(1)} %get-tuple-element.167), channel_id=1, source_target_pairs={{0,4},{2,6},{4,0},{6,2},{1,5},{3,7},{5,1},{7,3},{8,12},{10,14},{12... | collective-permute-start | bytes 479240 | tf_op jit(solution)/shard_map/ppermute | solution.py:581
  345.9 12.1 %collective-permute-start.55 = (bf16[208,384]{1,0:T(8,128)(2,1)S(1)}, bf16[208,384]{1,0:T(8,128)(2,1)S(1)}, u32[]{:S(2)}, u32[]{:S(2)}) collective-permute-start(bf16[208,384]{1,0:T(8,128)(2,1)S(1)} %get-tuple-element.166), channel_id=1, source_target_pairs={{0,6},{2,4},{4,2},{6,0},{1,7},{3,5},{5,3},{7,1},{8,14},{10,12},{12... | collective-permute-start | bytes 479240 | tf_op jit(solution)/shard_map/ppermute | solution.py:581
  358.2 7.4 %collective-permute-start.56 = (bf16[208,384]{1,0:T(8,128)(2,1)S(1)}, bf16[208,384]{1,0:T(8,128)(2,1)S(1)}, u32[]{:S(2)}, u32[]{:S(2)}) collective-permute-start(bf16[208,384]{1,0:T(8,128)(2,1)S(1)} %get-tuple-element.142), channel_id=1, source_target_pairs={{0,2},{2,0},{4,6},{6,4},{1,3},{3,1},{5,7},{7,5},{8,10},{10,8},{12,... | collective-permute-start | bytes 479240 | tf_op jit(solution)/shard_map/ppermute | solution.py:581
  360.5 14.1 %collective-permute-start.57 = (bf16[208,384]{1,0:T(8,128)(2,1)S(1)}, bf16[208,384]{1,0:T(8,128)(2,1)S(1)}, u32[]{:S(2)}, u32[]{:S(2)}) collective-permute-start(bf16[208,384]{1,0:T(8,128)(2,1)S(1)} %get-tuple-element.142), channel_id=1, source_target_pairs={{0,4},{2,6},{4,0},{6,2},{1,5},{3,7},{5,1},{7,3},{8,12},{10,14},{12... | collective-permute-start | bytes 479240 | tf_op jit(solution)/shard_map/ppermute | solution.py:581
  361.9 12.8 %collective-permute-start.58 = (bf16[208,384]{1,0:T(8,128)(2,1)S(1)}, bf16[208,384]{1,0:T(8,128)(2,1)S(1)}, u32[]{:S(2)}, u32[]{:S(2)}) collective-permute-start(bf16[208,384]{1,0:T(8,128)(2,1)S(1)} %get-tuple-element.142), channel_id=1, source_target_pairs={{0,6},{2,4},{4,2},{6,0},{1,7},{3,5},{5,3},{7,1},{8,14},{10,12},{12... | collective-permute-start | bytes 479240 | tf_op jit(solution)/shard_map/ppermute | solution.py:581
  375.2 8.0 %collective-permute-start.49 = (bf16[208,384]{1,0:T(8,128)(2,1)S(1)}, bf16[208,384]{1,0:T(8,128)(2,1)S(1)}, u32[]{:S(2)}, u32[]{:S(2)}) collective-permute-start(bf16[208,384]{1,0:T(8,128)(2,1)S(1)} %add_convert_fusion.10), channel_id=1, source_target_pairs={{0,2},{2,0},{4,6},{6,4},{1,3},{3,1},{5,7},{7,5},{8,10},{10,8},{12,... | collective-permute-start | bytes 479240 | tf_op jit(solution)/shard_map/ppermute | solution.py:581
  379.3 13.5 %collective-permute-start.50 = (bf16[208,384]{1,0:T(8,128)(2,1)S(1)}, bf16[208,384]{1,0:T(8,128)(2,1)S(1)}, u32[]{:S(2)}, u32[]{:S(2)}) collective-permute-start(bf16[208,384]{1,0:T(8,128)(2,1)S(1)} %add_convert_fusion.10), channel_id=1, source_target_pairs={{0,4},{2,6},{4,0},{6,2},{1,5},{3,7},{5,1},{7,3},{8,12},{10,14},{12... | collective-permute-start | bytes 479240 | tf_op jit(solution)/shard_map/ppermute | solution.py:581
  380.4 12.5 %collective-permute-start.51 = (bf16[208,384]{1,0:T(8,128)(2,1)S(1)}, bf16[208,384]{1,0:T(8,128)(2,1)S(1)}, u32[]{:S(2)}, u32[]{:S(2)}) collective-permute-start(bf16[208,384]{1,0:T(8,128)(2,1)S(1)} %add_convert_fusion.10), channel_id=1, source_target_pairs={{0,6},{2,4},{4,2},{6,0},{1,7},{3,5},{5,3},{7,1},{8,14},{10,12},{12... | collective-permute-start | bytes 479240 | tf_op jit(solution)/shard_map/ppermute | solution.py:581
  382.0 15.0 %collective-permute-start.37 = (bf16[1,1,208,1536]{3,2,1,0:T(8,128)(2,1)S(1)}, bf16[1,1,208,1536]{3,2,1,0:T(8,128)(2,1)S(1)}, u32[]{:S(2)}, u32[]{:S(2)}) collective-permute-start(bf16[1,1,208,1536]{3,2,1,0:T(8,128)(2,1)S(1)} %split.55), channel_id=1, source_target_pairs={{0,1},{1,0},{2,3},{3,2},{4,5},{5,4},{6,7},{7,6},{8,9},{9,8},{10,11... | collective-permute-start | bytes 1916936 | tf_op jit(solution)/shard_map/ppermute | solution.py:603
  397.2 6.8 %collective-permute-start.40 = (bf16[208,384]{1,0:T(8,128)(2,1)S(1)}, bf16[208,384]{1,0:T(8,128)(2,1)S(1)}, u32[]{:S(2)}, u32[]{:S(2)}) collective-permute-start(bf16[208,384]{1,0:T(8,128)(2,1)S(1)} %get-tuple-element.174), channel_id=1, source_target_pairs={{0,2},{2,0},{4,6},{6,4},{1,3},{3,1},{5,7},{7,5},{8,10},{10,8},{12,... | collective-permute-start | bytes 479240 | tf_op jit(solution)/shard_map/ppermute | solution.py:581
  397.8 14.6 %collective-permute-start.41 = (bf16[208,384]{1,0:T(8,128)(2,1)S(1)}, bf16[208,384]{1,0:T(8,128)(2,1)S(1)}, u32[]{:S(2)}, u32[]{:S(2)}) collective-permute-start(bf16[208,384]{1,0:T(8,128)(2,1)S(1)} %get-tuple-element.176), channel_id=1, source_target_pairs={{0,4},{2,6},{4,0},{6,2},{1,5},{3,7},{5,1},{7,3},{8,12},{10,14},{12... | collective-permute-start | bytes 479240 | tf_op jit(solution)/shard_map/ppermute | solution.py:581
  400.2 12.3 %collective-permute-start.42 = (bf16[208,384]{1,0:T(8,128)(2,1)S(1)}, bf16[208,384]{1,0:T(8,128)(2,1)S(1)}, u32[]{:S(2)}, u32[]{:S(2)}) collective-permute-start(bf16[208,384]{1,0:T(8,128)(2,1)S(1)} %get-tuple-element.175), channel_id=1, source_target_pairs={{0,6},{2,4},{4,2},{6,0},{1,7},{3,5},{5,3},{7,1},{8,14},{10,12},{12... | collective-permute-start | bytes 479240 | tf_op jit(solution)/shard_map/ppermute | solution.py:581
  401.9 30.9 %collective-permute-start.39 = (bf16[256,768]{1,0:T(8,128)(2,1)S(1)}, bf16[256,768]{1,0:T(8,128)(2,1)S(1)}, u32[]{:S(2)}, u32[]{:S(2)}) collective-permute-start(bf16[256,768]{1,0:T(8,128)(2,1)S(1)} %collective-permute-done.38), channel_id=1, source_target_pairs={{0,1},{1,0},{2,3},{3,2},{4,5},{5,4},{6,7},{7,6},{8,9},{9,8},{10,11... | collective-permute-start | bytes 1179656 | tf_op jit(solution)/shard_map/ppermute | solution.py:585
  412.6 7.5 %collective-permute-start.43 = (bf16[208,384]{1,0:T(8,128)(2,1)S(1)}, bf16[208,384]{1,0:T(8,128)(2,1)S(1)}, u32[]{:S(2)}, u32[]{:S(2)}) collective-permute-start(bf16[208,384]{1,0:T(8,128)(2,1)S(1)} %get-tuple-element.144), channel_id=1, source_target_pairs={{0,2},{2,0},{4,6},{6,4},{1,3},{3,1},{5,7},{7,5},{8,10},{10,8},{12,... | collective-permute-start | bytes 479240 | tf_op jit(solution)/shard_map/ppermute | solution.py:581
  414.9 14.5 %collective-permute-start.44 = (bf16[208,384]{1,0:T(8,128)(2,1)S(1)}, bf16[208,384]{1,0:T(8,128)(2,1)S(1)}, u32[]{:S(2)}, u32[]{:S(2)}) collective-permute-start(bf16[208,384]{1,0:T(8,128)(2,1)S(1)} %get-tuple-element.144), channel_id=1, source_target_pairs={{0,4},{2,6},{4,0},{6,2},{1,5},{3,7},{5,1},{7,3},{8,12},{10,14},{12... | collective-permute-start | bytes 479240 | tf_op jit(solution)/shard_map/ppermute | solution.py:581
  416.4 13.0 %collective-permute-start.45 = (bf16[208,384]{1,0:T(8,128)(2,1)S(1)}, bf16[208,384]{1,0:T(8,128)(2,1)S(1)}, u32[]{:S(2)}, u32[]{:S(2)}) collective-permute-start(bf16[208,384]{1,0:T(8,128)(2,1)S(1)} %get-tuple-element.144), channel_id=1, source_target_pairs={{0,6},{2,4},{4,2},{6,0},{1,7},{3,5},{5,3},{7,1},{8,14},{10,12},{12... | collective-permute-start | bytes 479240 | tf_op jit(solution)/shard_map/ppermute | solution.py:581
  (31 other events, 422.6 us)

commit v6 on v5

--- a/solution.py
+++ b/solution.py
@@ -623,9 +623,11 @@
 
     x_pieces = sequence_pieces(tokens_in)
     near_x = ctx_moved(x_pieces[1], 1)
-    x_pieces = x_pieces[:1] + [near_x] + [
-        ctx_moved(after(x_pieces[k], [near_x]), k) for k in range(2, C)
-    ]
+    before = [near_x]
+    x_pieces[1] = near_x
+    for k in [*range(3, C, 2), *range(2, C, 2)]:
+        x_pieces[k] = ctx_moved(after(x_pieces[k], before), k)
+        before = [x_pieces[k]]
     vectors = jnp.stack([output_bias, attn_gain, attn_shift, outer_bias, ffn_gain, ffn_shift])
     small = [
         spread(query_bias, half), spread(value_bias, half), spread(inner_bias, fhalf),
@@ -639,11 +641,11 @@
     high = chip_start(jnp.concatenate([high, small[:, D:]], axis=0), True)
     lows = both_cores(low, chip_end(after(low, [near_x]), False))
     highs = both_cores(high, chip_end(after(high, [near_x]), True))
-    halfway = [lows[1], highs[1], *x_pieces[2:]]
+    halfway = [lows[1], highs[1], *x_pieces[3::2]]
     inner = chip_start(after(inner_weight, halfway), False)
     outer = chip_start(after(outer_weight.T, halfway), True)
-    inner_got = chip_end(inner, False)
-    outer_got = chip_end(outer, True)
+    inner_got = chip_end(after(inner, x_pieces[2::2]), False)
+    outer_got = chip_end(after(outer, x_pieces[2::2]), True)
     cot_pieces = sequence_pieces(after(cotangent, [*x_pieces[1:], *lows, *highs]))
     cot_pieces = [ctx_moved(piece, k) for k, piece in enumerate(cot_pieces)]
     lengths = lax.dynamic_slice_in_dim(seq_lengths, (c * T + t) * ns, ns, 0)
@@ -717,23 +719,24 @@
     qkv_core = core_sum(keep, send)
     for k in even:
         ig[k] = ctx_moved(after(ins[k], ig[1::2]), k)
-    outer_x = after(outer_x[0, 0], [qkv_core])
+    outer_x = after(outer_x[0, 0], [qkv_core] + [ig[k] for k in even])
     outer_part = ctx_scatter(outer_x)
     early_ig = tp_moved(after(tuple(ig[k] for k in early), [qkv_core]))
     qkv_y, _ = y_sum(qkv_core)
     inner_x, _ = x_sum(after(inner_y, [outer_part]))
-    outer_g = ctx_gather(after(outer_part, [qkv_y]), outer_x)
-    inner_x = after(inner_x[0, 0], [ig[k] for k in even])
+    outer_g = ctx_gather(outer_part, outer_x)
+    inner_x = after(inner_x[0, 0], [qkv_y] + [ig[k] for k in even])
     inner_part = ctx_scatter(inner_x)
     qkv_x, _ = x_sum(qkv_y)
-    qkv_x = qkv_x[0, 0]
+    qkv_x = after(qkv_x[0, 0], [inner_part])
+    qkv_part = ctx_scatter(qkv_x)
     late_ig = tp_moved([after(ig[k], [qkv_x]) for k in even])
     early_lo, late_lo = (after(tuple(part), [qkv_core]) for part in (early_lo, late_lo))
     early_ig = after(tuple(early_ig), [qkv_x])
     layer_out = to_slots([(early, early_lo), (list(even), late_lo)], BF)
     input_grad = to_slots([(early, early_ig), (list(even), late_ig)], F32)
     inner_g = ctx_gather(inner_part, inner_x)
-    qkv_g = ctx_gather(ctx_scatter(qkv_x), qkv_x)
+    qkv_g = ctx_gather(qkv_part, qkv_x)
 
     def own(row, shape):
         whole = row.reshape(shape[0], shape[1] * F)

time: 437 us -> 414 us (0.947)
  waiting for transfers between devices: 141 us -> 124 us
  starting transfers between devices: 85.5 us -> 78.5 us
    ppermute x30, waiting for transfers between devices: 97.8 us -> 89 us  [ctx_moved(): return lax.ppermute(piece, 'ctx', xor_pairs(C, k)) if k else piece]
    ppermute x22, waiting for transfers between devices: 41.7 us -> 33.9 us  [swapped(): return lax.ppermute(array, axis, xor_pairs(lax.axis_size(axis), bit))]
    ppermute x30, starting transfers between devices: 62.7 us -> 58.2 us  [ctx_moved(): return lax.ppermute(piece, 'ctx', xor_pairs(C, k)) if k else piece]
    unnamed x77 -> x76, local copies, waits for them, and re-layouts: 8.9 us -> 9.74 us
    convert_element_type x7 -> x6, other arithmetic: 11.9 us -> 11.7 us  [added(): return (a.astype(F32) + b.astype(F32)).astype(BF)]
  transfers between devices with their start and end apart: 59 -> 59, of which waited for: 25 -> 25; matrix products, arithmetic and copies ran while one was open for 9% -> 9% of each run, Pallas kernels for 24% -> 25%
where the time goes in v6:
time: 414 us; the launch traced here: 413 us
  Pallas kernels  151 us (36%)
  waiting for transfers between devices  124 us (30%)
  starting transfers between devices  78.5 us (19%)
  local copies, waits for them, and re-layouts  37.2 us (9%)
  other arithmetic  20.2 us (5%)
    ppermute x30, waiting for transfers between devices, ctx_moved(): return lax.ppermute(piece, 'ctx', xor_pairs(C, k)) if k else piece  89 us
    ppermute x30, starting transfers between devices, ctx_moved(): return lax.ppermute(piece, 'ctx', xor_pairs(C, k)) if k else piece  58.2 us
    pallas_call x1, Pallas kernels, rows_call(): pl.pallas_call(functools.partial(rows_kernel, dims, FF), name='rows', gri...  46.7 us
    pallas_call x3, Pallas kernels, weight_call(): pl.pallas_call(functools.partial(weight_kernel, F, pers, sums is not None...  40 us
    ppermute x22, waiting for transfers between devices, swapped(): return lax.ppermute(array, axis, xor_pairs(lax.axis_size(axis), bit))  33.9 us
    pallas_call x1, Pallas kernels, front_call(): pl.pallas_call(functools.partial(front_kernel, dims), name='front', grid=...  29.9 us
    pallas_call x1, Pallas kernels, back_call(): pl.pallas_call(functools.partial(back_kernel, dims), name='back', grid=(n...  26.2 us
    ppermute x22, starting transfers between devices, swapped(): return lax.ppermute(array, axis, xor_pairs(lax.axis_size(axis), bit))  16.2 us
  transfers between devices with their start and end apart: 59, of which 25 were waited for; matrix products, arithmetic and copies ran while one was open for 9% of the time, Pallas kernels for 25%

profile of v6, /device:TPU:0, one launch (start us, length us, event | category | flops | bytes accessed | tf_op | source)
XLA Modules:
  0.0 412.5 jit_solution(7758603964829196043)
XLA Ops:
  8.4 3.0 collective-permute-start
  12.4 1.6 collective-permute-start.3
  14.0 2.3 constant_dynamic-slice_fusion.17
  16.3 1.6 collective-permute-start.1
  19.0 2.5 collective-permute-done.3
  21.6 5.0 %collective-permute-done.1.refs_1_ = bf16[256,768]{1,0:T(8,128)(2,1)S(1)} collective-permute-done((bf16[256,768]{1,0:T(8,128)(2,1)S(1)}, bf16[256,768]{1,0:T(8,128)(2,1)S(1)}, u32[]{:S(2)}, u32[]{:S(2)}) %collective-permute-start.1) | collective-permute-done | bytes 393248 | tf_op jit(solution)/shard_map/ppermute | solution.py:581
  27.5 3.8 collective-permute-start.5
  31.3 7.3 %collective-permute-done.5.refs_3_ = bf16[256,768]{1,0:T(8,128)(2,1)S(1)} collective-permute-done((bf16[256,768]{1,0:T(8,128)(2,1)S(1)}, bf16[256,768]{1,0:T(8,128)(2,1)S(1)}, u32[]{:S(2)}, u32[]{:S(2)}) %collective-permute-start.5) | collective-permute-done | bytes 393248 | tf_op jit(solution)/shard_map/ppermute | solution.py:581
  38.6 2.7 collective-permute-done.2.refs_5_
  41.6 1.5 collective-permute-start.7
  43.6 7.1 %collective-permute-start.8 = (bf16[256,768]{1,0:T(8,128)(2,1)S(1)}, bf16[256,768]{1,0:T(8,128)(2,1)S(1)}, u32[]{:S(2)}, u32[]{:S(2)}) collective-permute-start(bf16[256,768]{1,0:T(8,128)(2,1)S(1)} %bitcast.100), channel_id=1, source_target_pairs={{0,4},{2,6},{4,0},{6,2},{1,5},{3,7},{5,1},{7,3},{8,12},{10,14},{12... | collective-permute-start | bytes 1179656 | tf_op jit(solution)/shard_map/ppermute | solution.py:581
  51.2 3.0 collective-permute-done.7
  54.3 11.6 %collective-permute-done.8.refs_2_ = bf16[256,768]{1,0:T(8,128)(2,1)S(1)} collective-permute-done((bf16[256,768]{1,0:T(8,128)(2,1)S(1)}, bf16[256,768]{1,0:T(8,128)(2,1)S(1)}, u32[]{:S(2)}, u32[]{:S(2)}) %collective-permute-start.8) | collective-permute-done | bytes 393248 | tf_op jit(solution)/shard_map/ppermute | solution.py:581
  69.2 2.9 collective-permute-start.14
  72.1 1.5 collective-permute-start.15
  74.2 29.9 %front.1 = (bf16[4,256,768]{2,1,0:T(8,128)(2,1)}, bf16[768,2304]{1,0:T(8,128)(2,1)}, bf16[4,2,128,2304]{3,2,1,0:T(8,128)(2,1)}, bf16[12,1024,512]{2,1,0:T(8,128)...) custom-call(s32[4]{0:T(128)} %pad_add_fusion.meta, bf16[256,768]{1,0:T(8,128)(2,1)} %bitcast.98, ...), custom_call_target="tpu_custom_call" | custom-call | flops 3623878656 | bytes 40000000 | tf_op jit(solution)/shard_map/front/pallas_call | solution.py:162
  106.0 1.8 collective-permute-done.20.refs_18_
  107.8 1.7 collective-permute-done.17.refs_14_
  113.9 46.7 %rows.1 = (bf16[256,768]{1,0:T(8,128)(2,1)}, bf16[256,768]{1,0:T(8,128)(2,1)}, bf16[256,768]{1,0:T(8,128)(2,1)}, bf16[256,768]{1,0:T(8,128)(2,1)}, f32[4,256,768...) custom-call(s32[4]{0:T(128)} %pad_add_fusion.meta, ...), custom_call_target="tpu_custom_call" | custom-call | flops 21743271936 | bytes 50000000 | tf_op jit(solution)/shard_map/rows/pallas_call | solution.py:344
  160.5 2.4 collective-permute-start.22
  162.9 12.8 %weight_grad.3 = (bf16[2,2,208,1536]{3,2,1,0:T(8,128)(2,1)}, bf16[2,2,208,1536]{3,2,1,0:T(8,128)(2,1)}) custom-call(s32[4]{0:T(128)} %pad_add_fusion.meta, bf16[1024,768]{1,0:T(8,128)(2,1)} %bitcast.118, bf16[1024,3072]{1,0:T(8,128)(2,1)} %bitcast.114, f32[16,768]{1,0:T(8,128)} %get-tuple-element.102.refs_2_), custom_call_target="tpu_custom_call" | custom-call | flops 4831838208 | bytes 12582912 | tf_op jit(solution)/shard_map/weight_grad/pallas_call | solution.py:523
  175.7 2.5 collective-permute-start.23
  178.2 13.2 %weight_grad.4 = (bf16[2,2,208,1536]{3,2,1,0:T(8,128)(2,1)}, bf16[2,2,208,1536]{3,2,1,0:T(8,128)(2,1)}) custom-call(s32[4]{0:T(128)} %pad_add_fusion.meta, bf16[1024,768]{1,0:T(8,128)(2,1)} %bitcast.117, bf16[1024,3072]{1,0:T(8,128)(2,1)} %bitcast.113), custom_call_target="tpu_custom_call" | custom-call | flops 4831838208 | bytes 12582912 | tf_op jit(solution)/shard_map/weight_grad/pallas_call | solution.py:523
  191.5 5.3 %collective-permute-start.28 = (bf16[256,768]{1,0:T(8,128)(2,1)S(1)}, bf16[256,768]{1,0:T(8,128)(2,1)}, u32[]{:S(2)}, u32[]{:S(2)}) collective-permute-start(bf16[256,768]{1,0:T(8,128)(2,1)S(1)} %copy-done.32), channel_id=1, source_target_pairs={{0,4},{2,6},{4,0},{6,2},{1,5},{3,7},{5,1},{7,3},{8,12},{10,14},{12... | collective-permute-start | bytes 1179656 | tf_op jit(solution)/shard_map/ppermute | solution.py:581
  200.4 2.4 add_convert_fusion.2
  202.8 1.5 copy-done
  205.4 1.5 collective-permute-start.27
  206.9 26.2 %back.1 = bf16[4,2,128,2304]{3,2,1,0:T(8,128)(2,1)} custom-call(bf16[4,2,128,2304]{3,2,1,0:T(8,128)(2,1)} %get-tuple-element.98.qkv, bf16[4,2,128,768]{3,2,1,0:T(8,128)(2,1)} %get-tuple-element.88.ctx, bf16[4,2,128,768]{3,2,1,0:T(8,128)(2,1)} %bitcast.79, bf16[12,1024,512]{2,1,0:T(8,128)(2,1)} %get-tuple-element.113.e_ref, ...), custom_call_target="tpu_custom_call" | custom-call | flops 6442450944 | bytes 30000000 | tf_op jit(solution)/shard_map/back/pallas_call | solution.py:413
  233.7 3.2 add_convert_fusion.1
  239.1 1.6 add_convert_fusion.5
  241.8 1.6 collective-permute-start.29
  243.3 8.5 %input_grad.1 = (bf16[256,768]{1,0:T(8,128)(2,1)}, bf16[256,768]{1,0:T(8,128)(2,1)}, bf16[256,768]{1,0:T(8,128)(2,1)}, bf16[256,768]{1,0:T(8,128)(2,1)}) custom-call(bf16[4,256,2304]{2,1,0:T(8,128)(2,1)} %bitcast.75, bf16[768,2304]{1,0:T(8,128)(2,1)} %get-tuple-element.115.w, f32[4,256,768]{2,1,0:T(8,128)} %get-tuple-element.118.first), custom_call_target="tpu_custom_call" | custom-call | flops 3623878656 | bytes 15000000 | tf_op jit(solution)/shard_map/input_grad/pallas_call | solution.py:450
  252.0 1.5 collective-permute-start.32
  253.4 14.0 %weight_grad.5 = (bf16[2,2,208,1536]{3,2,1,0:T(8,128)(2,1)}, bf16[2,2,208,1536]{3,2,1,0:T(8,128)(2,1)}) custom-call(s32[4]{0:T(128)} %pad_add_fusion.meta, bf16[1024,768]{1,0:T(8,128)(2,1)} %bitcast.115, bf16[1024,768]{1,0:T(8,128)(2,1)} %bitcast.116, bf16[1024,2304]{1,0:T(8,128)(2,1)} %bitcast.76, bf16[1024,768]{1,0:T(8,128)(2,1)} %bitcast.78), custom_call_target="tpu_custom_call" | custom-call | flops 4831838208 | bytes 12582912 | tf_op jit(solution)/shard_map/weight_grad/pallas_call | solution.py:523
  267.8 3.0 collective-permute-done.31
  271.5 1.8 add_convert_fusion.3
  273.2 1.2 collective-permute-start.38
  274.4 1.2 fusion.1
  276.6 2.4 add_convert_fusion
  279.2 15.2 %collective-permute-done.38 = bf16[256,768]{1,0:T(8,128)(2,1)S(1)} collective-permute-done((bf16[256,768]{1,0:T(8,128)(2,1)}, bf16[256,768]{1,0:T(8,128)(2,1)S(1)}, u32[]{:S(2)}, u32[]{:S(2)}) %collective-permute-start.38) | collective-permute-done | bytes 393248 | tf_op jit(solution)/shard_map/ppermute | solution.py:581
  294.5 2.1 collective-permute-start.40
  296.6 2.3 collective-permute-start.41
  301.4 1.3 fusion.18
  302.7 1.3 fusion.17
  304.5 4.7 %collective-permute-done.40 = bf16[208,384]{1,0:T(8,128)(2,1)S(1)} collective-permute-done((bf16[208,384]{1,0:T(8,128)(2,1)S(1)}, bf16[208,384]{1,0:T(8,128)(2,1)S(1)}, u32[]{:S(2)}, u32[]{:S(2)}) %collective-permute-start.40) | collective-permute-done | bytes 159776 | tf_op jit(solution)/shard_map/ppermute | solution.py:581
  312.1 2.9 collective-permute-start.53
  315.2 4.3 %collective-permute-done.53 = bf16[208,384]{1,0:T(8,128)(2,1)S(1)} collective-permute-done((bf16[208,384]{1,0:T(8,128)(2,1)S(1)}, bf16[208,384]{1,0:T(8,128)(2,1)S(1)}, u32[]{:S(2)}, u32[]{:S(2)}) %collective-permute-start.53) | collective-permute-done | bytes 159776 | tf_op jit(solution)/shard_map/ppermute | solution.py:581
  319.4 2.2 collective-permute-start.55
  321.7 19.2 %collective-permute-done.42 = bf16[1,1,208,1536]{3,2,1,0:T(8,128)(2,1)S(1)} collective-permute-done((bf16[1,1,208,1536]{3,2,1,0:T(8,128)(2,1)S(1)}, bf16[1,1,208,1536]{3,2,1,0:T(8,128)(2,1)S(1)}, u32[]{:S(2)}, u32[]{:S(2)}) %collective-permute-start.42) | collective-permute-done | bytes 639008 | tf_op jit(solution)/shard_map/ppermute | solution.py:603
  341.5 2.1 collective-permute-start.44
  343.6 2.3 collective-permute-start.45
  346.1 2.6 collective-permute-done.43
  348.8 6.0 %collective-permute-done.44 = bf16[208,384]{1,0:T(8,128)(2,1)S(1)} collective-permute-done((bf16[208,384]{1,0:T(8,128)(2,1)S(1)}, bf16[208,384]{1,0:T(8,128)(2,1)S(1)}, u32[]{:S(2)}, u32[]{:S(2)}) %collective-permute-start.44) | collective-permute-done | bytes 159776 | tf_op jit(solution)/shard_map/ppermute | solution.py:581
  354.9 2.3 collective-permute-start.56
  359.7 2.3 collective-permute-start.58
  362.1 9.5 %collective-permute-done.57 = bf16[208,384]{1,0:T(8,128)(2,1)S(1)} collective-permute-done((bf16[208,384]{1,0:T(8,128)(2,1)S(1)}, bf16[208,384]{1,0:T(8,128)(2,1)S(1)}, u32[]{:S(2)}, u32[]{:S(2)}) %collective-permute-start.57) | collective-permute-done | bytes 159776 | tf_op jit(solution)/shard_map/ppermute | solution.py:581
  374.0 2.4 collective-permute-start.47
  376.9 1.9 collective-permute-start.49
  379.0 1.6 collective-permute-start.46
  381.5 8.6 %collective-permute-done.48 = bf16[208,384]{1,0:T(8,128)(2,1)S(1)} collective-permute-done((bf16[208,384]{1,0:T(8,128)(2,1)S(1)}, bf16[208,384]{1,0:T(8,128)(2,1)S(1)}, u32[]{:S(2)}, u32[]{:S(2)}) %collective-permute-start.48) | collective-permute-done | bytes 159776 | tf_op jit(solution)/shard_map/ppermute | solution.py:581
  390.2 2.3 collective-permute-start.50
  393.5 1.6 collective-permute-start.52
  395.1 2.1 collective-permute-done.50
  397.2 9.1 %collective-permute-done.51 = bf16[208,384]{1,0:T(8,128)(2,1)S(1)} collective-permute-done((bf16[208,384]{1,0:T(8,128)(2,1)S(1)}, bf16[208,384]{1,0:T(8,128)(2,1)S(1)}, u32[]{:S(2)}, u32[]{:S(2)}) %collective-permute-start.51) | collective-permute-done | bytes 159776 | tf_op jit(solution)/shard_map/ppermute | solution.py:581
  (246 shorter events, 53.6 us)
Async XLA Ops:
  8.4 10.6 %collective-permute-start = (bf16[1,208,768]{2,1,0:T(8,128)(2,1)S(1)}, bf16[1,208,768]{2,1,0:T(8,128)(2,1)S(1)}, u32[]{:S(2)}, u32[]{:S(2)}) collective-permute-start(bf16[1,208,768]{2,1,0:T(8,128)(2,1)S(1)} %maximum_bitcast_fusion), channel_id=1, source_target_pairs={{0,1},{1,0},{2,3},{3,2},{4,5},{5,4},{6,7},{7,6},{8,9},{9,8},{10,11... | collective-permute-start | bytes 958472 | tf_op jit(solution)/shard_map/ppermute | solution.py:603
  12.4 9.1 %collective-permute-start.3 = (bf16[1,208,768]{2,1,0:T(8,128)(2,1)S(1)}, bf16[1,208,768]{2,1,0:T(8,128)(2,1)S(1)}, u32[]{:S(2)}, u32[]{:S(2)}) collective-permute-start(bf16[1,208,768]{2,1,0:T(8,128)(2,1)S(1)} %maximum_bitcast_fusion.1), channel_id=1, source_target_pairs={{0,16},{8,24},{16,0},{24,8},{1,17},{9,25},{17,1},{25,9},{2,18},{10... | collective-permute-start | bytes 958472 | tf_op jit(solution)/shard_map/ppermute | solution.py:603
  16.3 10.3 %collective-permute-start.1 = (bf16[256,768]{1,0:T(8,128)(2,1)S(1)}, bf16[256,768]{1,0:T(8,128)(2,1)S(1)}, u32[]{:S(2)}, u32[]{:S(2)}) collective-permute-start(bf16[256,768]{1,0:T(8,128)(2,1)S(1)} %bitcast.104), channel_id=1, source_target_pairs={{0,2},{2,0},{4,6},{6,4},{1,3},{3,1},{5,7},{7,5},{8,10},{10,8},{12,... | collective-permute-start | bytes 1179656 | tf_op jit(solution)/shard_map/ppermute | solution.py:581
  19.0 48.3 %copy-start.11 = (bf16[2,208,768]{2,1,0:T(8,128)(2,1)}, bf16[2,208,768]{2,1,0:T(8,128)(2,1)S(1)}, u32[]{:S(2)}) copy-start(bf16[2,208,768]{2,1,0:T(8,128)(2,1)S(1)} %pad_maximum_fusion.2.refs_4_) | copy-start | bytes 1916932
  21.6 47.6 %copy-start.12 = (bf16[2,208,768]{2,1,0:T(8,128)(2,1)}, bf16[2,208,768]{2,1,0:T(8,128)(2,1)S(1)}, u32[]{:S(2)}) copy-start(bf16[2,208,768]{2,1,0:T(8,128)(2,1)S(1)} %pad_maximum_fusion.3.refs_8_) | copy-start | bytes 1916932
  21.6 46.4 %copy-start.35 = (s32[16]{0:T(128)S(1)}, s32[16]{0:T(128)}, u32[]{:S(2)}) copy-start(s32[16]{0:T(128)} %param.19) | copy-start | bytes 196
  21.6 46.5 %copy-start.10 = (bf16[16,128,768]{2,1,0:T(8,128)(2,1)S(1)}, bf16[16,128,768]{2,1,0:T(8,128)(2,1)}, u32[]{:S(2)}) copy-start(bf16[16,128,768]{2,1,0:T(8,128)(2,1)} %param.35) | copy-start | bytes 9437188
  26.6 14.7 %collective-permute-start.2 = (bf16[2,208,768]{2,1,0:T(8,128)(2,1)S(1)}, bf16[2,208,768]{2,1,0:T(8,128)(2,1)S(1)}, u32[]{:S(2)}, u32[]{:S(2)}) collective-permute-start(bf16[2,208,768]{2,1,0:T(8,128)(2,1)S(1)} %pad_maximum_fusion.2.refs_4_), channel_id=1, source_target_pairs={{0,16},{8,24},{16,0},{24,8},{1,17},{9,25},{17,1},{25,9},{2,18},{10... | collective-permute-start | bytes 1916936 | tf_op jit(solution)/shard_map/ppermute | solution.py:603
  27.1 14.4 %collective-permute-start.4 = (bf16[2,208,768]{2,1,0:T(8,128)(2,1)S(1)}, bf16[2,208,768]{2,1,0:T(8,128)(2,1)S(1)}, u32[]{:S(2)}, u32[]{:S(2)}) collective-permute-start(bf16[2,208,768]{2,1,0:T(8,128)(2,1)S(1)} %pad_maximum_fusion.3.refs_8_), channel_id=1, source_target_pairs={{0,1},{1,0},{2,3},{3,2},{4,5},{5,4},{6,7},{7,6},{8,9},{9,8},{10,11... | collective-permute-start | bytes 1916936 | tf_op jit(solution)/shard_map/ppermute | solution.py:603
  27.5 11.1 %collective-permute-start.5 = (bf16[256,768]{1,0:T(8,128)(2,1)S(1)}, bf16[256,768]{1,0:T(8,128)(2,1)S(1)}, u32[]{:S(2)}, u32[]{:S(2)}) collective-permute-start(bf16[256,768]{1,0:T(8,128)(2,1)S(1)} %bitcast.102), channel_id=1, source_target_pairs={{0,6},{2,4},{4,2},{6,0},{1,7},{3,5},{5,3},{7,1},{8,14},{10,12},{12... | collective-permute-start | bytes 1179656 | tf_op jit(solution)/shard_map/ppermute | solution.py:581
  41.6 12.6 %collective-permute-start.7 = (bf16[1,192,1536]{2,1,0:T(8,128)(2,1)S(1)}, bf16[1,192,1536]{2,1,0:T(8,128)(2,1)S(1)}, u32[]{:S(2)}, u32[]{:S(2)}) collective-permute-start(bf16[1,192,1536]{2,1,0:T(8,128)(2,1)S(1)} %bitcast.92), channel_id=1, source_target_pairs={{0,16},{8,24},{16,0},{24,8},{1,17},{9,25},{17,1},{25,9},{2,18},{10... | collective-permute-start | bytes 1769480 | tf_op jit(solution)/shard_map/ppermute | solution.py:603
  43.1 22.8 %collective-permute-start.6 = (bf16[1,192,1536]{2,1,0:T(8,128)(2,1)S(1)}, bf16[1,192,1536]{2,1,0:T(8,128)(2,1)S(1)}, u32[]{:S(2)}, u32[]{:S(2)}) collective-permute-start(bf16[1,192,1536]{2,1,0:T(8,128)(2,1)S(1)} %bitcast.94), channel_id=1, source_target_pairs={{0,1},{1,0},{2,3},{3,2},{4,5},{5,4},{6,7},{7,6},{8,9},{9,8},{10,11... | collective-permute-start | bytes 1769480 | tf_op jit(solution)/shard_map/ppermute | solution.py:603
  43.6 22.3 %collective-permute-start.8 = (bf16[256,768]{1,0:T(8,128)(2,1)S(1)}, bf16[256,768]{1,0:T(8,128)(2,1)S(1)}, u32[]{:S(2)}, u32[]{:S(2)}) collective-permute-start(bf16[256,768]{1,0:T(8,128)(2,1)S(1)} %bitcast.100), channel_id=1, source_target_pairs={{0,4},{2,6},{4,0},{6,2},{1,5},{3,7},{5,1},{7,3},{8,12},{10,14},{12... | collective-permute-start | bytes 1179656 | tf_op jit(solution)/shard_map/ppermute | solution.py:581
  50.7 16.7 %collective-permute-start.11 = (bf16[2,208,768]{2,1,0:T(8,128)(2,1)S(1)}, bf16[2,208,768]{2,1,0:T(8,128)(2,1)S(1)}, u32[]{:S(2)}, u32[]{:S(2)}) collective-permute-start(bf16[2,208,768]{2,1,0:T(8,128)(2,1)S(1)} %pad_maximum_fusion.3.refs_8_), channel_id=1, source_target_pairs={{0,8},{8,0},{16,24},{24,16},{1,9},{9,1},{17,25},{25,17},{2,10},{10... | collective-permute-start | bytes 1916936 | tf_op jit(solution)/shard_map/ppermute | solution.py:603
  50.7 17.3 %collective-permute-start.9 = (bf16[2,208,768]{2,1,0:T(8,128)(2,1)S(1)}, bf16[2,208,768]{2,1,0:T(8,128)(2,1)S(1)}, u32[]{:S(2)}, u32[]{:S(2)}) collective-permute-start(bf16[2,208,768]{2,1,0:T(8,128)(2,1)S(1)} %pad_maximum_fusion.2.refs_4_), channel_id=1, source_target_pairs={{0,8},{8,0},{16,24},{24,16},{1,9},{9,1},{17,25},{25,17},{2,10},{10... | collective-permute-start | bytes 1916936 | tf_op jit(solution)/shard_map/ppermute | solution.py:603
  54.2 13.8 %collective-permute-start.10 = (bf16[2,208,768]{2,1,0:T(8,128)(2,1)S(1)}, bf16[2,208,768]{2,1,0:T(8,128)(2,1)S(1)}, u32[]{:S(2)}, u32[]{:S(2)}) collective-permute-start(bf16[2,208,768]{2,1,0:T(8,128)(2,1)S(1)} %collective-permute-done.2.refs_5_), channel_id=1, source_target_pairs={{0,8},{8,0},{16,24},{24,16},{1,9},{9,1},{17,25},{25,17},{2,10},{10... | collective-permute-start | bytes 1916936 | tf_op jit(solution)/shard_map/ppermute | solution.py:603
  54.3 50.6 %copy-start.8 = (bf16[2,192,1536]{2,1,0:T(8,128)(2,1)}, bf16[2,192,1536]{2,1,0:T(8,128)(2,1)S(1)}, u32[]{:S(2)}) copy-start(bf16[2,192,1536]{2,1,0:T(8,128)(2,1)S(1)} %pad_maximum_fusion.1.refs_16_) | copy-start | bytes 3538948
  65.9 2.1 collective-permute-start.12
  66.7 38.8 %collective-permute-start.19 = (bf16[2,192,1536]{2,1,0:T(8,128)(2,1)S(1)}, bf16[2,192,1536]{2,1,0:T(8,128)(2,1)}, u32[]{:S(2)}, u32[]{:S(2)}) collective-permute-start(bf16[2,192,1536]{2,1,0:T(8,128)(2,1)S(1)} %pad_maximum_fusion.1.refs_16_), channel_id=1, source_target_pairs={{0,1},{1,0},{2,3},{3,2},{4,5},{5,4},{6,7},{7,6},{8,9},{9,8},{10,11... | collective-permute-start | bytes 3538952 | tf_op jit(solution)/shard_map/ppermute | solution.py:603
  67.4 38.2 %collective-permute-start.16 = (bf16[2,192,1536]{2,1,0:T(8,128)(2,1)S(1)}, bf16[2,192,1536]{2,1,0:T(8,128)(2,1)}, u32[]{:S(2)}, u32[]{:S(2)}) collective-permute-start(bf16[2,192,1536]{2,1,0:T(8,128)(2,1)S(1)} %pad_maximum_fusion.refs_12_), channel_id=1, source_target_pairs={{0,16},{8,24},{16,0},{24,8},{1,17},{9,25},{17,1},{25,9},{2,18},{10... | collective-permute-start | bytes 3538952 | tf_op jit(solution)/shard_map/ppermute | solution.py:603
  69.2 34.9 %collective-permute-start.13 = (bf16[256,768]{1,0:T(8,128)(2,1)}, bf16[256,768]{1,0:T(8,128)(2,1)S(1)}, u32[]{:S(2)}, u32[]{:S(2)}) collective-permute-start(bf16[256,768]{1,0:T(8,128)(2,1)} %bitcast.14), channel_id=1, source_target_pairs={{0,2},{2,0},{4,6},{6,4},{1,3},{3,1},{5,7},{7,5},{8,10},{10,8},{12,... | collective-permute-start | bytes 1179656 | tf_op jit(solution)/shard_map/ppermute | solution.py:581
  69.2 34.9 %collective-permute-start.14 = (bf16[256,768]{1,0:T(8,128)(2,1)S(1)}, bf16[256,768]{1,0:T(8,128)(2,1)S(1)}, u32[]{:S(2)}, u32[]{:S(2)}) collective-permute-start(bf16[256,768]{1,0:T(8,128)(2,1)S(1)} %bitcast.103), channel_id=1, source_target_pairs={{0,4},{2,6},{4,0},{6,2},{1,5},{3,7},{5,1},{7,3},{8,12},{10,14},{12... | collective-permute-start | bytes 1179656 | tf_op jit(solution)/shard_map/ppermute | solution.py:581
  72.1 32.0 %collective-permute-start.15 = (bf16[256,768]{1,0:T(8,128)(2,1)S(1)}, bf16[256,768]{1,0:T(8,128)(2,1)}, u32[]{:S(2)}, u32[]{:S(2)}) collective-permute-start(bf16[256,768]{1,0:T(8,128)(2,1)S(1)} %bitcast.101), channel_id=1, source_target_pairs={{0,6},{2,4},{4,2},{6,0},{1,7},{3,5},{5,3},{7,1},{8,14},{10,12},{12... | collective-permute-start | bytes 1179656 | tf_op jit(solution)/shard_map/ppermute | solution.py:581
  104.9 2.8 collective-permute-start.20
  104.9 4.5 %collective-permute-start.17 = (bf16[2,192,1536]{2,1,0:T(8,128)(2,1)S(1)}, bf16[2,192,1536]{2,1,0:T(8,128)(2,1)S(1)}, u32[]{:S(2)}, u32[]{:S(2)}) collective-permute-start(bf16[2,192,1536]{2,1,0:T(8,128)(2,1)S(1)} %pad_maximum_fusion.refs_12_), channel_id=1, source_target_pairs={{0,8},{8,0},{16,24},{24,16},{1,9},{9,1},{17,25},{25,17},{2,10},{10... | collective-permute-start | bytes 3538952 | tf_op jit(solution)/shard_map/ppermute | solution.py:603
  105.5 5.7 %collective-permute-start.21 = (bf16[2,192,1536]{2,1,0:T(8,128)(2,1)}, bf16[2,192,1536]{2,1,0:T(8,128)(2,1)S(1)}, u32[]{:S(2)}, u32[]{:S(2)}) collective-permute-start(bf16[2,192,1536]{2,1,0:T(8,128)(2,1)} %collective-permute-done.19.refs_17_), channel_id=1, source_target_pairs={{0,8},{8,0},{16,24},{24,16},{1,9},{9,1},{17,25},{25,17},{2,10},{10... | collective-permute-start | bytes 3538952 | tf_op jit(solution)/shard_map/ppermute | solution.py:603
  105.5 7.3 %collective-permute-start.18 = (bf16[2,192,1536]{2,1,0:T(8,128)(2,1)}, bf16[2,192,1536]{2,1,0:T(8,128)(2,1)S(1)}, u32[]{:S(2)}, u32[]{:S(2)}) collective-permute-start(bf16[2,192,1536]{2,1,0:T(8,128)(2,1)} %collective-permute-done.16.refs_13_), channel_id=1, source_target_pairs={{0,8},{8,0},{16,24},{24,16},{1,9},{9,1},{17,25},{25,17},{2,10},{10... | collective-permute-start | bytes 3538952 | tf_op jit(solution)/shard_map/ppermute | solution.py:603
  160.5 15.1 %collective-permute-start.22 = (bf16[256,768]{1,0:T(8,128)(2,1)}, bf16[256,768]{1,0:T(8,128)(2,1)S(1)}, u32[]{:S(2)}, u32[]{:S(2)}) collective-permute-start(bf16[256,768]{1,0:T(8,128)(2,1)} %get-tuple-element.95), channel_id=1, source_target_pairs={{0,2},{2,0},{4,6},{6,4},{1,3},{3,1},{5,7},{7,5},{8,10},{10,8},{12,... | collective-permute-start | bytes 1179656 | tf_op jit(solution)/shard_map/ppermute | solution.py:581
  175.7 24.7 %collective-permute-start.25 = (bf16[2,2,208,1536]{3,2,1,0:T(8,128)(2,1)}, bf16[2,2,208,1536]{3,2,1,0:T(8,128)(2,1)}, u32[]{:S(2)}, u32[]{:S(2)}) collective-permute-start(bf16[2,2,208,1536]{3,2,1,0:T(8,128)(2,1)} %get-tuple-element.105), channel_id=1, source_target_pairs={{0,8},{8,0},{16,24},{24,16},{1,9},{9,1},{17,25},{25,17},{2,10},{10... | collective-permute-start | bytes 7667720 | tf_op jit(solution)/shard_map/ppermute | solution.py:664
  175.7 15.7 %collective-permute-start.23 = (bf16[256,768]{1,0:T(8,128)(2,1)}, bf16[256,768]{1,0:T(8,128)(2,1)S(1)}, u32[]{:S(2)}, u32[]{:S(2)}) collective-permute-start(bf16[256,768]{1,0:T(8,128)(2,1)} %get-tuple-element.96), channel_id=1, source_target_pairs={{0,6},{2,4},{4,2},{6,0},{1,7},{3,5},{5,3},{7,1},{8,14},{10,12},{12... | collective-permute-start | bytes 1179656 | tf_op jit(solution)/shard_map/ppermute | solution.py:581
  191.4 42.3 %collective-permute-start.26 = (bf16[2,2,208,1536]{3,2,1,0:T(8,128)(2,1)}, bf16[2,2,208,1536]{3,2,1,0:T(8,128)(2,1)}, u32[]{:S(2)}, u32[]{:S(2)}) collective-permute-start(bf16[2,2,208,1536]{3,2,1,0:T(8,128)(2,1)} %get-tuple-element.111), channel_id=1, source_target_pairs={{0,8},{8,0},{16,24},{24,16},{1,9},{9,1},{17,25},{25,17},{2,10},{10... | collective-permute-start | bytes 7667720 | tf_op jit(solution)/shard_map/ppermute | solution.py:664
  191.5 41.6 %collective-permute-start.28 = (bf16[256,768]{1,0:T(8,128)(2,1)S(1)}, bf16[256,768]{1,0:T(8,128)(2,1)}, u32[]{:S(2)}, u32[]{:S(2)}) collective-permute-start(bf16[256,768]{1,0:T(8,128)(2,1)S(1)} %copy-done.32), channel_id=1, source_target_pairs={{0,4},{2,6},{4,0},{6,2},{1,5},{3,7},{5,1},{7,3},{8,12},{10,14},{12... | collective-permute-start | bytes 1179656 | tf_op jit(solution)/shard_map/ppermute | solution.py:581
  199.2 42.6 %collective-permute-start.24 = (bf16[768,768]{1,0:T(8,128)(2,1)}, bf16[768,768]{1,0:T(8,128)(2,1)}, u32[]{:S(2)}, u32[]{:S(2)}) collective-permute-start(bf16[768,768]{1,0:T(8,128)(2,1)} %constant_dynamic-update-slice_fusion), channel_id=1, source_target_pairs={{0,1},{1,0},{2,3},{3,2},{4,5},{5,4},{6,7},{7,6},{8,9},{9,8},{10,11... | collective-permute-start | bytes 3538952 | tf_op jit(solution)/shard_map/ppermute | solution.py:585
  205.4 33.5 %collective-permute-start.27 = (bf16[1,2,208,1536]{3,2,1,0:T(8,128)(2,1)}, bf16[1,2,208,1536]{3,2,1,0:T(8,128)(2,1)}, u32[]{:S(2)}, u32[]{:S(2)}) collective-permute-start(bf16[1,2,208,1536]{3,2,1,0:T(8,128)(2,1)} %split.49), channel_id=1, source_target_pairs={{0,16},{8,24},{16,0},{24,8},{1,17},{9,25},{17,1},{25,9},{2,18},{10... | collective-permute-start | bytes 3833864 | tf_op jit(solution)/shard_map/ppermute | solution.py:603
  233.1 34.4 %collective-permute-start.33 = (bf16[256,768]{1,0:T(8,128)(2,1)}, bf16[256,768]{1,0:T(8,128)(2,1)}, u32[]{:S(2)}, u32[]{:S(2)}) collective-permute-start(bf16[256,768]{1,0:T(8,128)(2,1)} %collective-permute-done.28), channel_id=1, source_target_pairs={{0,1},{1,0},{2,3},{3,2},{4,5},{5,4},{6,7},{7,6},{8,9},{9,8},{10,11... | collective-permute-start | bytes 1179656 | tf_op jit(solution)/shard_map/ppermute | solution.py:585
  238.1 29.7 %collective-permute-start.30 = (bf16[1,2,208,1536]{3,2,1,0:T(8,128)(2,1)}, bf16[1,2,208,1536]{3,2,1,0:T(8,128)(2,1)}, u32[]{:S(2)}, u32[]{:S(2)}) collective-permute-start(bf16[1,2,208,1536]{3,2,1,0:T(8,128)(2,1)} %split.51), channel_id=1, source_target_pairs={{0,16},{8,24},{16,0},{24,8},{1,17},{9,25},{17,1},{25,9},{2,18},{10... | collective-permute-start | bytes 3833864 | tf_op jit(solution)/shard_map/ppermute | solution.py:603
  241.8 28.9 %collective-permute-start.29 = (bf16[1,1,208,1536]{3,2,1,0:T(8,128)(2,1)S(1)}, bf16[1,1,208,1536]{3,2,1,0:T(8,128)(2,1)}, u32[]{:S(2)}, u32[]{:S(2)}) collective-permute-start(bf16[1,1,208,1536]{3,2,1,0:T(8,128)(2,1)S(1)} %split.50), channel_id=1, source_target_pairs={{0,1},{1,0},{2,3},{3,2},{4,5},{5,4},{6,7},{7,6},{8,9},{9,8},{10,11... | collective-permute-start | bytes 1916936 | tf_op jit(solution)/shard_map/ppermute | solution.py:603
  251.9 18.8 %collective-permute-start.31 = (bf16[256,768]{1,0:T(8,128)(2,1)}, bf16[256,768]{1,0:T(8,128)(2,1)S(1)}, u32[]{:S(2)}, u32[]{:S(2)}) collective-permute-start(bf16[256,768]{1,0:T(8,128)(2,1)} %get-tuple-element.120), channel_id=1, source_target_pairs={{0,2},{2,0},{4,6},{6,4},{1,3},{3,1},{5,7},{7,5},{8,10},{10,8},{12,... | collective-permute-start | bytes 1179656 | tf_op jit(solution)/shard_map/ppermute | solution.py:581
  252.0 18.8 %collective-permute-start.32 = (bf16[256,768]{1,0:T(8,128)(2,1)}, bf16[256,768]{1,0:T(8,128)(2,1)}, u32[]{:S(2)}, u32[]{:S(2)}) collective-permute-start(bf16[256,768]{1,0:T(8,128)(2,1)} %get-tuple-element.122), channel_id=1, source_target_pairs={{0,6},{2,4},{4,2},{6,0},{1,7},{3,5},{5,3},{7,1},{8,14},{10,12},{12... | collective-permute-start | bytes 1179656 | tf_op jit(solution)/shard_map/ppermute | solution.py:581
  271.5 5.2 %collective-permute-start.34 = (bf16[2,2,208,1536]{3,2,1,0:T(8,128)(2,1)}, bf16[2,2,208,1536]{3,2,1,0:T(8,128)(2,1)}, u32[]{:S(2)}, u32[]{:S(2)}) collective-permute-start(bf16[2,2,208,1536]{3,2,1,0:T(8,128)(2,1)} %get-tuple-element.127), channel_id=1, source_target_pairs={{0,8},{8,0},{16,24},{24,16},{1,9},{9,1},{17,25},{25,17},{2,10},{10... | collective-permute-start | bytes 7667720 | tf_op jit(solution)/shard_map/ppermute | solution.py:664
  273.2 21.1 %collective-permute-start.38 = (bf16[256,768]{1,0:T(8,128)(2,1)}, bf16[256,768]{1,0:T(8,128)(2,1)S(1)}, u32[]{:S(2)}, u32[]{:S(2)}) collective-permute-start(bf16[256,768]{1,0:T(8,128)(2,1)} %get-tuple-element.135), channel_id=1, source_target_pairs={{0,4},{2,6},{4,0},{6,2},{1,5},{3,7},{5,1},{7,3},{8,12},{10,14},{12... | collective-permute-start | bytes 1179656 | tf_op jit(solution)/shard_map/ppermute | solution.py:581
  294.4 10.1 %collective-permute-start.39 = (bf16[208,384]{1,0:T(8,128)(2,1)S(1)}, bf16[208,384]{1,0:T(8,128)(2,1)S(1)}, u32[]{:S(2)}, u32[]{:S(2)}) collective-permute-start(bf16[208,384]{1,0:T(8,128)(2,1)S(1)} %get-tuple-element.180), channel_id=1, source_target_pairs={{0,2},{2,0},{4,6},{6,4},{1,3},{3,1},{5,7},{7,5},{8,10},{10,8},{12,... | collective-permute-start | bytes 479240 | tf_op jit(solution)/shard_map/ppermute | solution.py:581
  294.5 14.7 %collective-permute-start.40 = (bf16[208,384]{1,0:T(8,128)(2,1)S(1)}, bf16[208,384]{1,0:T(8,128)(2,1)S(1)}, u32[]{:S(2)}, u32[]{:S(2)}) collective-permute-start(bf16[208,384]{1,0:T(8,128)(2,1)S(1)} %get-tuple-element.182), channel_id=1, source_target_pairs={{0,4},{2,6},{4,0},{6,2},{1,5},{3,7},{5,1},{7,3},{8,12},{10,14},{12... | collective-permute-start | bytes 479240 | tf_op jit(solution)/shard_map/ppermute | solution.py:581
  296.6 12.6 %collective-permute-start.41 = (bf16[208,384]{1,0:T(8,128)(2,1)S(1)}, bf16[208,384]{1,0:T(8,128)(2,1)S(1)}, u32[]{:S(2)}, u32[]{:S(2)}) collective-permute-start(bf16[208,384]{1,0:T(8,128)(2,1)S(1)} %get-tuple-element.181), channel_id=1, source_target_pairs={{0,6},{2,4},{4,2},{6,0},{1,7},{3,5},{5,3},{7,1},{8,14},{10,12},{12... | collective-permute-start | bytes 479240 | tf_op jit(solution)/shard_map/ppermute | solution.py:581
  298.9 42.2 %collective-permute-start.36 = (bf16[1,2,208,1536]{3,2,1,0:T(8,128)(2,1)S(1)}, bf16[1,2,208,1536]{3,2,1,0:T(8,128)(2,1)S(1)}, u32[]{:S(2)}, u32[]{:S(2)}) collective-permute-start(bf16[1,2,208,1536]{3,2,1,0:T(8,128)(2,1)S(1)} %split.53), channel_id=1, source_target_pairs={{0,16},{8,24},{16,0},{24,8},{1,17},{9,25},{17,1},{25,9},{2,18},{10... | collective-permute-start | bytes 3833864 | tf_op jit(solution)/shard_map/ppermute | solution.py:603
  300.7 78.1 %collective-permute-start.35 = (bf16[768,768]{1,0:T(8,128)(2,1)S(1)}, bf16[768,768]{1,0:T(8,128)(2,1)S(1)}, u32[]{:S(2)}, u32[]{:S(2)}) collective-permute-start(bf16[768,768]{1,0:T(8,128)(2,1)S(1)} %constant_dynamic-update-slice_fusion.3), channel_id=1, source_target_pairs={{0,1},{1,0},{2,3},{3,2},{4,5},{5,4},{6,7},{7,6},{8,9},{9,8},{10,11... | collective-permute-start | bytes 3538952 | tf_op jit(solution)/shard_map/ppermute | solution.py:585
  309.3 31.5 %collective-permute-start.42 = (bf16[1,1,208,1536]{3,2,1,0:T(8,128)(2,1)S(1)}, bf16[1,1,208,1536]{3,2,1,0:T(8,128)(2,1)S(1)}, u32[]{:S(2)}, u32[]{:S(2)}) collective-permute-start(bf16[1,1,208,1536]{3,2,1,0:T(8,128)(2,1)S(1)} %split.47), channel_id=1, source_target_pairs={{0,1},{1,0},{2,3},{3,2},{4,5},{5,4},{6,7},{7,6},{8,9},{9,8},{10,11... | collective-permute-start | bytes 1916936 | tf_op jit(solution)/shard_map/ppermute | solution.py:603
  312.1 7.4 %collective-permute-start.53 = (bf16[208,384]{1,0:T(8,128)(2,1)S(1)}, bf16[208,384]{1,0:T(8,128)(2,1)S(1)}, u32[]{:S(2)}, u32[]{:S(2)}) collective-permute-start(bf16[208,384]{1,0:T(8,128)(2,1)S(1)} %get-tuple-element.148), channel_id=1, source_target_pairs={{0,2},{2,0},{4,6},{6,4},{1,3},{3,1},{5,7},{7,5},{8,10},{10,8},{12,... | collective-permute-start | bytes 479240 | tf_op jit(solution)/shard_map/ppermute | solution.py:581
  315.0 28.6 %collective-permute-start.54 = (bf16[208,384]{1,0:T(8,128)(2,1)S(1)}, bf16[208,384]{1,0:T(8,128)(2,1)S(1)}, u32[]{:S(2)}, u32[]{:S(2)}) collective-permute-start(bf16[208,384]{1,0:T(8,128)(2,1)S(1)} %get-tuple-element.148), channel_id=1, source_target_pairs={{0,4},{2,6},{4,0},{6,2},{1,5},{3,7},{5,1},{7,3},{8,12},{10,14},{12... | collective-permute-start | bytes 479240 | tf_op jit(solution)/shard_map/ppermute | solution.py:581
  319.4 26.5 %collective-permute-start.55 = (bf16[208,384]{1,0:T(8,128)(2,1)S(1)}, bf16[208,384]{1,0:T(8,128)(2,1)S(1)}, u32[]{:S(2)}, u32[]{:S(2)}) collective-permute-start(bf16[208,384]{1,0:T(8,128)(2,1)S(1)} %get-tuple-element.148), channel_id=1, source_target_pairs={{0,6},{2,4},{4,2},{6,0},{1,7},{3,5},{5,3},{7,1},{8,14},{10,12},{12... | collective-permute-start | bytes 479240 | tf_op jit(solution)/shard_map/ppermute | solution.py:581
  341.5 7.3 %collective-permute-start.43 = (bf16[208,384]{1,0:T(8,128)(2,1)S(1)}, bf16[208,384]{1,0:T(8,128)(2,1)S(1)}, u32[]{:S(2)}, u32[]{:S(2)}) collective-permute-start(bf16[208,384]{1,0:T(8,128)(2,1)S(1)} %get-tuple-element.177), channel_id=1, source_target_pairs={{0,2},{2,0},{4,6},{6,4},{1,3},{3,1},{5,7},{7,5},{8,10},{10,8},{12,... | collective-permute-start | bytes 479240 | tf_op jit(solution)/shard_map/ppermute | solution.py:581
  341.5 13.3 %collective-permute-start.44 = (bf16[208,384]{1,0:T(8,128)(2,1)S(1)}, bf16[208,384]{1,0:T(8,128)(2,1)S(1)}, u32[]{:S(2)}, u32[]{:S(2)}) collective-permute-start(bf16[208,384]{1,0:T(8,128)(2,1)S(1)} %get-tuple-element.179), channel_id=1, source_target_pairs={{0,4},{2,6},{4,0},{6,2},{1,5},{3,7},{5,1},{7,3},{8,12},{10,14},{12... | collective-permute-start | bytes 479240 | tf_op jit(solution)/shard_map/ppermute | solution.py:581
  343.6 11.2 %collective-permute-start.45 = (bf16[208,384]{1,0:T(8,128)(2,1)S(1)}, bf16[208,384]{1,0:T(8,128)(2,1)S(1)}, u32[]{:S(2)}, u32[]{:S(2)}) collective-permute-start(bf16[208,384]{1,0:T(8,128)(2,1)S(1)} %get-tuple-element.178), channel_id=1, source_target_pairs={{0,6},{2,4},{4,2},{6,0},{1,7},{3,5},{5,3},{7,1},{8,14},{10,12},{12... | collective-permute-start | bytes 479240 | tf_op jit(solution)/shard_map/ppermute | solution.py:581
  354.9 7.2 %collective-permute-start.56 = (bf16[208,384]{1,0:T(8,128)(2,1)S(1)}, bf16[208,384]{1,0:T(8,128)(2,1)S(1)}, u32[]{:S(2)}, u32[]{:S(2)}) collective-permute-start(bf16[208,384]{1,0:T(8,128)(2,1)S(1)} %get-tuple-element.146), channel_id=1, source_target_pairs={{0,2},{2,0},{4,6},{6,4},{1,3},{3,1},{5,7},{7,5},{8,10},{10,8},{12,... | collective-permute-start | bytes 479240 | tf_op jit(solution)/shard_map/ppermute | solution.py:581
  358.4 15.3 %collective-permute-start.37 = (bf16[1,1,208,1536]{3,2,1,0:T(8,128)(2,1)S(1)}, bf16[1,1,208,1536]{3,2,1,0:T(8,128)(2,1)S(1)}, u32[]{:S(2)}, u32[]{:S(2)}) collective-permute-start(bf16[1,1,208,1536]{3,2,1,0:T(8,128)(2,1)S(1)} %split.55), channel_id=1, source_target_pairs={{0,1},{1,0},{2,3},{3,2},{4,5},{5,4},{6,7},{7,6},{8,9},{9,8},{10,11... | collective-permute-start | bytes 1916936 | tf_op jit(solution)/shard_map/ppermute | solution.py:603
  359.1 12.6 %collective-permute-start.57 = (bf16[208,384]{1,0:T(8,128)(2,1)S(1)}, bf16[208,384]{1,0:T(8,128)(2,1)S(1)}, u32[]{:S(2)}, u32[]{:S(2)}) collective-permute-start(bf16[208,384]{1,0:T(8,128)(2,1)S(1)} %get-tuple-element.146), channel_id=1, source_target_pairs={{0,4},{2,6},{4,0},{6,2},{1,5},{3,7},{5,1},{7,3},{8,12},{10,14},{12... | collective-permute-start | bytes 479240 | tf_op jit(solution)/shard_map/ppermute | solution.py:581
  359.7 11.9 %collective-permute-start.58 = (bf16[208,384]{1,0:T(8,128)(2,1)S(1)}, bf16[208,384]{1,0:T(8,128)(2,1)S(1)}, u32[]{:S(2)}, u32[]{:S(2)}) collective-permute-start(bf16[208,384]{1,0:T(8,128)(2,1)S(1)} %get-tuple-element.146), channel_id=1, source_target_pairs={{0,6},{2,4},{4,2},{6,0},{1,7},{3,5},{5,3},{7,1},{8,14},{10,12},{12... | collective-permute-start | bytes 479240 | tf_op jit(solution)/shard_map/ppermute | solution.py:581
  374.0 7.5 %collective-permute-start.47 = (bf16[208,384]{1,0:T(8,128)(2,1)S(1)}, bf16[208,384]{1,0:T(8,128)(2,1)S(1)}, u32[]{:S(2)}, u32[]{:S(2)}) collective-permute-start(bf16[208,384]{1,0:T(8,128)(2,1)S(1)} %get-tuple-element.174), channel_id=1, source_target_pairs={{0,2},{2,0},{4,6},{6,4},{1,3},{3,1},{5,7},{7,5},{8,10},{10,8},{12,... | collective-permute-start | bytes 479240 | tf_op jit(solution)/shard_map/ppermute | solution.py:581
  376.4 13.7 %collective-permute-start.48 = (bf16[208,384]{1,0:T(8,128)(2,1)S(1)}, bf16[208,384]{1,0:T(8,128)(2,1)S(1)}, u32[]{:S(2)}, u32[]{:S(2)}) collective-permute-start(bf16[208,384]{1,0:T(8,128)(2,1)S(1)} %get-tuple-element.176), channel_id=1, source_target_pairs={{0,4},{2,6},{4,0},{6,2},{1,5},{3,7},{5,1},{7,3},{8,12},{10,14},{12... | collective-permute-start | bytes 479240 | tf_op jit(solution)/shard_map/ppermute | solution.py:581
  376.9 13.2 %collective-permute-start.49 = (bf16[208,384]{1,0:T(8,128)(2,1)S(1)}, bf16[208,384]{1,0:T(8,128)(2,1)S(1)}, u32[]{:S(2)}, u32[]{:S(2)}) collective-permute-start(bf16[208,384]{1,0:T(8,128)(2,1)S(1)} %get-tuple-element.175), channel_id=1, source_target_pairs={{0,6},{2,4},{4,2},{6,0},{1,7},{3,5},{5,3},{7,1},{8,14},{10,12},{12... | collective-permute-start | bytes 479240 | tf_op jit(solution)/shard_map/ppermute | solution.py:581
  379.0 30.8 %collective-permute-start.46 = (bf16[256,768]{1,0:T(8,128)(2,1)S(1)}, bf16[256,768]{1,0:T(8,128)(2,1)S(1)}, u32[]{:S(2)}, u32[]{:S(2)}) collective-permute-start(bf16[256,768]{1,0:T(8,128)(2,1)S(1)} %collective-permute-done.38), channel_id=1, source_target_pairs={{0,1},{1,0},{2,3},{3,2},{4,5},{5,4},{6,7},{7,6},{8,9},{9,8},{10,11... | collective-permute-start | bytes 1179656 | tf_op jit(solution)/shard_map/ppermute | solution.py:585
  390.2 7.0 %collective-permute-start.50 = (bf16[208,384]{1,0:T(8,128)(2,1)S(1)}, bf16[208,384]{1,0:T(8,128)(2,1)S(1)}, u32[]{:S(2)}, u32[]{:S(2)}) collective-permute-start(bf16[208,384]{1,0:T(8,128)(2,1)S(1)} %get-tuple-element.150), channel_id=1, source_target_pairs={{0,2},{2,0},{4,6},{6,4},{1,3},{3,1},{5,7},{7,5},{8,10},{10,8},{12,... | collective-permute-start | bytes 479240 | tf_op jit(solution)/shard_map/ppermute | solution.py:581
  392.5 13.8 %collective-permute-start.51 = (bf16[208,384]{1,0:T(8,128)(2,1)S(1)}, bf16[208,384]{1,0:T(8,128)(2,1)S(1)}, u32[]{:S(2)}, u32[]{:S(2)}) collective-permute-start(bf16[208,384]{1,0:T(8,128)(2,1)S(1)} %get-tuple-element.150), channel_id=1, source_target_pairs={{0,4},{2,6},{4,0},{6,2},{1,5},{3,7},{5,1},{7,3},{8,12},{10,14},{12... | collective-permute-start | bytes 479240 | tf_op jit(solution)/shard_map/ppermute | solution.py:581
  393.5 12.8 %collective-permute-start.52 = (bf16[208,384]{1,0:T(8,128)(2,1)S(1)}, bf16[208,384]{1,0:T(8,128)(2,1)S(1)}, u32[]{:S(2)}, u32[]{:S(2)}) collective-permute-start(bf16[208,384]{1,0:T(8,128)(2,1)S(1)} %get-tuple-element.150), channel_id=1, source_target_pairs={{0,6},{2,4},{4,2},{6,0},{1,7},{3,5},{5,3},{7,1},{8,14},{10,12},{12... | collective-permute-start | bytes 479240 | tf_op jit(solution)/shard_map/ppermute | solution.py:581
  (31 other events, 385.5 us)

commit v7 on v6

--- a/solution.py
+++ b/solution.py
@@ -723,10 +723,10 @@
     outer_part = ctx_scatter(outer_x)
     early_ig = tp_moved(after(tuple(ig[k] for k in early), [qkv_core]))
     qkv_y, _ = y_sum(qkv_core)
-    inner_x, _ = x_sum(after(inner_y, [outer_part]))
-    outer_g = ctx_gather(outer_part, outer_x)
-    inner_x = after(inner_x[0, 0], [qkv_y] + [ig[k] for k in even])
+    inner_x, _ = x_sum(after(inner_y, [qkv_core]))
+    inner_x = after(inner_x[0, 0], [outer_part])
     inner_part = ctx_scatter(inner_x)
+    outer_g = ctx_gather(after(outer_part, [inner_part]), outer_x)
     qkv_x, _ = x_sum(qkv_y)
     qkv_x = after(qkv_x[0, 0], [inner_part])
     qkv_part = ctx_scatter(qkv_x)
@@ -735,7 +735,7 @@
     early_ig = after(tuple(early_ig), [qkv_x])
     layer_out = to_slots([(early, early_lo), (list(even), late_lo)], BF)
     input_grad = to_slots([(early, early_ig), (list(even), late_ig)], F32)
-    inner_g = ctx_gather(inner_part, inner_x)
+    inner_g = ctx_gather(after(inner_part, [qkv_y]), inner_x)
     qkv_g = ctx_gather(qkv_part, qkv_x)
 
     def own(row, shape):

time: 414 us -> 405 us (0.978)
  waiting for transfers between devices: 124 us -> 113 us
    ppermute x22, waiting for transfers between devices: 33.9 us -> 21.6 us  [swapped(): return lax.ppermute(array, axis, xor_pairs(lax.axis_size(axis), bit))]
  transfers between devices with their start and end apart: 59 -> 59, of which waited for: 25 -> 28; matrix products, arithmetic and copies ran while one was open for 9% -> 10% of each run, Pallas kernels for 25% -> 26%
where the time goes in v7:
time: 405 us; the launch traced here: 404 us
  Pallas kernels  151 us (37%)
  waiting for transfers between devices  113 us (28%)
  starting transfers between devices  80 us (20%)
  local copies, waits for them, and re-layouts  37.3 us (9%)
  other arithmetic  20.2 us (5%)
    ppermute x30, waiting for transfers between devices, ctx_moved(): return lax.ppermute(piece, 'ctx', xor_pairs(C, k)) if k else piece  90.8 us
    ppermute x30, starting transfers between devices, ctx_moved(): return lax.ppermute(piece, 'ctx', xor_pairs(C, k)) if k else piece  59.9 us
    pallas_call x1, Pallas kernels, rows_call(): pl.pallas_call(functools.partial(rows_kernel, dims, FF), name='rows', gri...  46.7 us
    pallas_call x3, Pallas kernels, weight_call(): pl.pallas_call(functools.partial(weight_kernel, F, pers, sums is not None...  40 us
    pallas_call x1, Pallas kernels, front_call(): pl.pallas_call(functools.partial(front_kernel, dims), name='front', grid=...  29.9 us
    pallas_call x1, Pallas kernels, back_call(): pl.pallas_call(functools.partial(back_kernel, dims), name='back', grid=(n...  26.2 us
    ppermute x22, waiting for transfers between devices, swapped(): return lax.ppermute(array, axis, xor_pairs(lax.axis_size(axis), bit))  21.6 us
    ppermute x22, starting transfers between devices, swapped(): return lax.ppermute(array, axis, xor_pairs(lax.axis_size(axis), bit))  16.1 us
  transfers between devices with their start and end apart: 59, of which 28 were waited for; matrix products, arithmetic and copies ran while one was open for 10% of the time, Pallas kernels for 26%

profile of v7, /device:TPU:0, one launch (start us, length us, event | category | flops | bytes accessed | tf_op | source)
XLA Modules:
  0.0 403.5 jit_solution(15630311953283055867)
XLA Ops:
  8.4 3.0 collective-permute-start
  12.4 1.6 collective-permute-start.3
  14.0 2.3 constant_dynamic-slice_fusion.17
  16.3 1.6 collective-permute-start.1
  19.0 2.5 collective-permute-done.3
  21.6 5.0 %collective-permute-done.1.refs_1_ = bf16[256,768]{1,0:T(8,128)(2,1)S(1)} collective-permute-done((bf16[256,768]{1,0:T(8,128)(2,1)S(1)}, bf16[256,768]{1,0:T(8,128)(2,1)S(1)}, u32[]{:S(2)}, u32[]{:S(2)}) %collective-permute-start.1) | collective-permute-done | bytes 393248 | tf_op jit(solution)/shard_map/ppermute | solution.py:581
  27.5 3.8 collective-permute-start.5
  31.3 7.3 %collective-permute-done.5.refs_3_ = bf16[256,768]{1,0:T(8,128)(2,1)S(1)} collective-permute-done((bf16[256,768]{1,0:T(8,128)(2,1)S(1)}, bf16[256,768]{1,0:T(8,128)(2,1)S(1)}, u32[]{:S(2)}, u32[]{:S(2)}) %collective-permute-start.5) | collective-permute-done | bytes 393248 | tf_op jit(solution)/shard_map/ppermute | solution.py:581
  38.6 2.7 collective-permute-done.2.refs_5_
  41.6 1.5 collective-permute-start.7
  43.6 7.1 %collective-permute-start.8 = (bf16[256,768]{1,0:T(8,128)(2,1)S(1)}, bf16[256,768]{1,0:T(8,128)(2,1)S(1)}, u32[]{:S(2)}, u32[]{:S(2)}) collective-permute-start(bf16[256,768]{1,0:T(8,128)(2,1)S(1)} %bitcast.100), channel_id=1, source_target_pairs={{0,4},{2,6},{4,0},{6,2},{1,5},{3,7},{5,1},{7,3},{8,12},{10,14},{12... | collective-permute-start | bytes 1179656 | tf_op jit(solution)/shard_map/ppermute | solution.py:581
  51.2 3.0 collective-permute-done.7
  54.3 11.6 %collective-permute-done.8.refs_2_ = bf16[256,768]{1,0:T(8,128)(2,1)S(1)} collective-permute-done((bf16[256,768]{1,0:T(8,128)(2,1)S(1)}, bf16[256,768]{1,0:T(8,128)(2,1)S(1)}, u32[]{:S(2)}, u32[]{:S(2)}) %collective-permute-start.8) | collective-permute-done | bytes 393248 | tf_op jit(solution)/shard_map/ppermute | solution.py:581
  69.2 2.9 collective-permute-start.14
  72.1 1.5 collective-permute-start.15
  74.2 29.9 %front.1 = (bf16[4,256,768]{2,1,0:T(8,128)(2,1)}, bf16[768,2304]{1,0:T(8,128)(2,1)}, bf16[4,2,128,2304]{3,2,1,0:T(8,128)(2,1)}, bf16[12,1024,512]{2,1,0:T(8,128)...) custom-call(s32[4]{0:T(128)} %pad_add_fusion.meta, bf16[256,768]{1,0:T(8,128)(2,1)} %bitcast.98, ...), custom_call_target="tpu_custom_call" | custom-call | flops 3623878656 | bytes 40000000 | tf_op jit(solution)/shard_map/front/pallas_call | solution.py:162
  106.0 1.8 collective-permute-done.20.refs_18_
  107.8 1.7 collective-permute-done.17.refs_14_
  113.9 46.7 %rows.1 = (bf16[256,768]{1,0:T(8,128)(2,1)}, bf16[256,768]{1,0:T(8,128)(2,1)}, bf16[256,768]{1,0:T(8,128)(2,1)}, bf16[256,768]{1,0:T(8,128)(2,1)}, f32[4,256,768...) custom-call(s32[4]{0:T(128)} %pad_add_fusion.meta, ...), custom_call_target="tpu_custom_call" | custom-call | flops 21743271936 | bytes 50000000 | tf_op jit(solution)/shard_map/rows/pallas_call | solution.py:344
  160.5 2.3 collective-permute-start.22
  162.9 12.8 %weight_grad.3 = (bf16[2,2,208,1536]{3,2,1,0:T(8,128)(2,1)}, bf16[2,2,208,1536]{3,2,1,0:T(8,128)(2,1)}) custom-call(s32[4]{0:T(128)} %pad_add_fusion.meta, bf16[1024,768]{1,0:T(8,128)(2,1)} %bitcast.118, bf16[1024,3072]{1,0:T(8,128)(2,1)} %bitcast.114, f32[16,768]{1,0:T(8,128)} %get-tuple-element.104.refs_2_), custom_call_target="tpu_custom_call" | custom-call | flops 4831838208 | bytes 12582912 | tf_op jit(solution)/shard_map/weight_grad/pallas_call | solution.py:523
  175.7 2.5 collective-permute-start.23
  178.2 13.2 %weight_grad.4 = (bf16[2,2,208,1536]{3,2,1,0:T(8,128)(2,1)}, bf16[2,2,208,1536]{3,2,1,0:T(8,128)(2,1)}) custom-call(s32[4]{0:T(128)} %pad_add_fusion.meta, bf16[1024,768]{1,0:T(8,128)(2,1)} %bitcast.117, bf16[1024,3072]{1,0:T(8,128)(2,1)} %bitcast.113), custom_call_target="tpu_custom_call" | custom-call | flops 4831838208 | bytes 12582912 | tf_op jit(solution)/shard_map/weight_grad/pallas_call | solution.py:523
  191.5 5.3 %collective-permute-start.28 = (bf16[256,768]{1,0:T(8,128)(2,1)S(1)}, bf16[256,768]{1,0:T(8,128)(2,1)}, u32[]{:S(2)}, u32[]{:S(2)}) collective-permute-start(bf16[256,768]{1,0:T(8,128)(2,1)S(1)} %copy-done.32), channel_id=1, source_target_pairs={{0,4},{2,6},{4,0},{6,2},{1,5},{3,7},{5,1},{7,3},{8,12},{10,14},{12... | collective-permute-start | bytes 1179656 | tf_op jit(solution)/shard_map/ppermute | solution.py:581
  200.3 2.4 add_convert_fusion.2
  202.8 1.5 copy-done
  205.4 1.5 collective-permute-start.27
  206.9 26.2 %back.1 = bf16[4,2,128,2304]{3,2,1,0:T(8,128)(2,1)} custom-call(bf16[4,2,128,2304]{3,2,1,0:T(8,128)(2,1)} %get-tuple-element.100.qkv, bf16[4,2,128,768]{3,2,1,0:T(8,128)(2,1)} %get-tuple-element.90.ctx, bf16[4,2,128,768]{3,2,1,0:T(8,128)(2,1)} %bitcast.79, bf16[12,1024,512]{2,1,0:T(8,128)(2,1)} %get-tuple-element.115.e_ref, ...), custom_call_target="tpu_custom_call" | custom-call | flops 6442450944 | bytes 30000000 | tf_op jit(solution)/shard_map/back/pallas_call | solution.py:413
  233.6 3.2 add_convert_fusion.1
  239.0 1.6 add_convert_fusion.5
  241.8 1.6 collective-permute-start.29
  243.3 8.5 %input_grad.1 = (bf16[256,768]{1,0:T(8,128)(2,1)}, bf16[256,768]{1,0:T(8,128)(2,1)}, bf16[256,768]{1,0:T(8,128)(2,1)}, bf16[256,768]{1,0:T(8,128)(2,1)}) custom-call(bf16[4,256,2304]{2,1,0:T(8,128)(2,1)} %bitcast.75, bf16[768,2304]{1,0:T(8,128)(2,1)} %get-tuple-element.117.w, f32[4,256,768]{2,1,0:T(8,128)} %get-tuple-element.120.first), custom_call_target="tpu_custom_call" | custom-call | flops 3623878656 | bytes 15000000 | tf_op jit(solution)/shard_map/input_grad/pallas_call | solution.py:450
  251.9 1.5 collective-permute-start.32
  253.4 14.0 %weight_grad.5 = (bf16[2,2,208,1536]{3,2,1,0:T(8,128)(2,1)}, bf16[2,2,208,1536]{3,2,1,0:T(8,128)(2,1)}) custom-call(s32[4]{0:T(128)} %pad_add_fusion.meta, bf16[1024,768]{1,0:T(8,128)(2,1)} %bitcast.115, bf16[1024,768]{1,0:T(8,128)(2,1)} %bitcast.116, bf16[1024,2304]{1,0:T(8,128)(2,1)} %bitcast.76, bf16[1024,768]{1,0:T(8,128)(2,1)} %bitcast.78), custom_call_target="tpu_custom_call" | custom-call | flops 4831838208 | bytes 12582912 | tf_op jit(solution)/shard_map/weight_grad/pallas_call | solution.py:523
  267.7 3.0 collective-permute-done.31
  271.4 1.8 add_convert_fusion.3
  274.4 1.3 fusion.2
  276.6 2.4 add_convert_fusion
  279.1 15.2 %collective-permute-done.39 = bf16[256,768]{1,0:T(8,128)(2,1)S(1)} collective-permute-done((bf16[256,768]{1,0:T(8,128)(2,1)}, bf16[256,768]{1,0:T(8,128)(2,1)S(1)}, u32[]{:S(2)}, u32[]{:S(2)}) %collective-permute-start.39) | collective-permute-done | bytes 393248 | tf_op jit(solution)/shard_map/ppermute | solution.py:581
  294.5 2.1 collective-permute-start.41
  296.6 2.3 collective-permute-start.42
  300.4 1.3 fusion.18
  301.7 1.3 fusion.17
  305.6 1.5 collective-permute-start.35
  307.1 2.1 collective-permute-done.41
  309.3 6.9 %collective-permute-done.38 = bf16[1,1,208,1536]{3,2,1,0:T(8,128)(2,1)S(1)} collective-permute-done((bf16[1,1,208,1536]{3,2,1,0:T(8,128)(2,1)S(1)}, bf16[1,1,208,1536]{3,2,1,0:T(8,128)(2,1)S(1)}, u32[]{:S(2)}, u32[]{:S(2)}) %collective-permute-start.38) | collective-permute-done | bytes 639008 | tf_op jit(solution)/shard_map/ppermute | solution.py:603
  316.5 2.1 collective-permute-start.44
  318.6 2.3 collective-permute-start.45
  322.0 1.5 collective-permute-done.43
  323.5 4.5 %collective-permute-done.44 = bf16[208,384]{1,0:T(8,128)(2,1)S(1)} collective-permute-done((bf16[208,384]{1,0:T(8,128)(2,1)S(1)}, bf16[208,384]{1,0:T(8,128)(2,1)S(1)}, u32[]{:S(2)}, u32[]{:S(2)}) %collective-permute-start.44) | collective-permute-done | bytes 159776 | tf_op jit(solution)/shard_map/ppermute | solution.py:581
  328.0 2.3 collective-permute-start.53
  330.5 2.4 collective-permute-start.55
  332.9 1.9 collective-permute-done.53
  334.9 8.6 %collective-permute-done.54 = bf16[208,384]{1,0:T(8,128)(2,1)S(1)} collective-permute-done((bf16[208,384]{1,0:T(8,128)(2,1)S(1)}, bf16[208,384]{1,0:T(8,128)(2,1)S(1)}, u32[]{:S(2)}, u32[]{:S(2)}) %collective-permute-start.54) | collective-permute-done | bytes 159776 | tf_op jit(solution)/shard_map/ppermute | solution.py:581
  345.1 2.8 collective-permute-start.56
  349.3 2.3 collective-permute-start.58
  352.4 9.2 %collective-permute-done.57 = bf16[208,384]{1,0:T(8,128)(2,1)S(1)} collective-permute-done((bf16[208,384]{1,0:T(8,128)(2,1)S(1)}, bf16[208,384]{1,0:T(8,128)(2,1)S(1)}, u32[]{:S(2)}, u32[]{:S(2)}) %collective-permute-start.57) | collective-permute-done | bytes 159776 | tf_op jit(solution)/shard_map/ppermute | solution.py:581
  363.9 3.0 collective-permute-start.47
  367.1 2.3 collective-permute-start.49
  371.4 8.8 %collective-permute-done.48 = bf16[208,384]{1,0:T(8,128)(2,1)S(1)} collective-permute-done((bf16[208,384]{1,0:T(8,128)(2,1)S(1)}, bf16[208,384]{1,0:T(8,128)(2,1)S(1)}, u32[]{:S(2)}, u32[]{:S(2)}) %collective-permute-start.48) | collective-permute-done | bytes 159776 | tf_op jit(solution)/shard_map/ppermute | solution.py:581
  380.3 3.3 collective-permute-start.50
  383.7 2.5 collective-permute-start.52
  386.2 2.2 collective-permute-done.50
  388.4 8.9 %collective-permute-done.51 = bf16[208,384]{1,0:T(8,128)(2,1)S(1)} collective-permute-done((bf16[208,384]{1,0:T(8,128)(2,1)S(1)}, bf16[208,384]{1,0:T(8,128)(2,1)S(1)}, u32[]{:S(2)}, u32[]{:S(2)}) %collective-permute-start.51) | collective-permute-done | bytes 159776 | tf_op jit(solution)/shard_map/ppermute | solution.py:581
  (248 shorter events, 54.5 us)
Async XLA Ops:
  8.4 10.6 %collective-permute-start = (bf16[1,208,768]{2,1,0:T(8,128)(2,1)S(1)}, bf16[1,208,768]{2,1,0:T(8,128)(2,1)S(1)}, u32[]{:S(2)}, u32[]{:S(2)}) collective-permute-start(bf16[1,208,768]{2,1,0:T(8,128)(2,1)S(1)} %maximum_bitcast_fusion), channel_id=1, source_target_pairs={{0,1},{1,0},{2,3},{3,2},{4,5},{5,4},{6,7},{7,6},{8,9},{9,8},{10,11... | collective-permute-start | bytes 958472 | tf_op jit(solution)/shard_map/ppermute | solution.py:603
  12.4 9.1 %collective-permute-start.3 = (bf16[1,208,768]{2,1,0:T(8,128)(2,1)S(1)}, bf16[1,208,768]{2,1,0:T(8,128)(2,1)S(1)}, u32[]{:S(2)}, u32[]{:S(2)}) collective-permute-start(bf16[1,208,768]{2,1,0:T(8,128)(2,1)S(1)} %maximum_bitcast_fusion.1), channel_id=1, source_target_pairs={{0,16},{8,24},{16,0},{24,8},{1,17},{9,25},{17,1},{25,9},{2,18},{10... | collective-permute-start | bytes 958472 | tf_op jit(solution)/shard_map/ppermute | solution.py:603
  16.3 10.3 %collective-permute-start.1 = (bf16[256,768]{1,0:T(8,128)(2,1)S(1)}, bf16[256,768]{1,0:T(8,128)(2,1)S(1)}, u32[]{:S(2)}, u32[]{:S(2)}) collective-permute-start(bf16[256,768]{1,0:T(8,128)(2,1)S(1)} %bitcast.104), channel_id=1, source_target_pairs={{0,2},{2,0},{4,6},{6,4},{1,3},{3,1},{5,7},{7,5},{8,10},{10,8},{12,... | collective-permute-start | bytes 1179656 | tf_op jit(solution)/shard_map/ppermute | solution.py:581
  19.0 48.3 %copy-start.11 = (bf16[2,208,768]{2,1,0:T(8,128)(2,1)}, bf16[2,208,768]{2,1,0:T(8,128)(2,1)S(1)}, u32[]{:S(2)}) copy-start(bf16[2,208,768]{2,1,0:T(8,128)(2,1)S(1)} %pad_maximum_fusion.2.refs_4_) | copy-start | bytes 1916932
  21.6 47.6 %copy-start.12 = (bf16[2,208,768]{2,1,0:T(8,128)(2,1)}, bf16[2,208,768]{2,1,0:T(8,128)(2,1)S(1)}, u32[]{:S(2)}) copy-start(bf16[2,208,768]{2,1,0:T(8,128)(2,1)S(1)} %pad_maximum_fusion.3.refs_8_) | copy-start | bytes 1916932
  21.6 46.4 %copy-start.35 = (s32[16]{0:T(128)S(1)}, s32[16]{0:T(128)}, u32[]{:S(2)}) copy-start(s32[16]{0:T(128)} %param.19) | copy-start | bytes 196
  21.6 46.5 %copy-start.10 = (bf16[16,128,768]{2,1,0:T(8,128)(2,1)S(1)}, bf16[16,128,768]{2,1,0:T(8,128)(2,1)}, u32[]{:S(2)}) copy-start(bf16[16,128,768]{2,1,0:T(8,128)(2,1)} %param.35) | copy-start | bytes 9437188
  26.6 14.7 %collective-permute-start.2 = (bf16[2,208,768]{2,1,0:T(8,128)(2,1)S(1)}, bf16[2,208,768]{2,1,0:T(8,128)(2,1)S(1)}, u32[]{:S(2)}, u32[]{:S(2)}) collective-permute-start(bf16[2,208,768]{2,1,0:T(8,128)(2,1)S(1)} %pad_maximum_fusion.2.refs_4_), channel_id=1, source_target_pairs={{0,16},{8,24},{16,0},{24,8},{1,17},{9,25},{17,1},{25,9},{2,18},{10... | collective-permute-start | bytes 1916936 | tf_op jit(solution)/shard_map/ppermute | solution.py:603
  27.1 14.4 %collective-permute-start.4 = (bf16[2,208,768]{2,1,0:T(8,128)(2,1)S(1)}, bf16[2,208,768]{2,1,0:T(8,128)(2,1)S(1)}, u32[]{:S(2)}, u32[]{:S(2)}) collective-permute-start(bf16[2,208,768]{2,1,0:T(8,128)(2,1)S(1)} %pad_maximum_fusion.3.refs_8_), channel_id=1, source_target_pairs={{0,1},{1,0},{2,3},{3,2},{4,5},{5,4},{6,7},{7,6},{8,9},{9,8},{10,11... | collective-permute-start | bytes 1916936 | tf_op jit(solution)/shard_map/ppermute | solution.py:603
  27.5 11.1 %collective-permute-start.5 = (bf16[256,768]{1,0:T(8,128)(2,1)S(1)}, bf16[256,768]{1,0:T(8,128)(2,1)S(1)}, u32[]{:S(2)}, u32[]{:S(2)}) collective-permute-start(bf16[256,768]{1,0:T(8,128)(2,1)S(1)} %bitcast.102), channel_id=1, source_target_pairs={{0,6},{2,4},{4,2},{6,0},{1,7},{3,5},{5,3},{7,1},{8,14},{10,12},{12... | collective-permute-start | bytes 1179656 | tf_op jit(solution)/shard_map/ppermute | solution.py:581
  41.6 12.6 %collective-permute-start.7 = (bf16[1,192,1536]{2,1,0:T(8,128)(2,1)S(1)}, bf16[1,192,1536]{2,1,0:T(8,128)(2,1)S(1)}, u32[]{:S(2)}, u32[]{:S(2)}) collective-permute-start(bf16[1,192,1536]{2,1,0:T(8,128)(2,1)S(1)} %bitcast.92), channel_id=1, source_target_pairs={{0,16},{8,24},{16,0},{24,8},{1,17},{9,25},{17,1},{25,9},{2,18},{10... | collective-permute-start | bytes 1769480 | tf_op jit(solution)/shard_map/ppermute | solution.py:603
  43.1 22.8 %collective-permute-start.6 = (bf16[1,192,1536]{2,1,0:T(8,128)(2,1)S(1)}, bf16[1,192,1536]{2,1,0:T(8,128)(2,1)S(1)}, u32[]{:S(2)}, u32[]{:S(2)}) collective-permute-start(bf16[1,192,1536]{2,1,0:T(8,128)(2,1)S(1)} %bitcast.94), channel_id=1, source_target_pairs={{0,1},{1,0},{2,3},{3,2},{4,5},{5,4},{6,7},{7,6},{8,9},{9,8},{10,11... | collective-permute-start | bytes 1769480 | tf_op jit(solution)/shard_map/ppermute | solution.py:603
  43.6 22.3 %collective-permute-start.8 = (bf16[256,768]{1,0:T(8,128)(2,1)S(1)}, bf16[256,768]{1,0:T(8,128)(2,1)S(1)}, u32[]{:S(2)}, u32[]{:S(2)}) collective-permute-start(bf16[256,768]{1,0:T(8,128)(2,1)S(1)} %bitcast.100), channel_id=1, source_target_pairs={{0,4},{2,6},{4,0},{6,2},{1,5},{3,7},{5,1},{7,3},{8,12},{10,14},{12... | collective-permute-start | bytes 1179656 | tf_op jit(solution)/shard_map/ppermute | solution.py:581
  50.7 16.7 %collective-permute-start.11 = (bf16[2,208,768]{2,1,0:T(8,128)(2,1)S(1)}, bf16[2,208,768]{2,1,0:T(8,128)(2,1)S(1)}, u32[]{:S(2)}, u32[]{:S(2)}) collective-permute-start(bf16[2,208,768]{2,1,0:T(8,128)(2,1)S(1)} %pad_maximum_fusion.3.refs_8_), channel_id=1, source_target_pairs={{0,8},{8,0},{16,24},{24,16},{1,9},{9,1},{17,25},{25,17},{2,10},{10... | collective-permute-start | bytes 1916936 | tf_op jit(solution)/shard_map/ppermute | solution.py:603
  50.7 17.3 %collective-permute-start.9 = (bf16[2,208,768]{2,1,0:T(8,128)(2,1)S(1)}, bf16[2,208,768]{2,1,0:T(8,128)(2,1)S(1)}, u32[]{:S(2)}, u32[]{:S(2)}) collective-permute-start(bf16[2,208,768]{2,1,0:T(8,128)(2,1)S(1)} %pad_maximum_fusion.2.refs_4_), channel_id=1, source_target_pairs={{0,8},{8,0},{16,24},{24,16},{1,9},{9,1},{17,25},{25,17},{2,10},{10... | collective-permute-start | bytes 1916936 | tf_op jit(solution)/shard_map/ppermute | solution.py:603
  54.2 13.8 %collective-permute-start.10 = (bf16[2,208,768]{2,1,0:T(8,128)(2,1)S(1)}, bf16[2,208,768]{2,1,0:T(8,128)(2,1)S(1)}, u32[]{:S(2)}, u32[]{:S(2)}) collective-permute-start(bf16[2,208,768]{2,1,0:T(8,128)(2,1)S(1)} %collective-permute-done.2.refs_5_), channel_id=1, source_target_pairs={{0,8},{8,0},{16,24},{24,16},{1,9},{9,1},{17,25},{25,17},{2,10},{10... | collective-permute-start | bytes 1916936 | tf_op jit(solution)/shard_map/ppermute | solution.py:603
  54.3 50.6 %copy-start.8 = (bf16[2,192,1536]{2,1,0:T(8,128)(2,1)}, bf16[2,192,1536]{2,1,0:T(8,128)(2,1)S(1)}, u32[]{:S(2)}) copy-start(bf16[2,192,1536]{2,1,0:T(8,128)(2,1)S(1)} %pad_maximum_fusion.1.refs_16_) | copy-start | bytes 3538948
  65.9 2.1 collective-permute-start.12
  66.7 38.8 %collective-permute-start.19 = (bf16[2,192,1536]{2,1,0:T(8,128)(2,1)S(1)}, bf16[2,192,1536]{2,1,0:T(8,128)(2,1)}, u32[]{:S(2)}, u32[]{:S(2)}) collective-permute-start(bf16[2,192,1536]{2,1,0:T(8,128)(2,1)S(1)} %pad_maximum_fusion.1.refs_16_), channel_id=1, source_target_pairs={{0,1},{1,0},{2,3},{3,2},{4,5},{5,4},{6,7},{7,6},{8,9},{9,8},{10,11... | collective-permute-start | bytes 3538952 | tf_op jit(solution)/shard_map/ppermute | solution.py:603
  67.4 38.1 %collective-permute-start.16 = (bf16[2,192,1536]{2,1,0:T(8,128)(2,1)S(1)}, bf16[2,192,1536]{2,1,0:T(8,128)(2,1)}, u32[]{:S(2)}, u32[]{:S(2)}) collective-permute-start(bf16[2,192,1536]{2,1,0:T(8,128)(2,1)S(1)} %pad_maximum_fusion.refs_12_), channel_id=1, source_target_pairs={{0,16},{8,24},{16,0},{24,8},{1,17},{9,25},{17,1},{25,9},{2,18},{10... | collective-permute-start | bytes 3538952 | tf_op jit(solution)/shard_map/ppermute | solution.py:603
  69.2 34.9 %collective-permute-start.13 = (bf16[256,768]{1,0:T(8,128)(2,1)}, bf16[256,768]{1,0:T(8,128)(2,1)S(1)}, u32[]{:S(2)}, u32[]{:S(2)}) collective-permute-start(bf16[256,768]{1,0:T(8,128)(2,1)} %bitcast.14), channel_id=1, source_target_pairs={{0,2},{2,0},{4,6},{6,4},{1,3},{3,1},{5,7},{7,5},{8,10},{10,8},{12,... | collective-permute-start | bytes 1179656 | tf_op jit(solution)/shard_map/ppermute | solution.py:581
  69.2 34.9 %collective-permute-start.14 = (bf16[256,768]{1,0:T(8,128)(2,1)S(1)}, bf16[256,768]{1,0:T(8,128)(2,1)S(1)}, u32[]{:S(2)}, u32[]{:S(2)}) collective-permute-start(bf16[256,768]{1,0:T(8,128)(2,1)S(1)} %bitcast.103), channel_id=1, source_target_pairs={{0,4},{2,6},{4,0},{6,2},{1,5},{3,7},{5,1},{7,3},{8,12},{10,14},{12... | collective-permute-start | bytes 1179656 | tf_op jit(solution)/shard_map/ppermute | solution.py:581
  72.1 32.0 %collective-permute-start.15 = (bf16[256,768]{1,0:T(8,128)(2,1)S(1)}, bf16[256,768]{1,0:T(8,128)(2,1)}, u32[]{:S(2)}, u32[]{:S(2)}) collective-permute-start(bf16[256,768]{1,0:T(8,128)(2,1)S(1)} %bitcast.101), channel_id=1, source_target_pairs={{0,6},{2,4},{4,2},{6,0},{1,7},{3,5},{5,3},{7,1},{8,14},{10,12},{12... | collective-permute-start | bytes 1179656 | tf_op jit(solution)/shard_map/ppermute | solution.py:581
  104.9 2.8 collective-permute-start.20
  104.9 4.5 %collective-permute-start.17 = (bf16[2,192,1536]{2,1,0:T(8,128)(2,1)S(1)}, bf16[2,192,1536]{2,1,0:T(8,128)(2,1)S(1)}, u32[]{:S(2)}, u32[]{:S(2)}) collective-permute-start(bf16[2,192,1536]{2,1,0:T(8,128)(2,1)S(1)} %pad_maximum_fusion.refs_12_), channel_id=1, source_target_pairs={{0,8},{8,0},{16,24},{24,16},{1,9},{9,1},{17,25},{25,17},{2,10},{10... | collective-permute-start | bytes 3538952 | tf_op jit(solution)/shard_map/ppermute | solution.py:603
  105.4 5.7 %collective-permute-start.21 = (bf16[2,192,1536]{2,1,0:T(8,128)(2,1)}, bf16[2,192,1536]{2,1,0:T(8,128)(2,1)S(1)}, u32[]{:S(2)}, u32[]{:S(2)}) collective-permute-start(bf16[2,192,1536]{2,1,0:T(8,128)(2,1)} %collective-permute-done.19.refs_17_), channel_id=1, source_target_pairs={{0,8},{8,0},{16,24},{24,16},{1,9},{9,1},{17,25},{25,17},{2,10},{10... | collective-permute-start | bytes 3538952 | tf_op jit(solution)/shard_map/ppermute | solution.py:603
  105.5 7.3 %collective-permute-start.18 = (bf16[2,192,1536]{2,1,0:T(8,128)(2,1)}, bf16[2,192,1536]{2,1,0:T(8,128)(2,1)S(1)}, u32[]{:S(2)}, u32[]{:S(2)}) collective-permute-start(bf16[2,192,1536]{2,1,0:T(8,128)(2,1)} %collective-permute-done.16.refs_13_), channel_id=1, source_target_pairs={{0,8},{8,0},{16,24},{24,16},{1,9},{9,1},{17,25},{25,17},{2,10},{10... | collective-permute-start | bytes 3538952 | tf_op jit(solution)/shard_map/ppermute | solution.py:603
  160.5 15.1 %collective-permute-start.22 = (bf16[256,768]{1,0:T(8,128)(2,1)}, bf16[256,768]{1,0:T(8,128)(2,1)S(1)}, u32[]{:S(2)}, u32[]{:S(2)}) collective-permute-start(bf16[256,768]{1,0:T(8,128)(2,1)} %get-tuple-element.97), channel_id=1, source_target_pairs={{0,2},{2,0},{4,6},{6,4},{1,3},{3,1},{5,7},{7,5},{8,10},{10,8},{12,... | collective-permute-start | bytes 1179656 | tf_op jit(solution)/shard_map/ppermute | solution.py:581
  175.6 24.7 %collective-permute-start.25 = (bf16[2,2,208,1536]{3,2,1,0:T(8,128)(2,1)}, bf16[2,2,208,1536]{3,2,1,0:T(8,128)(2,1)}, u32[]{:S(2)}, u32[]{:S(2)}) collective-permute-start(bf16[2,2,208,1536]{3,2,1,0:T(8,128)(2,1)} %get-tuple-element.107), channel_id=1, source_target_pairs={{0,8},{8,0},{16,24},{24,16},{1,9},{9,1},{17,25},{25,17},{2,10},{10... | collective-permute-start | bytes 7667720 | tf_op jit(solution)/shard_map/ppermute | solution.py:664
  175.7 15.7 %collective-permute-start.23 = (bf16[256,768]{1,0:T(8,128)(2,1)}, bf16[256,768]{1,0:T(8,128)(2,1)S(1)}, u32[]{:S(2)}, u32[]{:S(2)}) collective-permute-start(bf16[256,768]{1,0:T(8,128)(2,1)} %get-tuple-element.98), channel_id=1, source_target_pairs={{0,6},{2,4},{4,2},{6,0},{1,7},{3,5},{5,3},{7,1},{8,14},{10,12},{12... | collective-permute-start | bytes 1179656 | tf_op jit(solution)/shard_map/ppermute | solution.py:581
  191.4 42.3 %collective-permute-start.26 = (bf16[2,2,208,1536]{3,2,1,0:T(8,128)(2,1)}, bf16[2,2,208,1536]{3,2,1,0:T(8,128)(2,1)}, u32[]{:S(2)}, u32[]{:S(2)}) collective-permute-start(bf16[2,2,208,1536]{3,2,1,0:T(8,128)(2,1)} %get-tuple-element.113), channel_id=1, source_target_pairs={{0,8},{8,0},{16,24},{24,16},{1,9},{9,1},{17,25},{25,17},{2,10},{10... | collective-permute-start | bytes 7667720 | tf_op jit(solution)/shard_map/ppermute | solution.py:664
  191.5 41.6 %collective-permute-start.28 = (bf16[256,768]{1,0:T(8,128)(2,1)S(1)}, bf16[256,768]{1,0:T(8,128)(2,1)}, u32[]{:S(2)}, u32[]{:S(2)}) collective-permute-start(bf16[256,768]{1,0:T(8,128)(2,1)S(1)} %copy-done.32), channel_id=1, source_target_pairs={{0,4},{2,6},{4,0},{6,2},{1,5},{3,7},{5,1},{7,3},{8,12},{10,14},{12... | collective-permute-start | bytes 1179656 | tf_op jit(solution)/shard_map/ppermute | solution.py:581
  199.2 42.6 %collective-permute-start.24 = (bf16[768,768]{1,0:T(8,128)(2,1)}, bf16[768,768]{1,0:T(8,128)(2,1)}, u32[]{:S(2)}, u32[]{:S(2)}) collective-permute-start(bf16[768,768]{1,0:T(8,128)(2,1)} %constant_dynamic-update-slice_fusion), channel_id=1, source_target_pairs={{0,1},{1,0},{2,3},{3,2},{4,5},{5,4},{6,7},{7,6},{8,9},{9,8},{10,11... | collective-permute-start | bytes 3538952 | tf_op jit(solution)/shard_map/ppermute | solution.py:585
  205.4 33.5 %collective-permute-start.27 = (bf16[1,2,208,1536]{3,2,1,0:T(8,128)(2,1)}, bf16[1,2,208,1536]{3,2,1,0:T(8,128)(2,1)}, u32[]{:S(2)}, u32[]{:S(2)}) collective-permute-start(bf16[1,2,208,1536]{3,2,1,0:T(8,128)(2,1)} %split.49), channel_id=1, source_target_pairs={{0,16},{8,24},{16,0},{24,8},{1,17},{9,25},{17,1},{25,9},{2,18},{10... | collective-permute-start | bytes 3833864 | tf_op jit(solution)/shard_map/ppermute | solution.py:603
  233.1 34.4 %collective-permute-start.33 = (bf16[256,768]{1,0:T(8,128)(2,1)}, bf16[256,768]{1,0:T(8,128)(2,1)}, u32[]{:S(2)}, u32[]{:S(2)}) collective-permute-start(bf16[256,768]{1,0:T(8,128)(2,1)} %collective-permute-done.28), channel_id=1, source_target_pairs={{0,1},{1,0},{2,3},{3,2},{4,5},{5,4},{6,7},{7,6},{8,9},{9,8},{10,11... | collective-permute-start | bytes 1179656 | tf_op jit(solution)/shard_map/ppermute | solution.py:585
  238.1 29.7 %collective-permute-start.30 = (bf16[1,2,208,1536]{3,2,1,0:T(8,128)(2,1)}, bf16[1,2,208,1536]{3,2,1,0:T(8,128)(2,1)}, u32[]{:S(2)}, u32[]{:S(2)}) collective-permute-start(bf16[1,2,208,1536]{3,2,1,0:T(8,128)(2,1)} %split.51), channel_id=1, source_target_pairs={{0,16},{8,24},{16,0},{24,8},{1,17},{9,25},{17,1},{25,9},{2,18},{10... | collective-permute-start | bytes 3833864 | tf_op jit(solution)/shard_map/ppermute | solution.py:603
  241.8 28.9 %collective-permute-start.29 = (bf16[1,1,208,1536]{3,2,1,0:T(8,128)(2,1)S(1)}, bf16[1,1,208,1536]{3,2,1,0:T(8,128)(2,1)}, u32[]{:S(2)}, u32[]{:S(2)}) collective-permute-start(bf16[1,1,208,1536]{3,2,1,0:T(8,128)(2,1)S(1)} %split.50), channel_id=1, source_target_pairs={{0,1},{1,0},{2,3},{3,2},{4,5},{5,4},{6,7},{7,6},{8,9},{9,8},{10,11... | collective-permute-start | bytes 1916936 | tf_op jit(solution)/shard_map/ppermute | solution.py:603
  251.9 18.8 %collective-permute-start.31 = (bf16[256,768]{1,0:T(8,128)(2,1)}, bf16[256,768]{1,0:T(8,128)(2,1)S(1)}, u32[]{:S(2)}, u32[]{:S(2)}) collective-permute-start(bf16[256,768]{1,0:T(8,128)(2,1)} %get-tuple-element.122), channel_id=1, source_target_pairs={{0,2},{2,0},{4,6},{6,4},{1,3},{3,1},{5,7},{7,5},{8,10},{10,8},{12,... | collective-permute-start | bytes 1179656 | tf_op jit(solution)/shard_map/ppermute | solution.py:581
  251.9 18.8 %collective-permute-start.32 = (bf16[256,768]{1,0:T(8,128)(2,1)}, bf16[256,768]{1,0:T(8,128)(2,1)}, u32[]{:S(2)}, u32[]{:S(2)}) collective-permute-start(bf16[256,768]{1,0:T(8,128)(2,1)} %get-tuple-element.124), channel_id=1, source_target_pairs={{0,6},{2,4},{4,2},{6,0},{1,7},{3,5},{5,3},{7,1},{8,14},{10,12},{12... | collective-permute-start | bytes 1179656 | tf_op jit(solution)/shard_map/ppermute | solution.py:581
  271.4 5.2 %collective-permute-start.34 = (bf16[2,2,208,1536]{3,2,1,0:T(8,128)(2,1)}, bf16[2,2,208,1536]{3,2,1,0:T(8,128)(2,1)}, u32[]{:S(2)}, u32[]{:S(2)}) collective-permute-start(bf16[2,2,208,1536]{3,2,1,0:T(8,128)(2,1)} %get-tuple-element.129), channel_id=1, source_target_pairs={{0,8},{8,0},{16,24},{24,16},{1,9},{9,1},{17,25},{25,17},{2,10},{10... | collective-permute-start | bytes 7667720 | tf_op jit(solution)/shard_map/ppermute | solution.py:664
  273.2 21.1 %collective-permute-start.39 = (bf16[256,768]{1,0:T(8,128)(2,1)}, bf16[256,768]{1,0:T(8,128)(2,1)S(1)}, u32[]{:S(2)}, u32[]{:S(2)}) collective-permute-start(bf16[256,768]{1,0:T(8,128)(2,1)} %get-tuple-element.138), channel_id=1, source_target_pairs={{0,4},{2,6},{4,0},{6,2},{1,5},{3,7},{5,1},{7,3},{8,12},{10,14},{12... | collective-permute-start | bytes 1179656 | tf_op jit(solution)/shard_map/ppermute | solution.py:581
  294.4 11.2 %collective-permute-start.40 = (bf16[208,384]{1,0:T(8,128)(2,1)S(1)}, bf16[208,384]{1,0:T(8,128)(2,1)S(1)}, u32[]{:S(2)}, u32[]{:S(2)}) collective-permute-start(bf16[208,384]{1,0:T(8,128)(2,1)S(1)} %get-tuple-element.180), channel_id=1, source_target_pairs={{0,2},{2,0},{4,6},{6,4},{1,3},{3,1},{5,7},{7,5},{8,10},{10,8},{12,... | collective-permute-start | bytes 479240 | tf_op jit(solution)/shard_map/ppermute | solution.py:581
  294.5 14.7 %collective-permute-start.41 = (bf16[208,384]{1,0:T(8,128)(2,1)S(1)}, bf16[208,384]{1,0:T(8,128)(2,1)S(1)}, u32[]{:S(2)}, u32[]{:S(2)}) collective-permute-start(bf16[208,384]{1,0:T(8,128)(2,1)S(1)} %get-tuple-element.182), channel_id=1, source_target_pairs={{0,4},{2,6},{4,0},{6,2},{1,5},{3,7},{5,1},{7,3},{8,12},{10,14},{12... | collective-permute-start | bytes 479240 | tf_op jit(solution)/shard_map/ppermute | solution.py:581
  296.6 12.6 %collective-permute-start.42 = (bf16[208,384]{1,0:T(8,128)(2,1)S(1)}, bf16[208,384]{1,0:T(8,128)(2,1)S(1)}, u32[]{:S(2)}, u32[]{:S(2)}) collective-permute-start(bf16[208,384]{1,0:T(8,128)(2,1)S(1)} %get-tuple-element.181), channel_id=1, source_target_pairs={{0,6},{2,4},{4,2},{6,0},{1,7},{3,5},{5,3},{7,1},{8,14},{10,12},{12... | collective-permute-start | bytes 479240 | tf_op jit(solution)/shard_map/ppermute | solution.py:581
  298.9 17.3 %collective-permute-start.38 = (bf16[1,1,208,1536]{3,2,1,0:T(8,128)(2,1)S(1)}, bf16[1,1,208,1536]{3,2,1,0:T(8,128)(2,1)S(1)}, u32[]{:S(2)}, u32[]{:S(2)}) collective-permute-start(bf16[1,1,208,1536]{3,2,1,0:T(8,128)(2,1)S(1)} %split.46), channel_id=1, source_target_pairs={{0,1},{1,0},{2,3},{3,2},{4,5},{5,4},{6,7},{7,6},{8,9},{9,8},{10,11... | collective-permute-start | bytes 1916936 | tf_op jit(solution)/shard_map/ppermute | solution.py:603
  299.5 45.3 %collective-permute-start.36 = (bf16[1,2,208,1536]{3,2,1,0:T(8,128)(2,1)S(1)}, bf16[1,2,208,1536]{3,2,1,0:T(8,128)(2,1)S(1)}, u32[]{:S(2)}, u32[]{:S(2)}) collective-permute-start(bf16[1,2,208,1536]{3,2,1,0:T(8,128)(2,1)S(1)} %split.53), channel_id=1, source_target_pairs={{0,16},{8,24},{16,0},{24,8},{1,17},{9,25},{17,1},{25,9},{2,18},{10... | collective-permute-start | bytes 3833864 | tf_op jit(solution)/shard_map/ppermute | solution.py:603
  305.6 63.8 %collective-permute-start.35 = (bf16[768,768]{1,0:T(8,128)(2,1)S(1)}, bf16[768,768]{1,0:T(8,128)(2,1)S(1)}, u32[]{:S(2)}, u32[]{:S(2)}) collective-permute-start(bf16[768,768]{1,0:T(8,128)(2,1)S(1)} %constant_dynamic-update-slice_fusion.3), channel_id=1, source_target_pairs={{0,1},{1,0},{2,3},{3,2},{4,5},{5,4},{6,7},{7,6},{8,9},{9,8},{10,11... | collective-permute-start | bytes 3538952 | tf_op jit(solution)/shard_map/ppermute | solution.py:585
  316.4 7.0 %collective-permute-start.43 = (bf16[208,384]{1,0:T(8,128)(2,1)S(1)}, bf16[208,384]{1,0:T(8,128)(2,1)S(1)}, u32[]{:S(2)}, u32[]{:S(2)}) collective-permute-start(bf16[208,384]{1,0:T(8,128)(2,1)S(1)} %get-tuple-element.177), channel_id=1, source_target_pairs={{0,2},{2,0},{4,6},{6,4},{1,3},{3,1},{5,7},{7,5},{8,10},{10,8},{12,... | collective-permute-start | bytes 479240 | tf_op jit(solution)/shard_map/ppermute | solution.py:581
  316.5 11.4 %collective-permute-start.44 = (bf16[208,384]{1,0:T(8,128)(2,1)S(1)}, bf16[208,384]{1,0:T(8,128)(2,1)S(1)}, u32[]{:S(2)}, u32[]{:S(2)}) collective-permute-start(bf16[208,384]{1,0:T(8,128)(2,1)S(1)} %get-tuple-element.179), channel_id=1, source_target_pairs={{0,4},{2,6},{4,0},{6,2},{1,5},{3,7},{5,1},{7,3},{8,12},{10,14},{12... | collective-permute-start | bytes 479240 | tf_op jit(solution)/shard_map/ppermute | solution.py:581
  318.6 9.3 %collective-permute-start.45 = (bf16[208,384]{1,0:T(8,128)(2,1)S(1)}, bf16[208,384]{1,0:T(8,128)(2,1)S(1)}, u32[]{:S(2)}, u32[]{:S(2)}) collective-permute-start(bf16[208,384]{1,0:T(8,128)(2,1)S(1)} %get-tuple-element.178), channel_id=1, source_target_pairs={{0,6},{2,4},{4,2},{6,0},{1,7},{3,5},{5,3},{7,1},{8,14},{10,12},{12... | collective-permute-start | bytes 479240 | tf_op jit(solution)/shard_map/ppermute | solution.py:581
  328.0 6.9 %collective-permute-start.53 = (bf16[208,384]{1,0:T(8,128)(2,1)S(1)}, bf16[208,384]{1,0:T(8,128)(2,1)S(1)}, u32[]{:S(2)}, u32[]{:S(2)}) collective-permute-start(bf16[208,384]{1,0:T(8,128)(2,1)S(1)} %add_convert_fusion.11), channel_id=1, source_target_pairs={{0,2},{2,0},{4,6},{6,4},{1,3},{3,1},{5,7},{7,5},{8,10},{10,8},{12,... | collective-permute-start | bytes 479240 | tf_op jit(solution)/shard_map/ppermute | solution.py:581
  330.4 13.1 %collective-permute-start.54 = (bf16[208,384]{1,0:T(8,128)(2,1)S(1)}, bf16[208,384]{1,0:T(8,128)(2,1)S(1)}, u32[]{:S(2)}, u32[]{:S(2)}) collective-permute-start(bf16[208,384]{1,0:T(8,128)(2,1)S(1)} %add_convert_fusion.11), channel_id=1, source_target_pairs={{0,4},{2,6},{4,0},{6,2},{1,5},{3,7},{5,1},{7,3},{8,12},{10,14},{12... | collective-permute-start | bytes 479240 | tf_op jit(solution)/shard_map/ppermute | solution.py:581
  330.5 13.0 %collective-permute-start.55 = (bf16[208,384]{1,0:T(8,128)(2,1)S(1)}, bf16[208,384]{1,0:T(8,128)(2,1)S(1)}, u32[]{:S(2)}, u32[]{:S(2)}) collective-permute-start(bf16[208,384]{1,0:T(8,128)(2,1)S(1)} %add_convert_fusion.11), channel_id=1, source_target_pairs={{0,6},{2,4},{4,2},{6,0},{1,7},{3,5},{5,3},{7,1},{8,14},{10,12},{12... | collective-permute-start | bytes 479240 | tf_op jit(solution)/shard_map/ppermute | solution.py:581
  345.1 7.3 %collective-permute-start.56 = (bf16[208,384]{1,0:T(8,128)(2,1)S(1)}, bf16[208,384]{1,0:T(8,128)(2,1)S(1)}, u32[]{:S(2)}, u32[]{:S(2)}) collective-permute-start(bf16[208,384]{1,0:T(8,128)(2,1)S(1)} %add_convert_fusion.10), channel_id=1, source_target_pairs={{0,2},{2,0},{4,6},{6,4},{1,3},{3,1},{5,7},{7,5},{8,10},{10,8},{12,... | collective-permute-start | bytes 479240 | tf_op jit(solution)/shard_map/ppermute | solution.py:581
  348.5 13.1 %collective-permute-start.57 = (bf16[208,384]{1,0:T(8,128)(2,1)S(1)}, bf16[208,384]{1,0:T(8,128)(2,1)S(1)}, u32[]{:S(2)}, u32[]{:S(2)}) collective-permute-start(bf16[208,384]{1,0:T(8,128)(2,1)S(1)} %add_convert_fusion.10), channel_id=1, source_target_pairs={{0,4},{2,6},{4,0},{6,2},{1,5},{3,7},{5,1},{7,3},{8,12},{10,14},{12... | collective-permute-start | bytes 479240 | tf_op jit(solution)/shard_map/ppermute | solution.py:581
  348.7 15.0 %collective-permute-start.37 = (bf16[1,1,208,1536]{3,2,1,0:T(8,128)(2,1)S(1)}, bf16[1,1,208,1536]{3,2,1,0:T(8,128)(2,1)S(1)}, u32[]{:S(2)}, u32[]{:S(2)}) collective-permute-start(bf16[1,1,208,1536]{3,2,1,0:T(8,128)(2,1)S(1)} %split.55), channel_id=1, source_target_pairs={{0,1},{1,0},{2,3},{3,2},{4,5},{5,4},{6,7},{7,6},{8,9},{9,8},{10,11... | collective-permute-start | bytes 1916936 | tf_op jit(solution)/shard_map/ppermute | solution.py:603
  349.3 12.3 %collective-permute-start.58 = (bf16[208,384]{1,0:T(8,128)(2,1)S(1)}, bf16[208,384]{1,0:T(8,128)(2,1)S(1)}, u32[]{:S(2)}, u32[]{:S(2)}) collective-permute-start(bf16[208,384]{1,0:T(8,128)(2,1)S(1)} %add_convert_fusion.10), channel_id=1, source_target_pairs={{0,6},{2,4},{4,2},{6,0},{1,7},{3,5},{5,3},{7,1},{8,14},{10,12},{12... | collective-permute-start | bytes 479240 | tf_op jit(solution)/shard_map/ppermute | solution.py:581
  363.9 7.5 %collective-permute-start.47 = (bf16[208,384]{1,0:T(8,128)(2,1)S(1)}, bf16[208,384]{1,0:T(8,128)(2,1)S(1)}, u32[]{:S(2)}, u32[]{:S(2)}) collective-permute-start(bf16[208,384]{1,0:T(8,128)(2,1)S(1)} %get-tuple-element.174), channel_id=1, source_target_pairs={{0,2},{2,0},{4,6},{6,4},{1,3},{3,1},{5,7},{7,5},{8,10},{10,8},{12,... | collective-permute-start | bytes 479240 | tf_op jit(solution)/shard_map/ppermute | solution.py:581
  366.9 13.3 %collective-permute-start.48 = (bf16[208,384]{1,0:T(8,128)(2,1)S(1)}, bf16[208,384]{1,0:T(8,128)(2,1)S(1)}, u32[]{:S(2)}, u32[]{:S(2)}) collective-permute-start(bf16[208,384]{1,0:T(8,128)(2,1)S(1)} %get-tuple-element.176), channel_id=1, source_target_pairs={{0,4},{2,6},{4,0},{6,2},{1,5},{3,7},{5,1},{7,3},{8,12},{10,14},{12... | collective-permute-start | bytes 479240 | tf_op jit(solution)/shard_map/ppermute | solution.py:581
  367.1 13.1 %collective-permute-start.49 = (bf16[208,384]{1,0:T(8,128)(2,1)S(1)}, bf16[208,384]{1,0:T(8,128)(2,1)S(1)}, u32[]{:S(2)}, u32[]{:S(2)}) collective-permute-start(bf16[208,384]{1,0:T(8,128)(2,1)S(1)} %get-tuple-element.175), channel_id=1, source_target_pairs={{0,6},{2,4},{4,2},{6,0},{1,7},{3,5},{5,3},{7,1},{8,14},{10,12},{12... | collective-permute-start | bytes 479240 | tf_op jit(solution)/shard_map/ppermute | solution.py:581
  369.5 31.2 %collective-permute-start.46 = (bf16[256,768]{1,0:T(8,128)(2,1)S(1)}, bf16[256,768]{1,0:T(8,128)(2,1)S(1)}, u32[]{:S(2)}, u32[]{:S(2)}) collective-permute-start(bf16[256,768]{1,0:T(8,128)(2,1)S(1)} %collective-permute-done.39), channel_id=1, source_target_pairs={{0,1},{1,0},{2,3},{3,2},{4,5},{5,4},{6,7},{7,6},{8,9},{9,8},{10,11... | collective-permute-start | bytes 1179656 | tf_op jit(solution)/shard_map/ppermute | solution.py:585
  380.3 8.1 %collective-permute-start.50 = (bf16[208,384]{1,0:T(8,128)(2,1)S(1)}, bf16[208,384]{1,0:T(8,128)(2,1)S(1)}, u32[]{:S(2)}, u32[]{:S(2)}) collective-permute-start(bf16[208,384]{1,0:T(8,128)(2,1)S(1)} %get-tuple-element.150), channel_id=1, source_target_pairs={{0,2},{2,0},{4,6},{6,4},{1,3},{3,1},{5,7},{7,5},{8,10},{10,8},{12,... | collective-permute-start | bytes 479240 | tf_op jit(solution)/shard_map/ppermute | solution.py:581
  383.7 13.7 %collective-permute-start.51 = (bf16[208,384]{1,0:T(8,128)(2,1)S(1)}, bf16[208,384]{1,0:T(8,128)(2,1)S(1)}, u32[]{:S(2)}, u32[]{:S(2)}) collective-permute-start(bf16[208,384]{1,0:T(8,128)(2,1)S(1)} %get-tuple-element.150), channel_id=1, source_target_pairs={{0,4},{2,6},{4,0},{6,2},{1,5},{3,7},{5,1},{7,3},{8,12},{10,14},{12... | collective-permute-start | bytes 479240 | tf_op jit(solution)/shard_map/ppermute | solution.py:581
  383.7 13.6 %collective-permute-start.52 = (bf16[208,384]{1,0:T(8,128)(2,1)S(1)}, bf16[208,384]{1,0:T(8,128)(2,1)S(1)}, u32[]{:S(2)}, u32[]{:S(2)}) collective-permute-start(bf16[208,384]{1,0:T(8,128)(2,1)S(1)} %get-tuple-element.150), channel_id=1, source_target_pairs={{0,6},{2,4},{4,2},{6,0},{1,7},{3,5},{5,3},{7,1},{8,14},{10,12},{12... | collective-permute-start | bytes 479240 | tf_op jit(solution)/shard_map/ppermute | solution.py:581
  (31 other events, 358.8 us)

commit v8 on v7

--- a/solution.py
+++ b/solution.py
@@ -628,7 +628,8 @@
     for k in [*range(3, C, 2), *range(2, C, 2)]:
         x_pieces[k] = ctx_moved(after(x_pieces[k], before), k)
         before = [x_pieces[k]]
-    vectors = jnp.stack([output_bias, attn_gain, attn_shift, outer_bias, ffn_gain, ffn_shift])
+    vectors = [output_bias, attn_gain, attn_shift, outer_bias, ffn_gain, ffn_shift]
+    vectors = jnp.concatenate(vectors).reshape(len(vectors), Dl)
     small = [
         spread(query_bias, half), spread(value_bias, half), spread(inner_bias, fhalf),
         spread(vectors, D),
@@ -678,20 +679,27 @@
     def x_sum(total):
         return chip_sum(total, "tp", 1)
 
-    def ctx_scatter(total):
-        part = total.shape[1] // C
-        mine = 0.0
+    def ctx_scatter(totals):
+        part = totals[0].shape[1] // C
+        sums_in = []
         for k in range(C):
-            block = lax.dynamic_slice_in_dim(total, (c ^ k) * part, part, 1)
-            mine += ctx_moved(block, k).astype(F32)
-        return mine.astype(BF)
-
-    def ctx_gather(mine, like):
-        part = mine.shape[1]
-        out = like
+            blocks = [lax.dynamic_slice_in_dim(a, (c ^ k) * part, part, 1) for a in totals]
+            block = jnp.concatenate(blocks, axis=0) if len(blocks) > 1 else blocks[0]
+            sums_in.append(ctx_moved(block, k).astype(F32))
+        while len(sums_in) > 1:
+            sums_in = [a + b for a, b in zip(sums_in[::2], sums_in[1::2])]
+        return sums_in[0].astype(BF)
+
+    def ctx_gather(mine, likes):
+        rows, part = likes[0].shape[0], mine.shape[1]
+        outs = list(likes)
         for k in range(C):
-            out = lax.dynamic_update_slice_in_dim(out, ctx_moved(mine, k), (c ^ k) * part, 1)
-        return out.astype(F32)
+            got = ctx_moved(mine, k)
+            for i in range(len(likes)):
+                outs[i] = lax.dynamic_update_slice_in_dim(
+                    outs[i], got[i * rows : (i + 1) * rows], (c ^ k) * part, 1
+                )
+        return [out.astype(F32) for out in outs]
 
     outer_parts = weight_call(dims, meta, [(og, act)], sums)
     inner_parts = weight_call(dims, meta, [(after(nl, outer_parts), inner_low)])
@@ -719,24 +727,22 @@
     qkv_core = core_sum(keep, send)
     for k in even:
         ig[k] = ctx_moved(after(ins[k], ig[1::2]), k)
-    outer_x = after(outer_x[0, 0], [qkv_core] + [ig[k] for k in even])
-    outer_part = ctx_scatter(outer_x)
+    outer_x = after(outer_x[0, 0], [qkv_core])
     early_ig = tp_moved(after(tuple(ig[k] for k in early), [qkv_core]))
     qkv_y, _ = y_sum(qkv_core)
     inner_x, _ = x_sum(after(inner_y, [qkv_core]))
-    inner_x = after(inner_x[0, 0], [outer_part])
-    inner_part = ctx_scatter(inner_x)
-    outer_g = ctx_gather(after(outer_part, [inner_part]), outer_x)
+    inner_x = inner_x[0, 0]
+    two_parts = ctx_scatter([outer_x, inner_x])
+    outer_g, inner_g = ctx_gather(after(two_parts, [qkv_y] + [ig[k] for k in even]), [outer_x, inner_x])
     qkv_x, _ = x_sum(qkv_y)
-    qkv_x = after(qkv_x[0, 0], [inner_part])
-    qkv_part = ctx_scatter(qkv_x)
+    qkv_x = after(qkv_x[0, 0], [two_parts])
+    qkv_part = ctx_scatter([qkv_x])
     late_ig = tp_moved([after(ig[k], [qkv_x]) for k in even])
     early_lo, late_lo = (after(tuple(part), [qkv_core]) for part in (early_lo, late_lo))
     early_ig = after(tuple(early_ig), [qkv_x])
     layer_out = to_slots([(early, early_lo), (list(even), late_lo)], BF)
     input_grad = to_slots([(early, early_ig), (list(even), late_ig)], F32)
-    inner_g = ctx_gather(after(inner_part, [qkv_y]), inner_x)
-    qkv_g = ctx_gather(qkv_part, qkv_x)
+    (qkv_g,) = ctx_gather(qkv_part, [qkv_x])
 
     def own(row, shape):
         whole = row.reshape(shape[0], shape[1] * F)

time: 405 us -> 398 us (0.983)
  starting transfers between devices: 80 us -> 73.8 us
    ppermute x30 -> x24, starting transfers between devices: 59.9 us -> 54.7 us  [ctx_moved(): return lax.ppermute(piece, 'ctx', xor_pairs(C, k)) if k else piece]
    ppermute x30 -> x24, waiting for transfers between devices: 90.8 us -> 86 us  [ctx_moved(): return lax.ppermute(piece, 'ctx', xor_pairs(C, k)) if k else piece]
    concatenate x0 -> x1, local copies, waits for them, and re-layouts: none -> 4.09 us  [per_device(): vectors = jnp.concatenate(vectors).reshape(len(vectors), Dl)]
    convert_element_type x6 -> x7, other arithmetic: 11.7 us -> 11.9 us  [added(): return (a.astype(F32) + b.astype(F32)).astype(BF)]
  transfers between devices with their start and end apart: 59 -> 53, of which waited for: 28 -> 24; matrix products, arithmetic and copies ran while one was open for 10% -> 10% of each run, Pallas kernels for 26% -> 26%
where the time goes in v8:
time: 398 us; the launch traced here: 397 us
  Pallas kernels  151 us (38%)
  waiting for transfers between devices  112 us (28%)
  starting transfers between devices  73.8 us (19%)
  local copies, waits for them, and re-layouts  37.5 us (9%)
  other arithmetic  20.2 us (5%)
    ppermute x24, waiting for transfers between devices, ctx_moved(): return lax.ppermute(piece, 'ctx', xor_pairs(C, k)) if k else piece  86 us
    ppermute x24, starting transfers between devices, ctx_moved(): return lax.ppermute(piece, 'ctx', xor_pairs(C, k)) if k else piece  54.7 us
    pallas_call x1, Pallas kernels, rows_call(): pl.pallas_call(functools.partial(rows_kernel, dims, FF), name='rows', gri...  46.7 us
    pallas_call x3, Pallas kernels, weight_call(): pl.pallas_call(functools.partial(weight_kernel, F, pers, sums is not None...  40.1 us
    pallas_call x1, Pallas kernels, front_call(): pl.pallas_call(functools.partial(front_kernel, dims), name='front', grid=...  29.9 us
    pallas_call x1, Pallas kernels, back_call(): pl.pallas_call(functools.partial(back_kernel, dims), name='back', grid=(n...  26.2 us
    ppermute x22, waiting for transfers between devices, swapped(): return lax.ppermute(array, axis, xor_pairs(lax.axis_size(axis), bit))  25.3 us
    ppermute x22, starting transfers between devices, swapped(): return lax.ppermute(array, axis, xor_pairs(lax.axis_size(axis), bit))  16.1 us
  transfers between devices with their start and end apart: 53, of which 24 were waited for; matrix products, arithmetic and copies ran while one was open for 10% of the time, Pallas kernels for 26%

profile of v8, /device:TPU:0, one launch (start us, length us, event | category | flops | bytes accessed | tf_op | source)
XLA Modules:
  0.0 396.8 jit_solution(3047190596687793972)
XLA Ops:
  2.4 4.1 %concatenate.53 = bf16[1152]{0:T(1024)(128)(2,1)S(1)} concatenate(bf16[192]{0:T(256)(128)(2,1)} %param.26, bf16[192]{0:T(256)(128)(2,1)} %param.27, bf16[192]{0:T(256)(128)(2,1)} %param.28, bf16[192]{0:T(256)(128)(2,1)} %param.32, bf16[192]{0:T(256)(128)(2,1)} %param.33, bf16[192]{0:T(256)(128)(2,1)} %param.34), dimensions={0} | concatenate | bytes 4608 | tf_op jit(solution)/shard_map/concatenate | solution.py:632
  8.6 3.0 collective-permute-start
  12.6 1.6 collective-permute-start.3
  14.2 2.3 constant_dynamic-slice_fusion.15
  16.5 1.6 collective-permute-start.1
  19.2 2.5 collective-permute-done.3
  21.8 5.0 %collective-permute-done.1.refs_1_ = bf16[256,768]{1,0:T(8,128)(2,1)S(1)} collective-permute-done((bf16[256,768]{1,0:T(8,128)(2,1)S(1)}, bf16[256,768]{1,0:T(8,128)(2,1)S(1)}, u32[]{:S(2)}, u32[]{:S(2)}) %collective-permute-start.1) | collective-permute-done | bytes 393248 | tf_op jit(solution)/shard_map/ppermute | solution.py:581
  27.7 3.8 collective-permute-start.5
  31.5 7.3 %collective-permute-done.5.refs_3_ = bf16[256,768]{1,0:T(8,128)(2,1)S(1)} collective-permute-done((bf16[256,768]{1,0:T(8,128)(2,1)S(1)}, bf16[256,768]{1,0:T(8,128)(2,1)S(1)}, u32[]{:S(2)}, u32[]{:S(2)}) %collective-permute-start.5) | collective-permute-done | bytes 393248 | tf_op jit(solution)/shard_map/ppermute | solution.py:581
  38.8 2.7 collective-permute-done.2.refs_5_
  41.8 1.5 collective-permute-start.7
  43.8 7.1 %collective-permute-start.8 = (bf16[256,768]{1,0:T(8,128)(2,1)S(1)}, bf16[256,768]{1,0:T(8,128)(2,1)S(1)}, u32[]{:S(2)}, u32[]{:S(2)}) collective-permute-start(bf16[256,768]{1,0:T(8,128)(2,1)S(1)} %bitcast.108), channel_id=1, source_target_pairs={{0,4},{2,6},{4,0},{6,2},{1,5},{3,7},{5,1},{7,3},{8,12},{10,14},{12... | collective-permute-start | bytes 1179656 | tf_op jit(solution)/shard_map/ppermute | solution.py:581
  51.4 3.0 collective-permute-done.7
  54.5 11.6 %collective-permute-done.8.refs_2_ = bf16[256,768]{1,0:T(8,128)(2,1)S(1)} collective-permute-done((bf16[256,768]{1,0:T(8,128)(2,1)S(1)}, bf16[256,768]{1,0:T(8,128)(2,1)S(1)}, u32[]{:S(2)}, u32[]{:S(2)}) %collective-permute-start.8) | collective-permute-done | bytes 393248 | tf_op jit(solution)/shard_map/ppermute | solution.py:581
  68.3 1.1 constant_dynamic-slice_fusion.11
  69.4 2.9 collective-permute-start.14
  72.3 1.5 collective-permute-start.15
  74.4 29.9 %front.1 = (bf16[4,256,768]{2,1,0:T(8,128)(2,1)}, bf16[768,2304]{1,0:T(8,128)(2,1)}, bf16[4,2,128,2304]{3,2,1,0:T(8,128)(2,1)}, bf16[12,1024,512]{2,1,0:T(8,128)...) custom-call(s32[4]{0:T(128)} %pad_add_fusion.meta, bf16[256,768]{1,0:T(8,128)(2,1)} %bitcast.106, ...), custom_call_target="tpu_custom_call" | custom-call | flops 3623878656 | bytes 40000000 | tf_op jit(solution)/shard_map/front/pallas_call | solution.py:162
  106.2 1.8 collective-permute-done.20.refs_18_
  108.0 1.7 collective-permute-done.17.refs_14_
  114.1 46.7 %rows.1 = (bf16[256,768]{1,0:T(8,128)(2,1)}, bf16[256,768]{1,0:T(8,128)(2,1)}, bf16[256,768]{1,0:T(8,128)(2,1)}, bf16[256,768]{1,0:T(8,128)(2,1)}, f32[4,256,768...) custom-call(s32[4]{0:T(128)} %pad_add_fusion.meta, ...), custom_call_target="tpu_custom_call" | custom-call | flops 21743271936 | bytes 50000000 | tf_op jit(solution)/shard_map/rows/pallas_call | solution.py:344
  160.7 2.3 collective-permute-start.22
  163.1 12.9 %weight_grad.3 = (bf16[2,2,208,1536]{3,2,1,0:T(8,128)(2,1)}, bf16[2,2,208,1536]{3,2,1,0:T(8,128)(2,1)}) custom-call(s32[4]{0:T(128)} %pad_add_fusion.meta, bf16[1024,768]{1,0:T(8,128)(2,1)} %bitcast.126, bf16[1024,3072]{1,0:T(8,128)(2,1)} %bitcast.122, f32[16,768]{1,0:T(8,128)} %get-tuple-element.102.refs_2_), custom_call_target="tpu_custom_call" | custom-call | flops 4831838208 | bytes 12582912 | tf_op jit(solution)/shard_map/weight_grad/pallas_call | solution.py:523
  176.0 2.5 collective-permute-start.23
  178.5 13.2 %weight_grad.4 = (bf16[2,2,208,1536]{3,2,1,0:T(8,128)(2,1)}, bf16[2,2,208,1536]{3,2,1,0:T(8,128)(2,1)}) custom-call(s32[4]{0:T(128)} %pad_add_fusion.meta, bf16[1024,768]{1,0:T(8,128)(2,1)} %bitcast.125, bf16[1024,3072]{1,0:T(8,128)(2,1)} %bitcast.121), custom_call_target="tpu_custom_call" | custom-call | flops 4831838208 | bytes 12582912 | tf_op jit(solution)/shard_map/weight_grad/pallas_call | solution.py:523
  191.8 5.3 %collective-permute-start.28 = (bf16[256,768]{1,0:T(8,128)(2,1)S(1)}, bf16[256,768]{1,0:T(8,128)(2,1)}, u32[]{:S(2)}, u32[]{:S(2)}) collective-permute-start(bf16[256,768]{1,0:T(8,128)(2,1)S(1)} %copy-done.32), channel_id=1, source_target_pairs={{0,4},{2,6},{4,0},{6,2},{1,5},{3,7},{5,1},{7,3},{8,12},{10,14},{12... | collective-permute-start | bytes 1179656 | tf_op jit(solution)/shard_map/ppermute | solution.py:581
  199.5 1.2 collective-permute-start.24
  200.7 2.4 add_convert_fusion.2
  203.1 1.5 copy-done
  204.5 1.1 split.49
  205.7 1.5 collective-permute-start.27
  207.2 26.2 %back.1 = bf16[4,2,128,2304]{3,2,1,0:T(8,128)(2,1)} custom-call(bf16[4,2,128,2304]{3,2,1,0:T(8,128)(2,1)} %get-tuple-element.98.qkv, bf16[4,2,128,768]{3,2,1,0:T(8,128)(2,1)} %get-tuple-element.88.ctx, bf16[4,2,128,768]{3,2,1,0:T(8,128)(2,1)} %bitcast.87, bf16[12,1024,512]{2,1,0:T(8,128)(2,1)} %get-tuple-element.113.e_ref, ...), custom_call_target="tpu_custom_call" | custom-call | flops 6442450944 | bytes 30000000 | tf_op jit(solution)/shard_map/back/pallas_call | solution.py:413
  233.9 3.2 add_convert_fusion.1
  237.1 1.1 split.51
  239.3 1.6 add_convert_fusion.5
  242.1 1.6 collective-permute-start.29
  243.6 8.6 %input_grad.1 = (bf16[256,768]{1,0:T(8,128)(2,1)}, bf16[256,768]{1,0:T(8,128)(2,1)}, bf16[256,768]{1,0:T(8,128)(2,1)}, bf16[256,768]{1,0:T(8,128)(2,1)}) custom-call(bf16[4,256,2304]{2,1,0:T(8,128)(2,1)} %bitcast.83, bf16[768,2304]{1,0:T(8,128)(2,1)} %get-tuple-element.115.w, f32[4,256,768]{2,1,0:T(8,128)} %get-tuple-element.118.first), custom_call_target="tpu_custom_call" | custom-call | flops 3623878656 | bytes 15000000 | tf_op jit(solution)/shard_map/input_grad/pallas_call | solution.py:450
  252.3 1.5 collective-permute-start.32
  253.7 14.1 %weight_grad.5 = (bf16[2,2,208,1536]{3,2,1,0:T(8,128)(2,1)}, bf16[2,2,208,1536]{3,2,1,0:T(8,128)(2,1)}) custom-call(s32[4]{0:T(128)} %pad_add_fusion.meta, bf16[1024,768]{1,0:T(8,128)(2,1)} %bitcast.123, bf16[1024,768]{1,0:T(8,128)(2,1)} %bitcast.124, bf16[1024,2304]{1,0:T(8,128)(2,1)} %bitcast.84, bf16[1024,768]{1,0:T(8,128)(2,1)} %bitcast.86), custom_call_target="tpu_custom_call" | custom-call | flops 4831838208 | bytes 12582912 | tf_op jit(solution)/shard_map/weight_grad/pallas_call | solution.py:523
  268.0 3.0 collective-permute-done.31
  271.8 1.8 add_convert_fusion.3
  273.5 1.2 collective-permute-start.42
  274.7 1.2 fusion.1
  276.9 2.4 add_convert_fusion
  280.9 1.3 fusion.17
  282.3 1.3 fusion.16
  285.2 10.8 %collective-permute-done.38 = bf16[1,1,208,1536]{3,2,1,0:T(8,128)(2,1)S(1)} collective-permute-done((bf16[1,1,208,1536]{3,2,1,0:T(8,128)(2,1)S(1)}, bf16[1,1,208,1536]{3,2,1,0:T(8,128)(2,1)S(1)}, u32[]{:S(2)}, u32[]{:S(2)}) %collective-permute-start.38) | collective-permute-done | bytes 639008 | tf_op jit(solution)/shard_map/ppermute | solution.py:603
  296.3 1.2 collective-permute-start.39
  298.6 2.3 collective-permute-start.41
  303.0 7.3 %collective-permute-done.39 = bf16[416,384]{1,0:T(8,128)(2,1)S(1)} collective-permute-done((bf16[416,384]{1,0:T(8,128)(2,1)S(1)}, bf16[416,384]{1,0:T(8,128)(2,1)S(1)}, u32[]{:S(2)}, u32[]{:S(2)}) %collective-permute-start.39) | collective-permute-done | bytes 319520 | tf_op jit(solution)/shard_map/ppermute | solution.py:581
  310.8 11.7 %collective-permute-done.40 = bf16[416,384]{1,0:T(8,128)(2,1)S(1)} collective-permute-done((bf16[416,384]{1,0:T(8,128)(2,1)S(1)}, bf16[416,384]{1,0:T(8,128)(2,1)S(1)}, u32[]{:S(2)}, u32[]{:S(2)}) %collective-permute-start.40) | collective-permute-done | bytes 319520 | tf_op jit(solution)/shard_map/ppermute | solution.py:581
  323.1 5.6 %collective-permute-start.50 = (bf16[416,384]{1,0:T(8,128)(2,1)S(1)}, bf16[416,384]{1,0:T(8,128)(2,1)S(1)}, u32[]{:S(2)}, u32[]{:S(2)}) collective-permute-start(bf16[416,384]{1,0:T(8,128)(2,1)S(1)} %add_convert_fusion.9), channel_id=1, source_target_pairs={{0,2},{2,0},{4,6},{6,4},{1,3},{3,1},{5,7},{7,5},{8,10},{10,8},{12,... | collective-permute-start | bytes 958472 | tf_op jit(solution)/shard_map/ppermute | solution.py:581
  328.8 2.4 collective-permute-start.52
  331.8 7.5 %collective-permute-done.50 = bf16[416,384]{1,0:T(8,128)(2,1)S(1)} collective-permute-done((bf16[416,384]{1,0:T(8,128)(2,1)S(1)}, bf16[416,384]{1,0:T(8,128)(2,1)S(1)}, u32[]{:S(2)}, u32[]{:S(2)}) %collective-permute-start.50) | collective-permute-done | bytes 319520 | tf_op jit(solution)/shard_map/ppermute | solution.py:581
  339.3 14.2 %collective-permute-done.51 = bf16[416,384]{1,0:T(8,128)(2,1)S(1)} collective-permute-done((bf16[416,384]{1,0:T(8,128)(2,1)S(1)}, bf16[416,384]{1,0:T(8,128)(2,1)S(1)}, u32[]{:S(2)}, u32[]{:S(2)}) %collective-permute-start.51) | collective-permute-done | bytes 319520 | tf_op jit(solution)/shard_map/ppermute | solution.py:581
  355.4 1.1 slice.165
  357.8 4.6 %collective-permute-start.44 = (bf16[208,384]{1,0:T(8,128)(2,1)S(1)}, bf16[208,384]{1,0:T(8,128)(2,1)S(1)}, u32[]{:S(2)}, u32[]{:S(2)}) collective-permute-start(bf16[208,384]{1,0:T(8,128)(2,1)S(1)} %get-tuple-element.170), channel_id=1, source_target_pairs={{0,2},{2,0},{4,6},{6,4},{1,3},{3,1},{5,7},{7,5},{8,10},{10,8},{12,... | collective-permute-start | bytes 479240 | tf_op jit(solution)/shard_map/ppermute | solution.py:581
  362.4 2.4 collective-permute-start.46
  366.5 2.5 collective-permute-done.44
  369.0 5.3 %collective-permute-done.45 = bf16[208,384]{1,0:T(8,128)(2,1)S(1)} collective-permute-done((bf16[208,384]{1,0:T(8,128)(2,1)S(1)}, bf16[208,384]{1,0:T(8,128)(2,1)S(1)}, u32[]{:S(2)}, u32[]{:S(2)}) %collective-permute-start.45) | collective-permute-done | bytes 159776 | tf_op jit(solution)/shard_map/ppermute | solution.py:581
  374.4 3.0 collective-permute-start.47
  377.4 2.5 collective-permute-start.49
  379.9 1.9 collective-permute-done.47
  381.9 8.7 %collective-permute-done.48 = bf16[208,384]{1,0:T(8,128)(2,1)S(1)} collective-permute-done((bf16[208,384]{1,0:T(8,128)(2,1)S(1)}, bf16[208,384]{1,0:T(8,128)(2,1)S(1)}, u32[]{:S(2)}, u32[]{:S(2)}) %collective-permute-start.48) | collective-permute-done | bytes 159776 | tf_op jit(solution)/shard_map/ppermute | solution.py:581
  (229 shorter events, 43.8 us)
Async XLA Ops:
  8.6 10.6 %collective-permute-start = (bf16[1,208,768]{2,1,0:T(8,128)(2,1)S(1)}, bf16[1,208,768]{2,1,0:T(8,128)(2,1)S(1)}, u32[]{:S(2)}, u32[]{:S(2)}) collective-permute-start(bf16[1,208,768]{2,1,0:T(8,128)(2,1)S(1)} %maximum_bitcast_fusion), channel_id=1, source_target_pairs={{0,1},{1,0},{2,3},{3,2},{4,5},{5,4},{6,7},{7,6},{8,9},{9,8},{10,11... | collective-permute-start | bytes 958472 | tf_op jit(solution)/shard_map/ppermute | solution.py:603
  12.6 9.1 %collective-permute-start.3 = (bf16[1,208,768]{2,1,0:T(8,128)(2,1)S(1)}, bf16[1,208,768]{2,1,0:T(8,128)(2,1)S(1)}, u32[]{:S(2)}, u32[]{:S(2)}) collective-permute-start(bf16[1,208,768]{2,1,0:T(8,128)(2,1)S(1)} %maximum_bitcast_fusion.1), channel_id=1, source_target_pairs={{0,16},{8,24},{16,0},{24,8},{1,17},{9,25},{17,1},{25,9},{2,18},{10... | collective-permute-start | bytes 958472 | tf_op jit(solution)/shard_map/ppermute | solution.py:603
  14.2 27.5 %copy-start.13 = (bf16[1536,192]{0,1:T(8,128)(2,1)S(1)}, bf16[1536,192]{0,1:T(8,128)(2,1)}, u32[]{:S(2)}) copy-start(bf16[1536,192]{0,1:T(8,128)(2,1)} %param.31) | copy-start | bytes 1769476
  14.2 29.1 %copy-start.14 = (bf16[192,1536]{1,0:T(8,128)(2,1)S(1)}, bf16[192,1536]{1,0:T(8,128)(2,1)}, u32[]{:S(2)}) copy-start(bf16[192,1536]{1,0:T(8,128)(2,1)} %param.29) | copy-start | bytes 1769476
  16.5 10.3 %collective-permute-start.1 = (bf16[256,768]{1,0:T(8,128)(2,1)S(1)}, bf16[256,768]{1,0:T(8,128)(2,1)S(1)}, u32[]{:S(2)}, u32[]{:S(2)}) collective-permute-start(bf16[256,768]{1,0:T(8,128)(2,1)S(1)} %bitcast.112), channel_id=1, source_target_pairs={{0,2},{2,0},{4,6},{6,4},{1,3},{3,1},{5,7},{7,5},{8,10},{10,8},{12,... | collective-permute-start | bytes 1179656 | tf_op jit(solution)/shard_map/ppermute | solution.py:581
  19.2 48.3 %copy-start.11 = (bf16[2,208,768]{2,1,0:T(8,128)(2,1)}, bf16[2,208,768]{2,1,0:T(8,128)(2,1)S(1)}, u32[]{:S(2)}) copy-start(bf16[2,208,768]{2,1,0:T(8,128)(2,1)S(1)} %pad_maximum_fusion.2.refs_4_) | copy-start | bytes 1916932
  21.8 47.6 %copy-start.12 = (bf16[2,208,768]{2,1,0:T(8,128)(2,1)}, bf16[2,208,768]{2,1,0:T(8,128)(2,1)S(1)}, u32[]{:S(2)}) copy-start(bf16[2,208,768]{2,1,0:T(8,128)(2,1)S(1)} %pad_maximum_fusion.3.refs_8_) | copy-start | bytes 1916932
  21.8 46.4 %copy-start.35 = (s32[16]{0:T(128)S(1)}, s32[16]{0:T(128)}, u32[]{:S(2)}) copy-start(s32[16]{0:T(128)} %param.19) | copy-start | bytes 196
  21.8 46.5 %copy-start.10 = (bf16[16,128,768]{2,1,0:T(8,128)(2,1)S(1)}, bf16[16,128,768]{2,1,0:T(8,128)(2,1)}, u32[]{:S(2)}) copy-start(bf16[16,128,768]{2,1,0:T(8,128)(2,1)} %param.35) | copy-start | bytes 9437188
  26.8 27.6 %copy-start.29 = (bf16[256,768]{1,0:T(8,128)(2,1)}, bf16[256,768]{1,0:T(8,128)(2,1)S(1)}, u32[]{:S(2)}) copy-start(bf16[256,768]{1,0:T(8,128)(2,1)S(1)} %collective-permute-done.1.refs_1_) | copy-start | bytes 1179652
  26.8 14.7 %collective-permute-start.2 = (bf16[2,208,768]{2,1,0:T(8,128)(2,1)S(1)}, bf16[2,208,768]{2,1,0:T(8,128)(2,1)S(1)}, u32[]{:S(2)}, u32[]{:S(2)}) collective-permute-start(bf16[2,208,768]{2,1,0:T(8,128)(2,1)S(1)} %pad_maximum_fusion.2.refs_4_), channel_id=1, source_target_pairs={{0,16},{8,24},{16,0},{24,8},{1,17},{9,25},{17,1},{25,9},{2,18},{10... | collective-permute-start | bytes 1916936 | tf_op jit(solution)/shard_map/ppermute | solution.py:603
  27.3 14.4 %collective-permute-start.4 = (bf16[2,208,768]{2,1,0:T(8,128)(2,1)S(1)}, bf16[2,208,768]{2,1,0:T(8,128)(2,1)S(1)}, u32[]{:S(2)}, u32[]{:S(2)}) collective-permute-start(bf16[2,208,768]{2,1,0:T(8,128)(2,1)S(1)} %pad_maximum_fusion.3.refs_8_), channel_id=1, source_target_pairs={{0,1},{1,0},{2,3},{3,2},{4,5},{5,4},{6,7},{7,6},{8,9},{9,8},{10,11... | collective-permute-start | bytes 1916936 | tf_op jit(solution)/shard_map/ppermute | solution.py:603
  27.7 11.1 %collective-permute-start.5 = (bf16[256,768]{1,0:T(8,128)(2,1)S(1)}, bf16[256,768]{1,0:T(8,128)(2,1)S(1)}, u32[]{:S(2)}, u32[]{:S(2)}) collective-permute-start(bf16[256,768]{1,0:T(8,128)(2,1)S(1)} %bitcast.110), channel_id=1, source_target_pairs={{0,6},{2,4},{4,2},{6,0},{1,7},{3,5},{5,3},{7,1},{8,14},{10,12},{12... | collective-permute-start | bytes 1179656 | tf_op jit(solution)/shard_map/ppermute | solution.py:581
  41.5 27.9 %copy-start.23 = (bf16[2,208,768]{2,1,0:T(8,128)(2,1)}, bf16[2,208,768]{2,1,0:T(8,128)(2,1)S(1)}, u32[]{:S(2)}) copy-start(bf16[2,208,768]{2,1,0:T(8,128)(2,1)S(1)} %collective-permute-done.2.refs_5_) | copy-start | bytes 1916932
  41.8 26.5 %copy-start.24 = (bf16[2,208,768]{2,1,0:T(8,128)(2,1)}, bf16[2,208,768]{2,1,0:T(8,128)(2,1)S(1)}, u32[]{:S(2)}) copy-start(bf16[2,208,768]{2,1,0:T(8,128)(2,1)S(1)} %collective-permute-done.4.refs_9_) | copy-start | bytes 1916932
  41.8 12.6 %collective-permute-start.7 = (bf16[1,192,1536]{2,1,0:T(8,128)(2,1)S(1)}, bf16[1,192,1536]{2,1,0:T(8,128)(2,1)S(1)}, u32[]{:S(2)}, u32[]{:S(2)}) collective-permute-start(bf16[1,192,1536]{2,1,0:T(8,128)(2,1)S(1)} %bitcast.100), channel_id=1, source_target_pairs={{0,16},{8,24},{16,0},{24,8},{1,17},{9,25},{17,1},{25,9},{2,18},{10... | collective-permute-start | bytes 1769480 | tf_op jit(solution)/shard_map/ppermute | solution.py:603
  43.3 22.8 %collective-permute-start.6 = (bf16[1,192,1536]{2,1,0:T(8,128)(2,1)S(1)}, bf16[1,192,1536]{2,1,0:T(8,128)(2,1)S(1)}, u32[]{:S(2)}, u32[]{:S(2)}) collective-permute-start(bf16[1,192,1536]{2,1,0:T(8,128)(2,1)S(1)} %bitcast.102), channel_id=1, source_target_pairs={{0,1},{1,0},{2,3},{3,2},{4,5},{5,4},{6,7},{7,6},{8,9},{9,8},{10,11... | collective-permute-start | bytes 1769480 | tf_op jit(solution)/shard_map/ppermute | solution.py:603
  43.8 22.3 %collective-permute-start.8 = (bf16[256,768]{1,0:T(8,128)(2,1)S(1)}, bf16[256,768]{1,0:T(8,128)(2,1)S(1)}, u32[]{:S(2)}, u32[]{:S(2)}) collective-permute-start(bf16[256,768]{1,0:T(8,128)(2,1)S(1)} %bitcast.108), channel_id=1, source_target_pairs={{0,4},{2,6},{4,0},{6,2},{1,5},{3,7},{5,1},{7,3},{8,12},{10,14},{12... | collective-permute-start | bytes 1179656 | tf_op jit(solution)/shard_map/ppermute | solution.py:581
  50.9 16.7 %collective-permute-start.11 = (bf16[2,208,768]{2,1,0:T(8,128)(2,1)S(1)}, bf16[2,208,768]{2,1,0:T(8,128)(2,1)S(1)}, u32[]{:S(2)}, u32[]{:S(2)}) collective-permute-start(bf16[2,208,768]{2,1,0:T(8,128)(2,1)S(1)} %pad_maximum_fusion.3.refs_8_), channel_id=1, source_target_pairs={{0,8},{8,0},{16,24},{24,16},{1,9},{9,1},{17,25},{25,17},{2,10},{10... | collective-permute-start | bytes 1916936 | tf_op jit(solution)/shard_map/ppermute | solution.py:603
  50.9 17.3 %collective-permute-start.9 = (bf16[2,208,768]{2,1,0:T(8,128)(2,1)S(1)}, bf16[2,208,768]{2,1,0:T(8,128)(2,1)S(1)}, u32[]{:S(2)}, u32[]{:S(2)}) collective-permute-start(bf16[2,208,768]{2,1,0:T(8,128)(2,1)S(1)} %pad_maximum_fusion.2.refs_4_), channel_id=1, source_target_pairs={{0,8},{8,0},{16,24},{24,16},{1,9},{9,1},{17,25},{25,17},{2,10},{10... | collective-permute-start | bytes 1916936 | tf_op jit(solution)/shard_map/ppermute | solution.py:603
  54.4 13.8 %collective-permute-start.10 = (bf16[2,208,768]{2,1,0:T(8,128)(2,1)S(1)}, bf16[2,208,768]{2,1,0:T(8,128)(2,1)S(1)}, u32[]{:S(2)}, u32[]{:S(2)}) collective-permute-start(bf16[2,208,768]{2,1,0:T(8,128)(2,1)S(1)} %collective-permute-done.2.refs_5_), channel_id=1, source_target_pairs={{0,8},{8,0},{16,24},{24,16},{1,9},{9,1},{17,25},{25,17},{2,10},{10... | collective-permute-start | bytes 1916936 | tf_op jit(solution)/shard_map/ppermute | solution.py:603
  54.5 50.6 %copy-start.8 = (bf16[2,192,1536]{2,1,0:T(8,128)(2,1)}, bf16[2,192,1536]{2,1,0:T(8,128)(2,1)S(1)}, u32[]{:S(2)}) copy-start(bf16[2,192,1536]{2,1,0:T(8,128)(2,1)S(1)} %pad_maximum_fusion.1.refs_16_) | copy-start | bytes 3538948
  66.1 2.1 collective-permute-start.12
  66.9 38.8 %collective-permute-start.19 = (bf16[2,192,1536]{2,1,0:T(8,128)(2,1)S(1)}, bf16[2,192,1536]{2,1,0:T(8,128)(2,1)}, u32[]{:S(2)}, u32[]{:S(2)}) collective-permute-start(bf16[2,192,1536]{2,1,0:T(8,128)(2,1)S(1)} %pad_maximum_fusion.1.refs_16_), channel_id=1, source_target_pairs={{0,1},{1,0},{2,3},{3,2},{4,5},{5,4},{6,7},{7,6},{8,9},{9,8},{10,11... | collective-permute-start | bytes 3538952 | tf_op jit(solution)/shard_map/ppermute | solution.py:603
  67.5 37.6 %copy-start.9 = (bf16[2,192,1536]{2,1,0:T(8,128)(2,1)}, bf16[2,192,1536]{2,1,0:T(8,128)(2,1)S(1)}, u32[]{:S(2)}) copy-start(bf16[2,192,1536]{2,1,0:T(8,128)(2,1)S(1)} %pad_maximum_fusion.refs_12_) | copy-start | bytes 3538948
  67.6 38.2 %collective-permute-start.16 = (bf16[2,192,1536]{2,1,0:T(8,128)(2,1)S(1)}, bf16[2,192,1536]{2,1,0:T(8,128)(2,1)}, u32[]{:S(2)}, u32[]{:S(2)}) collective-permute-start(bf16[2,192,1536]{2,1,0:T(8,128)(2,1)S(1)} %pad_maximum_fusion.refs_12_), channel_id=1, source_target_pairs={{0,16},{8,24},{16,0},{24,8},{1,17},{9,25},{17,1},{25,9},{2,18},{10... | collective-permute-start | bytes 3538952 | tf_op jit(solution)/shard_map/ppermute | solution.py:603
  69.4 34.9 %collective-permute-start.13 = (bf16[256,768]{1,0:T(8,128)(2,1)}, bf16[256,768]{1,0:T(8,128)(2,1)S(1)}, u32[]{:S(2)}, u32[]{:S(2)}) collective-permute-start(bf16[256,768]{1,0:T(8,128)(2,1)} %bitcast.14), channel_id=1, source_target_pairs={{0,2},{2,0},{4,6},{6,4},{1,3},{3,1},{5,7},{7,5},{8,10},{10,8},{12,... | collective-permute-start | bytes 1179656 | tf_op jit(solution)/shard_map/ppermute | solution.py:581
  69.4 34.9 %collective-permute-start.14 = (bf16[256,768]{1,0:T(8,128)(2,1)S(1)}, bf16[256,768]{1,0:T(8,128)(2,1)S(1)}, u32[]{:S(2)}, u32[]{:S(2)}) collective-permute-start(bf16[256,768]{1,0:T(8,128)(2,1)S(1)} %bitcast.111), channel_id=1, source_target_pairs={{0,4},{2,6},{4,0},{6,2},{1,5},{3,7},{5,1},{7,3},{8,12},{10,14},{12... | collective-permute-start | bytes 1179656 | tf_op jit(solution)/shard_map/ppermute | solution.py:581
  72.3 32.0 %collective-permute-start.15 = (bf16[256,768]{1,0:T(8,128)(2,1)S(1)}, bf16[256,768]{1,0:T(8,128)(2,1)}, u32[]{:S(2)}, u32[]{:S(2)}) collective-permute-start(bf16[256,768]{1,0:T(8,128)(2,1)S(1)} %bitcast.109), channel_id=1, source_target_pairs={{0,6},{2,4},{4,2},{6,0},{1,7},{3,5},{5,3},{7,1},{8,14},{10,12},{12... | collective-permute-start | bytes 1179656 | tf_op jit(solution)/shard_map/ppermute | solution.py:581
  105.1 2.8 collective-permute-start.20
  105.2 4.5 %collective-permute-start.17 = (bf16[2,192,1536]{2,1,0:T(8,128)(2,1)S(1)}, bf16[2,192,1536]{2,1,0:T(8,128)(2,1)S(1)}, u32[]{:S(2)}, u32[]{:S(2)}) collective-permute-start(bf16[2,192,1536]{2,1,0:T(8,128)(2,1)S(1)} %pad_maximum_fusion.refs_12_), channel_id=1, source_target_pairs={{0,8},{8,0},{16,24},{24,16},{1,9},{9,1},{17,25},{25,17},{2,10},{10... | collective-permute-start | bytes 3538952 | tf_op jit(solution)/shard_map/ppermute | solution.py:603
  105.7 5.7 %collective-permute-start.21 = (bf16[2,192,1536]{2,1,0:T(8,128)(2,1)}, bf16[2,192,1536]{2,1,0:T(8,128)(2,1)S(1)}, u32[]{:S(2)}, u32[]{:S(2)}) collective-permute-start(bf16[2,192,1536]{2,1,0:T(8,128)(2,1)} %collective-permute-done.19.refs_17_), channel_id=1, source_target_pairs={{0,8},{8,0},{16,24},{24,16},{1,9},{9,1},{17,25},{25,17},{2,10},{10... | collective-permute-start | bytes 3538952 | tf_op jit(solution)/shard_map/ppermute | solution.py:603
  105.7 7.3 %collective-permute-start.18 = (bf16[2,192,1536]{2,1,0:T(8,128)(2,1)}, bf16[2,192,1536]{2,1,0:T(8,128)(2,1)S(1)}, u32[]{:S(2)}, u32[]{:S(2)}) collective-permute-start(bf16[2,192,1536]{2,1,0:T(8,128)(2,1)} %collective-permute-done.16.refs_13_), channel_id=1, source_target_pairs={{0,8},{8,0},{16,24},{24,16},{1,9},{9,1},{17,25},{25,17},{2,10},{10... | collective-permute-start | bytes 3538952 | tf_op jit(solution)/shard_map/ppermute | solution.py:603
  160.7 15.2 %collective-permute-start.22 = (bf16[256,768]{1,0:T(8,128)(2,1)}, bf16[256,768]{1,0:T(8,128)(2,1)S(1)}, u32[]{:S(2)}, u32[]{:S(2)}) collective-permute-start(bf16[256,768]{1,0:T(8,128)(2,1)} %get-tuple-element.95), channel_id=1, source_target_pairs={{0,2},{2,0},{4,6},{6,4},{1,3},{3,1},{5,7},{7,5},{8,10},{10,8},{12,... | collective-permute-start | bytes 1179656 | tf_op jit(solution)/shard_map/ppermute | solution.py:581
  175.9 24.7 %collective-permute-start.25 = (bf16[2,2,208,1536]{3,2,1,0:T(8,128)(2,1)}, bf16[2,2,208,1536]{3,2,1,0:T(8,128)(2,1)}, u32[]{:S(2)}, u32[]{:S(2)}) collective-permute-start(bf16[2,2,208,1536]{3,2,1,0:T(8,128)(2,1)} %get-tuple-element.105), channel_id=1, source_target_pairs={{0,8},{8,0},{16,24},{24,16},{1,9},{9,1},{17,25},{25,17},{2,10},{10... | collective-permute-start | bytes 7667720 | tf_op jit(solution)/shard_map/ppermute | solution.py:665
  176.0 15.7 %collective-permute-start.23 = (bf16[256,768]{1,0:T(8,128)(2,1)}, bf16[256,768]{1,0:T(8,128)(2,1)S(1)}, u32[]{:S(2)}, u32[]{:S(2)}) collective-permute-start(bf16[256,768]{1,0:T(8,128)(2,1)} %get-tuple-element.96), channel_id=1, source_target_pairs={{0,6},{2,4},{4,2},{6,0},{1,7},{3,5},{5,3},{7,1},{8,14},{10,12},{12... | collective-permute-start | bytes 1179656 | tf_op jit(solution)/shard_map/ppermute | solution.py:581
  191.6 42.3 %collective-permute-start.26 = (bf16[2,2,208,1536]{3,2,1,0:T(8,128)(2,1)}, bf16[2,2,208,1536]{3,2,1,0:T(8,128)(2,1)}, u32[]{:S(2)}, u32[]{:S(2)}) collective-permute-start(bf16[2,2,208,1536]{3,2,1,0:T(8,128)(2,1)} %get-tuple-element.111), channel_id=1, source_target_pairs={{0,8},{8,0},{16,24},{24,16},{1,9},{9,1},{17,25},{25,17},{2,10},{10... | collective-permute-start | bytes 7667720 | tf_op jit(solution)/shard_map/ppermute | solution.py:665
  191.8 41.6 %collective-permute-start.28 = (bf16[256,768]{1,0:T(8,128)(2,1)S(1)}, bf16[256,768]{1,0:T(8,128)(2,1)}, u32[]{:S(2)}, u32[]{:S(2)}) collective-permute-start(bf16[256,768]{1,0:T(8,128)(2,1)S(1)} %copy-done.32), channel_id=1, source_target_pairs={{0,4},{2,6},{4,0},{6,2},{1,5},{3,7},{5,1},{7,3},{8,12},{10,14},{12... | collective-permute-start | bytes 1179656 | tf_op jit(solution)/shard_map/ppermute | solution.py:581
  199.5 42.6 %collective-permute-start.24 = (bf16[768,768]{1,0:T(8,128)(2,1)}, bf16[768,768]{1,0:T(8,128)(2,1)}, u32[]{:S(2)}, u32[]{:S(2)}) collective-permute-start(bf16[768,768]{1,0:T(8,128)(2,1)} %constant_dynamic-update-slice_fusion), channel_id=1, source_target_pairs={{0,1},{1,0},{2,3},{3,2},{4,5},{5,4},{6,7},{7,6},{8,9},{9,8},{10,11... | collective-permute-start | bytes 3538952 | tf_op jit(solution)/shard_map/ppermute | solution.py:585
  205.7 33.4 %collective-permute-start.27 = (bf16[1,2,208,1536]{3,2,1,0:T(8,128)(2,1)}, bf16[1,2,208,1536]{3,2,1,0:T(8,128)(2,1)}, u32[]{:S(2)}, u32[]{:S(2)}) collective-permute-start(bf16[1,2,208,1536]{3,2,1,0:T(8,128)(2,1)} %split.49), channel_id=1, source_target_pairs={{0,16},{8,24},{16,0},{24,8},{1,17},{9,25},{17,1},{25,9},{2,18},{10... | collective-permute-start | bytes 3833864 | tf_op jit(solution)/shard_map/ppermute | solution.py:603
  233.4 34.4 %collective-permute-start.33 = (bf16[256,768]{1,0:T(8,128)(2,1)}, bf16[256,768]{1,0:T(8,128)(2,1)}, u32[]{:S(2)}, u32[]{:S(2)}) collective-permute-start(bf16[256,768]{1,0:T(8,128)(2,1)} %collective-permute-done.28), channel_id=1, source_target_pairs={{0,1},{1,0},{2,3},{3,2},{4,5},{5,4},{6,7},{7,6},{8,9},{9,8},{10,11... | collective-permute-start | bytes 1179656 | tf_op jit(solution)/shard_map/ppermute | solution.py:585
  238.3 29.7 %collective-permute-start.30 = (bf16[1,2,208,1536]{3,2,1,0:T(8,128)(2,1)}, bf16[1,2,208,1536]{3,2,1,0:T(8,128)(2,1)}, u32[]{:S(2)}, u32[]{:S(2)}) collective-permute-start(bf16[1,2,208,1536]{3,2,1,0:T(8,128)(2,1)} %split.51), channel_id=1, source_target_pairs={{0,16},{8,24},{16,0},{24,8},{1,17},{9,25},{17,1},{25,9},{2,18},{10... | collective-permute-start | bytes 3833864 | tf_op jit(solution)/shard_map/ppermute | solution.py:603
  242.1 29.0 %collective-permute-start.29 = (bf16[1,1,208,1536]{3,2,1,0:T(8,128)(2,1)S(1)}, bf16[1,1,208,1536]{3,2,1,0:T(8,128)(2,1)}, u32[]{:S(2)}, u32[]{:S(2)}) collective-permute-start(bf16[1,1,208,1536]{3,2,1,0:T(8,128)(2,1)S(1)} %split.50), channel_id=1, source_target_pairs={{0,1},{1,0},{2,3},{3,2},{4,5},{5,4},{6,7},{7,6},{8,9},{9,8},{10,11... | collective-permute-start | bytes 1916936 | tf_op jit(solution)/shard_map/ppermute | solution.py:603
  252.2 18.8 %collective-permute-start.31 = (bf16[256,768]{1,0:T(8,128)(2,1)}, bf16[256,768]{1,0:T(8,128)(2,1)S(1)}, u32[]{:S(2)}, u32[]{:S(2)}) collective-permute-start(bf16[256,768]{1,0:T(8,128)(2,1)} %get-tuple-element.120), channel_id=1, source_target_pairs={{0,2},{2,0},{4,6},{6,4},{1,3},{3,1},{5,7},{7,5},{8,10},{10,8},{12,... | collective-permute-start | bytes 1179656 | tf_op jit(solution)/shard_map/ppermute | solution.py:581
  252.3 18.7 %collective-permute-start.32 = (bf16[256,768]{1,0:T(8,128)(2,1)}, bf16[256,768]{1,0:T(8,128)(2,1)}, u32[]{:S(2)}, u32[]{:S(2)}) collective-permute-start(bf16[256,768]{1,0:T(8,128)(2,1)} %get-tuple-element.122), channel_id=1, source_target_pairs={{0,6},{2,4},{4,2},{6,0},{1,7},{3,5},{5,3},{7,1},{8,14},{10,12},{12... | collective-permute-start | bytes 1179656 | tf_op jit(solution)/shard_map/ppermute | solution.py:581
  271.8 5.2 %collective-permute-start.34 = (bf16[2,2,208,1536]{3,2,1,0:T(8,128)(2,1)}, bf16[2,2,208,1536]{3,2,1,0:T(8,128)(2,1)}, u32[]{:S(2)}, u32[]{:S(2)}) collective-permute-start(bf16[2,2,208,1536]{3,2,1,0:T(8,128)(2,1)} %get-tuple-element.127), channel_id=1, source_target_pairs={{0,8},{8,0},{16,24},{24,16},{1,9},{9,1},{17,25},{25,17},{2,10},{10... | collective-permute-start | bytes 7667720 | tf_op jit(solution)/shard_map/ppermute | solution.py:665
  273.5 49.5 %collective-permute-start.42 = (bf16[256,768]{1,0:T(8,128)(2,1)}, bf16[256,768]{1,0:T(8,128)(2,1)S(1)}, u32[]{:S(2)}, u32[]{:S(2)}) collective-permute-start(bf16[256,768]{1,0:T(8,128)(2,1)} %get-tuple-element.140), channel_id=1, source_target_pairs={{0,4},{2,6},{4,0},{6,2},{1,5},{3,7},{5,1},{7,3},{8,12},{10,14},{12... | collective-permute-start | bytes 1179656 | tf_op jit(solution)/shard_map/ppermute | solution.py:581
  279.5 16.5 %collective-permute-start.38 = (bf16[1,1,208,1536]{3,2,1,0:T(8,128)(2,1)S(1)}, bf16[1,1,208,1536]{3,2,1,0:T(8,128)(2,1)S(1)}, u32[]{:S(2)}, u32[]{:S(2)}) collective-permute-start(bf16[1,1,208,1536]{3,2,1,0:T(8,128)(2,1)S(1)} %split.47), channel_id=1, source_target_pairs={{0,1},{1,0},{2,3},{3,2},{4,5},{5,4},{6,7},{7,6},{8,9},{9,8},{10,11... | collective-permute-start | bytes 1916936 | tf_op jit(solution)/shard_map/ppermute | solution.py:603
  280.1 42.6 %collective-permute-start.36 = (bf16[1,2,208,1536]{3,2,1,0:T(8,128)(2,1)S(1)}, bf16[1,2,208,1536]{3,2,1,0:T(8,128)(2,1)S(1)}, u32[]{:S(2)}, u32[]{:S(2)}) collective-permute-start(bf16[1,2,208,1536]{3,2,1,0:T(8,128)(2,1)S(1)} %split.53), channel_id=1, source_target_pairs={{0,16},{8,24},{16,0},{24,8},{1,17},{9,25},{17,1},{25,9},{2,18},{10... | collective-permute-start | bytes 3833864 | tf_op jit(solution)/shard_map/ppermute | solution.py:603
  296.3 14.0 %collective-permute-start.39 = (bf16[416,384]{1,0:T(8,128)(2,1)S(1)}, bf16[416,384]{1,0:T(8,128)(2,1)S(1)}, u32[]{:S(2)}, u32[]{:S(2)}) collective-permute-start(bf16[416,384]{1,0:T(8,128)(2,1)S(1)} %pad_maximum_fusion.4), channel_id=1, source_target_pairs={{0,2},{2,0},{4,6},{6,4},{1,3},{3,1},{5,7},{7,5},{8,10},{10,8},{12,... | collective-permute-start | bytes 958472 | tf_op jit(solution)/shard_map/ppermute | solution.py:581
  297.5 25.1 %collective-permute-start.40 = (bf16[416,384]{1,0:T(8,128)(2,1)S(1)}, bf16[416,384]{1,0:T(8,128)(2,1)S(1)}, u32[]{:S(2)}, u32[]{:S(2)}) collective-permute-start(bf16[416,384]{1,0:T(8,128)(2,1)S(1)} %pad_maximum_fusion.5), channel_id=1, source_target_pairs={{0,4},{2,6},{4,0},{6,2},{1,5},{3,7},{5,1},{7,3},{8,12},{10,14},{12... | collective-permute-start | bytes 958472 | tf_op jit(solution)/shard_map/ppermute | solution.py:581
  298.6 24.0 %collective-permute-start.41 = (bf16[416,384]{1,0:T(8,128)(2,1)S(1)}, bf16[416,384]{1,0:T(8,128)(2,1)S(1)}, u32[]{:S(2)}, u32[]{:S(2)}) collective-permute-start(bf16[416,384]{1,0:T(8,128)(2,1)S(1)} %pad_maximum_fusion.6), channel_id=1, source_target_pairs={{0,6},{2,4},{4,2},{6,0},{1,7},{3,5},{5,3},{7,1},{8,14},{10,12},{12... | collective-permute-start | bytes 958472 | tf_op jit(solution)/shard_map/ppermute | solution.py:581
  310.3 54.5 %collective-permute-start.35 = (bf16[768,768]{1,0:T(8,128)(2,1)S(1)}, bf16[768,768]{1,0:T(8,128)(2,1)S(1)}, u32[]{:S(2)}, u32[]{:S(2)}) collective-permute-start(bf16[768,768]{1,0:T(8,128)(2,1)S(1)} %constant_dynamic-update-slice_fusion.3), channel_id=1, source_target_pairs={{0,1},{1,0},{2,3},{3,2},{4,5},{5,4},{6,7},{7,6},{8,9},{9,8},{10,11... | collective-permute-start | bytes 3538952 | tf_op jit(solution)/shard_map/ppermute | solution.py:585
  323.1 16.2 %collective-permute-start.50 = (bf16[416,384]{1,0:T(8,128)(2,1)S(1)}, bf16[416,384]{1,0:T(8,128)(2,1)S(1)}, u32[]{:S(2)}, u32[]{:S(2)}) collective-permute-start(bf16[416,384]{1,0:T(8,128)(2,1)S(1)} %add_convert_fusion.9), channel_id=1, source_target_pairs={{0,2},{2,0},{4,6},{6,4},{1,3},{3,1},{5,7},{7,5},{8,10},{10,8},{12,... | collective-permute-start | bytes 958472 | tf_op jit(solution)/shard_map/ppermute | solution.py:581
  328.7 24.9 %collective-permute-start.51 = (bf16[416,384]{1,0:T(8,128)(2,1)S(1)}, bf16[416,384]{1,0:T(8,128)(2,1)S(1)}, u32[]{:S(2)}, u32[]{:S(2)}) collective-permute-start(bf16[416,384]{1,0:T(8,128)(2,1)S(1)} %add_convert_fusion.9), channel_id=1, source_target_pairs={{0,4},{2,6},{4,0},{6,2},{1,5},{3,7},{5,1},{7,3},{8,12},{10,14},{12... | collective-permute-start | bytes 958472 | tf_op jit(solution)/shard_map/ppermute | solution.py:581
  328.8 24.9 %collective-permute-start.52 = (bf16[416,384]{1,0:T(8,128)(2,1)S(1)}, bf16[416,384]{1,0:T(8,128)(2,1)S(1)}, u32[]{:S(2)}, u32[]{:S(2)}) collective-permute-start(bf16[416,384]{1,0:T(8,128)(2,1)S(1)} %add_convert_fusion.9), channel_id=1, source_target_pairs={{0,6},{2,4},{4,2},{6,0},{1,7},{3,5},{5,3},{7,1},{8,14},{10,12},{12... | collective-permute-start | bytes 958472 | tf_op jit(solution)/shard_map/ppermute | solution.py:581
  331.2 26.4 %collective-permute-start.37 = (bf16[1,1,208,1536]{3,2,1,0:T(8,128)(2,1)S(1)}, bf16[1,1,208,1536]{3,2,1,0:T(8,128)(2,1)S(1)}, u32[]{:S(2)}, u32[]{:S(2)}) collective-permute-start(bf16[1,1,208,1536]{3,2,1,0:T(8,128)(2,1)S(1)} %split.55), channel_id=1, source_target_pairs={{0,1},{1,0},{2,3},{3,2},{4,5},{5,4},{6,7},{7,6},{8,9},{9,8},{10,11... | collective-permute-start | bytes 1916936 | tf_op jit(solution)/shard_map/ppermute | solution.py:603
  357.8 11.1 %collective-permute-start.44 = (bf16[208,384]{1,0:T(8,128)(2,1)S(1)}, bf16[208,384]{1,0:T(8,128)(2,1)S(1)}, u32[]{:S(2)}, u32[]{:S(2)}) collective-permute-start(bf16[208,384]{1,0:T(8,128)(2,1)S(1)} %get-tuple-element.170), channel_id=1, source_target_pairs={{0,2},{2,0},{4,6},{6,4},{1,3},{3,1},{5,7},{7,5},{8,10},{10,8},{12,... | collective-permute-start | bytes 479240 | tf_op jit(solution)/shard_map/ppermute | solution.py:581
  362.4 11.9 %collective-permute-start.45 = (bf16[208,384]{1,0:T(8,128)(2,1)S(1)}, bf16[208,384]{1,0:T(8,128)(2,1)S(1)}, u32[]{:S(2)}, u32[]{:S(2)}) collective-permute-start(bf16[208,384]{1,0:T(8,128)(2,1)S(1)} %get-tuple-element.172), channel_id=1, source_target_pairs={{0,4},{2,6},{4,0},{6,2},{1,5},{3,7},{5,1},{7,3},{8,12},{10,14},{12... | collective-permute-start | bytes 479240 | tf_op jit(solution)/shard_map/ppermute | solution.py:581
  362.4 11.8 %collective-permute-start.46 = (bf16[208,384]{1,0:T(8,128)(2,1)S(1)}, bf16[208,384]{1,0:T(8,128)(2,1)S(1)}, u32[]{:S(2)}, u32[]{:S(2)}) collective-permute-start(bf16[208,384]{1,0:T(8,128)(2,1)S(1)} %get-tuple-element.171), channel_id=1, source_target_pairs={{0,6},{2,4},{4,2},{6,0},{1,7},{3,5},{5,3},{7,1},{8,14},{10,12},{12... | collective-permute-start | bytes 479240 | tf_op jit(solution)/shard_map/ppermute | solution.py:581
  365.0 29.0 %collective-permute-start.43 = (bf16[256,768]{1,0:T(8,128)(2,1)S(1)}, bf16[256,768]{1,0:T(8,128)(2,1)S(1)}, u32[]{:S(2)}, u32[]{:S(2)}) collective-permute-start(bf16[256,768]{1,0:T(8,128)(2,1)S(1)} %collective-permute-done.42), channel_id=1, source_target_pairs={{0,1},{1,0},{2,3},{3,2},{4,5},{5,4},{6,7},{7,6},{8,9},{9,8},{10,11... | collective-permute-start | bytes 1179656 | tf_op jit(solution)/shard_map/ppermute | solution.py:585
  374.4 7.5 %collective-permute-start.47 = (bf16[208,384]{1,0:T(8,128)(2,1)S(1)}, bf16[208,384]{1,0:T(8,128)(2,1)S(1)}, u32[]{:S(2)}, u32[]{:S(2)}) collective-permute-start(bf16[208,384]{1,0:T(8,128)(2,1)S(1)} %get-tuple-element.146), channel_id=1, source_target_pairs={{0,2},{2,0},{4,6},{6,4},{1,3},{3,1},{5,7},{7,5},{8,10},{10,8},{12,... | collective-permute-start | bytes 479240 | tf_op jit(solution)/shard_map/ppermute | solution.py:581
  377.4 13.2 %collective-permute-start.48 = (bf16[208,384]{1,0:T(8,128)(2,1)S(1)}, bf16[208,384]{1,0:T(8,128)(2,1)S(1)}, u32[]{:S(2)}, u32[]{:S(2)}) collective-permute-start(bf16[208,384]{1,0:T(8,128)(2,1)S(1)} %get-tuple-element.146), channel_id=1, source_target_pairs={{0,4},{2,6},{4,0},{6,2},{1,5},{3,7},{5,1},{7,3},{8,12},{10,14},{12... | collective-permute-start | bytes 479240 | tf_op jit(solution)/shard_map/ppermute | solution.py:581
  377.4 13.1 %collective-permute-start.49 = (bf16[208,384]{1,0:T(8,128)(2,1)S(1)}, bf16[208,384]{1,0:T(8,128)(2,1)S(1)}, u32[]{:S(2)}, u32[]{:S(2)}) collective-permute-start(bf16[208,384]{1,0:T(8,128)(2,1)S(1)} %get-tuple-element.146), channel_id=1, source_target_pairs={{0,6},{2,4},{4,2},{6,0},{1,7},{3,5},{5,3},{7,1},{8,14},{10,12},{12... | collective-permute-start | bytes 479240 | tf_op jit(solution)/shard_map/ppermute | solution.py:581
  (25 other events, 173.3 us)

commit v9 on v8

--- a/solution.py
+++ b/solution.py
@@ -225,17 +225,21 @@
                 n = df * T + dt
                 rows = pl.ds(row, Dl)
                 copies.append((
-                    pltpu.make_async_copy(
+                    functools.partial(
+                        pltpu.make_async_copy,
                         vo[df, dt].at[pl.ds(0, Dl), pl.ds(half, half)],
                         wo.at[rows, pl.ds(dt * half, half)], sems.at[n]),
-                    pltpu.make_async_copy(
+                    functools.partial(
+                        pltpu.make_async_copy,
                         inner[df, dt],
                         wi.at[rows, pl.ds(dt * fhalf, fhalf)], sems.at[n_w + n]),
-                    pltpu.make_async_copy(
+                    functools.partial(
+                        pltpu.make_async_copy,
                         outer[df, dt],
                         wout.at[rows, pl.ds(dt * fhalf, fhalf)], sems.at[2 * n_w + n]),
                 ) + tuple(
-                    pltpu.make_async_copy(
+                    functools.partial(
+                        pltpu.make_async_copy,
                         (qk if part == 0 else vo)[df, dt].at[pl.ds(Dl, EXTRA)],
                         small.at[n, :, pl.ds(part * D, D)], sems.at[(3 + part) * n_w + n])
                     for part in range(2)
@@ -250,17 +254,15 @@
     @pl.when(k == 0)
     def _():
         copies = weight_copies()
-        for which in range(5):
+        for which in (3, 4, 0, 1, 2):
             for group in copies:
-                group[which].start()
+                group[which]().start()
         for copy in cot_copies():
             copy.start()
         sums[...] = jnp.zeros_like(sums)
-        for which in range(5):
+        for which in (3, 4, 0):
             for group in copies:
-                group[which].wait()
-        for copy in cot_copies():
-            copy.wait()
+                group[which]().wait()
         for dt in range(T):
             part = sum(small[df * T + dt, :EXTRA, :].astype(F32) for df in range(F))
             inner_bias[:, dt * fhalf : (dt + 1) * fhalf] = part[2:3]
@@ -280,6 +282,12 @@
     nl_out[0] = nl
     root = math.sqrt(2.0 / math.pi)
     chunk = 768
+
+    @pl.when(k == 0)
+    def _():
+        for group in weight_copies():
+            group[1]().wait()
+
     for j in range(FF // chunk):
         cols = slice(j * chunk, (j + 1) * chunk)
         pre = dot_nn(nl, wi[:, cols]) + inner_bias[:, cols]
@@ -290,6 +298,14 @@
         gp_s[:, cols] = hp + (0.5 * pre) * (1.0 - th * th) * (
             root + (3.0 * root * 0.044715) * square
         )
+
+    @pl.when(k == 0)
+    def _():
+        for group in weight_copies():
+            group[2]().wait()
+        for copy in cot_copies():
+            copy.wait()
+
     before2 = normed + dot_nt(act_out[0], wout[...]) + outer_bias
     xhat2, rstd2 = normalised(before2)
     row = lax.broadcasted_iota(jnp.int32, (R, 1), 0)

time: 398 us -> 397 us (level)
  no operation moved by 1% of the time
where the time goes in v9:
time: 397 us; the launch traced here: 396 us
  Pallas kernels  150 us (38%)
  waiting for transfers between devices  112 us (28%)
  starting transfers between devices  74.2 us (19%)
  local copies, waits for them, and re-layouts  37.5 us (9%)
  other arithmetic  20.2 us (5%)
    ppermute x24, waiting for transfers between devices, ctx_moved(): return lax.ppermute(piece, 'ctx', xor_pairs(C, k)) if k else piece  86.1 us
    ppermute x24, starting transfers between devices, ctx_moved(): return lax.ppermute(piece, 'ctx', xor_pairs(C, k)) if k else piece  55 us
    pallas_call x1, Pallas kernels, rows_call(): pl.pallas_call(functools.partial(rows_kernel, dims, FF), name='rows', gri...  45.9 us
    pallas_call x3, Pallas kernels, weight_call(): pl.pallas_call(functools.partial(weight_kernel, F, pers, sums is not None...  39.9 us
    pallas_call x1, Pallas kernels, front_call(): pl.pallas_call(functools.partial(front_kernel, dims), name='front', grid=...  29.9 us
    pallas_call x1, Pallas kernels, back_call(): pl.pallas_call(functools.partial(back_kernel, dims), name='back', grid=(n...  26.2 us
    ppermute x22, waiting for transfers between devices, swapped(): return lax.ppermute(array, axis, xor_pairs(lax.axis_size(axis), bit))  25.3 us
    ppermute x22, starting transfers between devices, swapped(): return lax.ppermute(array, axis, xor_pairs(lax.axis_size(axis), bit))  16.2 us
  transfers between devices with their start and end apart: 53, of which 24 were waited for; matrix products, arithmetic and copies ran while one was open for 10% of the time, Pallas kernels for 26%

profile of v9, /device:TPU:0, one launch (start us, length us, event | category | flops | bytes accessed | tf_op | source)
XLA Modules:
  0.0 396.0 jit_solution(6554669962974921194)
XLA Ops:
  2.4 4.1 %concatenate.53 = bf16[1152]{0:T(1024)(128)(2,1)S(1)} concatenate(bf16[192]{0:T(256)(128)(2,1)} %param.26, bf16[192]{0:T(256)(128)(2,1)} %param.27, bf16[192]{0:T(256)(128)(2,1)} %param.28, bf16[192]{0:T(256)(128)(2,1)} %param.32, bf16[192]{0:T(256)(128)(2,1)} %param.33, bf16[192]{0:T(256)(128)(2,1)} %param.34), dimensions={0} | concatenate | bytes 4608 | tf_op jit(solution)/shard_map/concatenate | solution.py:648
  8.6 3.0 collective-permute-start
  12.6 1.6 collective-permute-start.3
  14.2 2.3 constant_dynamic-slice_fusion.15
  16.5 1.6 collective-permute-start.1
  19.2 2.5 collective-permute-done.3
  21.8 5.0 %collective-permute-done.1.refs_1_ = bf16[256,768]{1,0:T(8,128)(2,1)S(1)} collective-permute-done((bf16[256,768]{1,0:T(8,128)(2,1)S(1)}, bf16[256,768]{1,0:T(8,128)(2,1)S(1)}, u32[]{:S(2)}, u32[]{:S(2)}) %collective-permute-start.1) | collective-permute-done | bytes 393248 | tf_op jit(solution)/shard_map/ppermute | solution.py:597
  27.7 3.8 collective-permute-start.5
  31.5 7.3 %collective-permute-done.5.refs_3_ = bf16[256,768]{1,0:T(8,128)(2,1)S(1)} collective-permute-done((bf16[256,768]{1,0:T(8,128)(2,1)S(1)}, bf16[256,768]{1,0:T(8,128)(2,1)S(1)}, u32[]{:S(2)}, u32[]{:S(2)}) %collective-permute-start.5) | collective-permute-done | bytes 393248 | tf_op jit(solution)/shard_map/ppermute | solution.py:597
  38.8 2.7 collective-permute-done.2.refs_5_
  41.8 1.5 collective-permute-start.7
  43.8 7.1 %collective-permute-start.8 = (bf16[256,768]{1,0:T(8,128)(2,1)S(1)}, bf16[256,768]{1,0:T(8,128)(2,1)S(1)}, u32[]{:S(2)}, u32[]{:S(2)}) collective-permute-start(bf16[256,768]{1,0:T(8,128)(2,1)S(1)} %bitcast.108), channel_id=1, source_target_pairs={{0,4},{2,6},{4,0},{6,2},{1,5},{3,7},{5,1},{7,3},{8,12},{10,14},{12... | collective-permute-start | bytes 1179656 | tf_op jit(solution)/shard_map/ppermute | solution.py:597
  51.4 3.0 collective-permute-done.7
  54.5 11.6 %collective-permute-done.8.refs_2_ = bf16[256,768]{1,0:T(8,128)(2,1)S(1)} collective-permute-done((bf16[256,768]{1,0:T(8,128)(2,1)S(1)}, bf16[256,768]{1,0:T(8,128)(2,1)S(1)}, u32[]{:S(2)}, u32[]{:S(2)}) %collective-permute-start.8) | collective-permute-done | bytes 393248 | tf_op jit(solution)/shard_map/ppermute | solution.py:597
  68.3 1.1 constant_dynamic-slice_fusion.11
  69.4 2.9 collective-permute-start.14
  72.3 1.5 collective-permute-start.15
  74.4 29.9 %front.1 = (bf16[4,256,768]{2,1,0:T(8,128)(2,1)}, bf16[768,2304]{1,0:T(8,128)(2,1)}, bf16[4,2,128,2304]{3,2,1,0:T(8,128)(2,1)}, bf16[12,1024,512]{2,1,0:T(8,128)...) custom-call(s32[4]{0:T(128)} %pad_add_fusion.meta, bf16[256,768]{1,0:T(8,128)(2,1)} %bitcast.106, ...), custom_call_target="tpu_custom_call" | custom-call | flops 3623878656 | bytes 40000000 | tf_op jit(solution)/shard_map/front/pallas_call | solution.py:162
  106.2 1.8 collective-permute-done.20.refs_18_
  108.0 1.7 collective-permute-done.17.refs_14_
  114.1 45.9 %rows.1 = (bf16[256,768]{1,0:T(8,128)(2,1)}, bf16[256,768]{1,0:T(8,128)(2,1)}, bf16[256,768]{1,0:T(8,128)(2,1)}, bf16[256,768]{1,0:T(8,128)(2,1)}, f32[4,256,768...) custom-call(s32[4]{0:T(128)} %pad_add_fusion.meta, ...), custom_call_target="tpu_custom_call" | custom-call | flops 21743271936 | bytes 50000000 | tf_op jit(solution)/shard_map/rows/pallas_call | solution.py:360
  160.0 2.3 collective-permute-start.22
  162.3 12.9 %weight_grad.3 = (bf16[2,2,208,1536]{3,2,1,0:T(8,128)(2,1)}, bf16[2,2,208,1536]{3,2,1,0:T(8,128)(2,1)}) custom-call(s32[4]{0:T(128)} %pad_add_fusion.meta, bf16[1024,768]{1,0:T(8,128)(2,1)} %bitcast.126, bf16[1024,3072]{1,0:T(8,128)(2,1)} %bitcast.122, f32[16,768]{1,0:T(8,128)} %get-tuple-element.102.refs_2_), custom_call_target="tpu_custom_call" | custom-call | flops 4831838208 | bytes 12582912 | tf_op jit(solution)/shard_map/weight_grad/pallas_call | solution.py:539
  175.2 2.5 collective-permute-start.23
  177.8 13.0 %weight_grad.4 = (bf16[2,2,208,1536]{3,2,1,0:T(8,128)(2,1)}, bf16[2,2,208,1536]{3,2,1,0:T(8,128)(2,1)}) custom-call(s32[4]{0:T(128)} %pad_add_fusion.meta, bf16[1024,768]{1,0:T(8,128)(2,1)} %bitcast.125, bf16[1024,3072]{1,0:T(8,128)(2,1)} %bitcast.121), custom_call_target="tpu_custom_call" | custom-call | flops 4831838208 | bytes 12582912 | tf_op jit(solution)/shard_map/weight_grad/pallas_call | solution.py:539
  190.9 5.6 %collective-permute-start.28 = (bf16[256,768]{1,0:T(8,128)(2,1)S(1)}, bf16[256,768]{1,0:T(8,128)(2,1)}, u32[]{:S(2)}, u32[]{:S(2)}) collective-permute-start(bf16[256,768]{1,0:T(8,128)(2,1)S(1)} %copy-done.32), channel_id=1, source_target_pairs={{0,4},{2,6},{4,0},{6,2},{1,5},{3,7},{5,1},{7,3},{8,12},{10,14},{12... | collective-permute-start | bytes 1179656 | tf_op jit(solution)/shard_map/ppermute | solution.py:597
  198.8 1.1 collective-permute-start.24
  199.9 2.4 add_convert_fusion.2
  202.3 1.5 copy-done
  203.8 1.1 split.49
  204.9 1.5 collective-permute-start.27
  206.4 26.2 %back.1 = bf16[4,2,128,2304]{3,2,1,0:T(8,128)(2,1)} custom-call(bf16[4,2,128,2304]{3,2,1,0:T(8,128)(2,1)} %get-tuple-element.98.qkv, bf16[4,2,128,768]{3,2,1,0:T(8,128)(2,1)} %get-tuple-element.88.ctx, bf16[4,2,128,768]{3,2,1,0:T(8,128)(2,1)} %bitcast.87, bf16[12,1024,512]{2,1,0:T(8,128)(2,1)} %get-tuple-element.113.e_ref, ...), custom_call_target="tpu_custom_call" | custom-call | flops 6442450944 | bytes 30000000 | tf_op jit(solution)/shard_map/back/pallas_call | solution.py:429
  233.2 3.2 add_convert_fusion.1
  236.4 1.1 split.51
  238.6 1.6 add_convert_fusion.5
  241.3 1.6 collective-permute-start.29
  242.9 8.5 %input_grad.1 = (bf16[256,768]{1,0:T(8,128)(2,1)}, bf16[256,768]{1,0:T(8,128)(2,1)}, bf16[256,768]{1,0:T(8,128)(2,1)}, bf16[256,768]{1,0:T(8,128)(2,1)}) custom-call(bf16[4,256,2304]{2,1,0:T(8,128)(2,1)} %bitcast.83, bf16[768,2304]{1,0:T(8,128)(2,1)} %get-tuple-element.115.w, f32[4,256,768]{2,1,0:T(8,128)} %get-tuple-element.118.first), custom_call_target="tpu_custom_call" | custom-call | flops 3623878656 | bytes 15000000 | tf_op jit(solution)/shard_map/input_grad/pallas_call | solution.py:466
  251.5 1.5 collective-permute-start.32
  253.0 14.1 %weight_grad.5 = (bf16[2,2,208,1536]{3,2,1,0:T(8,128)(2,1)}, bf16[2,2,208,1536]{3,2,1,0:T(8,128)(2,1)}) custom-call(s32[4]{0:T(128)} %pad_add_fusion.meta, bf16[1024,768]{1,0:T(8,128)(2,1)} %bitcast.123, bf16[1024,768]{1,0:T(8,128)(2,1)} %bitcast.124, bf16[1024,2304]{1,0:T(8,128)(2,1)} %bitcast.84, bf16[1024,768]{1,0:T(8,128)(2,1)} %bitcast.86), custom_call_target="tpu_custom_call" | custom-call | flops 4831838208 | bytes 12582912 | tf_op jit(solution)/shard_map/weight_grad/pallas_call | solution.py:539
  267.2 3.0 collective-permute-done.31
  271.0 1.8 add_convert_fusion.3
  272.8 1.2 collective-permute-start.42
  274.0 1.2 fusion.1
  276.2 2.4 add_convert_fusion
  280.3 1.3 fusion.17
  281.6 1.3 fusion.16
  284.5 10.7 %collective-permute-done.38 = bf16[1,1,208,1536]{3,2,1,0:T(8,128)(2,1)S(1)} collective-permute-done((bf16[1,1,208,1536]{3,2,1,0:T(8,128)(2,1)S(1)}, bf16[1,1,208,1536]{3,2,1,0:T(8,128)(2,1)S(1)}, u32[]{:S(2)}, u32[]{:S(2)}) %collective-permute-start.38) | collective-permute-done | bytes 639008 | tf_op jit(solution)/shard_map/ppermute | solution.py:619
  295.5 1.2 collective-permute-start.39
  297.9 2.3 collective-permute-start.41
  302.3 7.3 %collective-permute-done.39 = bf16[416,384]{1,0:T(8,128)(2,1)S(1)} collective-permute-done((bf16[416,384]{1,0:T(8,128)(2,1)S(1)}, bf16[416,384]{1,0:T(8,128)(2,1)S(1)}, u32[]{:S(2)}, u32[]{:S(2)}) %collective-permute-start.39) | collective-permute-done | bytes 319520 | tf_op jit(solution)/shard_map/ppermute | solution.py:597
  310.1 11.7 %collective-permute-done.40 = bf16[416,384]{1,0:T(8,128)(2,1)S(1)} collective-permute-done((bf16[416,384]{1,0:T(8,128)(2,1)S(1)}, bf16[416,384]{1,0:T(8,128)(2,1)S(1)}, u32[]{:S(2)}, u32[]{:S(2)}) %collective-permute-start.40) | collective-permute-done | bytes 319520 | tf_op jit(solution)/shard_map/ppermute | solution.py:597
  322.3 5.6 %collective-permute-start.50 = (bf16[416,384]{1,0:T(8,128)(2,1)S(1)}, bf16[416,384]{1,0:T(8,128)(2,1)S(1)}, u32[]{:S(2)}, u32[]{:S(2)}) collective-permute-start(bf16[416,384]{1,0:T(8,128)(2,1)S(1)} %add_convert_fusion.9), channel_id=1, source_target_pairs={{0,2},{2,0},{4,6},{6,4},{1,3},{3,1},{5,7},{7,5},{8,10},{10,8},{12,... | collective-permute-start | bytes 958472 | tf_op jit(solution)/shard_map/ppermute | solution.py:597
  328.0 2.4 collective-permute-start.52
  331.1 7.5 %collective-permute-done.50 = bf16[416,384]{1,0:T(8,128)(2,1)S(1)} collective-permute-done((bf16[416,384]{1,0:T(8,128)(2,1)S(1)}, bf16[416,384]{1,0:T(8,128)(2,1)S(1)}, u32[]{:S(2)}, u32[]{:S(2)}) %collective-permute-start.50) | collective-permute-done | bytes 319520 | tf_op jit(solution)/shard_map/ppermute | solution.py:597
  338.6 14.2 %collective-permute-done.51 = bf16[416,384]{1,0:T(8,128)(2,1)S(1)} collective-permute-done((bf16[416,384]{1,0:T(8,128)(2,1)S(1)}, bf16[416,384]{1,0:T(8,128)(2,1)S(1)}, u32[]{:S(2)}, u32[]{:S(2)}) %collective-permute-start.51) | collective-permute-done | bytes 319520 | tf_op jit(solution)/shard_map/ppermute | solution.py:597
  354.6 1.1 slice.165
  357.1 4.6 %collective-permute-start.44 = (bf16[208,384]{1,0:T(8,128)(2,1)S(1)}, bf16[208,384]{1,0:T(8,128)(2,1)S(1)}, u32[]{:S(2)}, u32[]{:S(2)}) collective-permute-start(bf16[208,384]{1,0:T(8,128)(2,1)S(1)} %get-tuple-element.170), channel_id=1, source_target_pairs={{0,2},{2,0},{4,6},{6,4},{1,3},{3,1},{5,7},{7,5},{8,10},{10,8},{12,... | collective-permute-start | bytes 479240 | tf_op jit(solution)/shard_map/ppermute | solution.py:597
  361.7 2.4 collective-permute-start.46
  365.7 2.5 collective-permute-done.44
  368.2 5.3 %collective-permute-done.45 = bf16[208,384]{1,0:T(8,128)(2,1)S(1)} collective-permute-done((bf16[208,384]{1,0:T(8,128)(2,1)S(1)}, bf16[208,384]{1,0:T(8,128)(2,1)S(1)}, u32[]{:S(2)}, u32[]{:S(2)}) %collective-permute-start.45) | collective-permute-done | bytes 159776 | tf_op jit(solution)/shard_map/ppermute | solution.py:597
  373.6 3.0 collective-permute-start.47
  376.7 2.5 collective-permute-start.49
  379.2 1.9 collective-permute-done.47
  381.2 8.7 %collective-permute-done.48 = bf16[208,384]{1,0:T(8,128)(2,1)S(1)} collective-permute-done((bf16[208,384]{1,0:T(8,128)(2,1)S(1)}, bf16[208,384]{1,0:T(8,128)(2,1)S(1)}, u32[]{:S(2)}, u32[]{:S(2)}) %collective-permute-start.48) | collective-permute-done | bytes 159776 | tf_op jit(solution)/shard_map/ppermute | solution.py:597
  (229 shorter events, 43.9 us)
Async XLA Ops:
  8.6 10.6 %collective-permute-start = (bf16[1,208,768]{2,1,0:T(8,128)(2,1)S(1)}, bf16[1,208,768]{2,1,0:T(8,128)(2,1)S(1)}, u32[]{:S(2)}, u32[]{:S(2)}) collective-permute-start(bf16[1,208,768]{2,1,0:T(8,128)(2,1)S(1)} %maximum_bitcast_fusion), channel_id=1, source_target_pairs={{0,1},{1,0},{2,3},{3,2},{4,5},{5,4},{6,7},{7,6},{8,9},{9,8},{10,11... | collective-permute-start | bytes 958472 | tf_op jit(solution)/shard_map/ppermute | solution.py:619
  12.6 9.1 %collective-permute-start.3 = (bf16[1,208,768]{2,1,0:T(8,128)(2,1)S(1)}, bf16[1,208,768]{2,1,0:T(8,128)(2,1)S(1)}, u32[]{:S(2)}, u32[]{:S(2)}) collective-permute-start(bf16[1,208,768]{2,1,0:T(8,128)(2,1)S(1)} %maximum_bitcast_fusion.1), channel_id=1, source_target_pairs={{0,16},{8,24},{16,0},{24,8},{1,17},{9,25},{17,1},{25,9},{2,18},{10... | collective-permute-start | bytes 958472 | tf_op jit(solution)/shard_map/ppermute | solution.py:619
  14.2 27.5 %copy-start.13 = (bf16[1536,192]{0,1:T(8,128)(2,1)S(1)}, bf16[1536,192]{0,1:T(8,128)(2,1)}, u32[]{:S(2)}) copy-start(bf16[1536,192]{0,1:T(8,128)(2,1)} %param.31) | copy-start | bytes 1769476
  14.2 29.1 %copy-start.14 = (bf16[192,1536]{1,0:T(8,128)(2,1)S(1)}, bf16[192,1536]{1,0:T(8,128)(2,1)}, u32[]{:S(2)}) copy-start(bf16[192,1536]{1,0:T(8,128)(2,1)} %param.29) | copy-start | bytes 1769476
  16.5 10.3 %collective-permute-start.1 = (bf16[256,768]{1,0:T(8,128)(2,1)S(1)}, bf16[256,768]{1,0:T(8,128)(2,1)S(1)}, u32[]{:S(2)}, u32[]{:S(2)}) collective-permute-start(bf16[256,768]{1,0:T(8,128)(2,1)S(1)} %bitcast.112), channel_id=1, source_target_pairs={{0,2},{2,0},{4,6},{6,4},{1,3},{3,1},{5,7},{7,5},{8,10},{10,8},{12,... | collective-permute-start | bytes 1179656 | tf_op jit(solution)/shard_map/ppermute | solution.py:597
  19.2 48.3 %copy-start.11 = (bf16[2,208,768]{2,1,0:T(8,128)(2,1)}, bf16[2,208,768]{2,1,0:T(8,128)(2,1)S(1)}, u32[]{:S(2)}) copy-start(bf16[2,208,768]{2,1,0:T(8,128)(2,1)S(1)} %pad_maximum_fusion.2.refs_4_) | copy-start | bytes 1916932
  21.8 47.6 %copy-start.12 = (bf16[2,208,768]{2,1,0:T(8,128)(2,1)}, bf16[2,208,768]{2,1,0:T(8,128)(2,1)S(1)}, u32[]{:S(2)}) copy-start(bf16[2,208,768]{2,1,0:T(8,128)(2,1)S(1)} %pad_maximum_fusion.3.refs_8_) | copy-start | bytes 1916932
  21.8 46.4 %copy-start.35 = (s32[16]{0:T(128)S(1)}, s32[16]{0:T(128)}, u32[]{:S(2)}) copy-start(s32[16]{0:T(128)} %param.19) | copy-start | bytes 196
  21.8 46.5 %copy-start.10 = (bf16[16,128,768]{2,1,0:T(8,128)(2,1)S(1)}, bf16[16,128,768]{2,1,0:T(8,128)(2,1)}, u32[]{:S(2)}) copy-start(bf16[16,128,768]{2,1,0:T(8,128)(2,1)} %param.35) | copy-start | bytes 9437188
  26.8 27.6 %copy-start.29 = (bf16[256,768]{1,0:T(8,128)(2,1)}, bf16[256,768]{1,0:T(8,128)(2,1)S(1)}, u32[]{:S(2)}) copy-start(bf16[256,768]{1,0:T(8,128)(2,1)S(1)} %collective-permute-done.1.refs_1_) | copy-start | bytes 1179652
  26.8 14.7 %collective-permute-start.2 = (bf16[2,208,768]{2,1,0:T(8,128)(2,1)S(1)}, bf16[2,208,768]{2,1,0:T(8,128)(2,1)S(1)}, u32[]{:S(2)}, u32[]{:S(2)}) collective-permute-start(bf16[2,208,768]{2,1,0:T(8,128)(2,1)S(1)} %pad_maximum_fusion.2.refs_4_), channel_id=1, source_target_pairs={{0,16},{8,24},{16,0},{24,8},{1,17},{9,25},{17,1},{25,9},{2,18},{10... | collective-permute-start | bytes 1916936 | tf_op jit(solution)/shard_map/ppermute | solution.py:619
  27.3 14.4 %collective-permute-start.4 = (bf16[2,208,768]{2,1,0:T(8,128)(2,1)S(1)}, bf16[2,208,768]{2,1,0:T(8,128)(2,1)S(1)}, u32[]{:S(2)}, u32[]{:S(2)}) collective-permute-start(bf16[2,208,768]{2,1,0:T(8,128)(2,1)S(1)} %pad_maximum_fusion.3.refs_8_), channel_id=1, source_target_pairs={{0,1},{1,0},{2,3},{3,2},{4,5},{5,4},{6,7},{7,6},{8,9},{9,8},{10,11... | collective-permute-start | bytes 1916936 | tf_op jit(solution)/shard_map/ppermute | solution.py:619
  27.7 11.1 %collective-permute-start.5 = (bf16[256,768]{1,0:T(8,128)(2,1)S(1)}, bf16[256,768]{1,0:T(8,128)(2,1)S(1)}, u32[]{:S(2)}, u32[]{:S(2)}) collective-permute-start(bf16[256,768]{1,0:T(8,128)(2,1)S(1)} %bitcast.110), channel_id=1, source_target_pairs={{0,6},{2,4},{4,2},{6,0},{1,7},{3,5},{5,3},{7,1},{8,14},{10,12},{12... | collective-permute-start | bytes 1179656 | tf_op jit(solution)/shard_map/ppermute | solution.py:597
  41.5 27.9 %copy-start.23 = (bf16[2,208,768]{2,1,0:T(8,128)(2,1)}, bf16[2,208,768]{2,1,0:T(8,128)(2,1)S(1)}, u32[]{:S(2)}) copy-start(bf16[2,208,768]{2,1,0:T(8,128)(2,1)S(1)} %collective-permute-done.2.refs_5_) | copy-start | bytes 1916932
  41.8 26.5 %copy-start.24 = (bf16[2,208,768]{2,1,0:T(8,128)(2,1)}, bf16[2,208,768]{2,1,0:T(8,128)(2,1)S(1)}, u32[]{:S(2)}) copy-start(bf16[2,208,768]{2,1,0:T(8,128)(2,1)S(1)} %collective-permute-done.4.refs_9_) | copy-start | bytes 1916932
  41.8 12.6 %collective-permute-start.7 = (bf16[1,192,1536]{2,1,0:T(8,128)(2,1)S(1)}, bf16[1,192,1536]{2,1,0:T(8,128)(2,1)S(1)}, u32[]{:S(2)}, u32[]{:S(2)}) collective-permute-start(bf16[1,192,1536]{2,1,0:T(8,128)(2,1)S(1)} %bitcast.100), channel_id=1, source_target_pairs={{0,16},{8,24},{16,0},{24,8},{1,17},{9,25},{17,1},{25,9},{2,18},{10... | collective-permute-start | bytes 1769480 | tf_op jit(solution)/shard_map/ppermute | solution.py:619
  43.3 22.8 %collective-permute-start.6 = (bf16[1,192,1536]{2,1,0:T(8,128)(2,1)S(1)}, bf16[1,192,1536]{2,1,0:T(8,128)(2,1)S(1)}, u32[]{:S(2)}, u32[]{:S(2)}) collective-permute-start(bf16[1,192,1536]{2,1,0:T(8,128)(2,1)S(1)} %bitcast.102), channel_id=1, source_target_pairs={{0,1},{1,0},{2,3},{3,2},{4,5},{5,4},{6,7},{7,6},{8,9},{9,8},{10,11... | collective-permute-start | bytes 1769480 | tf_op jit(solution)/shard_map/ppermute | solution.py:619
  43.8 22.3 %collective-permute-start.8 = (bf16[256,768]{1,0:T(8,128)(2,1)S(1)}, bf16[256,768]{1,0:T(8,128)(2,1)S(1)}, u32[]{:S(2)}, u32[]{:S(2)}) collective-permute-start(bf16[256,768]{1,0:T(8,128)(2,1)S(1)} %bitcast.108), channel_id=1, source_target_pairs={{0,4},{2,6},{4,0},{6,2},{1,5},{3,7},{5,1},{7,3},{8,12},{10,14},{12... | collective-permute-start | bytes 1179656 | tf_op jit(solution)/shard_map/ppermute | solution.py:597
  50.9 16.7 %collective-permute-start.11 = (bf16[2,208,768]{2,1,0:T(8,128)(2,1)S(1)}, bf16[2,208,768]{2,1,0:T(8,128)(2,1)S(1)}, u32[]{:S(2)}, u32[]{:S(2)}) collective-permute-start(bf16[2,208,768]{2,1,0:T(8,128)(2,1)S(1)} %pad_maximum_fusion.3.refs_8_), channel_id=1, source_target_pairs={{0,8},{8,0},{16,24},{24,16},{1,9},{9,1},{17,25},{25,17},{2,10},{10... | collective-permute-start | bytes 1916936 | tf_op jit(solution)/shard_map/ppermute | solution.py:619
  50.9 17.3 %collective-permute-start.9 = (bf16[2,208,768]{2,1,0:T(8,128)(2,1)S(1)}, bf16[2,208,768]{2,1,0:T(8,128)(2,1)S(1)}, u32[]{:S(2)}, u32[]{:S(2)}) collective-permute-start(bf16[2,208,768]{2,1,0:T(8,128)(2,1)S(1)} %pad_maximum_fusion.2.refs_4_), channel_id=1, source_target_pairs={{0,8},{8,0},{16,24},{24,16},{1,9},{9,1},{17,25},{25,17},{2,10},{10... | collective-permute-start | bytes 1916936 | tf_op jit(solution)/shard_map/ppermute | solution.py:619
  54.4 13.8 %collective-permute-start.10 = (bf16[2,208,768]{2,1,0:T(8,128)(2,1)S(1)}, bf16[2,208,768]{2,1,0:T(8,128)(2,1)S(1)}, u32[]{:S(2)}, u32[]{:S(2)}) collective-permute-start(bf16[2,208,768]{2,1,0:T(8,128)(2,1)S(1)} %collective-permute-done.2.refs_5_), channel_id=1, source_target_pairs={{0,8},{8,0},{16,24},{24,16},{1,9},{9,1},{17,25},{25,17},{2,10},{10... | collective-permute-start | bytes 1916936 | tf_op jit(solution)/shard_map/ppermute | solution.py:619
  54.5 50.6 %copy-start.8 = (bf16[2,192,1536]{2,1,0:T(8,128)(2,1)}, bf16[2,192,1536]{2,1,0:T(8,128)(2,1)S(1)}, u32[]{:S(2)}) copy-start(bf16[2,192,1536]{2,1,0:T(8,128)(2,1)S(1)} %pad_maximum_fusion.1.refs_16_) | copy-start | bytes 3538948
  66.1 2.1 collective-permute-start.12
  66.9 38.8 %collective-permute-start.19 = (bf16[2,192,1536]{2,1,0:T(8,128)(2,1)S(1)}, bf16[2,192,1536]{2,1,0:T(8,128)(2,1)}, u32[]{:S(2)}, u32[]{:S(2)}) collective-permute-start(bf16[2,192,1536]{2,1,0:T(8,128)(2,1)S(1)} %pad_maximum_fusion.1.refs_16_), channel_id=1, source_target_pairs={{0,1},{1,0},{2,3},{3,2},{4,5},{5,4},{6,7},{7,6},{8,9},{9,8},{10,11... | collective-permute-start | bytes 3538952 | tf_op jit(solution)/shard_map/ppermute | solution.py:619
  67.5 37.6 %copy-start.9 = (bf16[2,192,1536]{2,1,0:T(8,128)(2,1)}, bf16[2,192,1536]{2,1,0:T(8,128)(2,1)S(1)}, u32[]{:S(2)}) copy-start(bf16[2,192,1536]{2,1,0:T(8,128)(2,1)S(1)} %pad_maximum_fusion.refs_12_) | copy-start | bytes 3538948
  67.6 38.2 %collective-permute-start.16 = (bf16[2,192,1536]{2,1,0:T(8,128)(2,1)S(1)}, bf16[2,192,1536]{2,1,0:T(8,128)(2,1)}, u32[]{:S(2)}, u32[]{:S(2)}) collective-permute-start(bf16[2,192,1536]{2,1,0:T(8,128)(2,1)S(1)} %pad_maximum_fusion.refs_12_), channel_id=1, source_target_pairs={{0,16},{8,24},{16,0},{24,8},{1,17},{9,25},{17,1},{25,9},{2,18},{10... | collective-permute-start | bytes 3538952 | tf_op jit(solution)/shard_map/ppermute | solution.py:619
  69.4 34.9 %collective-permute-start.13 = (bf16[256,768]{1,0:T(8,128)(2,1)}, bf16[256,768]{1,0:T(8,128)(2,1)S(1)}, u32[]{:S(2)}, u32[]{:S(2)}) collective-permute-start(bf16[256,768]{1,0:T(8,128)(2,1)} %bitcast.14), channel_id=1, source_target_pairs={{0,2},{2,0},{4,6},{6,4},{1,3},{3,1},{5,7},{7,5},{8,10},{10,8},{12,... | collective-permute-start | bytes 1179656 | tf_op jit(solution)/shard_map/ppermute | solution.py:597
  69.4 34.9 %collective-permute-start.14 = (bf16[256,768]{1,0:T(8,128)(2,1)S(1)}, bf16[256,768]{1,0:T(8,128)(2,1)S(1)}, u32[]{:S(2)}, u32[]{:S(2)}) collective-permute-start(bf16[256,768]{1,0:T(8,128)(2,1)S(1)} %bitcast.111), channel_id=1, source_target_pairs={{0,4},{2,6},{4,0},{6,2},{1,5},{3,7},{5,1},{7,3},{8,12},{10,14},{12... | collective-permute-start | bytes 1179656 | tf_op jit(solution)/shard_map/ppermute | solution.py:597
  72.3 32.0 %collective-permute-start.15 = (bf16[256,768]{1,0:T(8,128)(2,1)S(1)}, bf16[256,768]{1,0:T(8,128)(2,1)}, u32[]{:S(2)}, u32[]{:S(2)}) collective-permute-start(bf16[256,768]{1,0:T(8,128)(2,1)S(1)} %bitcast.109), channel_id=1, source_target_pairs={{0,6},{2,4},{4,2},{6,0},{1,7},{3,5},{5,3},{7,1},{8,14},{10,12},{12... | collective-permute-start | bytes 1179656 | tf_op jit(solution)/shard_map/ppermute | solution.py:597
  105.1 2.8 collective-permute-start.20
  105.2 4.5 %collective-permute-start.17 = (bf16[2,192,1536]{2,1,0:T(8,128)(2,1)S(1)}, bf16[2,192,1536]{2,1,0:T(8,128)(2,1)S(1)}, u32[]{:S(2)}, u32[]{:S(2)}) collective-permute-start(bf16[2,192,1536]{2,1,0:T(8,128)(2,1)S(1)} %pad_maximum_fusion.refs_12_), channel_id=1, source_target_pairs={{0,8},{8,0},{16,24},{24,16},{1,9},{9,1},{17,25},{25,17},{2,10},{10... | collective-permute-start | bytes 3538952 | tf_op jit(solution)/shard_map/ppermute | solution.py:619
  105.7 5.7 %collective-permute-start.21 = (bf16[2,192,1536]{2,1,0:T(8,128)(2,1)}, bf16[2,192,1536]{2,1,0:T(8,128)(2,1)S(1)}, u32[]{:S(2)}, u32[]{:S(2)}) collective-permute-start(bf16[2,192,1536]{2,1,0:T(8,128)(2,1)} %collective-permute-done.19.refs_17_), channel_id=1, source_target_pairs={{0,8},{8,0},{16,24},{24,16},{1,9},{9,1},{17,25},{25,17},{2,10},{10... | collective-permute-start | bytes 3538952 | tf_op jit(solution)/shard_map/ppermute | solution.py:619
  105.7 7.3 %collective-permute-start.18 = (bf16[2,192,1536]{2,1,0:T(8,128)(2,1)}, bf16[2,192,1536]{2,1,0:T(8,128)(2,1)S(1)}, u32[]{:S(2)}, u32[]{:S(2)}) collective-permute-start(bf16[2,192,1536]{2,1,0:T(8,128)(2,1)} %collective-permute-done.16.refs_13_), channel_id=1, source_target_pairs={{0,8},{8,0},{16,24},{24,16},{1,9},{9,1},{17,25},{25,17},{2,10},{10... | collective-permute-start | bytes 3538952 | tf_op jit(solution)/shard_map/ppermute | solution.py:619
  160.0 15.2 %collective-permute-start.22 = (bf16[256,768]{1,0:T(8,128)(2,1)}, bf16[256,768]{1,0:T(8,128)(2,1)S(1)}, u32[]{:S(2)}, u32[]{:S(2)}) collective-permute-start(bf16[256,768]{1,0:T(8,128)(2,1)} %get-tuple-element.95), channel_id=1, source_target_pairs={{0,2},{2,0},{4,6},{6,4},{1,3},{3,1},{5,7},{7,5},{8,10},{10,8},{12,... | collective-permute-start | bytes 1179656 | tf_op jit(solution)/shard_map/ppermute | solution.py:597
  175.2 24.8 %collective-permute-start.25 = (bf16[2,2,208,1536]{3,2,1,0:T(8,128)(2,1)}, bf16[2,2,208,1536]{3,2,1,0:T(8,128)(2,1)}, u32[]{:S(2)}, u32[]{:S(2)}) collective-permute-start(bf16[2,2,208,1536]{3,2,1,0:T(8,128)(2,1)} %get-tuple-element.105), channel_id=1, source_target_pairs={{0,8},{8,0},{16,24},{24,16},{1,9},{9,1},{17,25},{25,17},{2,10},{10... | collective-permute-start | bytes 7667720 | tf_op jit(solution)/shard_map/ppermute | solution.py:681
  175.2 15.5 %collective-permute-start.23 = (bf16[256,768]{1,0:T(8,128)(2,1)}, bf16[256,768]{1,0:T(8,128)(2,1)S(1)}, u32[]{:S(2)}, u32[]{:S(2)}) collective-permute-start(bf16[256,768]{1,0:T(8,128)(2,1)} %get-tuple-element.96), channel_id=1, source_target_pairs={{0,6},{2,4},{4,2},{6,0},{1,7},{3,5},{5,3},{7,1},{8,14},{10,12},{12... | collective-permute-start | bytes 1179656 | tf_op jit(solution)/shard_map/ppermute | solution.py:597
  190.7 42.4 %collective-permute-start.26 = (bf16[2,2,208,1536]{3,2,1,0:T(8,128)(2,1)}, bf16[2,2,208,1536]{3,2,1,0:T(8,128)(2,1)}, u32[]{:S(2)}, u32[]{:S(2)}) collective-permute-start(bf16[2,2,208,1536]{3,2,1,0:T(8,128)(2,1)} %get-tuple-element.111), channel_id=1, source_target_pairs={{0,8},{8,0},{16,24},{24,16},{1,9},{9,1},{17,25},{25,17},{2,10},{10... | collective-permute-start | bytes 7667720 | tf_op jit(solution)/shard_map/ppermute | solution.py:681
  190.9 41.7 %collective-permute-start.28 = (bf16[256,768]{1,0:T(8,128)(2,1)S(1)}, bf16[256,768]{1,0:T(8,128)(2,1)}, u32[]{:S(2)}, u32[]{:S(2)}) collective-permute-start(bf16[256,768]{1,0:T(8,128)(2,1)S(1)} %copy-done.32), channel_id=1, source_target_pairs={{0,4},{2,6},{4,0},{6,2},{1,5},{3,7},{5,1},{7,3},{8,12},{10,14},{12... | collective-permute-start | bytes 1179656 | tf_op jit(solution)/shard_map/ppermute | solution.py:597
  198.8 42.5 %collective-permute-start.24 = (bf16[768,768]{1,0:T(8,128)(2,1)}, bf16[768,768]{1,0:T(8,128)(2,1)}, u32[]{:S(2)}, u32[]{:S(2)}) collective-permute-start(bf16[768,768]{1,0:T(8,128)(2,1)} %constant_dynamic-update-slice_fusion), channel_id=1, source_target_pairs={{0,1},{1,0},{2,3},{3,2},{4,5},{5,4},{6,7},{7,6},{8,9},{9,8},{10,11... | collective-permute-start | bytes 3538952 | tf_op jit(solution)/shard_map/ppermute | solution.py:601
  204.9 33.5 %collective-permute-start.27 = (bf16[1,2,208,1536]{3,2,1,0:T(8,128)(2,1)}, bf16[1,2,208,1536]{3,2,1,0:T(8,128)(2,1)}, u32[]{:S(2)}, u32[]{:S(2)}) collective-permute-start(bf16[1,2,208,1536]{3,2,1,0:T(8,128)(2,1)} %split.49), channel_id=1, source_target_pairs={{0,16},{8,24},{16,0},{24,8},{1,17},{9,25},{17,1},{25,9},{2,18},{10... | collective-permute-start | bytes 3833864 | tf_op jit(solution)/shard_map/ppermute | solution.py:619
  232.6 34.4 %collective-permute-start.33 = (bf16[256,768]{1,0:T(8,128)(2,1)}, bf16[256,768]{1,0:T(8,128)(2,1)}, u32[]{:S(2)}, u32[]{:S(2)}) collective-permute-start(bf16[256,768]{1,0:T(8,128)(2,1)} %collective-permute-done.28), channel_id=1, source_target_pairs={{0,1},{1,0},{2,3},{3,2},{4,5},{5,4},{6,7},{7,6},{8,9},{9,8},{10,11... | collective-permute-start | bytes 1179656 | tf_op jit(solution)/shard_map/ppermute | solution.py:601
  237.5 29.7 %collective-permute-start.30 = (bf16[1,2,208,1536]{3,2,1,0:T(8,128)(2,1)}, bf16[1,2,208,1536]{3,2,1,0:T(8,128)(2,1)}, u32[]{:S(2)}, u32[]{:S(2)}) collective-permute-start(bf16[1,2,208,1536]{3,2,1,0:T(8,128)(2,1)} %split.51), channel_id=1, source_target_pairs={{0,16},{8,24},{16,0},{24,8},{1,17},{9,25},{17,1},{25,9},{2,18},{10... | collective-permute-start | bytes 3833864 | tf_op jit(solution)/shard_map/ppermute | solution.py:619
  241.3 29.0 %collective-permute-start.29 = (bf16[1,1,208,1536]{3,2,1,0:T(8,128)(2,1)S(1)}, bf16[1,1,208,1536]{3,2,1,0:T(8,128)(2,1)}, u32[]{:S(2)}, u32[]{:S(2)}) collective-permute-start(bf16[1,1,208,1536]{3,2,1,0:T(8,128)(2,1)S(1)} %split.50), channel_id=1, source_target_pairs={{0,1},{1,0},{2,3},{3,2},{4,5},{5,4},{6,7},{7,6},{8,9},{9,8},{10,11... | collective-permute-start | bytes 1916936 | tf_op jit(solution)/shard_map/ppermute | solution.py:619
  251.4 18.8 %collective-permute-start.31 = (bf16[256,768]{1,0:T(8,128)(2,1)}, bf16[256,768]{1,0:T(8,128)(2,1)S(1)}, u32[]{:S(2)}, u32[]{:S(2)}) collective-permute-start(bf16[256,768]{1,0:T(8,128)(2,1)} %get-tuple-element.120), channel_id=1, source_target_pairs={{0,2},{2,0},{4,6},{6,4},{1,3},{3,1},{5,7},{7,5},{8,10},{10,8},{12,... | collective-permute-start | bytes 1179656 | tf_op jit(solution)/shard_map/ppermute | solution.py:597
  251.5 18.8 %collective-permute-start.32 = (bf16[256,768]{1,0:T(8,128)(2,1)}, bf16[256,768]{1,0:T(8,128)(2,1)}, u32[]{:S(2)}, u32[]{:S(2)}) collective-permute-start(bf16[256,768]{1,0:T(8,128)(2,1)} %get-tuple-element.122), channel_id=1, source_target_pairs={{0,6},{2,4},{4,2},{6,0},{1,7},{3,5},{5,3},{7,1},{8,14},{10,12},{12... | collective-permute-start | bytes 1179656 | tf_op jit(solution)/shard_map/ppermute | solution.py:597
  271.0 5.2 %collective-permute-start.34 = (bf16[2,2,208,1536]{3,2,1,0:T(8,128)(2,1)}, bf16[2,2,208,1536]{3,2,1,0:T(8,128)(2,1)}, u32[]{:S(2)}, u32[]{:S(2)}) collective-permute-start(bf16[2,2,208,1536]{3,2,1,0:T(8,128)(2,1)} %get-tuple-element.127), channel_id=1, source_target_pairs={{0,8},{8,0},{16,24},{24,16},{1,9},{9,1},{17,25},{25,17},{2,10},{10... | collective-permute-start | bytes 7667720 | tf_op jit(solution)/shard_map/ppermute | solution.py:681
  272.8 49.5 %collective-permute-start.42 = (bf16[256,768]{1,0:T(8,128)(2,1)}, bf16[256,768]{1,0:T(8,128)(2,1)S(1)}, u32[]{:S(2)}, u32[]{:S(2)}) collective-permute-start(bf16[256,768]{1,0:T(8,128)(2,1)} %get-tuple-element.140), channel_id=1, source_target_pairs={{0,4},{2,6},{4,0},{6,2},{1,5},{3,7},{5,1},{7,3},{8,12},{10,14},{12... | collective-permute-start | bytes 1179656 | tf_op jit(solution)/shard_map/ppermute | solution.py:597
  278.8 16.5 %collective-permute-start.38 = (bf16[1,1,208,1536]{3,2,1,0:T(8,128)(2,1)S(1)}, bf16[1,1,208,1536]{3,2,1,0:T(8,128)(2,1)S(1)}, u32[]{:S(2)}, u32[]{:S(2)}) collective-permute-start(bf16[1,1,208,1536]{3,2,1,0:T(8,128)(2,1)S(1)} %split.47), channel_id=1, source_target_pairs={{0,1},{1,0},{2,3},{3,2},{4,5},{5,4},{6,7},{7,6},{8,9},{9,8},{10,11... | collective-permute-start | bytes 1916936 | tf_op jit(solution)/shard_map/ppermute | solution.py:619
  279.4 42.7 %collective-permute-start.36 = (bf16[1,2,208,1536]{3,2,1,0:T(8,128)(2,1)S(1)}, bf16[1,2,208,1536]{3,2,1,0:T(8,128)(2,1)S(1)}, u32[]{:S(2)}, u32[]{:S(2)}) collective-permute-start(bf16[1,2,208,1536]{3,2,1,0:T(8,128)(2,1)S(1)} %split.53), channel_id=1, source_target_pairs={{0,16},{8,24},{16,0},{24,8},{1,17},{9,25},{17,1},{25,9},{2,18},{10... | collective-permute-start | bytes 3833864 | tf_op jit(solution)/shard_map/ppermute | solution.py:619
  295.5 14.0 %collective-permute-start.39 = (bf16[416,384]{1,0:T(8,128)(2,1)S(1)}, bf16[416,384]{1,0:T(8,128)(2,1)S(1)}, u32[]{:S(2)}, u32[]{:S(2)}) collective-permute-start(bf16[416,384]{1,0:T(8,128)(2,1)S(1)} %pad_maximum_fusion.4), channel_id=1, source_target_pairs={{0,2},{2,0},{4,6},{6,4},{1,3},{3,1},{5,7},{7,5},{8,10},{10,8},{12,... | collective-permute-start | bytes 958472 | tf_op jit(solution)/shard_map/ppermute | solution.py:597
  296.8 25.1 %collective-permute-start.40 = (bf16[416,384]{1,0:T(8,128)(2,1)S(1)}, bf16[416,384]{1,0:T(8,128)(2,1)S(1)}, u32[]{:S(2)}, u32[]{:S(2)}) collective-permute-start(bf16[416,384]{1,0:T(8,128)(2,1)S(1)} %pad_maximum_fusion.5), channel_id=1, source_target_pairs={{0,4},{2,6},{4,0},{6,2},{1,5},{3,7},{5,1},{7,3},{8,12},{10,14},{12... | collective-permute-start | bytes 958472 | tf_op jit(solution)/shard_map/ppermute | solution.py:597
  297.9 24.0 %collective-permute-start.41 = (bf16[416,384]{1,0:T(8,128)(2,1)S(1)}, bf16[416,384]{1,0:T(8,128)(2,1)S(1)}, u32[]{:S(2)}, u32[]{:S(2)}) collective-permute-start(bf16[416,384]{1,0:T(8,128)(2,1)S(1)} %pad_maximum_fusion.6), channel_id=1, source_target_pairs={{0,6},{2,4},{4,2},{6,0},{1,7},{3,5},{5,3},{7,1},{8,14},{10,12},{12... | collective-permute-start | bytes 958472 | tf_op jit(solution)/shard_map/ppermute | solution.py:597
  309.6 54.5 %collective-permute-start.35 = (bf16[768,768]{1,0:T(8,128)(2,1)S(1)}, bf16[768,768]{1,0:T(8,128)(2,1)S(1)}, u32[]{:S(2)}, u32[]{:S(2)}) collective-permute-start(bf16[768,768]{1,0:T(8,128)(2,1)S(1)} %constant_dynamic-update-slice_fusion.3), channel_id=1, source_target_pairs={{0,1},{1,0},{2,3},{3,2},{4,5},{5,4},{6,7},{7,6},{8,9},{9,8},{10,11... | collective-permute-start | bytes 3538952 | tf_op jit(solution)/shard_map/ppermute | solution.py:601
  322.3 16.2 %collective-permute-start.50 = (bf16[416,384]{1,0:T(8,128)(2,1)S(1)}, bf16[416,384]{1,0:T(8,128)(2,1)S(1)}, u32[]{:S(2)}, u32[]{:S(2)}) collective-permute-start(bf16[416,384]{1,0:T(8,128)(2,1)S(1)} %add_convert_fusion.9), channel_id=1, source_target_pairs={{0,2},{2,0},{4,6},{6,4},{1,3},{3,1},{5,7},{7,5},{8,10},{10,8},{12,... | collective-permute-start | bytes 958472 | tf_op jit(solution)/shard_map/ppermute | solution.py:597
  327.9 24.9 %collective-permute-start.51 = (bf16[416,384]{1,0:T(8,128)(2,1)S(1)}, bf16[416,384]{1,0:T(8,128)(2,1)S(1)}, u32[]{:S(2)}, u32[]{:S(2)}) collective-permute-start(bf16[416,384]{1,0:T(8,128)(2,1)S(1)} %add_convert_fusion.9), channel_id=1, source_target_pairs={{0,4},{2,6},{4,0},{6,2},{1,5},{3,7},{5,1},{7,3},{8,12},{10,14},{12... | collective-permute-start | bytes 958472 | tf_op jit(solution)/shard_map/ppermute | solution.py:597
  328.0 24.9 %collective-permute-start.52 = (bf16[416,384]{1,0:T(8,128)(2,1)S(1)}, bf16[416,384]{1,0:T(8,128)(2,1)S(1)}, u32[]{:S(2)}, u32[]{:S(2)}) collective-permute-start(bf16[416,384]{1,0:T(8,128)(2,1)S(1)} %add_convert_fusion.9), channel_id=1, source_target_pairs={{0,6},{2,4},{4,2},{6,0},{1,7},{3,5},{5,3},{7,1},{8,14},{10,12},{12... | collective-permute-start | bytes 958472 | tf_op jit(solution)/shard_map/ppermute | solution.py:597
  330.5 26.4 %collective-permute-start.37 = (bf16[1,1,208,1536]{3,2,1,0:T(8,128)(2,1)S(1)}, bf16[1,1,208,1536]{3,2,1,0:T(8,128)(2,1)S(1)}, u32[]{:S(2)}, u32[]{:S(2)}) collective-permute-start(bf16[1,1,208,1536]{3,2,1,0:T(8,128)(2,1)S(1)} %split.55), channel_id=1, source_target_pairs={{0,1},{1,0},{2,3},{3,2},{4,5},{5,4},{6,7},{7,6},{8,9},{9,8},{10,11... | collective-permute-start | bytes 1916936 | tf_op jit(solution)/shard_map/ppermute | solution.py:619
  357.1 11.1 %collective-permute-start.44 = (bf16[208,384]{1,0:T(8,128)(2,1)S(1)}, bf16[208,384]{1,0:T(8,128)(2,1)S(1)}, u32[]{:S(2)}, u32[]{:S(2)}) collective-permute-start(bf16[208,384]{1,0:T(8,128)(2,1)S(1)} %get-tuple-element.170), channel_id=1, source_target_pairs={{0,2},{2,0},{4,6},{6,4},{1,3},{3,1},{5,7},{7,5},{8,10},{10,8},{12,... | collective-permute-start | bytes 479240 | tf_op jit(solution)/shard_map/ppermute | solution.py:597
  361.7 11.9 %collective-permute-start.45 = (bf16[208,384]{1,0:T(8,128)(2,1)S(1)}, bf16[208,384]{1,0:T(8,128)(2,1)S(1)}, u32[]{:S(2)}, u32[]{:S(2)}) collective-permute-start(bf16[208,384]{1,0:T(8,128)(2,1)S(1)} %get-tuple-element.172), channel_id=1, source_target_pairs={{0,4},{2,6},{4,0},{6,2},{1,5},{3,7},{5,1},{7,3},{8,12},{10,14},{12... | collective-permute-start | bytes 479240 | tf_op jit(solution)/shard_map/ppermute | solution.py:597
  361.7 11.8 %collective-permute-start.46 = (bf16[208,384]{1,0:T(8,128)(2,1)S(1)}, bf16[208,384]{1,0:T(8,128)(2,1)S(1)}, u32[]{:S(2)}, u32[]{:S(2)}) collective-permute-start(bf16[208,384]{1,0:T(8,128)(2,1)S(1)} %get-tuple-element.171), channel_id=1, source_target_pairs={{0,6},{2,4},{4,2},{6,0},{1,7},{3,5},{5,3},{7,1},{8,14},{10,12},{12... | collective-permute-start | bytes 479240 | tf_op jit(solution)/shard_map/ppermute | solution.py:597
  364.3 29.0 %collective-permute-start.43 = (bf16[256,768]{1,0:T(8,128)(2,1)S(1)}, bf16[256,768]{1,0:T(8,128)(2,1)S(1)}, u32[]{:S(2)}, u32[]{:S(2)}) collective-permute-start(bf16[256,768]{1,0:T(8,128)(2,1)S(1)} %collective-permute-done.42), channel_id=1, source_target_pairs={{0,1},{1,0},{2,3},{3,2},{4,5},{5,4},{6,7},{7,6},{8,9},{9,8},{10,11... | collective-permute-start | bytes 1179656 | tf_op jit(solution)/shard_map/ppermute | solution.py:601
  373.6 7.5 %collective-permute-start.47 = (bf16[208,384]{1,0:T(8,128)(2,1)S(1)}, bf16[208,384]{1,0:T(8,128)(2,1)S(1)}, u32[]{:S(2)}, u32[]{:S(2)}) collective-permute-start(bf16[208,384]{1,0:T(8,128)(2,1)S(1)} %get-tuple-element.146), channel_id=1, source_target_pairs={{0,2},{2,0},{4,6},{6,4},{1,3},{3,1},{5,7},{7,5},{8,10},{10,8},{12,... | collective-permute-start | bytes 479240 | tf_op jit(solution)/shard_map/ppermute | solution.py:597
  376.6 13.2 %collective-permute-start.48 = (bf16[208,384]{1,0:T(8,128)(2,1)S(1)}, bf16[208,384]{1,0:T(8,128)(2,1)S(1)}, u32[]{:S(2)}, u32[]{:S(2)}) collective-permute-start(bf16[208,384]{1,0:T(8,128)(2,1)S(1)} %get-tuple-element.146), channel_id=1, source_target_pairs={{0,4},{2,6},{4,0},{6,2},{1,5},{3,7},{5,1},{7,3},{8,12},{10,14},{12... | collective-permute-start | bytes 479240 | tf_op jit(solution)/shard_map/ppermute | solution.py:597
  376.7 13.1 %collective-permute-start.49 = (bf16[208,384]{1,0:T(8,128)(2,1)S(1)}, bf16[208,384]{1,0:T(8,128)(2,1)S(1)}, u32[]{:S(2)}, u32[]{:S(2)}) collective-permute-start(bf16[208,384]{1,0:T(8,128)(2,1)S(1)} %get-tuple-element.146), channel_id=1, source_target_pairs={{0,6},{2,4},{4,2},{6,0},{1,7},{3,5},{5,3},{7,1},{8,14},{10,12},{12... | collective-permute-start | bytes 479240 | tf_op jit(solution)/shard_map/ppermute | solution.py:597
  (25 other events, 173.2 us)

commit v10 on v9

--- a/solution.py
+++ b/solution.py
@@ -641,7 +641,7 @@
     near_x = ctx_moved(x_pieces[1], 1)
     before = [near_x]
     x_pieces[1] = near_x
-    for k in [*range(3, C, 2), *range(2, C, 2)]:
+    for k in [*range(2, C, 2), *range(3, C, 2)]:
         x_pieces[k] = ctx_moved(after(x_pieces[k], before), k)
         before = [x_pieces[k]]
     vectors = [output_bias, attn_gain, attn_shift, outer_bias, ffn_gain, ffn_shift]
@@ -658,11 +658,11 @@
     high = chip_start(jnp.concatenate([high, small[:, D:]], axis=0), True)
     lows = both_cores(low, chip_end(after(low, [near_x]), False))
     highs = both_cores(high, chip_end(after(high, [near_x]), True))
-    halfway = [lows[1], highs[1], *x_pieces[3::2]]
+    halfway = [lows[1], highs[1], *x_pieces[2::2]]
     inner = chip_start(after(inner_weight, halfway), False)
     outer = chip_start(after(outer_weight.T, halfway), True)
-    inner_got = chip_end(after(inner, x_pieces[2::2]), False)
-    outer_got = chip_end(after(outer, x_pieces[2::2]), True)
+    inner_got = chip_end(after(inner, x_pieces[3::2]), False)
+    outer_got = chip_end(after(outer, x_pieces[3::2]), True)
     cot_pieces = sequence_pieces(after(cotangent, [*x_pieces[1:], *lows, *highs]))
     cot_pieces = [ctx_moved(piece, k) for k, piece in enumerate(cot_pieces)]
     lengths = lax.dynamic_slice_in_dim(seq_lengths, (c * T + t) * ns, ns, 0)

time: 397 us -> 399 us (level)
  transfers between devices with their start and end apart: 53 -> 53, of which waited for: 24 -> 22; matrix products, arithmetic and copies ran while one was open for 10% -> 10% of each run, Pallas kernels for 26% -> 26%
where the time goes in v10:
time: 399 us; the launch traced here: 397 us
  Pallas kernels  150 us (38%)
  waiting for transfers between devices  111 us (28%)
  starting transfers between devices  77.9 us (20%)
  local copies, waits for them, and re-layouts  36.5 us (9%)
  other arithmetic  20.2 us (5%)
    ppermute x24, waiting for transfers between devices, ctx_moved(): return lax.ppermute(piece, 'ctx', xor_pairs(C, k)) if k else piece  84.3 us
    ppermute x24, starting transfers between devices, ctx_moved(): return lax.ppermute(piece, 'ctx', xor_pairs(C, k)) if k else piece  56.5 us
    pallas_call x1, Pallas kernels, rows_call(): pl.pallas_call(functools.partial(rows_kernel, dims, FF), name='rows', gri...  45.9 us
    pallas_call x3, Pallas kernels, weight_call(): pl.pallas_call(functools.partial(weight_kernel, F, pers, sums is not None...  39.9 us
    pallas_call x1, Pallas kernels, front_call(): pl.pallas_call(functools.partial(front_kernel, dims), name='front', grid=...  29.9 us
    ppermute x22, waiting for transfers between devices, swapped(): return lax.ppermute(array, axis, xor_pairs(lax.axis_size(axis), bit))  26.3 us
    pallas_call x1, Pallas kernels, back_call(): pl.pallas_call(functools.partial(back_kernel, dims), name='back', grid=(n...  26.2 us
    ppermute x22, starting transfers between devices, swapped(): return lax.ppermute(array, axis, xor_pairs(lax.axis_size(axis), bit))  18.6 us
  transfers between devices with their start and end apart: 53, of which 22 were waited for; matrix products, arithmetic and copies ran while one was open for 10% of the time, Pallas kernels for 26%

profile of v10, /device:TPU:0, one launch (start us, length us, event | category | flops | bytes accessed | tf_op | source)
XLA Modules:
  0.0 397.3 jit_solution(6566176782830012547)
XLA Ops:
  2.4 4.1 %concatenate.53 = bf16[1152]{0:T(1024)(128)(2,1)S(1)} concatenate(bf16[192]{0:T(256)(128)(2,1)} %param.26, bf16[192]{0:T(256)(128)(2,1)} %param.27, bf16[192]{0:T(256)(128)(2,1)} %param.28, bf16[192]{0:T(256)(128)(2,1)} %param.32, bf16[192]{0:T(256)(128)(2,1)} %param.33, bf16[192]{0:T(256)(128)(2,1)} %param.34), dimensions={0} | concatenate | bytes 4608 | tf_op jit(solution)/shard_map/concatenate | solution.py:648
  8.6 3.0 collective-permute-start
  12.6 1.6 collective-permute-start.3
  14.2 2.3 constant_dynamic-slice_fusion.15
  16.5 1.6 collective-permute-start.1
  19.2 2.5 collective-permute-done.3
  21.8 5.0 %collective-permute-done.1.refs_1_ = bf16[256,768]{1,0:T(8,128)(2,1)S(1)} collective-permute-done((bf16[256,768]{1,0:T(8,128)(2,1)S(1)}, bf16[256,768]{1,0:T(8,128)(2,1)S(1)}, u32[]{:S(2)}, u32[]{:S(2)}) %collective-permute-start.1) | collective-permute-done | bytes 393248 | tf_op jit(solution)/shard_map/ppermute | solution.py:597
  27.7 2.7 collective-permute-start.5
  30.5 15.7 %collective-permute-done.5.refs_2_ = bf16[256,768]{1,0:T(8,128)(2,1)S(1)} collective-permute-done((bf16[256,768]{1,0:T(8,128)(2,1)S(1)}, bf16[256,768]{1,0:T(8,128)(2,1)S(1)}, u32[]{:S(2)}, u32[]{:S(2)}) %collective-permute-start.5) | collective-permute-done | bytes 393248 | tf_op jit(solution)/shard_map/ppermute | solution.py:597
  46.2 1.5 collective-permute-start.7
  47.7 1.5 collective-permute-start.6
  49.2 3.5 collective-permute-start.8
  53.2 7.5 %collective-permute-done.7 = bf16[1,192,1536]{2,1,0:T(8,128)(2,1)S(1)} collective-permute-done((bf16[1,192,1536]{2,1,0:T(8,128)(2,1)S(1)}, bf16[1,192,1536]{2,1,0:T(8,128)(2,1)S(1)}, u32[]{:S(2)}, u32[]{:S(2)}) %collective-permute-start.7) | collective-permute-done | bytes 589856 | tf_op jit(solution)/shard_map/ppermute | solution.py:619
  63.3 1.3 collective-permute-start.16
  64.7 1.1 constant_dynamic-slice_fusion.11
  65.9 6.2 %collective-permute-start.13 = (bf16[256,768]{1,0:T(8,128)(2,1)}, bf16[256,768]{1,0:T(8,128)(2,1)S(1)}, u32[]{:S(2)}, u32[]{:S(2)}) collective-permute-start(bf16[256,768]{1,0:T(8,128)(2,1)} %bitcast.14), channel_id=1, source_target_pairs={{0,2},{2,0},{4,6},{6,4},{1,3},{3,1},{5,7},{7,5},{8,10},{10,8},{12,... | collective-permute-start | bytes 1179656 | tf_op jit(solution)/shard_map/ppermute | solution.py:597
  72.1 2.4 collective-permute-start.15
  75.1 29.9 %front.1 = (bf16[4,256,768]{2,1,0:T(8,128)(2,1)}, bf16[768,2304]{1,0:T(8,128)(2,1)}, bf16[4,2,128,2304]{3,2,1,0:T(8,128)(2,1)}, bf16[12,1024,512]{2,1,0:T(8,128)...) custom-call(s32[4]{0:T(128)} %pad_add_fusion.meta, bf16[256,768]{1,0:T(8,128)(2,1)} %bitcast.106, ...), custom_call_target="tpu_custom_call" | custom-call | flops 3623878656 | bytes 40000000 | tf_op jit(solution)/shard_map/front/pallas_call | solution.py:162
  106.9 1.8 collective-permute-done.20.refs_18_
  108.7 1.7 collective-permute-done.17.refs_14_
  114.8 45.9 %rows.1 = (bf16[256,768]{1,0:T(8,128)(2,1)}, bf16[256,768]{1,0:T(8,128)(2,1)}, bf16[256,768]{1,0:T(8,128)(2,1)}, bf16[256,768]{1,0:T(8,128)(2,1)}, f32[4,256,768...) custom-call(s32[4]{0:T(128)} %pad_add_fusion.meta, ...), custom_call_target="tpu_custom_call" | custom-call | flops 21743271936 | bytes 50000000 | tf_op jit(solution)/shard_map/rows/pallas_call | solution.py:360
  160.6 4.0 collective-permute-start.22
  164.6 12.9 %weight_grad.3 = (bf16[2,2,208,1536]{3,2,1,0:T(8,128)(2,1)}, bf16[2,2,208,1536]{3,2,1,0:T(8,128)(2,1)}) custom-call(s32[4]{0:T(128)} %pad_add_fusion.meta, bf16[1024,768]{1,0:T(8,128)(2,1)} %bitcast.126, bf16[1024,3072]{1,0:T(8,128)(2,1)} %bitcast.122, f32[16,768]{1,0:T(8,128)} %get-tuple-element.102.refs_2_), custom_call_target="tpu_custom_call" | custom-call | flops 4831838208 | bytes 12582912 | tf_op jit(solution)/shard_map/weight_grad/pallas_call | solution.py:539
  177.5 1.2 collective-permute-start.23
  178.8 13.0 %weight_grad.4 = (bf16[2,2,208,1536]{3,2,1,0:T(8,128)(2,1)}, bf16[2,2,208,1536]{3,2,1,0:T(8,128)(2,1)}) custom-call(s32[4]{0:T(128)} %pad_add_fusion.meta, bf16[1024,768]{1,0:T(8,128)(2,1)} %bitcast.125, bf16[1024,3072]{1,0:T(8,128)(2,1)} %bitcast.121), custom_call_target="tpu_custom_call" | custom-call | flops 4831838208 | bytes 12582912 | tf_op jit(solution)/shard_map/weight_grad/pallas_call | solution.py:539
  191.9 5.6 %collective-permute-start.28 = (bf16[256,768]{1,0:T(8,128)(2,1)S(1)}, bf16[256,768]{1,0:T(8,128)(2,1)}, u32[]{:S(2)}, u32[]{:S(2)}) collective-permute-start(bf16[256,768]{1,0:T(8,128)(2,1)S(1)} %copy-done.32), channel_id=1, source_target_pairs={{0,4},{2,6},{4,0},{6,2},{1,5},{3,7},{5,1},{7,3},{8,12},{10,14},{12... | collective-permute-start | bytes 1179656 | tf_op jit(solution)/shard_map/ppermute | solution.py:597
  200.7 2.4 add_convert_fusion.2
  203.1 1.5 copy-done
  204.5 1.1 split.49
  205.7 1.3 collective-permute-start.27
  207.0 26.2 %back.1 = bf16[4,2,128,2304]{3,2,1,0:T(8,128)(2,1)} custom-call(bf16[4,2,128,2304]{3,2,1,0:T(8,128)(2,1)} %get-tuple-element.98.qkv, bf16[4,2,128,768]{3,2,1,0:T(8,128)(2,1)} %get-tuple-element.88.ctx, bf16[4,2,128,768]{3,2,1,0:T(8,128)(2,1)} %bitcast.87, bf16[12,1024,512]{2,1,0:T(8,128)(2,1)} %get-tuple-element.113.e_ref, ...), custom_call_target="tpu_custom_call" | custom-call | flops 6442450944 | bytes 30000000 | tf_op jit(solution)/shard_map/back/pallas_call | solution.py:429
  233.7 3.2 add_convert_fusion.1
  237.0 1.1 split.51
  238.1 1.3 collective-permute-start.30
  239.4 1.6 add_convert_fusion.5
  242.2 1.3 collective-permute-start.29
  243.4 8.6 %input_grad.1 = (bf16[256,768]{1,0:T(8,128)(2,1)}, bf16[256,768]{1,0:T(8,128)(2,1)}, bf16[256,768]{1,0:T(8,128)(2,1)}, bf16[256,768]{1,0:T(8,128)(2,1)}) custom-call(bf16[4,256,2304]{2,1,0:T(8,128)(2,1)} %bitcast.83, bf16[768,2304]{1,0:T(8,128)(2,1)} %get-tuple-element.115.w, f32[4,256,768]{2,1,0:T(8,128)} %get-tuple-element.118.first), custom_call_target="tpu_custom_call" | custom-call | flops 3623878656 | bytes 15000000 | tf_op jit(solution)/shard_map/input_grad/pallas_call | solution.py:466
  252.4 2.4 collective-permute-start.32
  254.8 14.1 %weight_grad.5 = (bf16[2,2,208,1536]{3,2,1,0:T(8,128)(2,1)}, bf16[2,2,208,1536]{3,2,1,0:T(8,128)(2,1)}) custom-call(s32[4]{0:T(128)} %pad_add_fusion.meta, bf16[1024,768]{1,0:T(8,128)(2,1)} %bitcast.123, bf16[1024,768]{1,0:T(8,128)(2,1)} %bitcast.124, bf16[1024,2304]{1,0:T(8,128)(2,1)} %bitcast.84, bf16[1024,768]{1,0:T(8,128)(2,1)} %bitcast.86), custom_call_target="tpu_custom_call" | custom-call | flops 4831838208 | bytes 12582912 | tf_op jit(solution)/shard_map/weight_grad/pallas_call | solution.py:539
  268.9 3.0 collective-permute-done.32
  272.0 1.8 add_convert_fusion.3
  273.8 2.0 collective-permute-start.42
  275.8 1.2 fusion.1
  277.1 2.4 add_convert_fusion
  280.3 1.3 collective-permute-start.36
  281.6 1.3 fusion.17
  282.9 1.3 fusion.16
  285.9 10.3 %collective-permute-done.38 = bf16[1,1,208,1536]{3,2,1,0:T(8,128)(2,1)S(1)} collective-permute-done((bf16[1,1,208,1536]{3,2,1,0:T(8,128)(2,1)S(1)}, bf16[1,1,208,1536]{3,2,1,0:T(8,128)(2,1)S(1)}, u32[]{:S(2)}, u32[]{:S(2)}) %collective-permute-start.38) | collective-permute-done | bytes 639008 | tf_op jit(solution)/shard_map/ppermute | solution.py:619
  297.4 2.0 collective-permute-start.40
  299.5 1.6 collective-permute-start.41
  303.2 7.8 %collective-permute-done.39 = bf16[416,384]{1,0:T(8,128)(2,1)S(1)} collective-permute-done((bf16[416,384]{1,0:T(8,128)(2,1)S(1)}, bf16[416,384]{1,0:T(8,128)(2,1)S(1)}, u32[]{:S(2)}, u32[]{:S(2)}) %collective-permute-start.39) | collective-permute-done | bytes 319520 | tf_op jit(solution)/shard_map/ppermute | solution.py:597
  311.6 10.9 %collective-permute-done.40 = bf16[416,384]{1,0:T(8,128)(2,1)S(1)} collective-permute-done((bf16[416,384]{1,0:T(8,128)(2,1)S(1)}, bf16[416,384]{1,0:T(8,128)(2,1)S(1)}, u32[]{:S(2)}, u32[]{:S(2)}) %collective-permute-start.40) | collective-permute-done | bytes 319520 | tf_op jit(solution)/shard_map/ppermute | solution.py:597
  323.0 5.6 %collective-permute-start.50 = (bf16[416,384]{1,0:T(8,128)(2,1)S(1)}, bf16[416,384]{1,0:T(8,128)(2,1)S(1)}, u32[]{:S(2)}, u32[]{:S(2)}) collective-permute-start(bf16[416,384]{1,0:T(8,128)(2,1)S(1)} %add_convert_fusion.9), channel_id=1, source_target_pairs={{0,2},{2,0},{4,6},{6,4},{1,3},{3,1},{5,7},{7,5},{8,10},{10,8},{12,... | collective-permute-start | bytes 958472 | tf_op jit(solution)/shard_map/ppermute | solution.py:597
  329.8 1.5 collective-permute-start.52
  332.0 7.8 %collective-permute-done.50 = bf16[416,384]{1,0:T(8,128)(2,1)S(1)} collective-permute-done((bf16[416,384]{1,0:T(8,128)(2,1)S(1)}, bf16[416,384]{1,0:T(8,128)(2,1)S(1)}, u32[]{:S(2)}, u32[]{:S(2)}) %collective-permute-start.50) | collective-permute-done | bytes 319520 | tf_op jit(solution)/shard_map/ppermute | solution.py:597
  339.9 13.9 %collective-permute-done.51 = bf16[416,384]{1,0:T(8,128)(2,1)S(1)} collective-permute-done((bf16[416,384]{1,0:T(8,128)(2,1)S(1)}, bf16[416,384]{1,0:T(8,128)(2,1)S(1)}, u32[]{:S(2)}, u32[]{:S(2)}) %collective-permute-start.51) | collective-permute-done | bytes 319520 | tf_op jit(solution)/shard_map/ppermute | solution.py:597
  355.6 1.1 slice.165
  358.0 4.5 %collective-permute-start.44 = (bf16[208,384]{1,0:T(8,128)(2,1)S(1)}, bf16[208,384]{1,0:T(8,128)(2,1)S(1)}, u32[]{:S(2)}, u32[]{:S(2)}) collective-permute-start(bf16[208,384]{1,0:T(8,128)(2,1)S(1)} %get-tuple-element.170), channel_id=1, source_target_pairs={{0,2},{2,0},{4,6},{6,4},{1,3},{3,1},{5,7},{7,5},{8,10},{10,8},{12,... | collective-permute-start | bytes 479240 | tf_op jit(solution)/shard_map/ppermute | solution.py:597
  363.5 1.5 collective-permute-start.46
  366.7 8.2 %collective-permute-done.45 = bf16[208,384]{1,0:T(8,128)(2,1)S(1)} collective-permute-done((bf16[208,384]{1,0:T(8,128)(2,1)S(1)}, bf16[208,384]{1,0:T(8,128)(2,1)S(1)}, u32[]{:S(2)}, u32[]{:S(2)}) %collective-permute-start.45) | collective-permute-done | bytes 159776 | tf_op jit(solution)/shard_map/ppermute | solution.py:597
  375.0 2.3 collective-permute-start.47
  378.4 1.5 collective-permute-start.49
  379.9 2.2 collective-permute-done.47
  382.2 8.9 %collective-permute-done.48 = bf16[208,384]{1,0:T(8,128)(2,1)S(1)} collective-permute-done((bf16[208,384]{1,0:T(8,128)(2,1)S(1)}, bf16[208,384]{1,0:T(8,128)(2,1)S(1)}, u32[]{:S(2)}, u32[]{:S(2)}) %collective-permute-start.48) | collective-permute-done | bytes 159776 | tf_op jit(solution)/shard_map/ppermute | solution.py:597
  (229 shorter events, 44.1 us)
Async XLA Ops:
  8.6 10.6 %collective-permute-start = (bf16[1,208,768]{2,1,0:T(8,128)(2,1)S(1)}, bf16[1,208,768]{2,1,0:T(8,128)(2,1)S(1)}, u32[]{:S(2)}, u32[]{:S(2)}) collective-permute-start(bf16[1,208,768]{2,1,0:T(8,128)(2,1)S(1)} %maximum_bitcast_fusion), channel_id=1, source_target_pairs={{0,1},{1,0},{2,3},{3,2},{4,5},{5,4},{6,7},{7,6},{8,9},{9,8},{10,11... | collective-permute-start | bytes 958472 | tf_op jit(solution)/shard_map/ppermute | solution.py:619
  12.6 9.1 %collective-permute-start.3 = (bf16[1,208,768]{2,1,0:T(8,128)(2,1)S(1)}, bf16[1,208,768]{2,1,0:T(8,128)(2,1)S(1)}, u32[]{:S(2)}, u32[]{:S(2)}) collective-permute-start(bf16[1,208,768]{2,1,0:T(8,128)(2,1)S(1)} %maximum_bitcast_fusion.1), channel_id=1, source_target_pairs={{0,16},{8,24},{16,0},{24,8},{1,17},{9,25},{17,1},{25,9},{2,18},{10... | collective-permute-start | bytes 958472 | tf_op jit(solution)/shard_map/ppermute | solution.py:619
  14.2 32.0 %copy-start.13 = (bf16[1536,192]{0,1:T(8,128)(2,1)S(1)}, bf16[1536,192]{0,1:T(8,128)(2,1)}, u32[]{:S(2)}) copy-start(bf16[1536,192]{0,1:T(8,128)(2,1)} %param.31) | copy-start | bytes 1769476
  14.2 33.5 %copy-start.14 = (bf16[192,1536]{1,0:T(8,128)(2,1)S(1)}, bf16[192,1536]{1,0:T(8,128)(2,1)}, u32[]{:S(2)}) copy-start(bf16[192,1536]{1,0:T(8,128)(2,1)} %param.29) | copy-start | bytes 1769476
  16.5 10.3 %collective-permute-start.1 = (bf16[256,768]{1,0:T(8,128)(2,1)S(1)}, bf16[256,768]{1,0:T(8,128)(2,1)S(1)}, u32[]{:S(2)}, u32[]{:S(2)}) collective-permute-start(bf16[256,768]{1,0:T(8,128)(2,1)S(1)} %bitcast.112), channel_id=1, source_target_pairs={{0,2},{2,0},{4,6},{6,4},{1,3},{3,1},{5,7},{7,5},{8,10},{10,8},{12,... | collective-permute-start | bytes 1179656 | tf_op jit(solution)/shard_map/ppermute | solution.py:597
  19.2 44.0 %copy-start.11 = (bf16[2,208,768]{2,1,0:T(8,128)(2,1)}, bf16[2,208,768]{2,1,0:T(8,128)(2,1)S(1)}, u32[]{:S(2)}) copy-start(bf16[2,208,768]{2,1,0:T(8,128)(2,1)S(1)} %pad_maximum_fusion.2.refs_4_) | copy-start | bytes 1916932
  21.8 44.1 %copy-start.12 = (bf16[2,208,768]{2,1,0:T(8,128)(2,1)}, bf16[2,208,768]{2,1,0:T(8,128)(2,1)S(1)}, u32[]{:S(2)}) copy-start(bf16[2,208,768]{2,1,0:T(8,128)(2,1)S(1)} %pad_maximum_fusion.3.refs_8_) | copy-start | bytes 1916932
  21.8 42.8 %copy-start.35 = (s32[16]{0:T(128)S(1)}, s32[16]{0:T(128)}, u32[]{:S(2)}) copy-start(s32[16]{0:T(128)} %param.19) | copy-start | bytes 196
  21.8 42.9 %copy-start.10 = (bf16[16,128,768]{2,1,0:T(8,128)(2,1)S(1)}, bf16[16,128,768]{2,1,0:T(8,128)(2,1)}, u32[]{:S(2)}) copy-start(bf16[16,128,768]{2,1,0:T(8,128)(2,1)} %param.35) | copy-start | bytes 9437188
  26.8 33.8 %copy-start.29 = (bf16[256,768]{1,0:T(8,128)(2,1)}, bf16[256,768]{1,0:T(8,128)(2,1)S(1)}, u32[]{:S(2)}) copy-start(bf16[256,768]{1,0:T(8,128)(2,1)S(1)} %collective-permute-done.1.refs_1_) | copy-start | bytes 1179652
  26.8 19.4 %collective-permute-start.2 = (bf16[2,208,768]{2,1,0:T(8,128)(2,1)S(1)}, bf16[2,208,768]{2,1,0:T(8,128)(2,1)S(1)}, u32[]{:S(2)}, u32[]{:S(2)}) collective-permute-start(bf16[2,208,768]{2,1,0:T(8,128)(2,1)S(1)} %pad_maximum_fusion.2.refs_4_), channel_id=1, source_target_pairs={{0,16},{8,24},{16,0},{24,8},{1,17},{9,25},{17,1},{25,9},{2,18},{10... | collective-permute-start | bytes 1916936 | tf_op jit(solution)/shard_map/ppermute | solution.py:619
  27.3 18.9 %collective-permute-start.4 = (bf16[2,208,768]{2,1,0:T(8,128)(2,1)S(1)}, bf16[2,208,768]{2,1,0:T(8,128)(2,1)S(1)}, u32[]{:S(2)}, u32[]{:S(2)}) collective-permute-start(bf16[2,208,768]{2,1,0:T(8,128)(2,1)S(1)} %pad_maximum_fusion.3.refs_8_), channel_id=1, source_target_pairs={{0,1},{1,0},{2,3},{3,2},{4,5},{5,4},{6,7},{7,6},{8,9},{9,8},{10,11... | collective-permute-start | bytes 1916936 | tf_op jit(solution)/shard_map/ppermute | solution.py:619
  27.7 18.5 %collective-permute-start.5 = (bf16[256,768]{1,0:T(8,128)(2,1)S(1)}, bf16[256,768]{1,0:T(8,128)(2,1)S(1)}, u32[]{:S(2)}, u32[]{:S(2)}) collective-permute-start(bf16[256,768]{1,0:T(8,128)(2,1)S(1)} %bitcast.110), channel_id=1, source_target_pairs={{0,4},{2,6},{4,0},{6,2},{1,5},{3,7},{5,1},{7,3},{8,12},{10,14},{12... | collective-permute-start | bytes 1179656 | tf_op jit(solution)/shard_map/ppermute | solution.py:597
  46.2 14.4 %collective-permute-start.7 = (bf16[1,192,1536]{2,1,0:T(8,128)(2,1)S(1)}, bf16[1,192,1536]{2,1,0:T(8,128)(2,1)S(1)}, u32[]{:S(2)}, u32[]{:S(2)}) collective-permute-start(bf16[1,192,1536]{2,1,0:T(8,128)(2,1)S(1)} %bitcast.100), channel_id=1, source_target_pairs={{0,16},{8,24},{16,0},{24,8},{1,17},{9,25},{17,1},{25,9},{2,18},{10... | collective-permute-start | bytes 1769480 | tf_op jit(solution)/shard_map/ppermute | solution.py:619
  47.7 14.0 %collective-permute-start.6 = (bf16[1,192,1536]{2,1,0:T(8,128)(2,1)S(1)}, bf16[1,192,1536]{2,1,0:T(8,128)(2,1)S(1)}, u32[]{:S(2)}, u32[]{:S(2)}) collective-permute-start(bf16[1,192,1536]{2,1,0:T(8,128)(2,1)S(1)} %bitcast.102), channel_id=1, source_target_pairs={{0,1},{1,0},{2,3},{3,2},{4,5},{5,4},{6,7},{7,6},{8,9},{9,8},{10,11... | collective-permute-start | bytes 1769480 | tf_op jit(solution)/shard_map/ppermute | solution.py:619
  49.2 12.3 %collective-permute-start.8 = (bf16[256,768]{1,0:T(8,128)(2,1)S(1)}, bf16[256,768]{1,0:T(8,128)(2,1)S(1)}, u32[]{:S(2)}, u32[]{:S(2)}) collective-permute-start(bf16[256,768]{1,0:T(8,128)(2,1)S(1)} %bitcast.108), channel_id=1, source_target_pairs={{0,6},{2,4},{4,2},{6,0},{1,7},{3,5},{5,3},{7,1},{8,14},{10,12},{12... | collective-permute-start | bytes 1179656 | tf_op jit(solution)/shard_map/ppermute | solution.py:597
  52.7 10.6 %collective-permute-start.11 = (bf16[2,208,768]{2,1,0:T(8,128)(2,1)S(1)}, bf16[2,208,768]{2,1,0:T(8,128)(2,1)S(1)}, u32[]{:S(2)}, u32[]{:S(2)}) collective-permute-start(bf16[2,208,768]{2,1,0:T(8,128)(2,1)S(1)} %pad_maximum_fusion.3.refs_8_), channel_id=1, source_target_pairs={{0,8},{8,0},{16,24},{24,16},{1,9},{9,1},{17,25},{25,17},{2,10},{10... | collective-permute-start | bytes 1916936 | tf_op jit(solution)/shard_map/ppermute | solution.py:619
  52.7 12.0 %collective-permute-start.9 = (bf16[2,208,768]{2,1,0:T(8,128)(2,1)S(1)}, bf16[2,208,768]{2,1,0:T(8,128)(2,1)S(1)}, u32[]{:S(2)}, u32[]{:S(2)}) collective-permute-start(bf16[2,208,768]{2,1,0:T(8,128)(2,1)S(1)} %pad_maximum_fusion.2.refs_4_), channel_id=1, source_target_pairs={{0,8},{8,0},{16,24},{24,16},{1,9},{9,1},{17,25},{25,17},{2,10},{10... | collective-permute-start | bytes 1916936 | tf_op jit(solution)/shard_map/ppermute | solution.py:619
  60.7 4.0 %collective-permute-start.10 = (bf16[2,208,768]{2,1,0:T(8,128)(2,1)S(1)}, bf16[2,208,768]{2,1,0:T(8,128)(2,1)S(1)}, u32[]{:S(2)}, u32[]{:S(2)}) collective-permute-start(bf16[2,208,768]{2,1,0:T(8,128)(2,1)S(1)} %collective-permute-done.2.refs_5_), channel_id=1, source_target_pairs={{0,8},{8,0},{16,24},{24,16},{1,9},{9,1},{17,25},{25,17},{2,10},{10... | collective-permute-start | bytes 1916936 | tf_op jit(solution)/shard_map/ppermute | solution.py:619
  60.8 45.0 %copy-start.8 = (bf16[2,192,1536]{2,1,0:T(8,128)(2,1)}, bf16[2,192,1536]{2,1,0:T(8,128)(2,1)S(1)}, u32[]{:S(2)}) copy-start(bf16[2,192,1536]{2,1,0:T(8,128)(2,1)S(1)} %pad_maximum_fusion.1.refs_16_) | copy-start | bytes 3538948
  61.5 3.2 collective-permute-start.12
  62.3 44.1 %collective-permute-start.19 = (bf16[2,192,1536]{2,1,0:T(8,128)(2,1)S(1)}, bf16[2,192,1536]{2,1,0:T(8,128)(2,1)}, u32[]{:S(2)}, u32[]{:S(2)}) collective-permute-start(bf16[2,192,1536]{2,1,0:T(8,128)(2,1)S(1)} %pad_maximum_fusion.1.refs_16_), channel_id=1, source_target_pairs={{0,1},{1,0},{2,3},{3,2},{4,5},{5,4},{6,7},{7,6},{8,9},{9,8},{10,11... | collective-permute-start | bytes 3538952 | tf_op jit(solution)/shard_map/ppermute | solution.py:619
  63.3 42.6 %copy-start.9 = (bf16[2,192,1536]{2,1,0:T(8,128)(2,1)}, bf16[2,192,1536]{2,1,0:T(8,128)(2,1)S(1)}, u32[]{:S(2)}) copy-start(bf16[2,192,1536]{2,1,0:T(8,128)(2,1)S(1)} %pad_maximum_fusion.refs_12_) | copy-start | bytes 3538948
  63.3 43.1 %collective-permute-start.16 = (bf16[2,192,1536]{2,1,0:T(8,128)(2,1)S(1)}, bf16[2,192,1536]{2,1,0:T(8,128)(2,1)}, u32[]{:S(2)}, u32[]{:S(2)}) collective-permute-start(bf16[2,192,1536]{2,1,0:T(8,128)(2,1)S(1)} %pad_maximum_fusion.refs_12_), channel_id=1, source_target_pairs={{0,16},{8,24},{16,0},{24,8},{1,17},{9,25},{17,1},{25,9},{2,18},{10... | collective-permute-start | bytes 3538952 | tf_op jit(solution)/shard_map/ppermute | solution.py:619
  65.9 39.1 %collective-permute-start.13 = (bf16[256,768]{1,0:T(8,128)(2,1)}, bf16[256,768]{1,0:T(8,128)(2,1)S(1)}, u32[]{:S(2)}, u32[]{:S(2)}) collective-permute-start(bf16[256,768]{1,0:T(8,128)(2,1)} %bitcast.14), channel_id=1, source_target_pairs={{0,2},{2,0},{4,6},{6,4},{1,3},{3,1},{5,7},{7,5},{8,10},{10,8},{12,... | collective-permute-start | bytes 1179656 | tf_op jit(solution)/shard_map/ppermute | solution.py:597
  72.1 32.9 %collective-permute-start.14 = (bf16[256,768]{1,0:T(8,128)(2,1)S(1)}, bf16[256,768]{1,0:T(8,128)(2,1)S(1)}, u32[]{:S(2)}, u32[]{:S(2)}) collective-permute-start(bf16[256,768]{1,0:T(8,128)(2,1)S(1)} %bitcast.111), channel_id=1, source_target_pairs={{0,4},{2,6},{4,0},{6,2},{1,5},{3,7},{5,1},{7,3},{8,12},{10,14},{12... | collective-permute-start | bytes 1179656 | tf_op jit(solution)/shard_map/ppermute | solution.py:597
  72.1 33.0 %collective-permute-start.15 = (bf16[256,768]{1,0:T(8,128)(2,1)S(1)}, bf16[256,768]{1,0:T(8,128)(2,1)}, u32[]{:S(2)}, u32[]{:S(2)}) collective-permute-start(bf16[256,768]{1,0:T(8,128)(2,1)S(1)} %bitcast.109), channel_id=1, source_target_pairs={{0,6},{2,4},{4,2},{6,0},{1,7},{3,5},{5,3},{7,1},{8,14},{10,12},{12... | collective-permute-start | bytes 1179656 | tf_op jit(solution)/shard_map/ppermute | solution.py:597
  105.8 2.8 collective-permute-start.20
  105.8 4.5 %collective-permute-start.17 = (bf16[2,192,1536]{2,1,0:T(8,128)(2,1)S(1)}, bf16[2,192,1536]{2,1,0:T(8,128)(2,1)S(1)}, u32[]{:S(2)}, u32[]{:S(2)}) collective-permute-start(bf16[2,192,1536]{2,1,0:T(8,128)(2,1)S(1)} %pad_maximum_fusion.refs_12_), channel_id=1, source_target_pairs={{0,8},{8,0},{16,24},{24,16},{1,9},{9,1},{17,25},{25,17},{2,10},{10... | collective-permute-start | bytes 3538952 | tf_op jit(solution)/shard_map/ppermute | solution.py:619
  106.3 5.7 %collective-permute-start.21 = (bf16[2,192,1536]{2,1,0:T(8,128)(2,1)}, bf16[2,192,1536]{2,1,0:T(8,128)(2,1)S(1)}, u32[]{:S(2)}, u32[]{:S(2)}) collective-permute-start(bf16[2,192,1536]{2,1,0:T(8,128)(2,1)} %collective-permute-done.19.refs_17_), channel_id=1, source_target_pairs={{0,8},{8,0},{16,24},{24,16},{1,9},{9,1},{17,25},{25,17},{2,10},{10... | collective-permute-start | bytes 3538952 | tf_op jit(solution)/shard_map/ppermute | solution.py:619
  106.4 7.3 %collective-permute-start.18 = (bf16[2,192,1536]{2,1,0:T(8,128)(2,1)}, bf16[2,192,1536]{2,1,0:T(8,128)(2,1)S(1)}, u32[]{:S(2)}, u32[]{:S(2)}) collective-permute-start(bf16[2,192,1536]{2,1,0:T(8,128)(2,1)} %collective-permute-done.16.refs_13_), channel_id=1, source_target_pairs={{0,8},{8,0},{16,24},{24,16},{1,9},{9,1},{17,25},{25,17},{2,10},{10... | collective-permute-start | bytes 3538952 | tf_op jit(solution)/shard_map/ppermute | solution.py:619
  160.6 16.8 %collective-permute-start.22 = (bf16[256,768]{1,0:T(8,128)(2,1)}, bf16[256,768]{1,0:T(8,128)(2,1)S(1)}, u32[]{:S(2)}, u32[]{:S(2)}) collective-permute-start(bf16[256,768]{1,0:T(8,128)(2,1)} %get-tuple-element.95), channel_id=1, source_target_pairs={{0,2},{2,0},{4,6},{6,4},{1,3},{3,1},{5,7},{7,5},{8,10},{10,8},{12,... | collective-permute-start | bytes 1179656 | tf_op jit(solution)/shard_map/ppermute | solution.py:597
  177.5 23.2 %collective-permute-start.25 = (bf16[2,2,208,1536]{3,2,1,0:T(8,128)(2,1)}, bf16[2,2,208,1536]{3,2,1,0:T(8,128)(2,1)}, u32[]{:S(2)}, u32[]{:S(2)}) collective-permute-start(bf16[2,2,208,1536]{3,2,1,0:T(8,128)(2,1)} %get-tuple-element.105), channel_id=1, source_target_pairs={{0,8},{8,0},{16,24},{24,16},{1,9},{9,1},{17,25},{25,17},{2,10},{10... | collective-permute-start | bytes 7667720 | tf_op jit(solution)/shard_map/ppermute | solution.py:681
  177.5 14.2 %collective-permute-start.23 = (bf16[256,768]{1,0:T(8,128)(2,1)}, bf16[256,768]{1,0:T(8,128)(2,1)S(1)}, u32[]{:S(2)}, u32[]{:S(2)}) collective-permute-start(bf16[256,768]{1,0:T(8,128)(2,1)} %get-tuple-element.96), channel_id=1, source_target_pairs={{0,6},{2,4},{4,2},{6,0},{1,7},{3,5},{5,3},{7,1},{8,14},{10,12},{12... | collective-permute-start | bytes 1179656 | tf_op jit(solution)/shard_map/ppermute | solution.py:597
  178.8 21.9 %copy-start.7 = (bf16[2,2,208,1536]{3,2,1,0:T(8,128)(2,1)S(1)}, bf16[2,2,208,1536]{3,2,1,0:T(8,128)(2,1)}, u32[]{:S(2)}) copy-start(bf16[2,2,208,1536]{3,2,1,0:T(8,128)(2,1)} %get-tuple-element.103) | copy-start | bytes 7667716
  191.7 42.0 %collective-permute-start.26 = (bf16[2,2,208,1536]{3,2,1,0:T(8,128)(2,1)}, bf16[2,2,208,1536]{3,2,1,0:T(8,128)(2,1)}, u32[]{:S(2)}, u32[]{:S(2)}) collective-permute-start(bf16[2,2,208,1536]{3,2,1,0:T(8,128)(2,1)} %get-tuple-element.111), channel_id=1, source_target_pairs={{0,8},{8,0},{16,24},{24,16},{1,9},{9,1},{17,25},{25,17},{2,10},{10... | collective-permute-start | bytes 7667720 | tf_op jit(solution)/shard_map/ppermute | solution.py:681
  191.9 41.3 %collective-permute-start.28 = (bf16[256,768]{1,0:T(8,128)(2,1)S(1)}, bf16[256,768]{1,0:T(8,128)(2,1)}, u32[]{:S(2)}, u32[]{:S(2)}) collective-permute-start(bf16[256,768]{1,0:T(8,128)(2,1)S(1)} %copy-done.32), channel_id=1, source_target_pairs={{0,4},{2,6},{4,0},{6,2},{1,5},{3,7},{5,1},{7,3},{8,12},{10,14},{12... | collective-permute-start | bytes 1179656 | tf_op jit(solution)/shard_map/ppermute | solution.py:597
  199.8 42.4 %collective-permute-start.24 = (bf16[768,768]{1,0:T(8,128)(2,1)}, bf16[768,768]{1,0:T(8,128)(2,1)}, u32[]{:S(2)}, u32[]{:S(2)}) collective-permute-start(bf16[768,768]{1,0:T(8,128)(2,1)} %constant_dynamic-update-slice_fusion), channel_id=1, source_target_pairs={{0,1},{1,0},{2,3},{3,2},{4,5},{5,4},{6,7},{7,6},{8,9},{9,8},{10,11... | collective-permute-start | bytes 3538952 | tf_op jit(solution)/shard_map/ppermute | solution.py:601
  205.7 33.8 %collective-permute-start.27 = (bf16[1,2,208,1536]{3,2,1,0:T(8,128)(2,1)}, bf16[1,2,208,1536]{3,2,1,0:T(8,128)(2,1)}, u32[]{:S(2)}, u32[]{:S(2)}) collective-permute-start(bf16[1,2,208,1536]{3,2,1,0:T(8,128)(2,1)} %split.49), channel_id=1, source_target_pairs={{0,16},{8,24},{16,0},{24,8},{1,17},{9,25},{17,1},{25,9},{2,18},{10... | collective-permute-start | bytes 3833864 | tf_op jit(solution)/shard_map/ppermute | solution.py:619
  233.2 35.7 %collective-permute-start.33 = (bf16[256,768]{1,0:T(8,128)(2,1)}, bf16[256,768]{1,0:T(8,128)(2,1)}, u32[]{:S(2)}, u32[]{:S(2)}) collective-permute-start(bf16[256,768]{1,0:T(8,128)(2,1)} %collective-permute-done.28), channel_id=1, source_target_pairs={{0,1},{1,0},{2,3},{3,2},{4,5},{5,4},{6,7},{7,6},{8,9},{9,8},{10,11... | collective-permute-start | bytes 1179656 | tf_op jit(solution)/shard_map/ppermute | solution.py:601
  238.1 30.7 %collective-permute-start.30 = (bf16[1,2,208,1536]{3,2,1,0:T(8,128)(2,1)}, bf16[1,2,208,1536]{3,2,1,0:T(8,128)(2,1)}, u32[]{:S(2)}, u32[]{:S(2)}) collective-permute-start(bf16[1,2,208,1536]{3,2,1,0:T(8,128)(2,1)} %split.51), channel_id=1, source_target_pairs={{0,16},{8,24},{16,0},{24,8},{1,17},{9,25},{17,1},{25,9},{2,18},{10... | collective-permute-start | bytes 3833864 | tf_op jit(solution)/shard_map/ppermute | solution.py:619
  242.2 29.8 %collective-permute-start.29 = (bf16[1,1,208,1536]{3,2,1,0:T(8,128)(2,1)S(1)}, bf16[1,1,208,1536]{3,2,1,0:T(8,128)(2,1)}, u32[]{:S(2)}, u32[]{:S(2)}) collective-permute-start(bf16[1,1,208,1536]{3,2,1,0:T(8,128)(2,1)S(1)} %split.50), channel_id=1, source_target_pairs={{0,1},{1,0},{2,3},{3,2},{4,5},{5,4},{6,7},{7,6},{8,9},{9,8},{10,11... | collective-permute-start | bytes 1916936 | tf_op jit(solution)/shard_map/ppermute | solution.py:619
  252.0 16.9 %collective-permute-start.31 = (bf16[256,768]{1,0:T(8,128)(2,1)}, bf16[256,768]{1,0:T(8,128)(2,1)S(1)}, u32[]{:S(2)}, u32[]{:S(2)}) collective-permute-start(bf16[256,768]{1,0:T(8,128)(2,1)} %get-tuple-element.120), channel_id=1, source_target_pairs={{0,2},{2,0},{4,6},{6,4},{1,3},{3,1},{5,7},{7,5},{8,10},{10,8},{12,... | collective-permute-start | bytes 1179656 | tf_op jit(solution)/shard_map/ppermute | solution.py:597
  252.4 19.6 %collective-permute-start.32 = (bf16[256,768]{1,0:T(8,128)(2,1)}, bf16[256,768]{1,0:T(8,128)(2,1)}, u32[]{:S(2)}, u32[]{:S(2)}) collective-permute-start(bf16[256,768]{1,0:T(8,128)(2,1)} %get-tuple-element.122), channel_id=1, source_target_pairs={{0,6},{2,4},{4,2},{6,0},{1,7},{3,5},{5,3},{7,1},{8,14},{10,12},{12... | collective-permute-start | bytes 1179656 | tf_op jit(solution)/shard_map/ppermute | solution.py:597
  271.9 5.2 %collective-permute-start.34 = (bf16[2,2,208,1536]{3,2,1,0:T(8,128)(2,1)}, bf16[2,2,208,1536]{3,2,1,0:T(8,128)(2,1)}, u32[]{:S(2)}, u32[]{:S(2)}) collective-permute-start(bf16[2,2,208,1536]{3,2,1,0:T(8,128)(2,1)} %get-tuple-element.127), channel_id=1, source_target_pairs={{0,8},{8,0},{16,24},{24,16},{1,9},{9,1},{17,25},{25,17},{2,10},{10... | collective-permute-start | bytes 7667720 | tf_op jit(solution)/shard_map/ppermute | solution.py:681
  273.8 49.2 %collective-permute-start.42 = (bf16[256,768]{1,0:T(8,128)(2,1)}, bf16[256,768]{1,0:T(8,128)(2,1)S(1)}, u32[]{:S(2)}, u32[]{:S(2)}) collective-permute-start(bf16[256,768]{1,0:T(8,128)(2,1)} %get-tuple-element.140), channel_id=1, source_target_pairs={{0,4},{2,6},{4,0},{6,2},{1,5},{3,7},{5,1},{7,3},{8,12},{10,14},{12... | collective-permute-start | bytes 1179656 | tf_op jit(solution)/shard_map/ppermute | solution.py:597
  279.7 16.5 %collective-permute-start.38 = (bf16[1,1,208,1536]{3,2,1,0:T(8,128)(2,1)S(1)}, bf16[1,1,208,1536]{3,2,1,0:T(8,128)(2,1)S(1)}, u32[]{:S(2)}, u32[]{:S(2)}) collective-permute-start(bf16[1,1,208,1536]{3,2,1,0:T(8,128)(2,1)S(1)} %split.47), channel_id=1, source_target_pairs={{0,1},{1,0},{2,3},{3,2},{4,5},{5,4},{6,7},{7,6},{8,9},{9,8},{10,11... | collective-permute-start | bytes 1916936 | tf_op jit(solution)/shard_map/ppermute | solution.py:619
  280.3 42.4 %collective-permute-start.36 = (bf16[1,2,208,1536]{3,2,1,0:T(8,128)(2,1)S(1)}, bf16[1,2,208,1536]{3,2,1,0:T(8,128)(2,1)S(1)}, u32[]{:S(2)}, u32[]{:S(2)}) collective-permute-start(bf16[1,2,208,1536]{3,2,1,0:T(8,128)(2,1)S(1)} %split.53), channel_id=1, source_target_pairs={{0,16},{8,24},{16,0},{24,8},{1,17},{9,25},{17,1},{25,9},{2,18},{10... | collective-permute-start | bytes 3833864 | tf_op jit(solution)/shard_map/ppermute | solution.py:619
  296.5 14.6 %collective-permute-start.39 = (bf16[416,384]{1,0:T(8,128)(2,1)S(1)}, bf16[416,384]{1,0:T(8,128)(2,1)S(1)}, u32[]{:S(2)}, u32[]{:S(2)}) collective-permute-start(bf16[416,384]{1,0:T(8,128)(2,1)S(1)} %pad_maximum_fusion.4), channel_id=1, source_target_pairs={{0,2},{2,0},{4,6},{6,4},{1,3},{3,1},{5,7},{7,5},{8,10},{10,8},{12,... | collective-permute-start | bytes 958472 | tf_op jit(solution)/shard_map/ppermute | solution.py:597
  297.4 25.1 %collective-permute-start.40 = (bf16[416,384]{1,0:T(8,128)(2,1)S(1)}, bf16[416,384]{1,0:T(8,128)(2,1)S(1)}, u32[]{:S(2)}, u32[]{:S(2)}) collective-permute-start(bf16[416,384]{1,0:T(8,128)(2,1)S(1)} %pad_maximum_fusion.5), channel_id=1, source_target_pairs={{0,4},{2,6},{4,0},{6,2},{1,5},{3,7},{5,1},{7,3},{8,12},{10,14},{12... | collective-permute-start | bytes 958472 | tf_op jit(solution)/shard_map/ppermute | solution.py:597
  299.5 23.0 %collective-permute-start.41 = (bf16[416,384]{1,0:T(8,128)(2,1)S(1)}, bf16[416,384]{1,0:T(8,128)(2,1)S(1)}, u32[]{:S(2)}, u32[]{:S(2)}) collective-permute-start(bf16[416,384]{1,0:T(8,128)(2,1)S(1)} %pad_maximum_fusion.6), channel_id=1, source_target_pairs={{0,6},{2,4},{4,2},{6,0},{1,7},{3,5},{5,3},{7,1},{8,14},{10,12},{12... | collective-permute-start | bytes 958472 | tf_op jit(solution)/shard_map/ppermute | solution.py:597
  311.1 53.9 %collective-permute-start.35 = (bf16[768,768]{1,0:T(8,128)(2,1)S(1)}, bf16[768,768]{1,0:T(8,128)(2,1)S(1)}, u32[]{:S(2)}, u32[]{:S(2)}) collective-permute-start(bf16[768,768]{1,0:T(8,128)(2,1)S(1)} %constant_dynamic-update-slice_fusion.3), channel_id=1, source_target_pairs={{0,1},{1,0},{2,3},{3,2},{4,5},{5,4},{6,7},{7,6},{8,9},{9,8},{10,11... | collective-permute-start | bytes 3538952 | tf_op jit(solution)/shard_map/ppermute | solution.py:601
  323.0 16.8 %collective-permute-start.50 = (bf16[416,384]{1,0:T(8,128)(2,1)S(1)}, bf16[416,384]{1,0:T(8,128)(2,1)S(1)}, u32[]{:S(2)}, u32[]{:S(2)}) collective-permute-start(bf16[416,384]{1,0:T(8,128)(2,1)S(1)} %add_convert_fusion.9), channel_id=1, source_target_pairs={{0,2},{2,0},{4,6},{6,4},{1,3},{3,1},{5,7},{7,5},{8,10},{10,8},{12,... | collective-permute-start | bytes 958472 | tf_op jit(solution)/shard_map/ppermute | solution.py:597
  328.7 25.4 %copy-start.5 = (bf16[16,128,768]{2,1,0:T(8,128)(2,1)}, bf16[16,128,768]{2,1,0:T(8,128)(2,1)S(1)}, u32[]{:S(2)}) copy-start(bf16[16,128,768]{2,1,0:T(8,128)(2,1)S(1)} %constant_dynamic-update-slice_fusion.10) | copy-start | bytes 9437188
  328.7 25.1 %collective-permute-start.51 = (bf16[416,384]{1,0:T(8,128)(2,1)S(1)}, bf16[416,384]{1,0:T(8,128)(2,1)S(1)}, u32[]{:S(2)}, u32[]{:S(2)}) collective-permute-start(bf16[416,384]{1,0:T(8,128)(2,1)S(1)} %add_convert_fusion.9), channel_id=1, source_target_pairs={{0,4},{2,6},{4,0},{6,2},{1,5},{3,7},{5,1},{7,3},{8,12},{10,14},{12... | collective-permute-start | bytes 958472 | tf_op jit(solution)/shard_map/ppermute | solution.py:597
  329.8 24.1 %collective-permute-start.52 = (bf16[416,384]{1,0:T(8,128)(2,1)S(1)}, bf16[416,384]{1,0:T(8,128)(2,1)S(1)}, u32[]{:S(2)}, u32[]{:S(2)}) collective-permute-start(bf16[416,384]{1,0:T(8,128)(2,1)S(1)} %add_convert_fusion.9), channel_id=1, source_target_pairs={{0,6},{2,4},{4,2},{6,0},{1,7},{3,5},{5,3},{7,1},{8,14},{10,12},{12... | collective-permute-start | bytes 958472 | tf_op jit(solution)/shard_map/ppermute | solution.py:597
  331.4 26.4 %collective-permute-start.37 = (bf16[1,1,208,1536]{3,2,1,0:T(8,128)(2,1)S(1)}, bf16[1,1,208,1536]{3,2,1,0:T(8,128)(2,1)S(1)}, u32[]{:S(2)}, u32[]{:S(2)}) collective-permute-start(bf16[1,1,208,1536]{3,2,1,0:T(8,128)(2,1)S(1)} %split.55), channel_id=1, source_target_pairs={{0,1},{1,0},{2,3},{3,2},{4,5},{5,4},{6,7},{7,6},{8,9},{9,8},{10,11... | collective-permute-start | bytes 1916936 | tf_op jit(solution)/shard_map/ppermute | solution.py:619
  358.0 8.7 %collective-permute-start.44 = (bf16[208,384]{1,0:T(8,128)(2,1)S(1)}, bf16[208,384]{1,0:T(8,128)(2,1)S(1)}, u32[]{:S(2)}, u32[]{:S(2)}) collective-permute-start(bf16[208,384]{1,0:T(8,128)(2,1)S(1)} %get-tuple-element.170), channel_id=1, source_target_pairs={{0,2},{2,0},{4,6},{6,4},{1,3},{3,1},{5,7},{7,5},{8,10},{10,8},{12,... | collective-permute-start | bytes 479240 | tf_op jit(solution)/shard_map/ppermute | solution.py:597
  362.5 12.4 %collective-permute-start.45 = (bf16[208,384]{1,0:T(8,128)(2,1)S(1)}, bf16[208,384]{1,0:T(8,128)(2,1)S(1)}, u32[]{:S(2)}, u32[]{:S(2)}) collective-permute-start(bf16[208,384]{1,0:T(8,128)(2,1)S(1)} %get-tuple-element.172), channel_id=1, source_target_pairs={{0,4},{2,6},{4,0},{6,2},{1,5},{3,7},{5,1},{7,3},{8,12},{10,14},{12... | collective-permute-start | bytes 479240 | tf_op jit(solution)/shard_map/ppermute | solution.py:597
  363.5 11.4 %collective-permute-start.46 = (bf16[208,384]{1,0:T(8,128)(2,1)S(1)}, bf16[208,384]{1,0:T(8,128)(2,1)S(1)}, u32[]{:S(2)}, u32[]{:S(2)}) collective-permute-start(bf16[208,384]{1,0:T(8,128)(2,1)S(1)} %get-tuple-element.171), channel_id=1, source_target_pairs={{0,6},{2,4},{4,2},{6,0},{1,7},{3,5},{5,3},{7,1},{8,14},{10,12},{12... | collective-permute-start | bytes 479240 | tf_op jit(solution)/shard_map/ppermute | solution.py:597
  365.1 29.3 %collective-permute-start.43 = (bf16[256,768]{1,0:T(8,128)(2,1)S(1)}, bf16[256,768]{1,0:T(8,128)(2,1)S(1)}, u32[]{:S(2)}, u32[]{:S(2)}) collective-permute-start(bf16[256,768]{1,0:T(8,128)(2,1)S(1)} %collective-permute-done.42), channel_id=1, source_target_pairs={{0,1},{1,0},{2,3},{3,2},{4,5},{5,4},{6,7},{7,6},{8,9},{9,8},{10,11... | collective-permute-start | bytes 1179656 | tf_op jit(solution)/shard_map/ppermute | solution.py:601
  375.0 7.1 %collective-permute-start.47 = (bf16[208,384]{1,0:T(8,128)(2,1)S(1)}, bf16[208,384]{1,0:T(8,128)(2,1)S(1)}, u32[]{:S(2)}, u32[]{:S(2)}) collective-permute-start(bf16[208,384]{1,0:T(8,128)(2,1)S(1)} %get-tuple-element.146), channel_id=1, source_target_pairs={{0,2},{2,0},{4,6},{6,4},{1,3},{3,1},{5,7},{7,5},{8,10},{10,8},{12,... | collective-permute-start | bytes 479240 | tf_op jit(solution)/shard_map/ppermute | solution.py:597
  377.3 13.7 %collective-permute-start.48 = (bf16[208,384]{1,0:T(8,128)(2,1)S(1)}, bf16[208,384]{1,0:T(8,128)(2,1)S(1)}, u32[]{:S(2)}, u32[]{:S(2)}) collective-permute-start(bf16[208,384]{1,0:T(8,128)(2,1)S(1)} %get-tuple-element.146), channel_id=1, source_target_pairs={{0,4},{2,6},{4,0},{6,2},{1,5},{3,7},{5,1},{7,3},{8,12},{10,14},{12... | collective-permute-start | bytes 479240 | tf_op jit(solution)/shard_map/ppermute | solution.py:597
  378.4 12.6 %collective-permute-start.49 = (bf16[208,384]{1,0:T(8,128)(2,1)S(1)}, bf16[208,384]{1,0:T(8,128)(2,1)S(1)}, u32[]{:S(2)}, u32[]{:S(2)}) collective-permute-start(bf16[208,384]{1,0:T(8,128)(2,1)S(1)} %get-tuple-element.146), channel_id=1, source_target_pairs={{0,6},{2,4},{4,2},{6,0},{1,7},{3,5},{5,3},{7,1},{8,14},{10,12},{12... | collective-permute-start | bytes 479240 | tf_op jit(solution)/shard_map/ppermute | solution.py:597
  (25 other events, 184.2 us)
